TPU v7x, 32 devices: a whole 2x2x4 slice. The times are simulated.
32 devices in a mesh: cfg: 2 (over y), win: 16 (over z, x, core).
Axes of the slice: x: 2, y: 2, z: 4, core: 2. Of those that a mesh axis runs over, the one named last changes fastest.
Arguments:
- latent: float32 [512, 4, 32], P('win'), may hold values from -6 to 6
- text_kv: bfloat16 [2, 2, 120, 576], P(None, None, None, 'cfg'), may hold values from -200 to 200, as said below
- modulation: float32 [20, 4, 1152], replicated, may hold values from -3 to 3
- qkv_weight: bfloat16 [1152, 3, 576], P(None, None, 'cfg'), may hold values from -0.1875 to 0.1875
- out_weight: bfloat16 [576, 1152], P('cfg'), may hold values from -0.25 to 0.25
- patch_weight: bfloat16 [16, 1152], replicated, may hold values from -1.5 to 1.5
- final_weight: bfloat16 [1152, 16], replicated, may hold values from -0.1875 to 0.1875
- offsets: int32 [16], P('win'), may hold values from 1 to 16
- blend_weights: int32 [16], P('win'), may hold values from 1 to 4
- step_index: int32 [1], replicated, may hold values from 0 to 999
Outputs:
- previous: float32 [512, 4, 32], P('win', None, 'cfg')
- noise: float32 [512, 4, 32], P('win', None, 'cfg')
Inputs may be any that keep to these rules, and one draw needn't show every extreme that they name: Window i starts offsets[i] columns before column i * 32. `text_kv`: keys and values of caption tokens.
All inputs are finite; a program needn't handle non-finite values.
Results may differ from a plain program's by a relative error of at most 0.024.
Values may be sent and summed in bfloat16 or wider, within the bound.
No kernel may reach another device: no remote copies, remote signals or barrier semaphores. Data moves between devices by JAX's collectives and lax.ppermute only.
A program may use at most 64 MiB of HBM per device.

v0:
```python
import math

import jax
import jax.numpy as jnp
from jax import lax
from jax.sharding import PartitionSpec as P

HEAD_DIM = 72
STEPS = 20


guidance_scale = 4.5
plan_length = 1000
norm_eps = 1e-06


def with_halo(array, sides, width):
    for axis, dim in sides:
        size, length = (lax.axis_size(axis), array.shape[dim])
        up = [(i, (i + 1) % size) for i in range(size)]
        down = [(j, i) for i, j in up]
        last = lax.slice_in_dim(array, length - width, length, axis=dim)
        first = lax.slice_in_dim(array, 0, width, axis=dim)
        before = lax.ppermute(last, axis, up)
        after = lax.ppermute(first, axis, down)
        array = jnp.concatenate([before, array, after], axis=dim)
    return array


def from_partner(value, axis, stride):
    mask = 2**stride
    pairs = [(source, source ^ mask) for source in range(lax.axis_size(axis))]
    return lax.ppermute(value, axis, pairs)


def from_behind(array, axis, by):
    size = lax.axis_size(axis)
    return lax.ppermute(array, axis, [(i, (i + by) % size) for i in range(size)])


def layer_norm(values):
    average = jnp.mean(values, axis=-1, keepdims=True)
    centered = values - average
    variance = jnp.mean(centered * centered, axis=-1, keepdims=True)
    return centered * lax.rsqrt(variance + norm_eps)


def positions(col_pairs, row_couples, model_width):
    quarter = model_width // 4
    frequency = jnp.exp(-math.log(10000.0) * jnp.arange(quarter, dtype=jnp.float32) / quarter)
    col_pos = jnp.arange(col_pairs, dtype=jnp.float32)[:, None] * frequency[None, :]
    row_pos = jnp.arange(row_couples, dtype=jnp.float32)[:, None] * frequency[None, :]
    col_part = jnp.concatenate([jnp.sin(col_pos), jnp.cos(col_pos)], axis=1)
    row_part = jnp.concatenate([jnp.sin(row_pos), jnp.cos(row_pos)], axis=1)
    half_width = model_width // 2
    pos_table = jnp.concatenate(
        [
            jnp.broadcast_to(row_part[None, :, :], (col_pairs, row_couples, half_width)),
            jnp.broadcast_to(col_part[:, None, :], (col_pairs, row_couples, half_width)),
        ],
        axis=2,
    )
    return pos_table.reshape(col_pairs * row_couples, model_width)


def plan(moment):
    train_grid = jnp.arange(plan_length, dtype=jnp.int32)
    beta_values = 0.0001 + (0.02 - 0.0001) * train_grid.astype(jnp.float32) / (plan_length - 1)
    alpha_bar = jnp.exp(jnp.cumsum(jnp.log(1.0 - beta_values)))
    stride = plan_length // STEPS
    earlier = moment - stride
    alpha_now = jnp.sum(jnp.where(train_grid == moment, alpha_bar, 0.0))
    alpha_before = jnp.sum(jnp.where(train_grid == earlier, alpha_bar, 0.0)) + jnp.where(
        earlier < 0, 1.0, 0.0
    )
    return (alpha_now, alpha_before)


def attend_branches(projected, text_pair, attn_width):
    token_count = projected.shape[0]
    head_count = attn_width // HEAD_DIM
    branches = text_pair.shape[0]
    queries = (
        projected[:, :attn_width].reshape(token_count, head_count, HEAD_DIM).transpose(1, 0, 2)
    )
    keys_own = (
        projected[:, attn_width : 2 * attn_width]
        .reshape(token_count, head_count, HEAD_DIM)
        .transpose(1, 0, 2)
    )
    values_own = (
        projected[:, 2 * attn_width :].reshape(token_count, head_count, HEAD_DIM).transpose(1, 0, 2)
    )
    text_keys = text_pair[:, 0].reshape(branches, -1, head_count, HEAD_DIM).transpose(2, 0, 1, 3)
    text_values = text_pair[:, 1].reshape(branches, -1, head_count, HEAD_DIM).transpose(2, 0, 1, 3)
    factor = 1.0 / math.sqrt(HEAD_DIM)

    def one_head(head_parts):
        query_tile, key_block, value_tile, caption_key_tile, caption_value_tile = head_parts
        own_scores = (
            jnp.einsum("qd,kd->qk", query_tile, key_block, preferred_element_type=jnp.float32)
            * factor
        )
        text_scores = (
            jnp.einsum(
                "cr,eor->eco", query_tile, caption_key_tile, preferred_element_type=jnp.float32
            )
            * factor
        )
        highest = jnp.maximum(jnp.max(own_scores, axis=-1)[None, :], jnp.max(text_scores, axis=-1))
        own_exp = jnp.exp(own_scores[None, :, :] - highest[:, :, None])
        text_exp = jnp.exp(text_scores - highest[:, :, None])
        totals = jnp.sum(own_exp, axis=-1) + jnp.sum(text_exp, axis=-1)
        self_softmax_weights = (own_exp / totals[:, :, None]).astype(jnp.bfloat16)
        caption_softmax_weights = (text_exp / totals[:, :, None]).astype(jnp.bfloat16)
        return jnp.einsum(
            "roz,zt->rot", self_softmax_weights, value_tile, preferred_element_type=jnp.float32
        ) + jnp.einsum(
            "mzc,mce->mze",
            caption_softmax_weights,
            caption_value_tile,
            preferred_element_type=jnp.float32,
        )

    attended = lax.map(one_head, (queries, keys_own, values_own, text_keys, text_values))
    return (
        attended.transpose(1, 2, 0, 3)
        .reshape(branches, token_count, attn_width)
        .astype(jnp.bfloat16)
    )


def on_device(
    latent,
    text_kv,
    modulation,
    qkv_weight,
    out_weight,
    patch_weight,
    final_weight,
    offsets,
    blend_weights,
    step_index,
):
    slab_cols = latent.shape[0]
    model_width = patch_weight.shape[1]
    half_attn = out_weight.shape[0]
    branch = lax.axis_index("cfg")
    extended = with_halo(latent, (("win", 0),), slab_cols)
    start_at = slab_cols - offsets[0]
    window = lax.dynamic_slice_in_dim(extended, start_at, 2 * slab_cols, 0)
    moment = step_index[0]
    selected = jnp.arange(STEPS, dtype=jnp.int32) == moment * STEPS // plan_length
    modulate = jnp.sum(jnp.where(selected[:, None, None], modulation, 0.0), axis=0)
    col_count, channels, row_count = window.shape
    col_pairs = col_count // 2
    row_couples = row_count // 2
    patches = window.reshape(col_pairs, 2, channels, row_couples, 2).transpose(0, 3, 1, 2, 4)
    patches = patches.reshape(col_pairs * row_couples, 4 * channels).astype(jnp.bfloat16)
    embedded = jnp.dot(patches, patch_weight, preferred_element_type=jnp.float32) + positions(
        col_pairs, row_couples, model_width
    )
    normed = (layer_norm(embedded) * (1.0 + modulate[1]) + modulate[0]).astype(jnp.bfloat16)
    w_qkv = qkv_weight.reshape(model_width, 3 * half_attn)
    projected = jnp.dot(normed, w_qkv, preferred_element_type=jnp.float32).astype(jnp.bfloat16)
    attended = attend_branches(projected, text_kv, half_attn)
    mixed_sum = lax.psum_scatter(
        jnp.einsum("btk,kd->btd", attended, out_weight, preferred_element_type=jnp.float32).astype(
            jnp.bfloat16
        ),
        "cfg",
        scatter_dimension=0,
        tiled=True,
    ).astype(jnp.float32)[0]
    residual = embedded + modulate[2] * mixed_sum
    final_norm = (layer_norm(residual) * (1.0 + modulate[3])).astype(jnp.bfloat16)
    noise_tokens = jnp.dot(final_norm, final_weight, preferred_element_type=jnp.float32)
    unpacked = noise_tokens.reshape(col_pairs, row_couples, 2, channels, 2).transpose(0, 2, 3, 1, 4)
    predicted = unpacked.reshape(col_count, channels, row_count)
    half_rows = row_count // 2
    own_first = branch * half_rows
    other_first = (1 - branch) * half_rows
    kept = lax.dynamic_slice_in_dim(predicted, own_first, half_rows, 2)
    handed = lax.dynamic_slice_in_dim(predicted, other_first, half_rows, 2)
    partner = from_partner(handed, "cfg", 0)
    conditional = jnp.where(branch == 0, kept, partner)
    unconditional = jnp.where(branch == 0, partner, kept)
    guided = unconditional + guidance_scale * (conditional - unconditional)
    weight_value = blend_weights[0].astype(jnp.float32)
    zero_index = jnp.zeros((), jnp.int32)
    extent = extended.shape[0]
    spread = lax.dynamic_update_slice(
        jnp.zeros((extent,) + guided.shape[1:], jnp.float32),
        weight_value * guided,
        (start_at, zero_index, zero_index),
    )
    coverage = lax.dynamic_update_slice(
        jnp.zeros((extent,), jnp.float32),
        jnp.full((2 * slab_cols,), weight_value, jnp.float32),
        (start_at,),
    )
    from_left = from_behind(
        (spread[slab_cols + slab_cols :], coverage[slab_cols + slab_cols :]), "win", 1
    )
    from_right = from_behind((spread[:slab_cols], coverage[:slab_cols]), "win", -1)
    numerator = spread[slab_cols : slab_cols + slab_cols] + from_left[0]
    numerator = numerator.at[slab_cols - slab_cols :].add(from_right[0])
    denominator = coverage[slab_cols : slab_cols + slab_cols] + from_left[1]
    denominator = denominator.at[slab_cols - slab_cols :].add(from_right[1])
    blended = numerator / denominator[:, None, None]
    latent_rows = lax.dynamic_slice_in_dim(latent, own_first, half_rows, 2)
    alpha_now, alpha_before = plan(moment)
    previous = (
        jnp.sqrt(alpha_before)
        * (latent_rows - jnp.sqrt(1.0 - alpha_now) * blended)
        / jnp.sqrt(alpha_now)
        + jnp.sqrt(1.0 - alpha_before) * blended
    )
    return (previous, blended)


def solution(mesh):
    in_specs = (
        P("win", None, None),
        P(None, None, None, "cfg"),
        P(),
        P(None, None, "cfg"),
        P("cfg", None),
        P(),
        P(),
        P("win"),
        P("win"),
        P(),
    )
    out_specs = (P("win", None, "cfg"), P("win", None, "cfg"))
    return jax.shard_map(
        on_device, mesh=mesh, in_specs=in_specs, out_specs=out_specs, check_vma=False
    )
```

profile of v0, /device:TPU:0, one launch (start us, length us, event | category | flops | bytes accessed | tf_op | source)
XLA Modules:
  0.0 131.5 jit_solution(4297236387091419841)
XLA Ops:
  7.2 1.0 copy.48
  8.8 5.0 %collective-permute-start.1 = (bf16[32,4,32]{0,2,1:T(8,128)(2,1)S(1)}, bf16[32,4,32]{0,2,1:T(8,128)(2,1)S(1)}, u32[]{:S(2)}, u32[]{:S(2)}) collective-permute-start(bf16[32,4,32]{0,2,1:T(8,128)(2,1)S(1)} %convert.17), channel_id=1, source_target_pairs={{1,0},{2,1},{3,2},{4,3},{5,4},{6,5},{7,6},{8,7},{9,8},{10,9},{11,1... | collective-permute-start | bytes 24584 | tf_op jit(solution)/shard_map/ppermute | solution.py:25
  14.9 1.7 %fusion.46 = (bf16[2,1,120,288]{2,3,1,0:T(8,128)(2,1)}, bf16[2,1,120,288]{2,3,1,0:T(8,128)(2,1)}) fusion(bf16[2,2,120,288]{2,3,1,0:T(8,128)(2,1)} %param.21), kind=kLoop, calls=%fused_computation.94 | loop fusion | bytes 552960 | tf_op jit(solution)/shard_map/slice | solution.py:95
  17.0 1.8 %pad_maximum_fusion = f32[32,16,1152]{2,1,0:T(8,128)} fusion(f32[32,16,576]{2,1,0:T(8,128)S(1)} %broadcast_in_dim.41, f32[32,16,576]{2,1,0:T(8,128)S(1)} %broadcast_in_dim.33), kind=kLoop, calls=%fused_computation.34 | loop fusion | flops 589824 | bytes 4718592 | tf_op jit(solution)/shard_map/concatenate | solution.py:56
  19.8 0.9 copy.52
  20.8 1.2 copy.53
  22.1 2.2 %fusion.50 = (f32[512]{0:T(512)S(1)}, f32[512,1152]{1,0:T(8,128)S(1)}) fusion(f32[512,1152]{1,0:T(8,128)} %bitcast.113, bf16[512,16]{0,1:T(8,128)(2,1)S(1)} %convert_element_type.55, bf16[16,1152]{1,0:T(8,128)(2,1)S(1)} %copy-done.7), kind=kOutput, calls=%fused_computation.98 | convolution fusion | flops 20053504 | bytes 4773888 | tf_op jit(solution)/shard_map/dot_general | solution.py:160
  24.8 1.5 %convolution_convert_fusion.1 = bf16[512,864]{0,1:T(8,128)(2,1)S(1)} fusion(bf16[1152,864]{0,1:T(8,128)(2,1)S(1)} %bitcast.112, f32[512,1152]{1,0:T(8,128)S(1)} %get-tuple-element.145, f32[1152]{0:T(1024)S(1)} %get-tuple-element.103, f32[1152]{0:T(1024)S(1)} %get-tuple-element.104, f32[512]{0:T(512)S(1)} %add_rsqrt_fusion.1, ...), kind=kOutput, calls=%fused_computation.41 | convolution fusion | flops 1022607360 | bytes 5248000 | tf_op jit(solution)/shard_map/dot_general | solution.py:165
  26.3 0.9 fusion.45
  27.2 1.0 copy.54
  28.2 38.4 %while.14 = (s32[]{:T(128)}, bf16[4,2,512,72]{2,3,0,1:T(8,128)(2,1)}, bf16[4,512,72]{1,2,0:T(8,128)(2,1)}, bf16[4,512,72]{2,1,0:T(8,128)(2,1)}, bf16[4,2,120,72]...) while((s32[]{:T(128)}, ...), condition=%wide.region_12.13_spmd, body=%wide.region_7.0_spmd.sunk | while | flops 152713728 | bytes 12811917 | solution.py:125
  28.2 1.2 fusion.67
  29.4 1.2 fusion.66
  30.6 1.3 copy.79
  31.9 1.9 %fusion.68 = f32[2,512]{1,0:T(2,128)S(1)} fusion(f32[2,512]{1,0:T(2,128)S(1)} %broadcast_maximum_fusion.2, f32[512,512]{1,0:T(8,128)} %copy.79), kind=kLoop, calls=%fused_computation.2.clone.1 | loop fusion | flops 1047552 | bytes 1056768 | tf_op jit(solution)/shard_map/while/body/eval_jaxpr/reduce_sum | solution.py:113
  34.0 2.0 %fusion.70 = f32[2,512,72]{1,2,0:T(8,128)S(1)} fusion(f32[2,512]{1,0:T(2,128)S(1)} %add.189, f32[2,512]{1,0:T(2,128)S(1)} %broadcast_maximum_fusion.2, f32[512,512]{1,0:T(8,128)} %copy.79, bf16[4,512,72]{1,2,0:T(8,128)(2,1)} %get-tuple-element.218, s32[]{:T(128)} %get-tuple-element.205), kind=kOutput, calls=%fused_computation.9.clone.1 | convolution fusion | flops 77070336 | bytes 1425920 | tf_op jit(solution)/shard_map/while/body/eval_jaxpr/roz,zt->rot/dot_general | solution.py:116
  36.0 1.0 fusion.71
  37.0 0.8 copy-done.10
  37.8 1.2 fusion.67
  39.0 1.2 fusion.66
  40.2 1.3 copy.79
  41.5 1.9 %fusion.68 = f32[2,512]{1,0:T(2,128)S(1)} fusion(f32[2,512]{1,0:T(2,128)S(1)} %broadcast_maximum_fusion.2, f32[512,512]{1,0:T(8,128)} %copy.79), kind=kLoop, calls=%fused_computation.2.clone.1 | loop fusion | flops 1047552 | bytes 1056768 | tf_op jit(solution)/shard_map/while/body/eval_jaxpr/reduce_sum | solution.py:113
  43.6 2.0 %fusion.70 = f32[2,512,72]{1,2,0:T(8,128)S(1)} fusion(f32[2,512]{1,0:T(2,128)S(1)} %add.189, f32[2,512]{1,0:T(2,128)S(1)} %broadcast_maximum_fusion.2, f32[512,512]{1,0:T(8,128)} %copy.79, bf16[4,512,72]{1,2,0:T(8,128)(2,1)} %get-tuple-element.218, s32[]{:T(128)} %get-tuple-element.205), kind=kOutput, calls=%fused_computation.9.clone.1 | convolution fusion | flops 77070336 | bytes 1425920 | tf_op jit(solution)/shard_map/while/body/eval_jaxpr/roz,zt->rot/dot_general | solution.py:116
  45.6 1.0 fusion.71
  46.6 0.8 copy-done.10
  47.4 1.2 fusion.67
  48.6 1.2 fusion.66
  49.8 1.3 copy.79
  51.1 1.9 %fusion.68 = f32[2,512]{1,0:T(2,128)S(1)} fusion(f32[2,512]{1,0:T(2,128)S(1)} %broadcast_maximum_fusion.2, f32[512,512]{1,0:T(8,128)} %copy.79), kind=kLoop, calls=%fused_computation.2.clone.1 | loop fusion | flops 1047552 | bytes 1056768 | tf_op jit(solution)/shard_map/while/body/eval_jaxpr/reduce_sum | solution.py:113
  53.2 2.0 %fusion.70 = f32[2,512,72]{1,2,0:T(8,128)S(1)} fusion(f32[2,512]{1,0:T(2,128)S(1)} %add.189, f32[2,512]{1,0:T(2,128)S(1)} %broadcast_maximum_fusion.2, f32[512,512]{1,0:T(8,128)} %copy.79, bf16[4,512,72]{1,2,0:T(8,128)(2,1)} %get-tuple-element.218, s32[]{:T(128)} %get-tuple-element.205), kind=kOutput, calls=%fused_computation.9.clone.1 | convolution fusion | flops 77070336 | bytes 1425920 | tf_op jit(solution)/shard_map/while/body/eval_jaxpr/roz,zt->rot/dot_general | solution.py:116
  55.2 1.0 fusion.71
  56.2 0.8 copy-done.10
  57.0 1.2 fusion.67
  58.2 1.2 fusion.66
  59.4 1.3 copy.79
  60.7 1.9 %fusion.68 = f32[2,512]{1,0:T(2,128)S(1)} fusion(f32[2,512]{1,0:T(2,128)S(1)} %broadcast_maximum_fusion.2, f32[512,512]{1,0:T(8,128)} %copy.79), kind=kLoop, calls=%fused_computation.2.clone.1 | loop fusion | flops 1047552 | bytes 1056768 | tf_op jit(solution)/shard_map/while/body/eval_jaxpr/reduce_sum | solution.py:113
  62.8 2.0 %fusion.70 = f32[2,512,72]{1,2,0:T(8,128)S(1)} fusion(f32[2,512]{1,0:T(2,128)S(1)} %add.189, f32[2,512]{1,0:T(2,128)S(1)} %broadcast_maximum_fusion.2, f32[512,512]{1,0:T(8,128)} %copy.79, bf16[4,512,72]{1,2,0:T(8,128)(2,1)} %get-tuple-element.218, s32[]{:T(128)} %get-tuple-element.205), kind=kOutput, calls=%fused_computation.9.clone.1 | convolution fusion | flops 77070336 | bytes 1425920 | tf_op jit(solution)/shard_map/while/body/eval_jaxpr/roz,zt->rot/dot_general | solution.py:116
  64.8 1.0 fusion.71
  66.6 4.2 %convolution_convert_fusion = bf16[2,512,1152]{2,1,0:T(8,128)(2,1)} fusion(bf16[2,512,288]{1,2,0:T(8,128)(2,1)} %bitcast.122, bf16[288,1152]{1,0:T(8,128)(2,1)} %param.24), kind=kOutput, calls=%fused_computation.32 | convolution fusion | flops 680656896 | bytes 3612672 | tf_op jit(solution)/shard_map/btk,kd->btd/dot_general | solution.py:168
  71.6 4.4 %collective-permute-start.6 = (f32[32]{0:T(128)S(1)}, f32[32]{0:T(128)S(1)}, u32[]{:S(2)}, u32[]{:S(2)}) collective-permute-start(f32[32]{0:T(128)S(1)} %get-tuple-element.143), channel_id=1, source_target_pairs={{0,15},{1,0},{2,1},{3,2},{4,3},{5,4},{6,5},{7,6},{8,7},{9,8},{10,9... | collective-permute-start | bytes 392 | tf_op jit(solution)/shard_map/ppermute | solution.py:38
  76.6 28.1 %reduce-scatter.2.cloned.1.call-done = bf16[1,512,1152]{2,1,0:T(8,128)(2,1)} async-done(((bf16[2,512,1152]{2,1,0:T(8,128)(2,1)}), bf16[1,512,1152]{2,1,0:T(8,128)(2,1)}) %reduce-scatter.2.cloned.1.call-update) | async-done | bytes 1179664 | tf_op jit(solution)/shard_map/reduce_scatter | solution.py:167
  104.7 2.5 %fusion.32 = f32[512]{0:T(512)S(1)} fusion(f32[512,1152]{1,0:T(8,128)} %copy-done.1, bf16[1,512,1152]{2,1,0:T(8,128)(2,1)} %reduce-scatter.2.cloned.1.call-done, f32[1152]{0:T(1024)S(1)} %get-tuple-element.101), kind=kLoop, calls=%fused_computation.48 | loop fusion | flops 2358784 | bytes 3545600 | tf_op jit(solution)/shard_map/reduce_sum | solution.py:42
  109.2 1.0 copy.58
  110.1 1.1 constant_dynamic-slice_fusion.1
  111.2 1.3 copy.65
  115.7 1.3 copy.66
  117.9 4.4 %collective-permute-start.4 = (f32[32,4,16]{0,2,1:T(8,128)S(1)}, f32[32,4,16]{0,2,1:T(8,128)S(1)}, u32[]{:S(2)}, u32[]{:S(2)}) collective-permute-start(f32[32,4,16]{0,2,1:T(8,128)S(1)} %get-tuple-element.137), channel_id=1, source_target_pairs={{0,15},{1,0},{2,1},{3,2},{4,3},{5,4},{6,5},{7,6},{8,7},{9,8},{10,9... | collective-permute-start | bytes 24584 | tf_op jit(solution)/shard_map/ppermute | solution.py:38
  122.4 1.5 %collective-permute-done.3 = f32[32,4,16]{0,2,1:T(8,128)S(1)} collective-permute-done((f32[32,4,16]{0,2,1:T(8,128)S(1)}, f32[32,4,16]{0,2,1:T(8,128)S(1)}, u32[]{:S(2)}, u32[]{:S(2)}) %collective-permute-start.3) | collective-permute-done | bytes 8224 | tf_op jit(solution)/shard_map/ppermute | solution.py:38
  (94 shorter events, 8.7 us)
Async XLA Ops:
  7.2 17.6 %copy-start = (bf16[1152,3,288]{0,2,1:T(8,128)(2,1)S(1)}, bf16[1152,3,288]{0,2,1:T(8,128)(2,1)}, u32[]{:S(2)}) copy-start(bf16[1152,3,288]{0,2,1:T(8,128)(2,1)} %param.23) | copy-start | bytes 5971972
  7.2 97.5 %reduce-scatter.2.cloned.1.call-start = ((), (), s32[]{:S(2)}) async-start(), calls=%async_computation.1 | async-start | bytes 3538944 | tf_op jit(solution)/shard_map/reduce_scatter | solution.py:167
  8.3 11.4 %copy-start.4 = (f32[32,4,32]{0,2,1:T(8,128)}, f32[32,4,32]{0,2,1:T(8,128)S(1)}, u32[]{:S(2)}) copy-start(f32[32,4,32]{0,2,1:T(8,128)S(1)} %copy.48) | copy-start | bytes 49156
  8.3 11.4 %collective-permute-start = (bf16[32,4,32]{0,2,1:T(8,128)(2,1)S(1)}, bf16[32,4,32]{0,2,1:T(8,128)(2,1)S(1)}, u32[]{:S(2)}, u32[]{:S(2)}) collective-permute-start(bf16[32,4,32]{0,2,1:T(8,128)(2,1)S(1)} %convert.17), channel_id=1, source_target_pairs={{0,1},{1,2},{2,3},{3,4},{4,5},{5,6},{6,7},{7,8},{8,9},{9,10},{10,1... | collective-permute-start | bytes 24584 | tf_op jit(solution)/shard_map/ppermute | solution.py:24
  8.8 10.8 %collective-permute-start.1 = (bf16[32,4,32]{0,2,1:T(8,128)(2,1)S(1)}, bf16[32,4,32]{0,2,1:T(8,128)(2,1)S(1)}, u32[]{:S(2)}, u32[]{:S(2)}) collective-permute-start(bf16[32,4,32]{0,2,1:T(8,128)(2,1)S(1)} %convert.17), channel_id=1, source_target_pairs={{1,0},{2,1},{3,2},{4,3},{5,4},{6,5},{7,6},{8,7},{9,8},{10,9},{11,1... | collective-permute-start | bytes 24584 | tf_op jit(solution)/shard_map/ppermute | solution.py:25
  16.9 1.8 %copy-start.6 = (f32[20,4,1152]{2,1,0:T(4,128)S(1)}, f32[20,4,1152]{2,1,0:T(4,128)}, u32[]{:S(2)}) copy-start(f32[20,4,1152]{2,1,0:T(4,128)} %param.22) | copy-start | bytes 1105924
  17.0 5.2 %copy-start.7 = (bf16[16,1152]{1,0:T(8,128)(2,1)S(1)}, bf16[16,1152]{1,0:T(8,128)(2,1)}, u32[]{:S(2)}) copy-start(bf16[16,1152]{1,0:T(8,128)(2,1)} %param.25) | copy-start | bytes 110596
  24.4 1.9 %copy-start.1 = (f32[512,1152]{1,0:T(8,128)}, f32[512,1152]{1,0:T(8,128)S(1)}, u32[]{:S(2)}) copy-start(f32[512,1152]{1,0:T(8,128)S(1)} %get-tuple-element.145) | copy-start | bytes 7077892
  34.0 2.0 %copy-start.9 = (bf16[4,2,512,72]{2,3,0,1:T(8,128)(2,1)S(1)}, bf16[4,2,512,72]{2,3,0,1:T(8,128)(2,1)}, u32[]{:S(2)}) copy-start(bf16[4,2,512,72]{2,3,0,1:T(8,128)(2,1)} %get-tuple-element.206) | copy-start | bytes 1769476 | tf_op jit(solution)/shard_map/while
  37.0 0.8 copy-start.10
  43.6 2.0 %copy-start.9 = (bf16[4,2,512,72]{2,3,0,1:T(8,128)(2,1)S(1)}, bf16[4,2,512,72]{2,3,0,1:T(8,128)(2,1)}, u32[]{:S(2)}) copy-start(bf16[4,2,512,72]{2,3,0,1:T(8,128)(2,1)} %get-tuple-element.206) | copy-start | bytes 1769476 | tf_op jit(solution)/shard_map/while
  46.6 0.8 copy-start.10
  53.2 2.0 %copy-start.9 = (bf16[4,2,512,72]{2,3,0,1:T(8,128)(2,1)S(1)}, bf16[4,2,512,72]{2,3,0,1:T(8,128)(2,1)}, u32[]{:S(2)}) copy-start(bf16[4,2,512,72]{2,3,0,1:T(8,128)(2,1)} %get-tuple-element.206) | copy-start | bytes 1769476 | tf_op jit(solution)/shard_map/while
  56.2 0.8 copy-start.10
  62.8 2.0 %copy-start.9 = (bf16[4,2,512,72]{2,3,0,1:T(8,128)(2,1)S(1)}, bf16[4,2,512,72]{2,3,0,1:T(8,128)(2,1)}, u32[]{:S(2)}) copy-start(bf16[4,2,512,72]{2,3,0,1:T(8,128)(2,1)} %get-tuple-element.206) | copy-start | bytes 1769476 | tf_op jit(solution)/shard_map/while
  65.8 0.8 copy-start.10
  71.6 50.8 %collective-permute-start.5 = (f32[32]{0:T(128)S(1)}, f32[32]{0:T(128)S(1)}, u32[]{:S(2)}, u32[]{:S(2)}) collective-permute-start(f32[32]{0:T(128)S(1)} %get-tuple-element.142), channel_id=1, source_target_pairs={{0,1},{1,2},{2,3},{3,4},{4,5},{5,6},{6,7},{7,8},{8,9},{9,10},{10,1... | collective-permute-start | bytes 392 | tf_op jit(solution)/shard_map/ppermute | solution.py:38
  71.6 50.8 %collective-permute-start.6 = (f32[32]{0:T(128)S(1)}, f32[32]{0:T(128)S(1)}, u32[]{:S(2)}, u32[]{:S(2)}) collective-permute-start(f32[32]{0:T(128)S(1)} %get-tuple-element.143), channel_id=1, source_target_pairs={{0,15},{1,0},{2,1},{3,2},{4,3},{5,4},{6,5},{7,6},{8,7},{9,8},{10,9... | collective-permute-start | bytes 392 | tf_op jit(solution)/shard_map/ppermute | solution.py:38
  104.7 2.7 %copy-start.2 = (f32[512,1152]{1,0:T(8,128)S(1)}, f32[512,1152]{1,0:T(8,128)}, u32[]{:S(2)}) copy-start(f32[512,1152]{1,0:T(8,128)} %copy-done.1) | copy-start | bytes 7077892
  104.7 3.0 %copy-start.3 = (bf16[1,512,1152]{2,1,0:T(8,128)(2,1)S(1)}, bf16[1,512,1152]{2,1,0:T(8,128)(2,1)}, u32[]{:S(2)}) copy-start(bf16[1,512,1152]{2,1,0:T(8,128)(2,1)} %reduce-scatter.2.cloned.1.call-done) | copy-start | bytes 3538948
  107.2 1.1 copy-start.8
  109.1 14.8 %copy-start.5 = (f32[32,4,32]{0,2,1:T(8,128)S(1)}, f32[32,4,32]{0,2,1:T(8,128)}, u32[]{:S(2)}) copy-start(f32[32,4,32]{0,2,1:T(8,128)} %copy-done.4) | copy-start | bytes 49156
  112.5 4.5 %collective-permute-start.2 = (f32[64,4,16]{0,2,1:T(8,128)S(1)}, f32[64,4,16]{0,2,1:T(8,128)S(1)}, u32[]{:S(2)}, u32[]{:S(2)}) collective-permute-start(f32[64,4,16]{0,2,1:T(8,128)S(1)} %copy.65), channel_id=1, source_target_pairs={{0,16},{16,0},{1,17},{17,1},{2,18},{18,2},{3,19},{19,3},{4,20},{20... | collective-permute-start | bytes 49160 | tf_op jit(solution)/shard_map/ppermute | solution.py:33
  117.9 6.0 %collective-permute-start.3 = (f32[32,4,16]{0,2,1:T(8,128)S(1)}, f32[32,4,16]{0,2,1:T(8,128)S(1)}, u32[]{:S(2)}, u32[]{:S(2)}) collective-permute-start(f32[32,4,16]{0,2,1:T(8,128)S(1)} %get-tuple-element.136), channel_id=1, source_target_pairs={{0,1},{1,2},{2,3},{3,4},{4,5},{5,6},{6,7},{7,8},{8,9},{9,10},{10,1... | collective-permute-start | bytes 24584 | tf_op jit(solution)/shard_map/ppermute | solution.py:38
  117.9 6.0 %collective-permute-start.4 = (f32[32,4,16]{0,2,1:T(8,128)S(1)}, f32[32,4,16]{0,2,1:T(8,128)S(1)}, u32[]{:S(2)}, u32[]{:S(2)}) collective-permute-start(f32[32,4,16]{0,2,1:T(8,128)S(1)} %get-tuple-element.137), channel_id=1, source_target_pairs={{0,15},{1,0},{2,1},{3,2},{4,3},{5,4},{6,5},{7,6},{8,7},{9,8},{10,9... | collective-permute-start | bytes 24584 | tf_op jit(solution)/shard_map/ppermute | solution.py:38
Sparse Core Ops, SparseCore 0:
  70.9 33.7 reduce-scatter.1
where the time goes:
time: 133 us; the launch traced here: 131 us
  matrix products  30.1 us (23%)
  waiting for transfers between devices  29.7 us (22%)
  local copies, waits for them, and re-layouts  22.1 us (17%)
  between operations  18.4 us (14%)
  other arithmetic  16 us (12%)
  starting transfers between devices  14.9 us (11%)
    reduce_scatter x1, waiting for transfers between devices, on_device(): lax.psum_scatter(jnp.einsum('btk,kd->btd', attended, out_weight, preferre...  28.1 us
    ppermute x4, starting transfers between devices, from_behind(): lax.ppermute(array, axis, [(i, (i + by) % size) for i in range(size)])  8.89 us
    reduce_sum x8, other arithmetic, one_head(): totals = jnp.sum(own_exp, axis=-1) + jnp.sum(text_exp, axis=-1)  8.02 us
    dot_general x4, matrix products, one_head(): jnp.einsum('roz,zt->rot', self_softmax_weights, value_tile, preferred_ele...  7.94 us
    mul x4, local copies, waits for them, and re-layouts, one_head(): jnp.einsum('qd,kd->qk', query_tile, key_block, preferred_element_type=jnp...  5.23 us
    ppermute x1, starting transfers between devices, with_halo(): after = lax.ppermute(first, axis, down)  5.02 us
    dot_general x4, matrix products, one_head(): jnp.einsum('qd,kd->qk', query_tile, key_block, preferred_element_type=jnp...  4.9 us
    dot_general x4, matrix products, one_head(): jnp.einsum('cr,eor->eco', query_tile, caption_key_tile, preferred_element...  4.7 us
  transfers between devices with their start and end apart: 8, of which 2 were waited for; matrix products, arithmetic and copies ran while one was open for 12% of the time, Pallas kernels for 0%

commit v1 on v0

v1 whole, which is shorter than its diff:
```python
import functools
import math

import jax
import jax.numpy as jnp
from jax import lax
from jax.experimental import pallas as pl
from jax.experimental.pallas import tpu as pltpu
from jax.sharding import PartitionSpec as P

HEAD_DIM = 72
STEPS = 20


guidance_scale = 4.5
plan_length = 1000
norm_eps = 1e-06

VM = pl.BlockSpec(memory_space=pltpu.VMEM)
SM = pl.BlockSpec(memory_space=pltpu.SMEM)


def shift(array, axis, by):
    size = lax.axis_size(axis)
    return lax.ppermute(array, axis, [(i, (i + by) % size) for i in range(size)])


def swap(array, axis):
    return lax.ppermute(array, axis, [(0, 1), (1, 0)])


def layer_norm(values):
    average = jnp.mean(values, axis=-1, keepdims=True)
    centered = values - average
    variance = jnp.mean(centered * centered, axis=-1, keepdims=True)
    return centered * lax.rsqrt(variance + norm_eps)


def position_tables(col_pairs, row_couples, model_width):
    quarter = model_width // 4
    frequency = jnp.exp(-math.log(10000.0) * jnp.arange(quarter, dtype=jnp.float32) / quarter)
    col_pos = jnp.arange(col_pairs, dtype=jnp.float32)[:, None] * frequency[None, :]
    row_pos = jnp.arange(row_couples, dtype=jnp.float32)[:, None] * frequency[None, :]
    half = 2 * quarter
    row_part = jnp.concatenate(
        [jnp.sin(row_pos), jnp.cos(row_pos), jnp.zeros((row_couples, half), jnp.float32)], axis=1
    )
    col_part = jnp.concatenate(
        [jnp.zeros((col_pairs, half), jnp.float32), jnp.sin(col_pos), jnp.cos(col_pos)], axis=1
    )
    return row_part, col_part


def plan(moment):
    train_grid = jnp.arange(plan_length, dtype=jnp.int32)
    beta_values = 0.0001 + (0.02 - 0.0001) * train_grid.astype(jnp.float32) / (plan_length - 1)
    alpha_bar = jnp.exp(jnp.cumsum(jnp.log(1.0 - beta_values)))
    stride = plan_length // STEPS
    earlier = moment - stride
    alpha_now = jnp.sum(jnp.where(train_grid == moment, alpha_bar, 0.0))
    alpha_before = jnp.sum(jnp.where(train_grid == earlier, alpha_bar, 0.0)) + jnp.where(
        earlier < 0, 1.0, 0.0
    )
    return (alpha_now, alpha_before)


def repeat_pairs(weight, repeats):
    rows, width = weight.shape
    values = weight.astype(jnp.float32)
    even = lax.broadcasted_iota(jnp.int32, (2 * repeats, width), 0) % 2 == 0
    parts = []
    for pair in range(rows // 2):
        parts.append(
            jnp.where(even, values[2 * pair : 2 * pair + 1, :], values[2 * pair + 1 : 2 * pair + 2, :])
        )
    return jnp.concatenate(parts, axis=0).astype(jnp.bfloat16)


def attend(proj_ref, text_ref, first, count):
    heads = proj_ref.shape[0] // 3
    branches = text_ref.shape[0]
    factor = math.log2(math.e) / math.sqrt(HEAD_DIM)
    feature = (((0,), (0,)), ((), ()))
    results = [[] for _ in range(branches)]
    for head in range(heads):
        rows = slice(head * HEAD_DIM, (head + 1) * HEAD_DIM)
        queries = proj_ref[head, :, pl.ds(first, count)]
        own_scores = lax.dot_general(
            proj_ref[heads + head], queries, feature, preferred_element_type=jnp.float32
        )
        own_highest = jnp.max(own_scores, axis=0, keepdims=True)
        own_exp = jnp.exp2((own_scores - own_highest) * factor)
        own_total = jnp.sum(own_exp, axis=0, keepdims=True)
        own_mix = jnp.dot(
            proj_ref[2 * heads + head],
            own_exp.astype(jnp.bfloat16),
            preferred_element_type=jnp.float32,
        )
        for branch in range(branches):
            text_scores = lax.dot_general(
                text_ref[branch, 0, rows, :], queries, feature, preferred_element_type=jnp.float32
            )
            highest = jnp.maximum(own_highest, jnp.max(text_scores, axis=0, keepdims=True))
            text_exp = jnp.exp2((text_scores - highest) * factor)
            lowered = jnp.exp2((own_highest - highest) * factor)
            total = lowered * own_total + jnp.sum(text_exp, axis=0, keepdims=True)
            text_mix = jnp.dot(
                text_ref[branch, 1, rows, :],
                text_exp.astype(jnp.bfloat16),
                preferred_element_type=jnp.float32,
            )
            results[branch].append((lowered * own_mix + text_mix) * (1.0 / total))
    return [jnp.concatenate(parts, axis=0).astype(jnp.bfloat16) for parts in results]


def project_kernel(
    step_ref,
    side_ref,
    offset_ref,
    modulation_ref,
    before_ref,
    own_ref,
    after_ref,
    row_ref,
    col_ref,
    patch_ref,
    weight_ref,
    text_ref,
    proj_ref,
    embedded_ref,
    sent_ref,
    extended_ref,
):
    slab_cols, channels, row_count = own_ref.shape
    col_pairs, row_couples = slab_cols, row_count // 2
    tokens = col_pairs * row_couples
    own_tokens = tokens // 2
    wide = 2 * channels * row_count
    for place, source in enumerate((before_ref, own_ref, after_ref)):
        for channel in range(channels):
            extended_ref[
                place * slab_cols : (place + 1) * slab_cols,
                channel * row_count : (channel + 1) * row_count,
            ] = source[:, channel, :]
    extended = extended_ref[...].astype(jnp.bfloat16)
    start_at = slab_cols - offset_ref[0]
    chosen = lax.broadcasted_iota(jnp.int32, (2 * col_pairs, 3 * slab_cols), 0)
    column = lax.broadcasted_iota(jnp.int32, (2 * col_pairs, 3 * slab_cols), 1)
    target = jnp.where(
        chosen < col_pairs, 2 * chosen, 2 * (chosen - col_pairs) + 1
    )
    pick = jnp.where(column == target + start_at, 1.0, 0.0).astype(jnp.bfloat16)
    picked = jnp.dot(pick, extended, preferred_element_type=jnp.float32)
    picked = jnp.concatenate([picked[:col_pairs], picked[col_pairs:]], axis=1)
    lane_couple = lax.broadcasted_iota(jnp.int32, (col_pairs, wide), 1) % row_count // 2
    spread = jnp.concatenate(
        [jnp.where(lane_couple == couple, picked, 0.0) for couple in range(row_couples)], axis=0
    ).astype(jnp.bfloat16)
    patch_wide = repeat_pairs(patch_ref[...], row_couples)
    embedded = jnp.dot(spread, patch_wide, preferred_element_type=jnp.float32)
    position = jnp.concatenate(
        [row_ref[couple : couple + 1, :] + col_ref[...] for couple in range(row_couples)], axis=0
    )
    embedded = embedded + position
    side = side_ref[0]
    normed = (
        layer_norm(embedded) * (1.0 + modulation_ref[0, 1:2, :]) + modulation_ref[0, 0:1, :]
    ).astype(jnp.bfloat16)

    @pl.when(side == 0)
    def _():
        embedded_ref[...] = embedded[:own_tokens]

    @pl.when(side != 0)
    def _():
        embedded_ref[...] = embedded[own_tokens:]

    heads = proj_ref.shape[0] // 3
    for kind in range(3):
        projected = lax.dot_general(
            weight_ref[kind],
            normed,
            (((1,), (1,)), ((), ())),
            preferred_element_type=jnp.float32,
        )
        for head in range(heads):
            proj_ref[kind * heads + head] = projected[
                head * HEAD_DIM : (head + 1) * HEAD_DIM
            ].astype(jnp.bfloat16)
    first = pl.multiple_of((1 - side) * own_tokens, own_tokens)
    for branch, value in enumerate(attend(proj_ref, text_ref, first, own_tokens)):
        sent_ref[branch] = value


def attend_kernel(side_ref, proj_ref, text_ref, weight_ref, mixed_ref):
    tokens = proj_ref.shape[2]
    own_tokens = tokens // 2
    first = pl.multiple_of(side_ref[0] * own_tokens, own_tokens)
    for branch, value in enumerate(attend(proj_ref, text_ref, first, own_tokens)):
        mixed_ref[branch] = lax.dot_general(
            value, weight_ref[...], (((0,), (0,)), ((), ())), preferred_element_type=jnp.float32
        ).astype(jnp.bfloat16)


def finish_kernel(
    step_ref,
    offset_ref,
    blend_ref,
    modulation_ref,
    embedded_ref,
    mixed_ref,
    received_ref,
    weight_ref,
    final_ref,
    left_ref,
    center_ref,
    right_ref,
    buffer_ref,
):
    slab_cols = left_ref.shape[0]
    col_pairs = slab_cols
    own_tokens = embedded_ref.shape[0]
    couples = own_tokens // col_pairs
    final_wide = repeat_pairs(final_ref[...], couples)
    wide = final_wide.shape[0]
    predicted = []
    for branch in range(2):
        other = lax.dot_general(
            received_ref[branch],
            weight_ref[...],
            (((0,), (0,)), ((), ())),
            preferred_element_type=jnp.float32,
        ).astype(jnp.bfloat16)
        mixed = mixed_ref[branch].astype(jnp.float32) + other.astype(jnp.float32)
        residual = embedded_ref[...] + modulation_ref[0, 2:3, :] * mixed
        final_norm = (layer_norm(residual) * (1.0 + modulation_ref[0, 3:4, :])).astype(jnp.bfloat16)
        predicted.append(
            lax.dot_general(
                final_norm,
                final_wide,
                (((1,), (1,)), ((), ())),
                preferred_element_type=jnp.float32,
            )
        )
    conditional, unconditional = predicted
    guided = unconditional + guidance_scale * (conditional - unconditional)
    lane_couple = lax.broadcasted_iota(jnp.int32, (col_pairs, wide), 1) % (2 * couples) // 2
    pairs = jnp.zeros((col_pairs, wide), jnp.float32)
    for couple in range(couples):
        pairs = pairs + jnp.where(
            lane_couple == couple, guided[couple * col_pairs : (couple + 1) * col_pairs], 0.0
        )
    weight_value = blend_ref[0].astype(jnp.float32)
    half = wide // 2
    is_noise = lax.broadcasted_iota(jnp.int32, (col_pairs, wide), 1) < half
    even = jnp.where(is_noise, weight_value * pairs, weight_value)
    odd = jnp.where(is_noise, weight_value * pltpu.roll(pairs, half, 1), weight_value)
    start_at = slab_cols - offset_ref[0]
    buffer_ref[...] = jnp.zeros_like(buffer_ref)
    buffer_ref[pl.ds(start_at, col_pairs, stride=2), :] = even
    buffer_ref[pl.ds(start_at + 1, col_pairs, stride=2), :] = odd
    left_ref[...] = buffer_ref[:slab_cols]
    center_ref[...] = buffer_ref[slab_cols : 2 * slab_cols]
    right_ref[...] = buffer_ref[2 * slab_cols : 3 * slab_cols]


def blend_kernel(
    side_ref, plan_ref, center_ref, left_ref, right_ref, latent_ref, previous_ref, noise_ref
):
    channels, half_rows = noise_ref.shape[1:]
    total = center_ref[...] + left_ref[...] + right_ref[...]
    blended = total / pltpu.roll(total, total.shape[1] // 2, 1)
    first = side_ref[0] == 0
    for channel in range(channels):
        noise = blended[:, channel * half_rows : (channel + 1) * half_rows]
        rows = latent_ref[:, channel, :]
        rows = jnp.where(first, rows[:, :half_rows], rows[:, half_rows:])
        noise_ref[:, channel, :] = noise
        previous_ref[:, channel, :] = (
            plan_ref[0] * (rows - plan_ref[1] * noise) / plan_ref[2] + plan_ref[3] * noise
        )


def on_device(
    latent,
    text_kv,
    modulation,
    qkv_weight,
    out_weight,
    patch_weight,
    final_weight,
    offsets,
    blend_weights,
    step_index,
):
    slab_cols, channels, row_count = latent.shape
    model_width = patch_weight.shape[1]
    half_attn = out_weight.shape[0]
    heads = half_attn // HEAD_DIM
    branches = text_kv.shape[0]
    col_pairs, row_couples = slab_cols, row_count // 2
    tokens = col_pairs * row_couples
    own_tokens = tokens // 2
    half_rows = row_count // 2
    side = lax.axis_index("cfg").astype(jnp.int32).reshape(1)

    before = shift(latent, "win", 1)
    after = shift(latent, "win", -1)
    other_weight = swap(out_weight, "cfg")

    row_part, col_part = position_tables(col_pairs, row_couples, model_width)
    weight = jnp.transpose(qkv_weight, (1, 2, 0))
    text = jnp.transpose(text_kv, (0, 1, 3, 2))
    final = jnp.transpose(final_weight, (1, 0))
    moment = step_index[0]
    alpha_now, alpha_before = plan(moment)
    plan_values = jnp.stack(
        [
            jnp.sqrt(alpha_before),
            jnp.sqrt(1.0 - alpha_now),
            jnp.sqrt(alpha_now),
            jnp.sqrt(1.0 - alpha_before),
        ]
    )

    modulation_spec = pl.BlockSpec(
        (1, 4, model_width), lambda i, step: (step[0] * STEPS // plan_length, 0, 0)
    )
    bf16, f32 = jnp.bfloat16, jnp.float32
    shape = jax.ShapeDtypeStruct
    projected, embedded, sent = pl.pallas_call(
        project_kernel,
        out_shape=(
            shape((3 * heads, HEAD_DIM, tokens), bf16),
            shape((own_tokens, model_width), f32),
            shape((branches, half_attn, own_tokens), bf16),
        ),
        grid_spec=pltpu.PrefetchScalarGridSpec(
            num_scalar_prefetch=1,
            grid=(1,),
            in_specs=[SM, SM, modulation_spec] + [VM] * 8,
            out_specs=(VM, VM, VM),
            scratch_shapes=[pltpu.VMEM((3 * slab_cols, channels * row_count), f32)],
        ),
        name="project",
        cost_estimate=pl.CostEstimate(flops=2 * 10**9, bytes_accessed=8 * 10**6, transcendentals=10**6),
    )(
        step_index, side, offsets, modulation, before, latent, after,
        row_part, col_part, patch_weight, weight, text,
    )
    received = swap(sent, "cfg")
    mixed = pl.pallas_call(
        attend_kernel,
        out_shape=shape((branches, own_tokens, model_width), bf16),
        in_specs=[SM] + [VM] * 3,
        out_specs=VM,
        name="attend",
        cost_estimate=pl.CostEstimate(flops=10**9, bytes_accessed=8 * 10**6, transcendentals=10**6),
    )(side, projected, text, out_weight)
    left, center, right = pl.pallas_call(
        finish_kernel,
        out_shape=tuple(shape((slab_cols, 2 * channels * half_rows), f32) for _ in range(3)),
        grid_spec=pltpu.PrefetchScalarGridSpec(
            num_scalar_prefetch=1,
            grid=(1,),
            in_specs=[SM, SM, modulation_spec] + [VM] * 5,
            out_specs=(VM, VM, VM),
            scratch_shapes=[pltpu.VMEM((3 * slab_cols + 8, 2 * channels * half_rows), f32)],
        ),
        name="finish",
        cost_estimate=pl.CostEstimate(flops=10**9, bytes_accessed=4 * 10**6, transcendentals=10**3),
    )(
        step_index, offsets, blend_weights, modulation, embedded, mixed, received,
        other_weight, final,
    )
    from_left = shift(right, "win", 1)
    from_right = shift(left, "win", -1)
    previous, noise = pl.pallas_call(
        blend_kernel,
        out_shape=tuple(shape((slab_cols, channels, half_rows), f32) for _ in range(2)),
        in_specs=[SM, SM] + [VM] * 4,
        out_specs=(VM, VM),
        name="blend",
    )(side, plan_values, center, from_left, from_right, latent)
    return (previous, noise)


def solution(mesh):
    in_specs = (
        P("win", None, None),
        P(None, None, None, "cfg"),
        P(),
        P(None, None, "cfg"),
        P("cfg", None),
        P(),
        P(),
        P("win"),
        P("win"),
        P(),
    )
    out_specs = (P("win", None, "cfg"), P("win", None, "cfg"))
    return jax.shard_map(
        on_device, mesh=mesh, in_specs=in_specs, out_specs=out_specs, check_vma=False
    )
```

time: 133 us -> 49 us (0.37)
  matrix products: 30.1 us -> 0 us
  waiting for transfers between devices: 29.7 us -> 1.01 us
  Pallas kernels: 0 us -> 21.9 us
  local copies, waits for them, and re-layouts: 22.1 us -> 6.9 us
  other arithmetic: 16 us -> 1.96 us
  between operations: 18.4 us -> 4.77 us
  starting transfers between devices: 14.9 us -> 12 us
    dot_general x20 -> x0, matrix products: 30.1 us -> none  [the longest x4 7.94 us: one_head(): jnp.einsum('roz,zt->rot', self_softmax_weights, value_tile, preferred_ele...]
    reduce_scatter x1 -> x0, waiting for transfers between devices: 28.1 us -> none  [on_device(): lax.psum_scatter(jnp.einsum('btk,kd->btd', attended, out_weight, preferre...]
    pallas_call x0 -> x4, Pallas kernels: none -> 21.9 us  [the longest x1 8.54 us: on_device(): pl.pallas_call(project_kernel, out_shape=(shape((3 * heads, HEAD_DIM, tok...]
    reduce_sum x12 -> x0, other arithmetic: 11.6 us -> none  [the longest x8 8.02 us: one_head(): totals = jnp.sum(own_exp, axis=-1) + jnp.sum(text_exp, axis=-1)]
    mul x4 -> x0, local copies, waits for them, and re-layouts: 5.23 us -> none  [one_head(): jnp.einsum('qd,kd->qk', query_tile, key_block, preferred_element_type=jnp...]
    while x16 -> x0, local copies, waits for them, and re-layouts: 3.32 us -> none
    pallas_call x0 -> x2, local copies, waits for them, and re-layouts: none -> 3.06 us  [on_device(): pl.pallas_call(blend_kernel, out_shape=tuple((shape((slab_cols, channels,...]
    ppermute x7 -> x6, starting transfers between devices: 14.8 us -> 12 us  [the longest x4 10 us: shift(): lax.ppermute(array, axis, [(i, (i + by) % size) for i in range(size)])]
  transfers between devices with their start and end apart: 8 -> 6, of which waited for: 2 -> 1; matrix products, arithmetic and copies ran while one was open for 12% -> 7% of each run, Pallas kernels for 0% -> 31%
where the time goes in v1:
time: 49 us; the launch traced here: 48.6 us
  Pallas kernels  21.9 us (45%)
  starting transfers between devices  12 us (24%)
  local copies, waits for them, and re-layouts  6.9 us (14%)
  between operations  4.77 us (10%)
  other arithmetic  1.96 us (4%)
  waiting for transfers between devices  1.01 us (2%)
    ppermute x4, starting transfers between devices, shift(): lax.ppermute(array, axis, [(i, (i + by) % size) for i in range(size)])  10 us
    pallas_call x1, Pallas kernels, on_device(): pl.pallas_call(project_kernel, out_shape=(shape((3 * heads, HEAD_DIM, tok...  8.54 us
    pallas_call x1, Pallas kernels, on_device(): pl.pallas_call(attend_kernel, out_shape=shape((branches, own_tokens, mode...  6.47 us
    pallas_call x1, Pallas kernels, on_device(): pl.pallas_call(finish_kernel, out_shape=tuple((shape((slab_cols, 2 * chan...  4.69 us
    pallas_call x2, local copies, waits for them, and re-layouts, on_device(): pl.pallas_call(blend_kernel, out_shape=tuple((shape((slab_cols, channels,...  3.06 us
    pallas_call x1, Pallas kernels, on_device(): pl.pallas_call(blend_kernel, out_shape=tuple((shape((slab_cols, channels,...  2.2 us
    unnamed x12, local copies, waits for them, and re-layouts  2.17 us
    ppermute x2, starting transfers between devices, swap(): return lax.ppermute(array, axis, [(0, 1), (1, 0)])  2.02 us
  transfers between devices with their start and end apart: 6, of which 1 were waited for; matrix products, arithmetic and copies ran while one was open for 7% of the time, Pallas kernels for 31%

profile of v1, /device:TPU:0, one launch (start us, length us, event | category | flops | bytes accessed | tf_op | source)
XLA Modules:
  0.0 48.6 jit_solution(4979877622839768818)
XLA Ops:
  0.6 0.5 %collective-permute-start = (f32[32,4,32]{2,1,0:T(4,128)}, f32[32,4,32]{2,1,0:T(4,128)S(1)}, u32[]{:S(2)}, u32[]{:S(2)}) collective-permute-start(f32[32,4,32]{2,1,0:T(4,128)} %latent_ref.1), channel_id=1, source_target_pairs={{0,1},{1,2},{2,3},{3,4},{4,5},{5,6},{6,7},{7,8},{8,9},{9,10},{10,1... | collective-permute-start | bytes 49160 | tf_op jit(solution)/shard_map/ppermute | solution.py:25
  1.2 5.0 %collective-permute-start.1 = (f32[32,4,32]{2,1,0:T(4,128)}, f32[32,4,32]{2,1,0:T(4,128)S(1)}, u32[]{:S(2)}, u32[]{:S(2)}) collective-permute-start(f32[32,4,32]{2,1,0:T(4,128)} %latent_ref.1), channel_id=1, source_target_pairs={{0,15},{1,0},{2,1},{3,2},{4,3},{5,4},{6,5},{7,6},{8,7},{9,8},{10,9... | collective-permute-start | bytes 49160 | tf_op jit(solution)/shard_map/ppermute | solution.py:25
  6.2 1.9 %collective-permute-start.3 = (bf16[288,1152]{1,0:T(8,128)(2,1)}, bf16[288,1152]{1,0:T(8,128)(2,1)S(1)}, u32[]{:S(2)}, u32[]{:S(2)}) collective-permute-start(bf16[288,1152]{1,0:T(8,128)(2,1)} %weight_ref.1), channel_id=1, source_target_pairs={{0,16},{16,0},{1,17},{17,1},{2,18},{18,2},{3,19},{19,3},{4,20},{20... | collective-permute-start | bytes 1990664 | tf_op jit(solution)/shard_map/ppermute | solution.py:29
  8.1 0.2 fusion
  8.3 0.1 fusion.2
  8.5 0.3 reduce-window.9
  8.7 0.1 slice.10
  8.8 0.1 slice_reduce_fusion
  10.3 0.7 %concatenate.7.col_ref = f32[32,1152]{1,0:T(8,128)} concatenate(f32[32,576]{1,0:T(8,128)S(1)} %broadcast_in_dim.17, f32[32,288]{1,0:T(8,128)S(1)} %get-tuple-element.21, f32[32,288]{1,0:T(8,128)S(1)} %get-tuple-element.20), dimensions={1} | concatenate | bytes 294912 | tf_op jit(solution)/shard_map/concatenate | solution.py:48
  11.0 0.7 %concatenate.6.row_ref = f32[16,1152]{1,0:T(8,128)} concatenate(f32[16,288]{1,0:T(8,128)S(1)} %get-tuple-element.23, f32[16,288]{1,0:T(8,128)S(1)} %get-tuple-element.22, f32[16,576]{1,0:T(8,128)S(1)} %broadcast_in_dim.16), dimensions={1} | concatenate | bytes 147456 | tf_op jit(solution)/shard_map/concatenate | solution.py:45
  11.8 0.0 collective-permute-done.before_ref
  11.8 0.0 copy-start.4
  11.8 0.0 collective-permute-done.1.after_ref
  11.8 0.0 copy-start.5
  11.8 0.6 %copy-done.4 = f32[32,4,32]{2,1,0:T(4,128)} copy-done((f32[32,4,32]{2,1,0:T(4,128)}, f32[32,4,32]{2,1,0:T(4,128)S(1)}, u32[]{:S(2)}) %copy-start.4) | copy-done | bytes 16408
  12.4 0.0 copy-done.5
  12.4 8.5 %project.1 = (bf16[12,72,512]{2,1,0:T(8,128)(2,1)}, f32[256,1152]{1,0:T(8,128)}, bf16[2,288,256]{2,1,0:T(8,128)(2,1)}) custom-call(s32[1]{0:T(128)} %copy.18.step_ref, s32[1]{0:T(128)} %bitcast.side_ref, s32[1]{0:T(128)S(6)} %copy.16.offset_ref, f32[20,4,1152]{2,1,0:T(4,128)} %modulation_ref.3, f32[32,4,32]{2,1,0:T(4,128)} %copy-done.4, ...), custom_call_target="tpu_custom_call" | custom-call | flops 2000000000 | bytes 8000000 | tf_op jit(solution)/shard_map/project/pallas_call | solution.py:331
  21.0 0.1 collective-permute-start.2
  21.0 0.1 add_bitcast_fusion
  21.1 0.6 %select_reduce_fusion = (f32[]{:T(128)}, f32[]{:T(128)}) fusion(f32[1024]{0:T(1024)S(1)} %add_bitcast_fusion, s32[]{:T(128)} %bitcast.14, s32[]{:T(128)S(6)} %sub.15), kind=kLoop, calls=%fused_computation.7 | loop fusion | flops 5998 | bytes 4016 | tf_op jit(solution)/shard_map/reduce_sum | solution.py:60
  24.5 6.5 %attend.1.mixed_ref = bf16[2,256,1152]{2,1,0:T(8,128)(2,1)} custom-call(s32[1]{0:T(128)} %bitcast.side_ref, bf16[12,72,512]{2,1,0:T(8,128)(2,1)} %get-tuple-element.9.proj_ref, bf16[2,2,288,120]{3,2,1,0:T(8,128)(2,1)} %bitcast.18, bf16[288,1152]{1,0:T(8,128)(2,1)} %weight_ref.1), custom_call_target="tpu_custom_call" | custom-call | flops 1000000000 | bytes 8000000 | tf_op jit(solution)/shard_map/attend/pallas_call | solution.py:352
  31.0 0.0 collective-permute-done.2.received_ref
  31.0 0.0 copy-start.1
  31.0 0.0 collective-permute-done.3.weight_ref
  31.0 0.0 copy-start
  31.0 0.7 %copy-done.1 = bf16[2,288,256]{2,1,0:T(8,128)(2,1)} copy-done((bf16[2,288,256]{2,1,0:T(8,128)(2,1)}, bf16[2,288,256]{2,1,0:T(8,128)(2,1)S(1)}, u32[]{:S(2)}) %copy-start.1) | copy-done | bytes 294936
  31.7 0.2 copy-done
  31.9 4.7 %finish.1 = (f32[32,128]{1,0:T(8,128)}, f32[32,128]{1,0:T(8,128)}, f32[32,128]{1,0:T(8,128)}) custom-call(s32[1]{0:T(128)} %copy.18.step_ref, s32[1]{0:T(128)S(6)} %copy.16.offset_ref, s32[1]{0:T(128)S(6)} %copy.17.blend_ref, f32[20,4,1152]{2,1,0:T(4,128)} %modulation_ref.3, f32[256,1152]{1,0:T(8,128)} %get-tuple-element.8.embedded_ref, ...), custom_call_target="tpu_custom_call" | custom-call | flops 1000000000 | bytes 4000000 | tf_op jit(solution)/shard_map/finish/pallas_call | solution.py:360
  36.6 0.0 collective-permute-start.4
  36.6 4.4 %collective-permute-start.5 = (f32[32,128]{1,0:T(8,128)}, f32[32,128]{1,0:T(8,128)S(1)}, u32[]{:S(2)}, u32[]{:S(2)}) collective-permute-start(f32[32,128]{1,0:T(8,128)} %get-tuple-element.13), channel_id=1, source_target_pairs={{0,15},{1,0},{2,1},{3,2},{4,3},{5,4},{6,5},{7,6},{8,7},{9,8},{10,9... | collective-permute-start | bytes 49160 | tf_op jit(solution)/shard_map/ppermute | solution.py:25
  41.0 0.6 %pad_maximum_fusion.plan_ref = f32[4]{0:T(128)} fusion(f32[1]{0:T(128)} %bitcast.7, f32[1]{0:T(128)} %bitcast.6, f32[1]{0:T(128)} %bitcast.5, f32[1]{0:T(128)} %bitcast.4), kind=kLoop, calls=%fused_computation.16 | loop fusion | flops 12 | bytes 32 | tf_op jit(solution)/shard_map/stack | solution.py:317
  41.7 1.0 %collective-permute-done.4.left_ref = f32[32,128]{1,0:T(8,128)S(1)} collective-permute-done((f32[32,128]{1,0:T(8,128)}, f32[32,128]{1,0:T(8,128)S(1)}, u32[]{:S(2)}, u32[]{:S(2)}) %collective-permute-start.4) | collective-permute-done | bytes 16416 | tf_op jit(solution)/shard_map/ppermute | solution.py:25
  42.7 0.0 copy-start.2
  42.7 0.0 collective-permute-done.5.right_ref
  42.7 0.0 copy-start.3
  42.7 0.6 %copy-done.2 = f32[32,128]{1,0:T(8,128)} copy-done((f32[32,128]{1,0:T(8,128)}, f32[32,128]{1,0:T(8,128)S(1)}, u32[]{:S(2)}) %copy-start.2) | copy-done | bytes 16408
  43.3 0.0 copy-done.3
  43.3 2.2 %blend.1 = (f32[32,4,16]{2,1,0:T(4,128)}, f32[32,4,16]{2,1,0:T(4,128)}) custom-call(s32[1]{0:T(128)} %bitcast.side_ref, f32[4]{0:T(128)} %pad_maximum_fusion.plan_ref, f32[32,128]{1,0:T(8,128)} %get-tuple-element.11.center_ref, f32[32,128]{1,0:T(8,128)} %copy-done.2, f32[32,128]{1,0:T(8,128)} %copy-done.3, f32[32,4,32]{2,1,0:T(4,128)} %latent_ref.1), custom_call_target="tpu_custom_call" | custom-call | tf_op jit(solution)/shard_map/blend/pallas_call | solution.py:378
  45.5 1.5 %copy.14 = f32[32,4,16]{0,2,1:T(8,128)} copy(f32[32,4,16]{2,1,0:T(4,128)} %get-tuple-element.16) | data formatting | bytes 16384 | tf_op jit(solution)/shard_map/blend/pallas_call | solution.py:378
  47.0 1.5 %copy.15 = f32[32,4,16]{0,2,1:T(8,128)} copy(f32[32,4,16]{2,1,0:T(4,128)} %get-tuple-element.17) | data formatting | bytes 16384 | tf_op jit(solution)/shard_map/blend/pallas_call | solution.py:378
  (6 shorter events, 0.1 us)
Async XLA Ops:
  0.6 11.1 %collective-permute-start = (f32[32,4,32]{2,1,0:T(4,128)}, f32[32,4,32]{2,1,0:T(4,128)S(1)}, u32[]{:S(2)}, u32[]{:S(2)}) collective-permute-start(f32[32,4,32]{2,1,0:T(4,128)} %latent_ref.1), channel_id=1, source_target_pairs={{0,1},{1,2},{2,3},{3,4},{4,5},{5,6},{6,7},{7,8},{8,9},{9,10},{10,1... | collective-permute-start | bytes 49160 | tf_op jit(solution)/shard_map/ppermute | solution.py:25
  1.2 10.6 %collective-permute-start.1 = (f32[32,4,32]{2,1,0:T(4,128)}, f32[32,4,32]{2,1,0:T(4,128)S(1)}, u32[]{:S(2)}, u32[]{:S(2)}) collective-permute-start(f32[32,4,32]{2,1,0:T(4,128)} %latent_ref.1), channel_id=1, source_target_pairs={{0,15},{1,0},{2,1},{3,2},{4,3},{5,4},{6,5},{7,6},{8,7},{9,8},{10,9... | collective-permute-start | bytes 49160 | tf_op jit(solution)/shard_map/ppermute | solution.py:25
  6.2 24.8 %collective-permute-start.3 = (bf16[288,1152]{1,0:T(8,128)(2,1)}, bf16[288,1152]{1,0:T(8,128)(2,1)S(1)}, u32[]{:S(2)}, u32[]{:S(2)}) collective-permute-start(bf16[288,1152]{1,0:T(8,128)(2,1)} %weight_ref.1), channel_id=1, source_target_pairs={{0,16},{16,0},{1,17},{17,1},{2,18},{18,2},{3,19},{19,3},{4,20},{20... | collective-permute-start | bytes 1990664 | tf_op jit(solution)/shard_map/ppermute | solution.py:29
  11.8 0.6 %copy-start.4 = (f32[32,4,32]{2,1,0:T(4,128)}, f32[32,4,32]{2,1,0:T(4,128)S(1)}, u32[]{:S(2)}) copy-start(f32[32,4,32]{2,1,0:T(4,128)S(1)} %collective-permute-done.before_ref) | copy-start | bytes 49156
  11.8 0.6 %copy-start.5 = (f32[32,4,32]{2,1,0:T(4,128)}, f32[32,4,32]{2,1,0:T(4,128)S(1)}, u32[]{:S(2)}) copy-start(f32[32,4,32]{2,1,0:T(4,128)S(1)} %collective-permute-done.1.after_ref) | copy-start | bytes 49156
  21.0 10.0 %collective-permute-start.2 = (bf16[2,288,256]{2,1,0:T(8,128)(2,1)}, bf16[2,288,256]{2,1,0:T(8,128)(2,1)S(1)}, u32[]{:S(2)}, u32[]{:S(2)}) collective-permute-start(bf16[2,288,256]{2,1,0:T(8,128)(2,1)} %get-tuple-element.10), channel_id=1, source_target_pairs={{0,16},{16,0},{1,17},{17,1},{2,18},{18,2},{3,19},{19,3},{4,20},{20... | collective-permute-start | bytes 884744 | tf_op jit(solution)/shard_map/ppermute | solution.py:29
  31.0 0.7 %copy-start.1 = (bf16[2,288,256]{2,1,0:T(8,128)(2,1)}, bf16[2,288,256]{2,1,0:T(8,128)(2,1)S(1)}, u32[]{:S(2)}) copy-start(bf16[2,288,256]{2,1,0:T(8,128)(2,1)S(1)} %collective-permute-done.2.received_ref) | copy-start | bytes 884740
  31.0 0.9 %copy-start = (bf16[288,1152]{1,0:T(8,128)(2,1)}, bf16[288,1152]{1,0:T(8,128)(2,1)S(1)}, u32[]{:S(2)}) copy-start(bf16[288,1152]{1,0:T(8,128)(2,1)S(1)} %collective-permute-done.3.weight_ref) | copy-start | bytes 1990660
  36.6 6.1 %collective-permute-start.4 = (f32[32,128]{1,0:T(8,128)}, f32[32,128]{1,0:T(8,128)S(1)}, u32[]{:S(2)}, u32[]{:S(2)}) collective-permute-start(f32[32,128]{1,0:T(8,128)} %get-tuple-element.12), channel_id=1, source_target_pairs={{0,1},{1,2},{2,3},{3,4},{4,5},{5,6},{6,7},{7,8},{8,9},{9,10},{10,1... | collective-permute-start | bytes 49160 | tf_op jit(solution)/shard_map/ppermute | solution.py:25
  36.6 6.1 %collective-permute-start.5 = (f32[32,128]{1,0:T(8,128)}, f32[32,128]{1,0:T(8,128)S(1)}, u32[]{:S(2)}, u32[]{:S(2)}) collective-permute-start(f32[32,128]{1,0:T(8,128)} %get-tuple-element.13), channel_id=1, source_target_pairs={{0,15},{1,0},{2,1},{3,2},{4,3},{5,4},{6,5},{7,6},{8,7},{9,8},{10,9... | collective-permute-start | bytes 49160 | tf_op jit(solution)/shard_map/ppermute | solution.py:25
  42.7 0.6 %copy-start.2 = (f32[32,128]{1,0:T(8,128)}, f32[32,128]{1,0:T(8,128)S(1)}, u32[]{:S(2)}) copy-start(f32[32,128]{1,0:T(8,128)S(1)} %collective-permute-done.4.left_ref) | copy-start | bytes 49156
  42.7 0.6 %copy-start.3 = (f32[32,128]{1,0:T(8,128)}, f32[32,128]{1,0:T(8,128)S(1)}, u32[]{:S(2)}) copy-start(f32[32,128]{1,0:T(8,128)S(1)} %collective-permute-done.5.right_ref) | copy-start | bytes 49156

commit v2 on v1

v2 whole, which is shorter than its diff:
```python
import math

import jax
import jax.numpy as jnp
from jax import lax
from jax.experimental import pallas as pl
from jax.experimental.pallas import tpu as pltpu
from jax.sharding import PartitionSpec as P


HEAD_DIM = 72
STEPS = 20


guidance_scale = 4.5
plan_length = 1000
norm_eps = 1e-06

VM = pl.BlockSpec(memory_space=pltpu.VMEM)
SM = pl.BlockSpec(memory_space=pltpu.SMEM)
GRANT = 24 * 2**20


def swap_ring(array, axis, odd):
    size = lax.axis_size(axis)
    pairs = []
    for left in range(odd, size, 2):
        right = (left + 1) % size
        pairs += [(left, right), (right, left)]
    return lax.ppermute(array, axis, pairs)


def swap(array, axis):
    return lax.ppermute(array, axis, [(0, 1), (1, 0)])


def layer_norm(values):
    average = jnp.mean(values, axis=-1, keepdims=True)
    centered = values - average
    variance = jnp.mean(centered * centered, axis=-1, keepdims=True)
    return centered * lax.rsqrt(variance + norm_eps)


def repeat_pairs(weight, repeats):
    rows, width = weight.shape
    values = weight.astype(jnp.float32)
    even = lax.broadcasted_iota(jnp.int32, (2 * repeats, width), 0) % 2 == 0
    parts = []
    for pair in range(rows // 2):
        parts.append(
            jnp.where(even, values[2 * pair : 2 * pair + 1, :], values[2 * pair + 1 : 2 * pair + 2, :])
        )
    return jnp.concatenate(parts, axis=0).astype(jnp.bfloat16)


def prepare_kernel(
    step_ref,
    blend_ref,
    latent_source,
    patch_source,
    modulation_ref,
    weight_ref,
    text_ref,
    out_ref,
    final_ref,
    position_ref,
    patch_wide_ref,
    plan_ref,
    rows_ref,
    modulate_copy,
    weight_copy,
    text_copy,
    out_copy,
    final_copy,
    latent_ref,
    patch_ref,
    semaphores,
):
    row = step_ref[0] * STEPS // plan_length
    copies = [
        pltpu.make_async_copy(source, target, semaphores.at[place])
        for place, (source, target) in enumerate(
            (
                (latent_source, latent_ref),
                (patch_source, patch_ref),
                (modulation_ref.at[row], modulate_copy),
                (weight_ref, weight_copy),
                (text_ref, text_copy),
                (out_ref, out_copy),
                (final_ref, final_copy),
            )
        )
    ]
    for copy in copies:
        copy.start()
    _, model_width = position_ref.shape
    slab_cols, channels, row_count = latent_ref.shape
    row_couples = row_count // 2
    quarter = model_width // 4

    def table(count, first):
        lane = lax.broadcasted_iota(jnp.int32, (count, model_width), 1)
        place = lax.broadcasted_iota(jnp.int32, (count, model_width), 0).astype(jnp.float32)
        frequency = jnp.exp(-math.log(10000.0) * (lane % quarter).astype(jnp.float32) / quarter)
        angle = place * frequency
        values = jnp.where(lane // quarter % 2 == 0, jnp.sin(angle), jnp.cos(angle))
        return jnp.where(lane // (2 * quarter) == first, values, 0.0)

    plan_ref[4:5, :] = jnp.full((1, plan_ref.shape[1]), blend_ref[0].astype(jnp.float32))
    row_part = table(row_couples, 0)
    col_part = table(slab_cols, 1)
    for couple in range(row_couples):
        position_ref[couple * slab_cols : (couple + 1) * slab_cols, :] = (
            row_part[couple : couple + 1, :] + col_part
        )
    copies[1].wait()
    patch_wide_ref[...] = repeat_pairs(patch_ref[...], row_couples)

    moment = step_ref[0]
    index = lax.broadcasted_iota(jnp.int32, (8, 128), 0) * 128 + lax.broadcasted_iota(
        jnp.int32, (8, 128), 1
    )
    train = jnp.minimum(index, plan_length - 1).astype(jnp.float32)
    beta_values = 0.0001 + (0.02 - 0.0001) * train / (plan_length - 1)
    logs = jnp.log(1.0 - beta_values)

    def alpha_bar(last):
        kept = jnp.where((index <= last) & (index < plan_length), logs, 0.0)
        kept = jnp.sum(jnp.sum(kept, axis=0, keepdims=True), axis=1, keepdims=True)
        return jnp.exp(kept)

    alpha_now = alpha_bar(moment)
    alpha_before = alpha_bar(moment - plan_length // STEPS)
    for place, value in enumerate(
        (
            jnp.sqrt(alpha_before),
            jnp.sqrt(1.0 - alpha_now),
            jnp.sqrt(alpha_now),
            jnp.sqrt(1.0 - alpha_before),
        )
    ):
        plan_ref[place : place + 1, :] = jnp.broadcast_to(value, (1, plan_ref.shape[1]))

    half_rows = row_count // 2
    side = lax.axis_index("cfg")
    copies[0].wait()
    for channel in range(channels):
        turned = jnp.transpose(latent_ref[:, channel, :], (1, 0))
        rows_ref[channel * half_rows : (channel + 1) * half_rows, :] = jnp.where(
            side == 0, turned[:half_rows], turned[half_rows:]
        )
    for copy in copies[2:]:
        copy.wait()


def attend(proj_ref, text_ref, first, count):
    heads = proj_ref.shape[0] // 3
    branches = text_ref.shape[0]
    factor = math.log2(math.e) / math.sqrt(HEAD_DIM)
    feature = (((0,), (0,)), ((), ()))
    results = [[] for _ in range(branches)]
    for head in range(heads):
        rows = slice(head * HEAD_DIM, (head + 1) * HEAD_DIM)
        queries = proj_ref[head, :, pl.ds(first, count)]
        own_scores = lax.dot_general(
            proj_ref[heads + head], queries, feature, preferred_element_type=jnp.float32
        )
        own_highest = jnp.max(own_scores, axis=0, keepdims=True)
        own_exp = jnp.exp2((own_scores - own_highest) * factor)
        own_total = jnp.sum(own_exp, axis=0, keepdims=True)
        own_mix = jnp.dot(
            proj_ref[2 * heads + head],
            own_exp.astype(jnp.bfloat16),
            preferred_element_type=jnp.float32,
        )
        for branch in range(branches):
            text_scores = lax.dot_general(
                text_ref[branch, 0, rows, :], queries, feature, preferred_element_type=jnp.float32
            )
            highest = jnp.maximum(own_highest, jnp.max(text_scores, axis=0, keepdims=True))
            text_exp = jnp.exp2((text_scores - highest) * factor)
            lowered = jnp.exp2((own_highest - highest) * factor)
            total = lowered * own_total + jnp.sum(text_exp, axis=0, keepdims=True)
            text_mix = jnp.dot(
                text_ref[branch, 1, rows, :],
                text_exp.astype(jnp.bfloat16),
                preferred_element_type=jnp.float32,
            )
            results[branch].append((lowered * own_mix + text_mix) * (1.0 / total))
    return [jnp.concatenate(parts, axis=0).astype(jnp.bfloat16) for parts in results]


def project_kernel(
    offset_ref,
    modulation_ref,
    near_ref,
    own_ref,
    far_ref,
    position_ref,
    patch_ref,
    weight_ref,
    text_ref,
    proj_ref,
    embedded_ref,
    sent_ref,
    extended_ref,
):
    slab_cols, channels, row_count = own_ref.shape
    col_pairs, row_couples = slab_cols, row_count // 2
    tokens = col_pairs * row_couples
    own_tokens = tokens // 2
    wide = 2 * channels * row_count
    even = lax.axis_index("win") % 2 == 0
    for channel in range(channels):
        near, far = near_ref[:, channel, :], far_ref[:, channel, :]
        values = (jnp.where(even, far, near), own_ref[:, channel, :], jnp.where(even, near, far))
        for place, value in enumerate(values):
            extended_ref[
                place * slab_cols : (place + 1) * slab_cols,
                channel * row_count : (channel + 1) * row_count,
            ] = value
    extended = extended_ref[...].astype(jnp.bfloat16)
    start_at = slab_cols - offset_ref[0]
    chosen = lax.broadcasted_iota(jnp.int32, (2 * col_pairs, 3 * slab_cols), 0)
    column = lax.broadcasted_iota(jnp.int32, (2 * col_pairs, 3 * slab_cols), 1)
    target = jnp.where(
        chosen < col_pairs, 2 * chosen, 2 * (chosen - col_pairs) + 1
    )
    pick = jnp.where(column == target + start_at, 1.0, 0.0).astype(jnp.bfloat16)
    picked = jnp.dot(pick, extended, preferred_element_type=jnp.float32)
    picked = jnp.concatenate([picked[:col_pairs], picked[col_pairs:]], axis=1)
    lane_couple = lax.broadcasted_iota(jnp.int32, (col_pairs, wide), 1) % row_count // 2
    spread = jnp.concatenate(
        [jnp.where(lane_couple == couple, picked, 0.0) for couple in range(row_couples)], axis=0
    ).astype(jnp.bfloat16)
    embedded = jnp.dot(spread, patch_ref[...], preferred_element_type=jnp.float32)
    embedded = embedded + position_ref[...]
    side = lax.axis_index("cfg")
    normed = (
        layer_norm(embedded) * (1.0 + modulation_ref[1:2, :]) + modulation_ref[0:1, :]
    ).astype(jnp.bfloat16)

    @pl.when(side == 0)
    def _():
        embedded_ref[...] = embedded[:own_tokens]

    @pl.when(side != 0)
    def _():
        embedded_ref[...] = embedded[own_tokens:]

    heads = proj_ref.shape[0] // 3
    for kind in range(3):
        projected = lax.dot_general(
            weight_ref[kind],
            normed,
            (((1,), (1,)), ((), ())),
            preferred_element_type=jnp.float32,
        )
        for head in range(heads):
            proj_ref[kind * heads + head] = projected[
                head * HEAD_DIM : (head + 1) * HEAD_DIM
            ].astype(jnp.bfloat16)
    first = pl.multiple_of((1 - side) * own_tokens, own_tokens)
    for branch, value in enumerate(attend(proj_ref, text_ref, first, own_tokens)):
        sent_ref[branch] = value


def attend_kernel(proj_ref, text_ref, weight_ref, mixed_ref):
    tokens = proj_ref.shape[2]
    own_tokens = tokens // 2
    first = pl.multiple_of(lax.axis_index("cfg") * own_tokens, own_tokens)
    for branch, value in enumerate(attend(proj_ref, text_ref, first, own_tokens)):
        mixed_ref[branch] = lax.dot_general(
            value, weight_ref[...], (((0,), (0,)), ((), ())), preferred_element_type=jnp.float32
        ).astype(jnp.bfloat16)


def finish_kernel(
    offset_ref,
    plan_ref,
    modulation_ref,
    embedded_ref,
    mixed_ref,
    received_ref,
    weight_ref,
    final_ref,
    near_ref,
    center_ref,
    far_ref,
    buffer_ref,
):
    slab_cols = center_ref.shape[0]
    col_pairs = slab_cols
    own_tokens = embedded_ref.shape[0]
    couples = own_tokens // col_pairs
    final_wide = repeat_pairs(final_ref[...], couples)
    wide = final_wide.shape[0]
    predicted = []
    for branch in range(2):
        other = lax.dot_general(
            received_ref[branch],
            weight_ref[...],
            (((0,), (0,)), ((), ())),
            preferred_element_type=jnp.float32,
        ).astype(jnp.bfloat16)
        mixed = mixed_ref[branch].astype(jnp.float32) + other.astype(jnp.float32)
        residual = embedded_ref[...] + modulation_ref[2:3, :] * mixed
        final_norm = (layer_norm(residual) * (1.0 + modulation_ref[3:4, :])).astype(jnp.bfloat16)
        predicted.append(
            lax.dot_general(
                final_norm,
                final_wide,
                (((1,), (1,)), ((), ())),
                preferred_element_type=jnp.float32,
            )
        )
    conditional, unconditional = predicted
    guided = unconditional + guidance_scale * (conditional - unconditional)
    lane_couple = lax.broadcasted_iota(jnp.int32, (col_pairs, wide), 1) % (2 * couples) // 2
    pairs = jnp.zeros((col_pairs, wide), jnp.float32)
    for couple in range(couples):
        pairs = pairs + jnp.where(
            lane_couple == couple, guided[couple * col_pairs : (couple + 1) * col_pairs], 0.0
        )
    weight_value = plan_ref[4:5, :wide]
    half = wide // 2
    is_noise = lax.broadcasted_iota(jnp.int32, (col_pairs, wide), 1) < half
    even = jnp.where(is_noise, weight_value * pairs, weight_value)
    odd = jnp.where(is_noise, weight_value * pltpu.roll(pairs, half, 1), weight_value)
    start_at = slab_cols - offset_ref[0]
    buffer_ref[...] = jnp.zeros_like(buffer_ref)
    buffer_ref[pl.ds(start_at, col_pairs, stride=2), :] = even
    buffer_ref[pl.ds(start_at + 1, col_pairs, stride=2), :] = odd
    center_ref[...] = buffer_ref[slab_cols : 2 * slab_cols]
    even_place = lax.axis_index("win") % 2 == 0
    left, right = buffer_ref[:slab_cols], buffer_ref[2 * slab_cols : 3 * slab_cols]
    near_ref[...] = jnp.where(even_place, right, left)
    far_ref[...] = jnp.where(even_place, left, right)


def blend_kernel(plan_ref, center_ref, near_ref, far_ref, rows_ref, previous_ref, noise_ref):
    channels, half_rows, slab_cols = noise_ref.shape
    total = jnp.transpose(center_ref[...] + near_ref[...] + far_ref[...], (1, 0))
    half = total.shape[0] // 2
    noise = total[:half] / total[half:]
    scale = plan_ref[:, :slab_cols]
    previous = (
        scale[0:1] * (rows_ref[...] - scale[1:2] * noise) / scale[2:3] + scale[3:4] * noise
    )
    for channel in range(channels):
        rows = slice(channel * half_rows, (channel + 1) * half_rows)
        noise_ref[channel] = noise[rows]
        previous_ref[channel] = previous[rows]


def on_device(
    latent,
    text_kv,
    modulation,
    qkv_weight,
    out_weight,
    patch_weight,
    final_weight,
    offsets,
    blend_weights,
    step_index,
):
    slab_cols, channels, row_count = latent.shape
    model_width = patch_weight.shape[1]
    half_attn = out_weight.shape[0]
    heads = half_attn // HEAD_DIM
    branches = text_kv.shape[0]
    col_pairs, row_couples = slab_cols, row_count // 2
    tokens = col_pairs * row_couples
    own_tokens = tokens // 2
    half_rows = row_count // 2
    far = swap_ring(latent, "win", 1)
    near = swap_ring(latent, "win", 0)
    other_weight = swap(out_weight, "cfg")

    weight = jnp.transpose(qkv_weight, (1, 2, 0))
    text = jnp.transpose(text_kv, (0, 1, 3, 2))
    final = jnp.transpose(final_weight, (1, 0))

    bf16, f32 = jnp.bfloat16, jnp.float32
    shape = jax.ShapeDtypeStruct
    wide = 2 * channels * half_rows
    position, patch_wide, plan_values, rows, modulate, weight, text, out_own, final, own = pl.pallas_call(
        prepare_kernel,
        out_shape=(
            shape((tokens, model_width), f32),
            shape((2 * channels * row_count, model_width), bf16),
            shape((8, max(wide, slab_cols)), f32),
            shape((channels * half_rows, slab_cols), f32),
            shape(modulation.shape[1:], f32),
            shape(weight.shape, bf16),
            shape(text.shape, bf16),
            shape(out_weight.shape, bf16),
            shape(final.shape, bf16),
            shape(latent.shape, f32),
        ),
        in_specs=[SM, SM] + [pl.BlockSpec(memory_space=pltpu.HBM)] * 7,
        out_specs=(VM,) * 10,
        scratch_shapes=[
            pltpu.VMEM(patch_weight.shape, bf16),
            pltpu.SemaphoreType.DMA((7,)),
        ],
        name="prepare",
        compiler_params=pltpu.CompilerParams(vmem_limit_bytes=GRANT),
        cost_estimate=pl.CostEstimate(flops=10**7, bytes_accessed=10**6, transcendentals=10**5),
    )(
        step_index,
        blend_weights,
        *(
            pltpu.with_memory_space_constraint(array, pltpu.HBM)
            for array in (latent, patch_weight, modulation, weight, text, out_weight, final)
        ),
    )
    projected, embedded, sent = pl.pallas_call(
        project_kernel,
        out_shape=(
            shape((3 * heads, HEAD_DIM, tokens), bf16),
            shape((own_tokens, model_width), f32),
            shape((branches, half_attn, own_tokens), bf16),
        ),
        in_specs=[SM] + [VM] * 8,
        out_specs=(VM, VM, VM),
        scratch_shapes=[pltpu.VMEM((3 * slab_cols, channels * row_count), f32)],
        name="project",
        compiler_params=pltpu.CompilerParams(vmem_limit_bytes=GRANT),
        cost_estimate=pl.CostEstimate(flops=2 * 10**9, bytes_accessed=8 * 10**6, transcendentals=10**6),
    )(offsets, modulate, near, own, far, position, patch_wide, weight, text)
    received = swap(sent, "cfg")
    mixed = pl.pallas_call(
        attend_kernel,
        out_shape=shape((branches, own_tokens, model_width), bf16),
        in_specs=[VM] * 3,
        out_specs=VM,
        name="attend",
        compiler_params=pltpu.CompilerParams(vmem_limit_bytes=GRANT),
        cost_estimate=pl.CostEstimate(flops=10**9, bytes_accessed=8 * 10**6, transcendentals=10**6),
    )(projected, text, out_own)
    to_near, center, to_far = pl.pallas_call(
        finish_kernel,
        out_shape=tuple(shape((slab_cols, wide), f32) for _ in range(3)),
        in_specs=[SM] + [VM] * 7,
        out_specs=(VM, VM, VM),
        scratch_shapes=[pltpu.VMEM((3 * slab_cols + 8, wide), f32)],
        name="finish",
        compiler_params=pltpu.CompilerParams(vmem_limit_bytes=GRANT),
        cost_estimate=pl.CostEstimate(flops=10**9, bytes_accessed=4 * 10**6, transcendentals=10**3),
    )(
        offsets, plan_values, modulate, embedded, mixed, received,
        other_weight, final,
    )
    from_far = swap_ring(to_far, "win", 1)
    from_near = swap_ring(to_near, "win", 0)
    previous, noise = pl.pallas_call(
        blend_kernel,
        out_shape=tuple(shape((channels, half_rows, slab_cols), f32) for _ in range(2)),
        in_specs=[VM] * 5,
        out_specs=(VM, VM),
        name="blend",
        compiler_params=pltpu.CompilerParams(vmem_limit_bytes=GRANT),
    )(plan_values, center, from_near, from_far, rows)
    return (jnp.transpose(previous, (2, 0, 1)), jnp.transpose(noise, (2, 0, 1)))


def solution(mesh):
    in_specs = (
        P("win", None, None),
        P(None, None, None, "cfg"),
        P(),
        P(None, None, "cfg"),
        P("cfg", None),
        P(),
        P(),
        P("win"),
        P("win"),
        P(),
    )
    out_specs = (P("win", None, "cfg"), P("win", None, "cfg"))
    return jax.shard_map(
        on_device, mesh=mesh, in_specs=in_specs, out_specs=out_specs, check_vma=False
    )
```

time: 49 us -> 34.4 us (0.70)
  Pallas kernels: 21.9 us -> 14.8 us
  local copies, waits for them, and re-layouts: 6.9 us -> 0 us
  waiting for transfers between devices: 1.01 us -> 3.85 us
  between operations: 4.77 us -> 2.63 us
  other arithmetic: 1.96 us -> 0 us
  starting transfers between devices: 12 us -> 12.9 us
    pallas_call x2 -> x0, local copies, waits for them, and re-layouts: 3.06 us -> none  [on_device(): pl.pallas_call(blend_kernel, out_shape=tuple((shape((slab_cols, channels,...]
    pallas_call x1, Pallas kernels: 8.54 us -> 5.91 us  [on_device(): pl.pallas_call(project_kernel, out_shape=(shape((3 * heads, HEAD_DIM, tok...]
    pallas_call x1, Pallas kernels: 6.47 us -> 3.99 us  [on_device(): pl.pallas_call(attend_kernel, out_shape=shape((branches, own_tokens, mode...]
    ppermute x2, waiting for transfers between devices: 0.01 us -> 2.4 us  [swap(): return lax.ppermute(array, axis, [(0, 1), (1, 0)])]
    unnamed x12 -> x0, local copies, waits for them, and re-layouts: 2.17 us -> none
    pallas_call x2 -> x3, Pallas kernels: 6.89 us -> 4.94 us  [the longest x1 2.28 us: on_device(): pl.pallas_call(finish_kernel, out_shape=tuple((shape((slab_cols, wide), f...]
    ppermute x2, starting transfers between devices: 2.02 us -> 3.65 us  [swap(): return lax.ppermute(array, axis, [(0, 1), (1, 0)])]
    concatenate x2 -> x0, local copies, waits for them, and re-layouts: 1.46 us -> none  [the longest x1 0.74 us: position_tables(): jnp.concatenate([jnp.zeros((col_pairs, half), jnp.float32), jnp.sin(col_p...]
  transfers between devices with their start and end apart: 6 -> 6, of which waited for: 1 -> 2; matrix products, arithmetic and copies ran while one was open for 7% -> 0% of each run, Pallas kernels for 31% -> 35%
where the time goes in v2:
time: 34.4 us; the launch traced here: 34.2 us
  Pallas kernels  14.8 us (43%)
  starting transfers between devices  12.9 us (38%)
  waiting for transfers between devices  3.85 us (11%)
  between operations  2.63 us (8%)
    ppermute x4, starting transfers between devices, swap_ring(): return lax.ppermute(array, axis, pairs)  9.22 us
    pallas_call x1, Pallas kernels, on_device(): pl.pallas_call(project_kernel, out_shape=(shape((3 * heads, HEAD_DIM, tok...  5.91 us
    pallas_call x1, Pallas kernels, on_device(): pl.pallas_call(attend_kernel, out_shape=shape((branches, own_tokens, mode...  3.99 us
    ppermute x2, starting transfers between devices, swap(): return lax.ppermute(array, axis, [(0, 1), (1, 0)])  3.65 us
    ppermute x2, waiting for transfers between devices, swap(): return lax.ppermute(array, axis, [(0, 1), (1, 0)])  2.4 us
    pallas_call x1, Pallas kernels, on_device(): pl.pallas_call(finish_kernel, out_shape=tuple((shape((slab_cols, wide), f...  2.28 us
    pallas_call x1, Pallas kernels, on_device(): pl.pallas_call(prepare_kernel, out_shape=(shape((tokens, model_width), f3...  1.92 us
    ppermute x4, waiting for transfers between devices, swap_ring(): return lax.ppermute(array, axis, pairs)  1.45 us
  transfers between devices with their start and end apart: 6, of which 2 were waited for; matrix products, arithmetic and copies ran while one was open for 0% of the time, Pallas kernels for 35%

profile of v2, /device:TPU:0, one launch (start us, length us, event | category | flops | bytes accessed | tf_op | source)
XLA Modules:
  0.0 34.2 jit_solution(9107735409246299740)
XLA Ops:
  0.6 3.1 %collective-permute-start.3 = (bf16[288,1152]{1,0:T(8,128)(2,1)}, bf16[288,1152]{1,0:T(8,128)(2,1)S(1)}, u32[]{:S(2)}, u32[]{:S(2)}) collective-permute-start(bf16[288,1152]{1,0:T(8,128)(2,1)} %out_ref.1), channel_id=1, source_target_pairs={{0,16},{16,0},{1,17},{17,1},{2,18},{18,2},{3,19},{19,3},{4,20},{20... | collective-permute-start | bytes 1990664 | tf_op jit(solution)/shard_map/ppermute | solution.py:34
  3.7 0.0 collective-permute-start
  3.7 4.6 %collective-permute-start.1 = (f32[32,4,32]{2,1,0:T(4,128)}, f32[32,4,32]{2,1,0:T(4,128)S(1)}, u32[]{:S(2)}, u32[]{:S(2)}) collective-permute-start(f32[32,4,32]{2,1,0:T(4,128)} %latent_source.1), channel_id=1, source_target_pairs={{1,2},{2,1},{3,4},{4,3},{5,6},{6,5},{7,8},{8,7},{9,10},{10,9},{11,... | collective-permute-start | bytes 49160 | tf_op jit(solution)/shard_map/ppermute | solution.py:30
  10.3 1.9 %prepare.1 = (f32[512,1152]{1,0:T(8,128)S(1)}, bf16[256,1152]{1,0:T(8,128)(2,1)S(1)}, f32[8,128]{1,0:T(8,128)S(1)}, f32[64,32]{1,0:T(8,128)S(1)}, f32[4,1152]{1,...) custom-call(s32[1]{0:T(128)S(6)} %copy.14.step_ref, ...), custom_call_target="tpu_custom_call" | custom-call | flops 10000000 | bytes 1000000 | tf_op jit(solution)/shard_map/prepare/pallas_call | solution.py:388
  12.2 0.0 collective-permute-done.near_ref
  12.2 0.0 collective-permute-done.1.far_ref
  12.2 5.9 %project.1 = (bf16[12,72,512]{2,1,0:T(8,128)(2,1)S(1)}, f32[256,1152]{1,0:T(8,128)S(1)}, bf16[2,288,256]{2,1,0:T(8,128)(2,1)S(1)}) custom-call(s32[1]{0:T(128)S(6)} %copy.12.offset_ref, f32[4,1152]{1,0:T(4,128)S(1)} %get-tuple-element.21.modulation_ref, f32[32,4,32]{2,1,0:T(4,128)S(1)} %collective-permute-done.near_ref, ...), custom_call_target="tpu_custom_call" | custom-call | flops 2000000000 | bytes 8000000 | tf_op jit(solution)/shard_map/project/pallas_call | solution.py:419
  18.1 0.6 %collective-permute-start.2 = (bf16[2,288,256]{2,1,0:T(8,128)(2,1)S(1)}, bf16[2,288,256]{2,1,0:T(8,128)(2,1)S(1)}, u32[]{:S(2)}, u32[]{:S(2)}) collective-permute-start(bf16[2,288,256]{2,1,0:T(8,128)(2,1)S(1)} %get-tuple-element.30), channel_id=1, source_target_pairs={{0,16},{16,0},{1,17},{17,1},{2,18},{18,2},{3,19},{19,3},{4,20},{20... | collective-permute-start | bytes 884744 | tf_op jit(solution)/shard_map/ppermute | solution.py:34
  18.7 4.0 %attend.1.mixed_ref = bf16[2,256,1152]{2,1,0:T(8,128)(2,1)S(1)} custom-call(bf16[12,72,512]{2,1,0:T(8,128)(2,1)S(1)} %get-tuple-element.28.proj_ref, bf16[2,2,288,120]{3,2,1,0:T(8,128)(2,1)S(1)} %get-tuple-element.26.text_ref, bf16[288,1152]{1,0:T(8,128)(2,1)S(1)} %get-tuple-element.29.weight_ref), custom_call_target="tpu_custom_call" | custom-call | flops 1000000000 | bytes 8000000 | tf_op jit(solution)/shard_map/attend/pallas_call | solution.py:434
  22.7 2.4 %collective-permute-done.2.received_ref = bf16[2,288,256]{2,1,0:T(8,128)(2,1)S(1)} collective-permute-done((bf16[2,288,256]{2,1,0:T(8,128)(2,1)S(1)}, bf16[2,288,256]{2,1,0:T(8,128)(2,1)S(1)}, u32[]{:S(2)}, u32[]{:S(2)}) %collective-permute-start.2) | collective-permute-done | bytes 294944 | tf_op jit(solution)/shard_map/ppermute | solution.py:34
  25.1 0.0 collective-permute-done.3.weight_ref
  25.1 2.3 %finish.1 = (f32[32,128]{1,0:T(8,128)S(1)}, f32[32,128]{1,0:T(8,128)S(1)}, f32[32,128]{1,0:T(8,128)S(1)}) custom-call(s32[1]{0:T(128)S(6)} %copy.12.offset_ref, f32[8,128]{1,0:T(8,128)S(1)} %get-tuple-element.20.plan_ref, f32[4,1152]{1,0:T(4,128)S(1)} %get-tuple-element.21.modulation_ref, f32[256,1152]{1,0:T(8,128)S(1)} %get-tuple-element.27.embedded_ref, ...), custom_call_target="tpu_custom_call" | custom-call | flops 1000000000 | bytes 4000000 | tf_op jit(solution)/shard_map/finish/pallas_call | solution.py:443
  27.4 0.1 collective-permute-start.4
  27.5 4.5 %collective-permute-start.5 = (f32[32,128]{1,0:T(8,128)S(1)}, f32[32,128]{1,0:T(8,128)S(1)}, u32[]{:S(2)}, u32[]{:S(2)}) collective-permute-start(f32[32,128]{1,0:T(8,128)S(1)} %get-tuple-element.34), channel_id=1, source_target_pairs={{1,2},{2,1},{3,4},{4,3},{5,6},{6,5},{7,8},{8,7},{9,10},{10,9},{11,... | collective-permute-start | bytes 49160 | tf_op jit(solution)/shard_map/ppermute | solution.py:30
  32.0 0.0 collective-permute-done.4.near_ref
  32.0 1.4 %collective-permute-done.5.far_ref = f32[32,128]{1,0:T(8,128)S(1)} collective-permute-done((f32[32,128]{1,0:T(8,128)S(1)}, f32[32,128]{1,0:T(8,128)S(1)}, u32[]{:S(2)}, u32[]{:S(2)}) %collective-permute-start.5) | collective-permute-done | bytes 16416 | tf_op jit(solution)/shard_map/ppermute | solution.py:30
  33.4 0.7 %blend.1 = (f32[4,16,32]{2,1,0:T(8,128)}, f32[4,16,32]{2,1,0:T(8,128)}) custom-call(f32[8,128]{1,0:T(8,128)S(1)} %get-tuple-element.20.plan_ref, f32[32,128]{1,0:T(8,128)S(1)} %get-tuple-element.32.center_ref, f32[32,128]{1,0:T(8,128)S(1)} %collective-permute-done.4.near_ref, f32[32,128]{1,0:T(8,128)S(1)} %collective-permute-done.5.far_ref, ...), custom_call_target="tpu_custom_call" | custom-call | tf_op jit(solution)/shard_map/blend/pallas_call | solution.py:458
Async XLA Ops:
  0.6 24.5 %collective-permute-start.3 = (bf16[288,1152]{1,0:T(8,128)(2,1)}, bf16[288,1152]{1,0:T(8,128)(2,1)S(1)}, u32[]{:S(2)}, u32[]{:S(2)}) collective-permute-start(bf16[288,1152]{1,0:T(8,128)(2,1)} %out_ref.1), channel_id=1, source_target_pairs={{0,16},{16,0},{1,17},{17,1},{2,18},{18,2},{3,19},{19,3},{4,20},{20... | collective-permute-start | bytes 1990664 | tf_op jit(solution)/shard_map/ppermute | solution.py:34
  3.7 8.5 %collective-permute-start = (f32[32,4,32]{2,1,0:T(4,128)}, f32[32,4,32]{2,1,0:T(4,128)S(1)}, u32[]{:S(2)}, u32[]{:S(2)}) collective-permute-start(f32[32,4,32]{2,1,0:T(4,128)} %latent_source.1), channel_id=1, source_target_pairs={{0,1},{1,0},{2,3},{3,2},{4,5},{5,4},{6,7},{7,6},{8,9},{9,8},{10,11... | collective-permute-start | bytes 49160 | tf_op jit(solution)/shard_map/ppermute | solution.py:30
  3.7 8.5 %collective-permute-start.1 = (f32[32,4,32]{2,1,0:T(4,128)}, f32[32,4,32]{2,1,0:T(4,128)S(1)}, u32[]{:S(2)}, u32[]{:S(2)}) collective-permute-start(f32[32,4,32]{2,1,0:T(4,128)} %latent_source.1), channel_id=1, source_target_pairs={{1,2},{2,1},{3,4},{4,3},{5,6},{6,5},{7,8},{8,7},{9,10},{10,9},{11,... | collective-permute-start | bytes 49160 | tf_op jit(solution)/shard_map/ppermute | solution.py:30
  18.1 7.0 %collective-permute-start.2 = (bf16[2,288,256]{2,1,0:T(8,128)(2,1)S(1)}, bf16[2,288,256]{2,1,0:T(8,128)(2,1)S(1)}, u32[]{:S(2)}, u32[]{:S(2)}) collective-permute-start(bf16[2,288,256]{2,1,0:T(8,128)(2,1)S(1)} %get-tuple-element.30), channel_id=1, source_target_pairs={{0,16},{16,0},{1,17},{17,1},{2,18},{18,2},{3,19},{19,3},{4,20},{20... | collective-permute-start | bytes 884744 | tf_op jit(solution)/shard_map/ppermute | solution.py:34
  27.4 4.6 %collective-permute-start.4 = (f32[32,128]{1,0:T(8,128)S(1)}, f32[32,128]{1,0:T(8,128)S(1)}, u32[]{:S(2)}, u32[]{:S(2)}) collective-permute-start(f32[32,128]{1,0:T(8,128)S(1)} %get-tuple-element.33), channel_id=1, source_target_pairs={{0,1},{1,0},{2,3},{3,2},{4,5},{5,4},{6,7},{7,6},{8,9},{9,8},{10,11... | collective-permute-start | bytes 49160 | tf_op jit(solution)/shard_map/ppermute | solution.py:30
  27.5 6.0 %collective-permute-start.5 = (f32[32,128]{1,0:T(8,128)S(1)}, f32[32,128]{1,0:T(8,128)S(1)}, u32[]{:S(2)}, u32[]{:S(2)}) collective-permute-start(f32[32,128]{1,0:T(8,128)S(1)} %get-tuple-element.34), channel_id=1, source_target_pairs={{1,2},{2,1},{3,4},{4,3},{5,6},{6,5},{7,8},{8,7},{9,10},{10,9},{11,... | collective-permute-start | bytes 49160 | tf_op jit(solution)/shard_map/ppermute | solution.py:30

commit v3 on v2

--- a/solution.py
+++ b/solution.py
@@ -1,3 +1,4 @@
+import functools
 import math
 
 import jax
@@ -53,9 +54,16 @@
     return jnp.concatenate(parts, axis=0).astype(jnp.bfloat16)
 
 
+def cut_kernel(weight_ref, part_ref, semaphore):
+    count = part_ref.shape[0]
+    first = pl.multiple_of(lax.axis_index("win") % 2 * count, count)
+    copy = pltpu.make_async_copy(weight_ref.at[pl.ds(first, count)], part_ref, semaphore)
+    copy.start()
+    copy.wait()
+
+
 def prepare_kernel(
     step_ref,
-    blend_ref,
     latent_source,
     patch_source,
     modulation_ref,
@@ -98,21 +106,27 @@
     row_couples = row_count // 2
     quarter = model_width // 4
 
-    def table(count, first):
-        lane = lax.broadcasted_iota(jnp.int32, (count, model_width), 1)
-        place = lax.broadcasted_iota(jnp.int32, (count, model_width), 0).astype(jnp.float32)
+    half = 2 * quarter
+
+    def table(count, first, lanes):
+        lane = first + lax.broadcasted_iota(jnp.int32, (count, lanes), 1)
+        place = lax.broadcasted_iota(jnp.int32, (count, lanes), 0).astype(jnp.float32)
         frequency = jnp.exp(-math.log(10000.0) * (lane % quarter).astype(jnp.float32) / quarter)
-        angle = place * frequency
-        values = jnp.where(lane // quarter % 2 == 0, jnp.sin(angle), jnp.cos(angle))
-        return jnp.where(lane // (2 * quarter) == first, values, 0.0)
-
-    plan_ref[4:5, :] = jnp.full((1, plan_ref.shape[1]), blend_ref[0].astype(jnp.float32))
-    row_part = table(row_couples, 0)
-    col_part = table(slab_cols, 1)
+        phase = jnp.where(lane // quarter % 2 == 0, 0.0, 0.5 * math.pi)
+        return jnp.sin(place * frequency + phase)
+
+    below, above = half // 128 * 128, -(-half // 128) * 128
+    row_part = table(row_couples, 0, above)
+    col_part = table(slab_cols, below, model_width - below)
+    lane = below + lax.broadcasted_iota(jnp.int32, (slab_cols, above - below), 1)
     for couple in range(row_couples):
-        position_ref[couple * slab_cols : (couple + 1) * slab_cols, :] = (
-            row_part[couple : couple + 1, :] + col_part
-        )
+        rows = slice(couple * slab_cols, (couple + 1) * slab_cols)
+        line = jnp.broadcast_to(row_part[couple : couple + 1, :], (slab_cols, above))
+        position_ref[rows, :below] = line[:, :below]
+        position_ref[rows, below:above] = jnp.where(
+            lane < half, line[:, below:], col_part[:, : above - below]
+        )
+        position_ref[rows, above:] = col_part[:, above - below :]
     copies[1].wait()
     patch_wide_ref[...] = repeat_pairs(patch_ref[...], row_couples)
 
@@ -277,18 +291,24 @@
 
 def finish_kernel(
     offset_ref,
-    plan_ref,
+    blend_ref,
     modulation_ref,
     embedded_ref,
     mixed_ref,
     received_ref,
     weight_ref,
+    neighbour_ref,
     final_ref,
     near_ref,
     center_ref,
     far_ref,
     buffer_ref,
 ):
+    count = weight_ref.shape[0]
+    parity = lax.axis_index("win") % 2
+    mine = pl.multiple_of(parity * count, count)
+    theirs = pl.multiple_of((1 - parity) * count, count)
+    feature = (((0,), (0,)), ((), ()))
     slab_cols = center_ref.shape[0]
     col_pairs = slab_cols
     own_tokens = embedded_ref.shape[0]
@@ -298,12 +318,17 @@
     predicted = []
     for branch in range(2):
         other = lax.dot_general(
-            received_ref[branch],
+            received_ref[branch, pl.ds(mine, count), :],
             weight_ref[...],
-            (((0,), (0,)), ((), ())),
+            feature,
             preferred_element_type=jnp.float32,
-        ).astype(jnp.bfloat16)
-        mixed = mixed_ref[branch].astype(jnp.float32) + other.astype(jnp.float32)
+        ) + lax.dot_general(
+            received_ref[branch, pl.ds(theirs, count), :],
+            neighbour_ref[...],
+            feature,
+            preferred_element_type=jnp.float32,
+        )
+        mixed = mixed_ref[branch].astype(jnp.float32) + other
         residual = embedded_ref[...] + modulation_ref[2:3, :] * mixed
         final_norm = (layer_norm(residual) * (1.0 + modulation_ref[3:4, :])).astype(jnp.bfloat16)
         predicted.append(
@@ -322,7 +347,7 @@
         pairs = pairs + jnp.where(
             lane_couple == couple, guided[couple * col_pairs : (couple + 1) * col_pairs], 0.0
         )
-    weight_value = plan_ref[4:5, :wide]
+    weight_value = blend_ref[0].astype(jnp.float32)
     half = wide // 2
     is_noise = lax.broadcasted_iota(jnp.int32, (col_pairs, wide), 1) < half
     even = jnp.where(is_noise, weight_value * pairs, weight_value)
@@ -376,7 +401,18 @@
     half_rows = row_count // 2
     far = swap_ring(latent, "win", 1)
     near = swap_ring(latent, "win", 0)
-    other_weight = swap(out_weight, "cfg")
+    hbm = pl.BlockSpec(memory_space=pltpu.HBM)
+    keep = functools.partial(pltpu.with_memory_space_constraint, memory_space=pltpu.HBM)
+    part = pl.pallas_call(
+        cut_kernel,
+        out_shape=jax.ShapeDtypeStruct((half_attn // 2, model_width), out_weight.dtype),
+        in_specs=[hbm],
+        out_specs=VM,
+        scratch_shapes=[pltpu.SemaphoreType.DMA],
+        name="cut",
+        compiler_params=pltpu.CompilerParams(vmem_limit_bytes=GRANT),
+    )(keep(out_weight))
+    other_weight = swap(part, "cfg")
 
     weight = jnp.transpose(qkv_weight, (1, 2, 0))
     text = jnp.transpose(text_kv, (0, 1, 3, 2))
@@ -399,7 +435,7 @@
             shape(final.shape, bf16),
             shape(latent.shape, f32),
         ),
-        in_specs=[SM, SM] + [pl.BlockSpec(memory_space=pltpu.HBM)] * 7,
+        in_specs=[SM] + [hbm] * 7,
         out_specs=(VM,) * 10,
         scratch_shapes=[
             pltpu.VMEM(patch_weight.shape, bf16),
@@ -410,11 +446,7 @@
         cost_estimate=pl.CostEstimate(flops=10**7, bytes_accessed=10**6, transcendentals=10**5),
     )(
         step_index,
-        blend_weights,
-        *(
-            pltpu.with_memory_space_constraint(array, pltpu.HBM)
-            for array in (latent, patch_weight, modulation, weight, text, out_weight, final)
-        ),
+        *map(keep, (latent, patch_weight, modulation, weight, text, out_weight, final)),
     )
     projected, embedded, sent = pl.pallas_call(
         project_kernel,
@@ -431,6 +463,7 @@
         cost_estimate=pl.CostEstimate(flops=2 * 10**9, bytes_accessed=8 * 10**6, transcendentals=10**6),
     )(offsets, modulate, near, own, far, position, patch_wide, weight, text)
     received = swap(sent, "cfg")
+    neighbour_weight = swap_ring(other_weight, "win", 0)
     mixed = pl.pallas_call(
         attend_kernel,
         out_shape=shape((branches, own_tokens, model_width), bf16),
@@ -443,15 +476,15 @@
     to_near, center, to_far = pl.pallas_call(
         finish_kernel,
         out_shape=tuple(shape((slab_cols, wide), f32) for _ in range(3)),
-        in_specs=[SM] + [VM] * 7,
+        in_specs=[SM, SM] + [VM] * 7,
         out_specs=(VM, VM, VM),
         scratch_shapes=[pltpu.VMEM((3 * slab_cols + 8, wide), f32)],
         name="finish",
         compiler_params=pltpu.CompilerParams(vmem_limit_bytes=GRANT),
         cost_estimate=pl.CostEstimate(flops=10**9, bytes_accessed=4 * 10**6, transcendentals=10**3),
     )(
-        offsets, plan_values, modulate, embedded, mixed, received,
-        other_weight, final,
+        offsets, blend_weights, modulate, embedded, mixed, received,
+        other_weight, neighbour_weight, final,
     )
     from_far = swap_ring(to_far, "win", 1)
     from_near = swap_ring(to_near, "win", 0)

time: 34.4 us -> 37.6 us (1.093)
  starting transfers between devices: 12.9 us -> 14.2 us
  Pallas kernels: 14.8 us -> 16 us
  waiting for transfers between devices: 3.85 us -> 4.64 us
    ppermute x2, starting transfers between devices: 3.65 us -> 4.7 us  [swap(): return lax.ppermute(array, axis, [(0, 1), (1, 0)])]
    pallas_call x0 -> x1, Pallas kernels: none -> 1 us  [on_device(): pl.pallas_call(cut_kernel, out_shape=jax.ShapeDtypeStruct((half_attn // 2...]
    ppermute x2, waiting for transfers between devices: 2.4 us -> 3.19 us  [swap(): return lax.ppermute(array, axis, [(0, 1), (1, 0)])]
    ppermute x4 -> x5, starting transfers between devices: 9.22 us -> 9.48 us  [swap_ring(): return lax.ppermute(array, axis, pairs)]
    ppermute x4 -> x5, waiting for transfers between devices: 1.45 us -> 1.45 us  [swap_ring(): return lax.ppermute(array, axis, pairs)]
  transfers between devices with their start and end apart: 6 -> 7, of which waited for: 2 -> 2; matrix products, arithmetic and copies ran while one was open for 0% -> 0% of each run, Pallas kernels for 35% -> 32%
where the time goes in v3:
time: 37.6 us; the launch traced here: 37.4 us
  Pallas kernels  16 us (43%)
  starting transfers between devices  14.2 us (38%)
  waiting for transfers between devices  4.64 us (12%)
  between operations  2.65 us (7%)
    ppermute x5, starting transfers between devices, swap_ring(): return lax.ppermute(array, axis, pairs)  9.48 us
    pallas_call x1, Pallas kernels, on_device(): pl.pallas_call(project_kernel, out_shape=(shape((3 * heads, HEAD_DIM, tok...  5.91 us
    ppermute x2, starting transfers between devices, swap(): return lax.ppermute(array, axis, [(0, 1), (1, 0)])  4.7 us
    pallas_call x1, Pallas kernels, on_device(): pl.pallas_call(attend_kernel, out_shape=shape((branches, own_tokens, mode...  3.99 us
    ppermute x2, waiting for transfers between devices, swap(): return lax.ppermute(array, axis, [(0, 1), (1, 0)])  3.19 us
    pallas_call x1, Pallas kernels, on_device(): pl.pallas_call(finish_kernel, out_shape=tuple((shape((slab_cols, wide), f...  2.39 us
    pallas_call x1, Pallas kernels, on_device(): pl.pallas_call(prepare_kernel, out_shape=(shape((tokens, model_width), f3...  1.93 us
    ppermute x5, waiting for transfers between devices, swap_ring(): return lax.ppermute(array, axis, pairs)  1.45 us
  transfers between devices with their start and end apart: 7, of which 2 were waited for; matrix products, arithmetic and copies ran while one was open for 0% of the time, Pallas kernels for 32%

profile of v3, /device:TPU:0, one launch (start us, length us, event | category | flops | bytes accessed | tf_op | source)
XLA Modules:
  0.0 37.4 jit_solution(9403250502527483582)
XLA Ops:
  0.6 1.0 %cut.1 = bf16[144,1152]{1,0:T(8,128)(2,1)S(1)} custom-call(bf16[288,1152]{1,0:T(8,128)(2,1)} %weight_ref.1), custom_call_target="tpu_custom_call" | custom-call | tf_op jit(solution)/shard_map/cut/pallas_call | solution.py:406
  1.6 3.1 %collective-permute-start.3 = (bf16[144,1152]{1,0:T(8,128)(2,1)S(1)}, bf16[144,1152]{1,0:T(8,128)(2,1)S(1)}, u32[]{:S(2)}, u32[]{:S(2)}) collective-permute-start(bf16[144,1152]{1,0:T(8,128)(2,1)S(1)} %cut.1), channel_id=1, source_target_pairs={{0,16},{16,0},{1,17},{17,1},{2,18},{18,2},{3,19},{19,3},{4,20},{20... | collective-permute-start | bytes 995336 | tf_op jit(solution)/shard_map/ppermute | solution.py:35
  4.7 0.0 collective-permute-start
  4.7 4.6 %collective-permute-start.1 = (f32[32,4,32]{2,1,0:T(4,128)}, f32[32,4,32]{2,1,0:T(4,128)S(1)}, u32[]{:S(2)}, u32[]{:S(2)}) collective-permute-start(f32[32,4,32]{2,1,0:T(4,128)} %latent_source.1), channel_id=1, source_target_pairs={{1,2},{2,1},{3,4},{4,3},{5,6},{6,5},{7,8},{8,7},{9,10},{10,9},{11,... | collective-permute-start | bytes 49160 | tf_op jit(solution)/shard_map/ppermute | solution.py:31
  10.6 1.9 %prepare.1 = (f32[512,1152]{1,0:T(8,128)S(1)}, bf16[256,1152]{1,0:T(8,128)(2,1)S(1)}, f32[8,128]{1,0:T(8,128)S(1)}, f32[64,32]{1,0:T(8,128)S(1)}, f32[4,1152]{1,...) custom-call(s32[1]{0:T(128)S(6)} %copy.14.step_ref, ...), custom_call_target="tpu_custom_call" | custom-call | flops 10000000 | bytes 1000000 | tf_op jit(solution)/shard_map/prepare/pallas_call | solution.py:424
  12.6 0.0 collective-permute-done.3.weight_ref
  12.6 0.1 collective-permute-start.4
  12.7 0.0 collective-permute-done.near_ref
  12.7 0.0 collective-permute-done.1.far_ref
  12.7 5.9 %project.1 = (bf16[12,72,512]{2,1,0:T(8,128)(2,1)S(1)}, f32[256,1152]{1,0:T(8,128)S(1)}, bf16[2,288,256]{2,1,0:T(8,128)(2,1)S(1)}) custom-call(s32[1]{0:T(128)S(6)} %copy.12.offset_ref, f32[4,1152]{1,0:T(4,128)S(1)} %get-tuple-element.21.modulation_ref, f32[32,4,32]{2,1,0:T(4,128)S(1)} %collective-permute-done.near_ref, ...), custom_call_target="tpu_custom_call" | custom-call | flops 2000000000 | bytes 8000000 | tf_op jit(solution)/shard_map/project/pallas_call | solution.py:451
  18.6 1.6 %collective-permute-start.2 = (bf16[2,288,256]{2,1,0:T(8,128)(2,1)S(1)}, bf16[2,288,256]{2,1,0:T(8,128)(2,1)S(1)}, u32[]{:S(2)}, u32[]{:S(2)}) collective-permute-start(bf16[2,288,256]{2,1,0:T(8,128)(2,1)S(1)} %get-tuple-element.30), channel_id=1, source_target_pairs={{0,16},{16,0},{1,17},{17,1},{2,18},{18,2},{3,19},{19,3},{4,20},{20... | collective-permute-start | bytes 884744 | tf_op jit(solution)/shard_map/ppermute | solution.py:35
  20.9 4.0 %attend.1.mixed_ref = bf16[2,256,1152]{2,1,0:T(8,128)(2,1)S(1)} custom-call(bf16[12,72,512]{2,1,0:T(8,128)(2,1)S(1)} %get-tuple-element.28.proj_ref, bf16[2,2,288,120]{3,2,1,0:T(8,128)(2,1)S(1)} %get-tuple-element.26.text_ref, bf16[288,1152]{1,0:T(8,128)(2,1)S(1)} %get-tuple-element.29.weight_ref), custom_call_target="tpu_custom_call" | custom-call | flops 1000000000 | bytes 8000000 | tf_op jit(solution)/shard_map/attend/pallas_call | solution.py:467
  24.9 3.2 %collective-permute-done.2.received_ref = bf16[2,288,256]{2,1,0:T(8,128)(2,1)S(1)} collective-permute-done((bf16[2,288,256]{2,1,0:T(8,128)(2,1)S(1)}, bf16[2,288,256]{2,1,0:T(8,128)(2,1)S(1)}, u32[]{:S(2)}, u32[]{:S(2)}) %collective-permute-start.2) | collective-permute-done | bytes 294944 | tf_op jit(solution)/shard_map/ppermute | solution.py:35
  28.1 0.0 collective-permute-done.4.neighbour_ref
  28.1 2.4 %finish.1 = (f32[32,128]{1,0:T(8,128)S(1)}, f32[32,128]{1,0:T(8,128)S(1)}, f32[32,128]{1,0:T(8,128)S(1)}) custom-call(s32[1]{0:T(128)S(6)} %copy.12.offset_ref, s32[1]{0:T(128)S(6)} %copy.13.blend_ref, f32[4,1152]{1,0:T(4,128)S(1)} %get-tuple-element.21.modulation_ref, f32[256,1152]{1,0:T(8,128)S(1)} %get-tuple-element.27.embedded_ref, ...), custom_call_target="tpu_custom_call" | custom-call | flops 1000000000 | bytes 4000000 | tf_op jit(solution)/shard_map/finish/pallas_call | solution.py:476
  30.5 0.1 collective-permute-start.5
  30.5 4.7 %collective-permute-start.6 = (f32[32,128]{1,0:T(8,128)S(1)}, f32[32,128]{1,0:T(8,128)S(1)}, u32[]{:S(2)}, u32[]{:S(2)}) collective-permute-start(f32[32,128]{1,0:T(8,128)S(1)} %get-tuple-element.34), channel_id=1, source_target_pairs={{1,2},{2,1},{3,4},{4,3},{5,6},{6,5},{7,8},{8,7},{9,10},{10,9},{11,... | collective-permute-start | bytes 49160 | tf_op jit(solution)/shard_map/ppermute | solution.py:31
  35.2 0.0 collective-permute-done.5.near_ref
  35.2 1.4 %collective-permute-done.6.far_ref = f32[32,128]{1,0:T(8,128)S(1)} collective-permute-done((f32[32,128]{1,0:T(8,128)S(1)}, f32[32,128]{1,0:T(8,128)S(1)}, u32[]{:S(2)}, u32[]{:S(2)}) %collective-permute-start.6) | collective-permute-done | bytes 16416 | tf_op jit(solution)/shard_map/ppermute | solution.py:31
  36.7 0.7 %blend.1 = (f32[4,16,32]{2,1,0:T(8,128)}, f32[4,16,32]{2,1,0:T(8,128)}) custom-call(f32[8,128]{1,0:T(8,128)S(1)} %get-tuple-element.20.plan_ref, f32[32,128]{1,0:T(8,128)S(1)} %get-tuple-element.32.center_ref, f32[32,128]{1,0:T(8,128)S(1)} %collective-permute-done.5.near_ref, f32[32,128]{1,0:T(8,128)S(1)} %collective-permute-done.6.far_ref, ...), custom_call_target="tpu_custom_call" | custom-call | tf_op jit(solution)/shard_map/blend/pallas_call | solution.py:491
Async XLA Ops:
  1.6 10.9 %collective-permute-start.3 = (bf16[144,1152]{1,0:T(8,128)(2,1)S(1)}, bf16[144,1152]{1,0:T(8,128)(2,1)S(1)}, u32[]{:S(2)}, u32[]{:S(2)}) collective-permute-start(bf16[144,1152]{1,0:T(8,128)(2,1)S(1)} %cut.1), channel_id=1, source_target_pairs={{0,16},{16,0},{1,17},{17,1},{2,18},{18,2},{3,19},{19,3},{4,20},{20... | collective-permute-start | bytes 995336 | tf_op jit(solution)/shard_map/ppermute | solution.py:35
  4.7 8.0 %collective-permute-start = (f32[32,4,32]{2,1,0:T(4,128)}, f32[32,4,32]{2,1,0:T(4,128)S(1)}, u32[]{:S(2)}, u32[]{:S(2)}) collective-permute-start(f32[32,4,32]{2,1,0:T(4,128)} %latent_source.1), channel_id=1, source_target_pairs={{0,1},{1,0},{2,3},{3,2},{4,5},{5,4},{6,7},{7,6},{8,9},{9,8},{10,11... | collective-permute-start | bytes 49160 | tf_op jit(solution)/shard_map/ppermute | solution.py:31
  4.7 8.0 %collective-permute-start.1 = (f32[32,4,32]{2,1,0:T(4,128)}, f32[32,4,32]{2,1,0:T(4,128)S(1)}, u32[]{:S(2)}, u32[]{:S(2)}) collective-permute-start(f32[32,4,32]{2,1,0:T(4,128)} %latent_source.1), channel_id=1, source_target_pairs={{1,2},{2,1},{3,4},{4,3},{5,6},{6,5},{7,8},{8,7},{9,10},{10,9},{11,... | collective-permute-start | bytes 49160 | tf_op jit(solution)/shard_map/ppermute | solution.py:31
  12.6 15.5 %collective-permute-start.4 = (bf16[144,1152]{1,0:T(8,128)(2,1)S(1)}, bf16[144,1152]{1,0:T(8,128)(2,1)S(1)}, u32[]{:S(2)}, u32[]{:S(2)}) collective-permute-start(bf16[144,1152]{1,0:T(8,128)(2,1)S(1)} %collective-permute-done.3.weight_ref), channel_id=1, source_target_pairs={{0,1},{1,0},{2,3},{3,2},{4,5},{5,4},{6,7},{7,6},{8,9},{9,8},{10,11... | collective-permute-start | bytes 995336 | tf_op jit(solution)/shard_map/ppermute | solution.py:31
  18.6 9.5 %collective-permute-start.2 = (bf16[2,288,256]{2,1,0:T(8,128)(2,1)S(1)}, bf16[2,288,256]{2,1,0:T(8,128)(2,1)S(1)}, u32[]{:S(2)}, u32[]{:S(2)}) collective-permute-start(bf16[2,288,256]{2,1,0:T(8,128)(2,1)S(1)} %get-tuple-element.30), channel_id=1, source_target_pairs={{0,16},{16,0},{1,17},{17,1},{2,18},{18,2},{3,19},{19,3},{4,20},{20... | collective-permute-start | bytes 884744 | tf_op jit(solution)/shard_map/ppermute | solution.py:35
  30.5 4.8 %collective-permute-start.5 = (f32[32,128]{1,0:T(8,128)S(1)}, f32[32,128]{1,0:T(8,128)S(1)}, u32[]{:S(2)}, u32[]{:S(2)}) collective-permute-start(f32[32,128]{1,0:T(8,128)S(1)} %get-tuple-element.33), channel_id=1, source_target_pairs={{0,1},{1,0},{2,3},{3,2},{4,5},{5,4},{6,7},{7,6},{8,9},{9,8},{10,11... | collective-permute-start | bytes 49160 | tf_op jit(solution)/shard_map/ppermute | solution.py:31
  30.5 6.1 %collective-permute-start.6 = (f32[32,128]{1,0:T(8,128)S(1)}, f32[32,128]{1,0:T(8,128)S(1)}, u32[]{:S(2)}, u32[]{:S(2)}) collective-permute-start(f32[32,128]{1,0:T(8,128)S(1)} %get-tuple-element.34), channel_id=1, source_target_pairs={{1,2},{2,1},{3,4},{4,3},{5,6},{6,5},{7,8},{8,7},{9,10},{10,9},{11,... | collective-permute-start | bytes 49160 | tf_op jit(solution)/shard_map/ppermute | solution.py:31

commit v4 on v3

--- a/solution.py
+++ b/solution.py
@@ -33,6 +33,21 @@
 
 def swap(array, axis):
     return lax.ppermute(array, axis, [(0, 1), (1, 0)])
+
+
+def swap_even(array, axis, ring):
+    size = lax.axis_size(ring)
+    pairs = [
+        (side * size + place, (1 - side) * size + place)
+        for side in range(2)
+        for place in range(0, size, 2)
+    ]
+    return lax.ppermute(array, (axis, ring), pairs)
+
+
+def even_to_odd(array, axis):
+    size = lax.axis_size(axis)
+    return lax.ppermute(array, axis, [(place, place + 1) for place in range(0, size, 2)])
 
 
 def layer_norm(values):
@@ -54,32 +69,16 @@
     return jnp.concatenate(parts, axis=0).astype(jnp.bfloat16)
 
 
-def cut_kernel(weight_ref, part_ref, semaphore):
-    count = part_ref.shape[0]
-    first = pl.multiple_of(lax.axis_index("win") % 2 * count, count)
-    copy = pltpu.make_async_copy(weight_ref.at[pl.ds(first, count)], part_ref, semaphore)
-    copy.start()
-    copy.wait()
-
-
 def prepare_kernel(
     step_ref,
     latent_source,
     patch_source,
     modulation_ref,
-    weight_ref,
-    text_ref,
-    out_ref,
-    final_ref,
     position_ref,
     patch_wide_ref,
     plan_ref,
     rows_ref,
     modulate_copy,
-    weight_copy,
-    text_copy,
-    out_copy,
-    final_copy,
     latent_ref,
     patch_ref,
     semaphores,
@@ -92,10 +91,6 @@
                 (latent_source, latent_ref),
                 (patch_source, patch_ref),
                 (modulation_ref.at[row], modulate_copy),
-                (weight_ref, weight_copy),
-                (text_ref, text_copy),
-                (out_ref, out_copy),
-                (final_ref, final_copy),
             )
         )
     ]
@@ -167,13 +162,13 @@
         copy.wait()
 
 
-def attend(proj_ref, text_ref, first, count):
+def attend(proj_ref, text_ref, first, count, chosen):
     heads = proj_ref.shape[0] // 3
     branches = text_ref.shape[0]
     factor = math.log2(math.e) / math.sqrt(HEAD_DIM)
     feature = (((0,), (0,)), ((), ()))
     results = [[] for _ in range(branches)]
-    for head in range(heads):
+    for head in chosen:
         rows = slice(head * HEAD_DIM, (head + 1) * HEAD_DIM)
         queries = proj_ref[head, :, pl.ds(first, count)]
         own_scores = lax.dot_general(
@@ -212,13 +207,20 @@
     far_ref,
     position_ref,
     patch_ref,
-    weight_ref,
-    text_ref,
+    weight_source,
+    text_source,
     proj_ref,
     embedded_ref,
+    text_ref,
     sent_ref,
     extended_ref,
+    weight_ref,
+    semaphores,
 ):
+    weight_copy = pltpu.make_async_copy(weight_source, weight_ref, semaphores.at[0])
+    text_copy = pltpu.make_async_copy(text_source, text_ref, semaphores.at[1])
+    weight_copy.start()
+    text_copy.start()
     slab_cols, channels, row_count = own_ref.shape
     col_pairs, row_couples = slab_cols, row_count // 2
     tokens = col_pairs * row_couples
@@ -263,6 +265,7 @@
         embedded_ref[...] = embedded[own_tokens:]
 
     heads = proj_ref.shape[0] // 3
+    weight_copy.wait()
     for kind in range(3):
         projected = lax.dot_general(
             weight_ref[kind],
@@ -275,15 +278,33 @@
                 head * HEAD_DIM : (head + 1) * HEAD_DIM
             ].astype(jnp.bfloat16)
     first = pl.multiple_of((1 - side) * own_tokens, own_tokens)
-    for branch, value in enumerate(attend(proj_ref, text_ref, first, own_tokens)):
+    text_copy.wait()
+    for branch, value in enumerate(
+        attend(proj_ref, text_ref, first, own_tokens, range(heads // 2))
+    ):
         sent_ref[branch] = value
 
 
-def attend_kernel(proj_ref, text_ref, weight_ref, mixed_ref):
+def second_kernel(proj_ref, text_ref, sent_ref):
+    heads = proj_ref.shape[0] // 3
+    own_tokens = proj_ref.shape[2] // 2
+    first = pl.multiple_of((1 - lax.axis_index("cfg")) * own_tokens, own_tokens)
+    for branch, value in enumerate(
+        attend(proj_ref, text_ref, first, own_tokens, range(heads // 2, heads))
+    ):
+        sent_ref[branch] = value
+
+
+def attend_kernel(proj_ref, text_ref, weight_source, mixed_ref, weight_ref, semaphore):
+    weight_copy = pltpu.make_async_copy(weight_source, weight_ref, semaphore)
+    weight_copy.start()
+    heads = proj_ref.shape[0] // 3
     tokens = proj_ref.shape[2]
     own_tokens = tokens // 2
     first = pl.multiple_of(lax.axis_index("cfg") * own_tokens, own_tokens)
-    for branch, value in enumerate(attend(proj_ref, text_ref, first, own_tokens)):
+    values = attend(proj_ref, text_ref, first, own_tokens, range(heads))
+    weight_copy.wait()
+    for branch, value in enumerate(values):
         mixed_ref[branch] = lax.dot_general(
             value, weight_ref[...], (((0,), (0,)), ((), ())), preferred_element_type=jnp.float32
         ).astype(jnp.bfloat16)
@@ -295,7 +316,8 @@
     modulation_ref,
     embedded_ref,
     mixed_ref,
-    received_ref,
+    early_ref,
+    late_ref,
     weight_ref,
     neighbour_ref,
     final_ref,
@@ -304,10 +326,9 @@
     far_ref,
     buffer_ref,
 ):
-    count = weight_ref.shape[0]
-    parity = lax.axis_index("win") % 2
-    mine = pl.multiple_of(parity * count, count)
-    theirs = pl.multiple_of((1 - parity) * count, count)
+    even_place = lax.axis_index("win") % 2 == 0
+    other_weight = jnp.where(even_place, weight_ref[...], neighbour_ref[...])
+    count = early_ref.shape[1]
     feature = (((0,), (0,)), ((), ()))
     slab_cols = center_ref.shape[0]
     col_pairs = slab_cols
@@ -318,13 +339,13 @@
     predicted = []
     for branch in range(2):
         other = lax.dot_general(
-            received_ref[branch, pl.ds(mine, count), :],
-            weight_ref[...],
+            early_ref[branch],
+            other_weight[:count],
             feature,
             preferred_element_type=jnp.float32,
         ) + lax.dot_general(
-            received_ref[branch, pl.ds(theirs, count), :],
-            neighbour_ref[...],
+            late_ref[branch],
+            other_weight[count:],
             feature,
             preferred_element_type=jnp.float32,
         )
@@ -357,7 +378,6 @@
     buffer_ref[pl.ds(start_at, col_pairs, stride=2), :] = even
     buffer_ref[pl.ds(start_at + 1, col_pairs, stride=2), :] = odd
     center_ref[...] = buffer_ref[slab_cols : 2 * slab_cols]
-    even_place = lax.axis_index("win") % 2 == 0
     left, right = buffer_ref[:slab_cols], buffer_ref[2 * slab_cols : 3 * slab_cols]
     near_ref[...] = jnp.where(even_place, right, left)
     far_ref[...] = jnp.where(even_place, left, right)
@@ -403,16 +423,7 @@
     near = swap_ring(latent, "win", 0)
     hbm = pl.BlockSpec(memory_space=pltpu.HBM)
     keep = functools.partial(pltpu.with_memory_space_constraint, memory_space=pltpu.HBM)
-    part = pl.pallas_call(
-        cut_kernel,
-        out_shape=jax.ShapeDtypeStruct((half_attn // 2, model_width), out_weight.dtype),
-        in_specs=[hbm],
-        out_specs=VM,
-        scratch_shapes=[pltpu.SemaphoreType.DMA],
-        name="cut",
-        compiler_params=pltpu.CompilerParams(vmem_limit_bytes=GRANT),
-    )(keep(out_weight))
-    other_weight = swap(part, "cfg")
+    other_weight = swap_even(out_weight, "cfg", "win")
 
     weight = jnp.transpose(qkv_weight, (1, 2, 0))
     text = jnp.transpose(text_kv, (0, 1, 3, 2))
@@ -421,7 +432,7 @@
     bf16, f32 = jnp.bfloat16, jnp.float32
     shape = jax.ShapeDtypeStruct
     wide = 2 * channels * half_rows
-    position, patch_wide, plan_values, rows, modulate, weight, text, out_own, final, own = pl.pallas_call(
+    position, patch_wide, plan_values, rows, modulate, own = pl.pallas_call(
         prepare_kernel,
         out_shape=(
             shape((tokens, model_width), f32),
@@ -429,61 +440,73 @@
             shape((8, max(wide, slab_cols)), f32),
             shape((channels * half_rows, slab_cols), f32),
             shape(modulation.shape[1:], f32),
-            shape(weight.shape, bf16),
-            shape(text.shape, bf16),
-            shape(out_weight.shape, bf16),
-            shape(final.shape, bf16),
             shape(latent.shape, f32),
         ),
-        in_specs=[SM] + [hbm] * 7,
-        out_specs=(VM,) * 10,
+        in_specs=[SM] + [hbm] * 3,
+        out_specs=(VM,) * 6,
         scratch_shapes=[
             pltpu.VMEM(patch_weight.shape, bf16),
-            pltpu.SemaphoreType.DMA((7,)),
+            pltpu.SemaphoreType.DMA((3,)),
         ],
         name="prepare",
         compiler_params=pltpu.CompilerParams(vmem_limit_bytes=GRANT),
         cost_estimate=pl.CostEstimate(flops=10**7, bytes_accessed=10**6, transcendentals=10**5),
     )(
         step_index,
-        *map(keep, (latent, patch_weight, modulation, weight, text, out_weight, final)),
-    )
-    projected, embedded, sent = pl.pallas_call(
+        *map(keep, (latent, patch_weight, modulation)),
+    )
+    projected, embedded, text, sent = pl.pallas_call(
         project_kernel,
         out_shape=(
             shape((3 * heads, HEAD_DIM, tokens), bf16),
             shape((own_tokens, model_width), f32),
-            shape((branches, half_attn, own_tokens), bf16),
+            shape(text.shape, bf16),
+            shape((branches, half_attn // 2, own_tokens), bf16),
         ),
-        in_specs=[SM] + [VM] * 8,
-        out_specs=(VM, VM, VM),
-        scratch_shapes=[pltpu.VMEM((3 * slab_cols, channels * row_count), f32)],
+        in_specs=[SM] + [VM] * 6 + [hbm] * 2,
+        out_specs=(VM,) * 4,
+        scratch_shapes=[
+            pltpu.VMEM((3 * slab_cols, channels * row_count), f32),
+            pltpu.VMEM(weight.shape, bf16),
+            pltpu.SemaphoreType.DMA((2,)),
+        ],
         name="project",
         compiler_params=pltpu.CompilerParams(vmem_limit_bytes=GRANT),
         cost_estimate=pl.CostEstimate(flops=2 * 10**9, bytes_accessed=8 * 10**6, transcendentals=10**6),
-    )(offsets, modulate, near, own, far, position, patch_wide, weight, text)
-    received = swap(sent, "cfg")
-    neighbour_weight = swap_ring(other_weight, "win", 0)
+    )(offsets, modulate, near, own, far, position, patch_wide, keep(weight), keep(text))
+    early = swap(sent, "cfg")
+    sent = pl.pallas_call(
+        second_kernel,
+        out_shape=shape((branches, half_attn // 2, own_tokens), bf16),
+        in_specs=[VM] * 2,
+        out_specs=VM,
+        name="second",
+        compiler_params=pltpu.CompilerParams(vmem_limit_bytes=GRANT),
+        cost_estimate=pl.CostEstimate(flops=10**9, bytes_accessed=10**6, transcendentals=10**6),
+    )(projected, text)
+    late = swap(sent, "cfg")
+    neighbour_weight = even_to_odd(other_weight, "win")
     mixed = pl.pallas_call(
         attend_kernel,
         out_shape=shape((branches, own_tokens, model_width), bf16),
-        in_specs=[VM] * 3,
+        in_specs=[VM] * 2 + [hbm],
         out_specs=VM,
+        scratch_shapes=[pltpu.VMEM(out_weight.shape, bf16), pltpu.SemaphoreType.DMA],
         name="attend",
         compiler_params=pltpu.CompilerParams(vmem_limit_bytes=GRANT),
         cost_estimate=pl.CostEstimate(flops=10**9, bytes_accessed=8 * 10**6, transcendentals=10**6),
-    )(projected, text, out_own)
+    )(projected, text, keep(out_weight))
     to_near, center, to_far = pl.pallas_call(
         finish_kernel,
         out_shape=tuple(shape((slab_cols, wide), f32) for _ in range(3)),
-        in_specs=[SM, SM] + [VM] * 7,
+        in_specs=[SM, SM] + [VM] * 8,
         out_specs=(VM, VM, VM),
         scratch_shapes=[pltpu.VMEM((3 * slab_cols + 8, wide), f32)],
         name="finish",
         compiler_params=pltpu.CompilerParams(vmem_limit_bytes=GRANT),
         cost_estimate=pl.CostEstimate(flops=10**9, bytes_accessed=4 * 10**6, transcendentals=10**3),
     )(
-        offsets, blend_weights, modulate, embedded, mixed, received,
+        offsets, blend_weights, modulate, embedded, mixed, early, late,
         other_weight, neighbour_weight, final,
     )
     from_far = swap_ring(to_far, "win", 1)

time: 37.6 us -> 46.2 us (1.23)
  waiting for transfers between devices: 4.64 us -> 10.9 us
  starting transfers between devices: 14.2 us -> 17.5 us
  Pallas kernels: 16 us -> 14.8 us
    ppermute x0 -> x2, waiting for transfers between devices: none -> 8.85 us  [the longest x1 8.85 us: swap_even(): return lax.ppermute(array, (axis, ring), pairs)]
    ppermute x0 -> x2, starting transfers between devices: none -> 6.23 us  [the longest x1 4.91 us: swap_even(): return lax.ppermute(array, (axis, ring), pairs)]
    ppermute x2, waiting for transfers between devices: 3.19 us -> 0.01 us  [swap(): return lax.ppermute(array, axis, [(0, 1), (1, 0)])]
    ppermute x2, starting transfers between devices: 4.7 us -> 2.09 us  [swap(): return lax.ppermute(array, axis, [(0, 1), (1, 0)])]
    pallas_call x1, Pallas kernels: 5.91 us -> 4.63 us  [on_device(): pl.pallas_call(project_kernel, out_shape=(shape((3 * heads, HEAD_DIM, tok...]
    pallas_call x1, Pallas kernels: 1.93 us -> 1.09 us  [on_device(): pl.pallas_call(prepare_kernel, out_shape=(shape((tokens, model_width), f3...]
    pallas_call x1, Pallas kernels: 1 us -> 1.83 us  [on_device(): pl.pallas_call(second_kernel, out_shape=shape((branches, half_attn // 2,...]
    ppermute x5 -> x4, waiting for transfers between devices: 1.45 us -> 2.02 us  [swap_ring(): return lax.ppermute(array, axis, pairs)]
  transfers between devices with their start and end apart: 7 -> 8, of which waited for: 2 -> 2; matrix products, arithmetic and copies ran while one was open for 0% -> 0% of each run, Pallas kernels for 32% -> 26%
where the time goes in v4:
time: 46.2 us; the launch traced here: 45.9 us
  starting transfers between devices  17.5 us (38%)
  Pallas kernels  14.8 us (32%)
  waiting for transfers between devices  10.9 us (24%)
  between operations  2.7 us (6%)
    ppermute x4, starting transfers between devices, swap_ring(): return lax.ppermute(array, axis, pairs)  9.18 us
    ppermute x1, waiting for transfers between devices, swap_even(): return lax.ppermute(array, (axis, ring), pairs)  8.85 us
    ppermute x1, starting transfers between devices, swap_even(): return lax.ppermute(array, (axis, ring), pairs)  4.91 us
    pallas_call x1, Pallas kernels, on_device(): pl.pallas_call(project_kernel, out_shape=(shape((3 * heads, HEAD_DIM, tok...  4.63 us
    pallas_call x1, Pallas kernels, on_device(): pl.pallas_call(attend_kernel, out_shape=shape((branches, own_tokens, mode...  4.18 us
    pallas_call x1, Pallas kernels, on_device(): pl.pallas_call(finish_kernel, out_shape=tuple((shape((slab_cols, wide), f...  2.37 us
    ppermute x2, starting transfers between devices, swap(): return lax.ppermute(array, axis, [(0, 1), (1, 0)])  2.09 us
    ppermute x4, waiting for transfers between devices, swap_ring(): return lax.ppermute(array, axis, pairs)  2.02 us
  transfers between devices with their start and end apart: 8, of which 2 were waited for; matrix products, arithmetic and copies ran while one was open for 0% of the time, Pallas kernels for 26%

profile of v4, /device:TPU:0, one launch (start us, length us, event | category | flops | bytes accessed | tf_op | source)
XLA Modules:
  0.0 45.9 jit_solution(8521419123457468225)
XLA Ops:
  0.6 4.9 %collective-permute-start.4 = (bf16[288,1152]{1,0:T(8,128)(2,1)}, bf16[288,1152]{1,0:T(8,128)(2,1)S(1)}, u32[]{:S(2)}, u32[]{:S(2)}) collective-permute-start(bf16[288,1152]{1,0:T(8,128)(2,1)} %weight_source.1), channel_id=1, source_target_pairs={{0,16},{2,18},{4,20},{6,22},{8,24},{10,26},{12,28},{14,30},{16,0},... | collective-permute-start | bytes 1990664 | tf_op jit(solution)/shard_map/ppermute | solution.py:45
  5.5 8.8 %collective-permute-done.4.weight_ref = bf16[288,1152]{1,0:T(8,128)(2,1)S(1)} collective-permute-done((bf16[288,1152]{1,0:T(8,128)(2,1)}, bf16[288,1152]{1,0:T(8,128)(2,1)S(1)}, u32[]{:S(2)}, u32[]{:S(2)}) %collective-permute-start.4) | collective-permute-done | bytes 663584 | tf_op jit(solution)/shard_map/ppermute | solution.py:45
  14.4 1.3 %collective-permute-start.5 = (bf16[288,1152]{1,0:T(8,128)(2,1)S(1)}, bf16[288,1152]{1,0:T(8,128)(2,1)S(1)}, u32[]{:S(2)}, u32[]{:S(2)}) collective-permute-start(bf16[288,1152]{1,0:T(8,128)(2,1)S(1)} %collective-permute-done.4.weight_ref), channel_id=1, source_target_pairs={{0,1},{2,3},{4,5},{6,7},{8,9},{10,11},{12,13},{14,15},{16,17},{18,... | collective-permute-start | bytes 1990664 | tf_op jit(solution)/shard_map/ppermute | solution.py:50
  15.7 0.1 collective-permute-start
  15.8 5.1 %collective-permute-start.1 = (f32[32,4,32]{2,1,0:T(4,128)}, f32[32,4,32]{2,1,0:T(4,128)S(1)}, u32[]{:S(2)}, u32[]{:S(2)}) collective-permute-start(f32[32,4,32]{2,1,0:T(4,128)} %latent_source.1), channel_id=1, source_target_pairs={{1,2},{2,1},{3,4},{4,3},{5,6},{6,5},{7,8},{8,7},{9,10},{10,9},{11,... | collective-permute-start | bytes 49160 | tf_op jit(solution)/shard_map/ppermute | solution.py:31
  22.2 1.1 %prepare.1 = (f32[512,1152]{1,0:T(8,128)S(1)}, bf16[256,1152]{1,0:T(8,128)(2,1)S(1)}, f32[8,128]{1,0:T(8,128)S(1)}, f32[64,32]{1,0:T(8,128)S(1)}, f32[4,1152]{1,0:T(4,128)S(1)}, /*index=5*/f32[32,4,32]{2,1,0:T(4,128)S(1)}) custom-call(s32[1]{0:T(128)S(6)} %copy.14.step_ref, f32[32,4,32]{2,1,0:T(4,128)} %latent_source.1, bf16[16,1152]{1,0:T(8,128)(2,1)} %patch_source.1, ...), custom_call_target="tpu_custom_call" | custom-call | flops 10000000 | bytes 1000000 | tf_op jit(solution)/shard_map/prepare/pallas_call | solution.py:435
  23.3 0.0 collective-permute-done.near_ref
  23.3 0.0 collective-permute-done.1.far_ref
  23.3 4.6 %project.1 = (bf16[12,72,512]{2,1,0:T(8,128)(2,1)S(1)}, f32[256,1152]{1,0:T(8,128)S(1)}, bf16[2,2,288,120]{3,2,1,0:T(8,128)(2,1)S(1)}, bf16[2,144,256]{2,1,0:T(8,128)(2,1)S(1)}) custom-call(s32[1]{0:T(128)S(6)} %copy.12.offset_ref, f32[4,1152]{1,0:T(4,128)S(1)} %get-tuple-element.18.modulation_ref, f32[32,4,32]{2,1,0:T(4,128)S(1)} %collective-permute-done.near_ref, ...), custom_call_target="tpu_custom_call" | custom-call | flops 2000000000 | bytes 8000000 | tf_op jit(solution)/shard_map/project/pallas_call | solution.py:458
  28.0 1.8 %second.1 = bf16[2,144,256]{2,1,0:T(8,128)(2,1)S(1)} custom-call(bf16[12,72,512]{2,1,0:T(8,128)(2,1)S(1)} %get-tuple-element.23.proj_ref, bf16[2,2,288,120]{3,2,1,0:T(8,128)(2,1)S(1)} %get-tuple-element.24.text_ref), custom_call_target="tpu_custom_call" | custom-call | flops 1000000000 | bytes 1000000 | tf_op jit(solution)/shard_map/second/pallas_call | solution.py:478
  29.8 0.0 copy-start
  29.8 1.6 %collective-permute-start.3 = (bf16[2,144,256]{2,1,0:T(8,128)(2,1)S(1)}, bf16[2,144,256]{2,1,0:T(8,128)(2,1)S(1)}, u32[]{:S(2)}, u32[]{:S(2)}) collective-permute-start(bf16[2,144,256]{2,1,0:T(8,128)(2,1)S(1)} %second.1), channel_id=1, source_target_pairs={{0,16},{16,0},{1,17},{17,1},{2,18},{18,2},{3,19},{19,3},{4,20},{20... | collective-permute-start | bytes 442376 | tf_op jit(solution)/shard_map/ppermute | solution.py:35
  31.4 0.5 %collective-permute-start.2 = (bf16[2,144,256]{2,1,0:T(8,128)(2,1)S(1)}, bf16[2,144,256]{2,1,0:T(8,128)(2,1)S(1)}, u32[]{:S(2)}, u32[]{:S(2)}) collective-permute-start(bf16[2,144,256]{2,1,0:T(8,128)(2,1)S(1)} %get-tuple-element.25), channel_id=1, source_target_pairs={{0,16},{16,0},{1,17},{17,1},{2,18},{18,2},{3,19},{19,3},{4,20},{20... | collective-permute-start | bytes 442376 | tf_op jit(solution)/shard_map/ppermute | solution.py:35
  32.6 4.2 %attend.1.mixed_ref = bf16[2,256,1152]{2,1,0:T(8,128)(2,1)S(1)} custom-call(bf16[12,72,512]{2,1,0:T(8,128)(2,1)S(1)} %get-tuple-element.23.proj_ref, bf16[2,2,288,120]{3,2,1,0:T(8,128)(2,1)S(1)} %get-tuple-element.24.text_ref, bf16[288,1152]{1,0:T(8,128)(2,1)} %weight_source.1), custom_call_target="tpu_custom_call" | custom-call | flops 1000000000 | bytes 8000000 | tf_op jit(solution)/shard_map/attend/pallas_call | solution.py:489
  36.8 0.0 collective-permute-done.3.late_ref
  36.8 0.0 collective-permute-done.2.early_ref
  36.8 0.0 collective-permute-done.5.neighbour_ref
  36.8 0.0 copy-done
  36.8 2.4 %finish.1 = (f32[32,128]{1,0:T(8,128)S(1)}, f32[32,128]{1,0:T(8,128)S(1)}, f32[32,128]{1,0:T(8,128)S(1)}) custom-call(s32[1]{0:T(128)S(6)} %copy.12.offset_ref, s32[1]{0:T(128)S(6)} %copy.13.blend_ref, f32[4,1152]{1,0:T(4,128)S(1)} %get-tuple-element.18.modulation_ref, f32[256,1152]{1,0:T(8,128)S(1)} %get-tuple-element.22.embedded_ref, ...), custom_call_target="tpu_custom_call" | custom-call | flops 1000000000 | bytes 4000000 | tf_op jit(solution)/shard_map/finish/pallas_call | solution.py:499
  39.2 0.1 collective-permute-start.6
  39.3 3.9 %collective-permute-start.7 = (f32[32,128]{1,0:T(8,128)S(1)}, f32[32,128]{1,0:T(8,128)S(1)}, u32[]{:S(2)}, u32[]{:S(2)}) collective-permute-start(f32[32,128]{1,0:T(8,128)S(1)} %get-tuple-element.28), channel_id=1, source_target_pairs={{1,2},{2,1},{3,4},{4,3},{5,6},{6,5},{7,8},{8,7},{9,10},{10,9},{11,... | collective-permute-start | bytes 49160 | tf_op jit(solution)/shard_map/ppermute | solution.py:31
  43.2 0.0 collective-permute-done.6.near_ref
  43.2 2.0 %collective-permute-done.7.far_ref = f32[32,128]{1,0:T(8,128)S(1)} collective-permute-done((f32[32,128]{1,0:T(8,128)S(1)}, f32[32,128]{1,0:T(8,128)S(1)}, u32[]{:S(2)}, u32[]{:S(2)}) %collective-permute-start.7) | collective-permute-done | bytes 16416 | tf_op jit(solution)/shard_map/ppermute | solution.py:31
  45.2 0.7 %blend.1 = (f32[4,16,32]{2,1,0:T(8,128)}, f32[4,16,32]{2,1,0:T(8,128)}) custom-call(f32[8,128]{1,0:T(8,128)S(1)} %get-tuple-element.17.plan_ref, f32[32,128]{1,0:T(8,128)S(1)} %get-tuple-element.26.center_ref, f32[32,128]{1,0:T(8,128)S(1)} %collective-permute-done.6.near_ref, f32[32,128]{1,0:T(8,128)S(1)} %collective-permute-done.7.far_ref, ...), custom_call_target="tpu_custom_call" | custom-call | tf_op jit(solution)/shard_map/blend/pallas_call | solution.py:514
Async XLA Ops:
  0.6 13.8 %collective-permute-start.4 = (bf16[288,1152]{1,0:T(8,128)(2,1)}, bf16[288,1152]{1,0:T(8,128)(2,1)S(1)}, u32[]{:S(2)}, u32[]{:S(2)}) collective-permute-start(bf16[288,1152]{1,0:T(8,128)(2,1)} %weight_source.1), channel_id=1, source_target_pairs={{0,16},{2,18},{4,20},{6,22},{8,24},{10,26},{12,28},{14,30},{16,0},... | collective-permute-start | bytes 1990664 | tf_op jit(solution)/shard_map/ppermute | solution.py:45
  14.4 22.4 %collective-permute-start.5 = (bf16[288,1152]{1,0:T(8,128)(2,1)S(1)}, bf16[288,1152]{1,0:T(8,128)(2,1)S(1)}, u32[]{:S(2)}, u32[]{:S(2)}) collective-permute-start(bf16[288,1152]{1,0:T(8,128)(2,1)S(1)} %collective-permute-done.4.weight_ref), channel_id=1, source_target_pairs={{0,1},{2,3},{4,5},{6,7},{8,9},{10,11},{12,13},{14,15},{16,17},{18,... | collective-permute-start | bytes 1990664 | tf_op jit(solution)/shard_map/ppermute | solution.py:50
  15.7 7.6 %collective-permute-start = (f32[32,4,32]{2,1,0:T(4,128)}, f32[32,4,32]{2,1,0:T(4,128)S(1)}, u32[]{:S(2)}, u32[]{:S(2)}) collective-permute-start(f32[32,4,32]{2,1,0:T(4,128)} %latent_source.1), channel_id=1, source_target_pairs={{0,1},{1,0},{2,3},{3,2},{4,5},{5,4},{6,7},{7,6},{8,9},{9,8},{10,11... | collective-permute-start | bytes 49160 | tf_op jit(solution)/shard_map/ppermute | solution.py:31
  15.8 7.5 %collective-permute-start.1 = (f32[32,4,32]{2,1,0:T(4,128)}, f32[32,4,32]{2,1,0:T(4,128)S(1)}, u32[]{:S(2)}, u32[]{:S(2)}) collective-permute-start(f32[32,4,32]{2,1,0:T(4,128)} %latent_source.1), channel_id=1, source_target_pairs={{1,2},{2,1},{3,4},{4,3},{5,6},{6,5},{7,8},{8,7},{9,10},{10,9},{11,... | collective-permute-start | bytes 49160 | tf_op jit(solution)/shard_map/ppermute | solution.py:31
  29.8 7.0 %copy-start = (bf16[1152,16]{0,1:T(8,128)(2,1)S(1)}, bf16[1152,16]{0,1:T(8,128)(2,1)}, u32[]{:S(2)}) copy-start(bf16[1152,16]{0,1:T(8,128)(2,1)} %param.16) | copy-start | bytes 110596
  29.8 6.9 %collective-permute-start.3 = (bf16[2,144,256]{2,1,0:T(8,128)(2,1)S(1)}, bf16[2,144,256]{2,1,0:T(8,128)(2,1)S(1)}, u32[]{:S(2)}, u32[]{:S(2)}) collective-permute-start(bf16[2,144,256]{2,1,0:T(8,128)(2,1)S(1)} %second.1), channel_id=1, source_target_pairs={{0,16},{16,0},{1,17},{17,1},{2,18},{18,2},{3,19},{19,3},{4,20},{20... | collective-permute-start | bytes 442376 | tf_op jit(solution)/shard_map/ppermute | solution.py:35
  31.4 5.4 %collective-permute-start.2 = (bf16[2,144,256]{2,1,0:T(8,128)(2,1)S(1)}, bf16[2,144,256]{2,1,0:T(8,128)(2,1)S(1)}, u32[]{:S(2)}, u32[]{:S(2)}) collective-permute-start(bf16[2,144,256]{2,1,0:T(8,128)(2,1)S(1)} %get-tuple-element.25), channel_id=1, source_target_pairs={{0,16},{16,0},{1,17},{17,1},{2,18},{18,2},{3,19},{19,3},{4,20},{20... | collective-permute-start | bytes 442376 | tf_op jit(solution)/shard_map/ppermute | solution.py:35
  39.2 4.0 %collective-permute-start.6 = (f32[32,128]{1,0:T(8,128)S(1)}, f32[32,128]{1,0:T(8,128)S(1)}, u32[]{:S(2)}, u32[]{:S(2)}) collective-permute-start(f32[32,128]{1,0:T(8,128)S(1)} %get-tuple-element.27), channel_id=1, source_target_pairs={{0,1},{1,0},{2,3},{3,2},{4,5},{5,4},{6,7},{7,6},{8,9},{9,8},{10,11... | collective-permute-start | bytes 49160 | tf_op jit(solution)/shard_map/ppermute | solution.py:31
  39.3 5.9 %collective-permute-start.7 = (f32[32,128]{1,0:T(8,128)S(1)}, f32[32,128]{1,0:T(8,128)S(1)}, u32[]{:S(2)}, u32[]{:S(2)}) collective-permute-start(f32[32,128]{1,0:T(8,128)S(1)} %get-tuple-element.28), channel_id=1, source_target_pairs={{1,2},{2,1},{3,4},{4,3},{5,6},{6,5},{7,8},{8,7},{9,10},{10,9},{11,... | collective-permute-start | bytes 49160 | tf_op jit(solution)/shard_map/ppermute | solution.py:31

commit v5 on v4

v5 whole, which is shorter than its diff:
```python
import functools
import math

import jax
import jax.numpy as jnp
from jax import lax
from jax.experimental import pallas as pl
from jax.experimental.pallas import tpu as pltpu
from jax.sharding import PartitionSpec as P


HEAD_DIM = 72
STEPS = 20


guidance_scale = 4.5
plan_length = 1000
norm_eps = 1e-06

VM = pl.BlockSpec(memory_space=pltpu.VMEM)
SM = pl.BlockSpec(memory_space=pltpu.SMEM)
GRANT = 24 * 2**20


def swap_ring(array, axis, odd):
    size = lax.axis_size(axis)
    pairs = []
    for left in range(odd, size, 2):
        right = (left + 1) % size
        pairs += [(left, right), (right, left)]
    return lax.ppermute(array, axis, pairs)


def swap(array, axis):
    return lax.ppermute(array, axis, [(0, 1), (1, 0)])


def swap_across(array, axis, step):
    size = lax.axis_size(axis)
    return lax.ppermute(array, axis, [(place, place ^ step) for place in range(size)])


def layer_norm(values):
    average = jnp.mean(values, axis=-1, keepdims=True)
    centered = values - average
    variance = jnp.mean(centered * centered, axis=-1, keepdims=True)
    return centered * lax.rsqrt(variance + norm_eps)


def repeat_pairs(weight, repeats):
    rows, width = weight.shape
    values = weight.astype(jnp.float32)
    even = lax.broadcasted_iota(jnp.int32, (2 * repeats, width), 0) % 2 == 0
    parts = []
    for pair in range(rows // 2):
        parts.append(
            jnp.where(even, values[2 * pair : 2 * pair + 1, :], values[2 * pair + 1 : 2 * pair + 2, :])
        )
    return jnp.concatenate(parts, axis=0).astype(jnp.bfloat16)


def prepare_kernel(
    step_ref,
    offset_ref,
    latent_source,
    patch_source,
    modulation_ref,
    out_source,
    row_ref,
    col_ref,
    patch_wide_ref,
    start_ref,
    modulate_copy,
    latent_copy,
    quarter_copy,
    patch_ref,
    semaphores,
):
    count = quarter_copy.shape[0]
    quarter_first = pl.multiple_of(lax.axis_index("win") % 4 * count, 8)
    row = step_ref[0] * STEPS // plan_length
    copies = [
        pltpu.make_async_copy(source, target, semaphores.at[place])
        for place, (source, target) in enumerate(
            (
                (patch_source, patch_ref),
                (modulation_ref.at[row], modulate_copy),
                (latent_source, latent_copy),
                (out_source.at[pl.ds(quarter_first, count)], quarter_copy),
            )
        )
    ]
    for copy in copies:
        copy.start()
    slab_cols, _, row_count = latent_copy.shape
    model_width = patch_ref.shape[1]
    quarter = model_width // 4

    def table(target_ref, first):
        count, lanes = target_ref.shape
        lane = first + lax.broadcasted_iota(jnp.int32, (count, lanes), 1)
        place = lax.broadcasted_iota(jnp.int32, (count, lanes), 0).astype(jnp.float32)
        frequency = jnp.exp(-math.log(10000.0) * (lane % quarter).astype(jnp.float32) / quarter)
        phase = jnp.where(lane // quarter % 2 == 0, 0.0, 0.5 * math.pi)
        target_ref[...] = jnp.sin(place * frequency + phase)

    table(row_ref, 0)
    table(col_ref, model_width - col_ref.shape[1])
    is_start = lax.broadcasted_iota(jnp.int32, start_ref.shape, 0) == 0
    start_ref[...] = jnp.where(is_start, slab_cols - offset_ref[0], step_ref[0])
    copies[0].wait()
    patch_wide_ref[...] = repeat_pairs(patch_ref[...], row_count // 2)
    for copy in copies[1:]:
        copy.wait()


def coefficient_kernel(start_ref, latent_ref, plan_ref, rows_ref):
    _, channels, row_count = latent_ref.shape
    moment = start_ref[1:2, :128]
    index = lax.broadcasted_iota(jnp.int32, (8, 128), 0) * 128 + lax.broadcasted_iota(
        jnp.int32, (8, 128), 1
    )
    train = jnp.minimum(index, plan_length - 1).astype(jnp.float32)
    beta_values = 0.0001 + (0.02 - 0.0001) * train / (plan_length - 1)
    logs = jnp.log(1.0 - beta_values)

    def alpha_bar(last):
        kept = jnp.where((index <= last) & (index < plan_length), logs, 0.0)
        kept = jnp.sum(jnp.sum(kept, axis=0, keepdims=True), axis=1, keepdims=True)
        return jnp.exp(kept)

    alpha_now = alpha_bar(moment)
    alpha_before = alpha_bar(moment - plan_length // STEPS)
    for place, value in enumerate(
        (
            jnp.sqrt(alpha_before),
            jnp.sqrt(1.0 - alpha_now),
            jnp.sqrt(alpha_now),
            jnp.sqrt(1.0 - alpha_before),
        )
    ):
        plan_ref[place : place + 1, :] = jnp.broadcast_to(value, (1, plan_ref.shape[1]))

    half_rows = row_count // 2
    side = lax.axis_index("cfg")
    for channel in range(channels):
        turned = jnp.transpose(latent_ref[:, channel, :], (1, 0))
        rows_ref[channel * half_rows : (channel + 1) * half_rows, :] = jnp.where(
            side == 0, turned[:half_rows], turned[half_rows:]
        )


def attend(proj_ref, text_ref, first, count, chosen, finished):
    heads = proj_ref.shape[0] // 3
    branches = text_ref.shape[0]
    feature = (((0,), (0,)), ((), ()))

    def score(head):
        rows = slice(head * HEAD_DIM, (head + 1) * HEAD_DIM)
        queries = proj_ref[head, :, pl.ds(first, count)]
        return [
            lax.dot_general(keys, queries, feature, preferred_element_type=jnp.float32)
            for keys in [proj_ref[heads + head]]
            + [text_ref[branch, 0, rows, :] for branch in range(branches)]
        ]

    def weigh(scores):
        own_highest = jnp.max(scores[0], axis=0, keepdims=True)
        own_exp = jnp.exp2(scores[0] - own_highest)
        own = (own_exp.astype(jnp.bfloat16), jnp.sum(own_exp, axis=0, keepdims=True))
        texts = []
        for text_scores in scores[1:]:
            highest = jnp.maximum(own_highest, jnp.max(text_scores, axis=0, keepdims=True))
            text_exp = jnp.exp2(text_scores - highest)
            lowered = jnp.exp2(own_highest - highest)
            total = lowered * own[1] + jnp.sum(text_exp, axis=0, keepdims=True)
            texts.append((text_exp.astype(jnp.bfloat16), lowered, 1.0 / total))
        return own[0], texts

    def mix(head, own_exp, texts):
        rows = slice(head * HEAD_DIM, (head + 1) * HEAD_DIM)
        own_mix = jnp.dot(
            proj_ref[2 * heads + head], own_exp, preferred_element_type=jnp.float32
        )
        results = []
        for branch, (text_exp, lowered, inverse) in enumerate(texts):
            text_mix = jnp.dot(
                text_ref[branch, 1, rows, :], text_exp, preferred_element_type=jnp.float32
            )
            results.append((lowered * own_mix + text_mix) * inverse)
        return jnp.concatenate(results, axis=1)

    chosen = list(chosen)
    mixed = []

    def take(place, weights):
        mixed.append(mix(chosen[place], *weights))
        if place % 2:
            finished(place // 2, jnp.concatenate(mixed[-2:], axis=0).astype(jnp.bfloat16))

    ahead = score(chosen[0])
    before = None
    for place, head in enumerate(chosen):
        scores = ahead
        if place + 1 < len(chosen):
            ahead = score(chosen[place + 1])
        weights = weigh(scores)
        if before is not None:
            take(place - 1, before)
        before = weights
    take(len(chosen) - 1, before)


def keep_pair(target_ref, place, pair):
    target_ref[...] = pair


def project_kernel(
    start_ref,
    modulation_ref,
    near_ref,
    own_ref,
    far_ref,
    row_ref,
    col_ref,
    patch_ref,
    weight_source,
    text_source,
    proj_ref,
    embedded_ref,
    text_ref,
    sent_ref,
    extended_ref,
    weight_ref,
    semaphores,
):
    weight_copy = pltpu.make_async_copy(weight_source, weight_ref, semaphores.at[0])
    text_copy = pltpu.make_async_copy(text_source, text_ref, semaphores.at[1])
    weight_copy.start()
    text_copy.start()
    slab_cols, channels, row_count = own_ref.shape
    col_pairs, row_couples = slab_cols, row_count // 2
    tokens = col_pairs * row_couples
    own_tokens = tokens // 2
    wide = 2 * channels * row_count
    even = lax.axis_index("win") % 2 == 0
    for channel in range(channels):
        near, far = near_ref[:, channel, :], far_ref[:, channel, :]
        values = (jnp.where(even, far, near), own_ref[:, channel, :], jnp.where(even, near, far))
        for place, value in enumerate(values):
            extended_ref[
                place * slab_cols : (place + 1) * slab_cols,
                channel * row_count : (channel + 1) * row_count,
            ] = value
    extended = extended_ref[...].astype(jnp.bfloat16)
    start_at = start_ref[0:1, : 3 * slab_cols]
    chosen = lax.broadcasted_iota(jnp.int32, (2 * col_pairs, 3 * slab_cols), 0)
    column = lax.broadcasted_iota(jnp.int32, (2 * col_pairs, 3 * slab_cols), 1)
    target = jnp.where(
        chosen < col_pairs, 2 * chosen, 2 * (chosen - col_pairs) + 1
    )
    pick = jnp.where(column == target + start_at, 1.0, 0.0).astype(jnp.bfloat16)
    picked = jnp.dot(pick, extended, preferred_element_type=jnp.float32)
    picked = jnp.concatenate([picked[:col_pairs], picked[col_pairs:]], axis=1)
    lane_couple = lax.broadcasted_iota(jnp.int32, (col_pairs, wide), 1) % row_count // 2
    spread = jnp.concatenate(
        [jnp.where(lane_couple == couple, picked, 0.0) for couple in range(row_couples)], axis=0
    ).astype(jnp.bfloat16)
    side = lax.axis_index("cfg")
    heads = proj_ref.shape[0] // 3
    chunks = [slice(place * own_tokens, (place + 1) * own_tokens) for place in range(2)]

    couples = row_couples // 2
    model_width = patch_ref.shape[1]
    below, above = model_width - col_ref.shape[1], row_ref.shape[1]
    is_row = below + lax.broadcasted_iota(jnp.int32, (col_pairs, above - below), 1)
    is_row = is_row < model_width // 2

    def position(couple):
        line = jnp.broadcast_to(row_ref[couple : couple + 1, :], (col_pairs, above))
        column = col_ref[...]
        both = jnp.where(is_row, line[:, below:], column[:, : above - below])
        return jnp.concatenate([line[:, :below], both, column[:, above - below :]], axis=1)

    def embed(place):
        chunk = chunks[place]
        embedded = jnp.dot(spread[chunk], patch_ref[...], preferred_element_type=jnp.float32)
        embedded = embedded + jnp.concatenate(
            [position(couple) for couple in range(row_couples)[place * couples :][:couples]], axis=0
        )

        @pl.when(side == place)
        def _():
            embedded_ref[...] = embedded

        return embedded

    def norm(embedded):
        return (
            layer_norm(embedded) * (1.0 + modulation_ref[1:2, :]) + modulation_ref[0:1, :]
        ).astype(jnp.bfloat16)

    def project(place, normed):
        projected = lax.dot_general(
            weight_ref[...],
            normed,
            (((1,), (1,)), ((), ())),
            preferred_element_type=jnp.float32,
        )
        for head in range(3 * heads):
            part = projected[head * HEAD_DIM : (head + 1) * HEAD_DIM]
            if head < heads:
                part = part * (math.log2(math.e) / math.sqrt(HEAD_DIM))
            proj_ref[head, :, chunks[place]] = part.astype(jnp.bfloat16)

    normed = norm(embed(0))
    later = embed(1)
    weight_copy.wait()
    project(0, normed)
    project(1, norm(later))
    first = pl.multiple_of((1 - side) * own_tokens, own_tokens)
    text_copy.wait()
    attend(proj_ref, text_ref, first, own_tokens, range(heads // 2), functools.partial(keep_pair, sent_ref))


def second_kernel(proj_ref, text_ref, sent_ref):
    heads = proj_ref.shape[0] // 3
    own_tokens = proj_ref.shape[2] // 2
    first = pl.multiple_of((1 - lax.axis_index("cfg")) * own_tokens, own_tokens)
    attend(proj_ref, text_ref, first, own_tokens, range(heads // 2, heads), functools.partial(keep_pair, sent_ref))


def attend_kernel(proj_ref, text_ref, weight_source, mixed_ref, weight_ref, semaphore):
    weight_copy = pltpu.make_async_copy(weight_source, weight_ref, semaphore)
    weight_copy.start()
    heads = proj_ref.shape[0] // 3
    tokens = proj_ref.shape[2]
    own_tokens = tokens // 2
    first = pl.multiple_of(lax.axis_index("cfg") * own_tokens, own_tokens)
    weight_copy.wait()
    pairs = []

    def finished(place, pair):
        pairs.append(pair)

    attend(proj_ref, text_ref, first, own_tokens, range(heads), finished)
    mixed_ref[...] = lax.dot_general(
        jnp.concatenate(pairs, axis=0),
        weight_ref[...],
        (((0,), (0,)), ((), ())),
        preferred_element_type=jnp.float32,
    ).astype(jnp.bfloat16)


def finish_kernel(
    start_source,
    blend_ref,
    modulation_ref,
    embedded_ref,
    mixed_ref,
    early_ref,
    late_ref,
    weight_ref,
    core_ref,
    cross_ref,
    core_cross_ref,
    final_ref,
    near_ref,
    center_ref,
    far_ref,
    buffer_ref,
    start_ref,
    semaphore,
):
    start_copy = pltpu.make_async_copy(start_source, start_ref, semaphore)
    start_copy.start()
    even_place = lax.axis_index("win") % 2 == 0
    lower_pair = lax.axis_index("win") % 4 < 2

    def join(mine, neighbour):
        mine, neighbour = mine[...].astype(jnp.float32), neighbour[...].astype(jnp.float32)
        first = jnp.where(even_place, mine, neighbour)
        second = jnp.where(even_place, neighbour, mine)
        return jnp.concatenate([first, second], axis=0).astype(jnp.bfloat16)

    feature = (((0,), (0,)), ((), ()))
    early, late = early_ref[...], late_ref[...]
    other = lax.dot_general(
        jnp.where(lower_pair, early, late),
        join(weight_ref, core_ref),
        feature,
        preferred_element_type=jnp.float32,
    ) + lax.dot_general(
        jnp.where(lower_pair, late, early),
        join(cross_ref, core_cross_ref),
        feature,
        preferred_element_type=jnp.float32,
    )
    slab_cols = center_ref.shape[0]
    col_pairs = slab_cols
    own_tokens = embedded_ref.shape[0]
    couples = own_tokens // col_pairs
    final_wide = repeat_pairs(final_ref[...], couples)
    wide = final_wide.shape[0]
    predicted = []
    for branch in range(2):
        rows = slice(branch * own_tokens, (branch + 1) * own_tokens)
        mixed = mixed_ref[rows, :].astype(jnp.float32) + other[rows]
        residual = embedded_ref[...] + modulation_ref[2:3, :] * mixed
        final_norm = (layer_norm(residual) * (1.0 + modulation_ref[3:4, :])).astype(jnp.bfloat16)
        predicted.append(
            lax.dot_general(
                final_norm,
                final_wide,
                (((1,), (1,)), ((), ())),
                preferred_element_type=jnp.float32,
            )
        )
    conditional, unconditional = predicted
    guided = unconditional + guidance_scale * (conditional - unconditional)
    lane_couple = lax.broadcasted_iota(jnp.int32, (col_pairs, wide), 1) % (2 * couples) // 2
    pairs = jnp.zeros((col_pairs, wide), jnp.float32)
    for couple in range(couples):
        pairs = pairs + jnp.where(
            lane_couple == couple, guided[couple * col_pairs : (couple + 1) * col_pairs], 0.0
        )
    weight_value = blend_ref[0].astype(jnp.float32)
    half = wide // 2
    is_noise = lax.broadcasted_iota(jnp.int32, (col_pairs, wide), 1) < half
    even = jnp.where(is_noise, weight_value * pairs, weight_value)
    odd = jnp.where(is_noise, weight_value * pltpu.roll(pairs, half, 1), weight_value)
    start_copy.wait()
    start_at = start_ref[0, 0]
    buffer_ref[...] = jnp.zeros_like(buffer_ref)
    buffer_ref[pl.ds(start_at, col_pairs, stride=2), :] = even
    buffer_ref[pl.ds(start_at + 1, col_pairs, stride=2), :] = odd
    center_ref[...] = buffer_ref[slab_cols : 2 * slab_cols]
    left, right = buffer_ref[:slab_cols], buffer_ref[2 * slab_cols : 3 * slab_cols]
    near_ref[...] = jnp.where(even_place, right, left)
    far_ref[...] = jnp.where(even_place, left, right)


def blend_kernel(plan_ref, center_ref, near_ref, far_ref, rows_ref, previous_ref, noise_ref):
    channels, half_rows, slab_cols = noise_ref.shape
    total = jnp.transpose(center_ref[...] + near_ref[...] + far_ref[...], (1, 0))
    half = total.shape[0] // 2
    noise = total[:half] / total[half:]
    scale = plan_ref[:, :slab_cols]
    previous = (
        scale[0:1] * (rows_ref[...] - scale[1:2] * noise) / scale[2:3] + scale[3:4] * noise
    )
    for channel in range(channels):
        rows = slice(channel * half_rows, (channel + 1) * half_rows)
        noise_ref[channel] = noise[rows]
        previous_ref[channel] = previous[rows]


def on_device(
    latent,
    text_kv,
    modulation,
    qkv_weight,
    out_weight,
    patch_weight,
    final_weight,
    offsets,
    blend_weights,
    step_index,
):
    slab_cols, channels, row_count = latent.shape
    model_width = patch_weight.shape[1]
    half_attn = out_weight.shape[0]
    heads = half_attn // HEAD_DIM
    branches = text_kv.shape[0]
    col_pairs, row_couples = slab_cols, row_count // 2
    tokens = col_pairs * row_couples
    own_tokens = tokens // 2
    half_rows = row_count // 2
    far = swap_ring(latent, "win", 1)
    near = swap_ring(latent, "win", 0)
    hbm = pl.BlockSpec(memory_space=pltpu.HBM)
    keep = functools.partial(pltpu.with_memory_space_constraint, memory_space=pltpu.HBM)
    weight = jnp.transpose(qkv_weight, (1, 2, 0)).reshape(3 * half_attn, model_width)
    text = jnp.transpose(text_kv, (0, 1, 3, 2))
    final = jnp.transpose(final_weight, (1, 0))

    bf16, f32 = jnp.bfloat16, jnp.float32
    shape = jax.ShapeDtypeStruct
    wide = 2 * channels * half_rows
    half_width = model_width // 2
    below, above = half_width // 128 * 128, -(-half_width // 128) * 128
    row_part, col_part, patch_wide, start, modulate, own, quarter = pl.pallas_call(
        prepare_kernel,
        out_shape=(
            shape((row_couples, above), f32),
            shape((col_pairs, model_width - below), f32),
            shape((2 * channels * row_count, model_width), bf16),
            shape((8, -(-3 * slab_cols // 128) * 128), jnp.int32),
            shape(modulation.shape[1:], f32),
            shape(latent.shape, f32),
            shape((half_attn // 4, model_width), bf16),
        ),
        grid_spec=pltpu.PrefetchScalarGridSpec(
            num_scalar_prefetch=2,
            grid=(1,),
            in_specs=[hbm] * 4,
            out_specs=(VM,) * 7,
            scratch_shapes=[
                pltpu.VMEM(patch_weight.shape, bf16),
                pltpu.SemaphoreType.DMA((4,)),
            ],
        ),
        name="prepare",
        compiler_params=pltpu.CompilerParams(vmem_limit_bytes=GRANT),
        cost_estimate=pl.CostEstimate(flops=10**7, bytes_accessed=10**6, transcendentals=10**5),
    )(step_index, offsets, *map(keep, (latent, patch_weight, modulation, out_weight)))
    other_weight = swap(quarter, "cfg")
    projected, embedded, text, sent = pl.pallas_call(
        project_kernel,
        out_shape=(
            shape((3 * heads, HEAD_DIM, tokens), bf16),
            shape((own_tokens, model_width), f32),
            shape(text.shape, bf16),
            shape((half_attn // 2, branches * own_tokens), bf16),
        ),
        in_specs=[VM] * 8 + [hbm] * 2,
        out_specs=(VM,) * 4,
        scratch_shapes=[
            pltpu.VMEM((3 * slab_cols, channels * row_count), f32),
            pltpu.VMEM(weight.shape, bf16),
            pltpu.SemaphoreType.DMA((2,)),
        ],
        name="project",
        compiler_params=pltpu.CompilerParams(vmem_limit_bytes=GRANT),
        cost_estimate=pl.CostEstimate(flops=2 * 10**9, bytes_accessed=8 * 10**6, transcendentals=10**6),
    )(
        start, modulate, near, own, far, row_part, col_part, patch_wide, keep(weight), keep(text)
    )
    early = swap(sent, "cfg")
    sent = pl.pallas_call(
        second_kernel,
        out_shape=shape((half_attn // 2, branches * own_tokens), bf16),
        in_specs=[VM] * 2,
        out_specs=VM,
        name="second",
        compiler_params=pltpu.CompilerParams(vmem_limit_bytes=GRANT),
        cost_estimate=pl.CostEstimate(flops=10**9, bytes_accessed=10**6, transcendentals=10**6),
    )(projected, text)
    late = swap(sent, "cfg")
    cross_weight = swap_across(other_weight, "win", 2)
    core_weight = swap_across(other_weight, "win", 1)
    core_cross_weight = swap_across(cross_weight, "win", 1)
    mixed = pl.pallas_call(
        attend_kernel,
        out_shape=shape((branches * own_tokens, model_width), bf16),
        in_specs=[VM] * 2 + [hbm],
        out_specs=VM,
        scratch_shapes=[pltpu.VMEM(out_weight.shape, bf16), pltpu.SemaphoreType.DMA],
        name="attend",
        compiler_params=pltpu.CompilerParams(vmem_limit_bytes=GRANT),
        cost_estimate=pl.CostEstimate(flops=10**9, bytes_accessed=8 * 10**6, transcendentals=10**6),
    )(projected, text, keep(out_weight))
    plan_values, rows = pl.pallas_call(
        coefficient_kernel,
        out_shape=(
            shape((8, -(-slab_cols // 128) * 128), f32),
            shape((channels * half_rows, slab_cols), f32),
        ),
        in_specs=[VM, VM],
        out_specs=(VM, VM),
        name="coefficient",
        compiler_params=pltpu.CompilerParams(vmem_limit_bytes=GRANT),
        cost_estimate=pl.CostEstimate(flops=10**5, bytes_accessed=10**5, transcendentals=10**4),
    )(start, own)
    to_near, center, to_far = pl.pallas_call(
        finish_kernel,
        out_shape=tuple(shape((slab_cols, wide), f32) for _ in range(3)),
        in_specs=[VM, SM] + [VM] * 10,
        out_specs=(VM, VM, VM),
        scratch_shapes=[
            pltpu.VMEM((3 * slab_cols + 8, wide), f32),
            pltpu.SMEM(start.shape, jnp.int32),
            pltpu.SemaphoreType.DMA,
        ],
        name="finish",
        compiler_params=pltpu.CompilerParams(vmem_limit_bytes=GRANT),
        cost_estimate=pl.CostEstimate(flops=10**9, bytes_accessed=4 * 10**6, transcendentals=10**3),
    )(
        start, blend_weights, modulate, embedded, mixed, early, late,
        other_weight, core_weight, cross_weight, core_cross_weight, final,
    )
    from_far = swap_ring(to_far, "win", 1)
    from_near = swap_ring(to_near, "win", 0)
    previous, noise = pl.pallas_call(
        blend_kernel,
        out_shape=tuple(shape((channels, half_rows, slab_cols), f32) for _ in range(2)),
        in_specs=[VM] * 5,
        out_specs=(VM, VM),
        name="blend",
        compiler_params=pltpu.CompilerParams(vmem_limit_bytes=GRANT),
    )(plan_values, center, from_near, from_far, rows)
    return (jnp.transpose(previous, (2, 0, 1)), jnp.transpose(noise, (2, 0, 1)))


def solution(mesh):
    in_specs = (
        P("win", None, None),
        P(None, None, None, "cfg"),
        P(),
        P(None, None, "cfg"),
        P("cfg", None),
        P(),
        P(),
        P("win"),
        P("win"),
        P(),
    )
    out_specs = (P("win", None, "cfg"), P("win", None, "cfg"))
    return jax.shard_map(
        on_device, mesh=mesh, in_specs=in_specs, out_specs=out_specs, check_vma=False
    )
```

time: 46.2 us -> 34.4 us (0.74)
  waiting for transfers between devices: 10.9 us -> 3.45 us
  Pallas kernels: 14.8 us -> 12 us
  starting transfers between devices: 17.5 us -> 16.1 us
    ppermute x2 -> x3, waiting for transfers between devices: 8.85 us -> 0.01 us  [swap_across(): lax.ppermute(array, axis, [(place, place ^ step) for place in range(size)])]
    ppermute x2 -> x3, starting transfers between devices: 6.23 us -> 1.82 us  [swap_across(): lax.ppermute(array, axis, [(place, place ^ step) for place in range(size)])]
    ppermute x2 -> x3, starting transfers between devices: 2.09 us -> 5.22 us  [swap(): return lax.ppermute(array, axis, [(0, 1), (1, 0)])]
    pallas_call x3 -> x4, Pallas kernels: 7.1 us -> 5.14 us  [the longest x1 3.21 us: on_device(): pl.pallas_call(attend_kernel, out_shape=shape((branches * own_tokens, mod...]
    ppermute x2 -> x3, waiting for transfers between devices: 0.01 us -> 1.02 us  [swap(): return lax.ppermute(array, axis, [(0, 1), (1, 0)])]
    pallas_call x1, Pallas kernels: 4.63 us -> 4.05 us  [on_device(): pl.pallas_call(project_kernel, out_shape=(shape((3 * heads, HEAD_DIM, tok...]
  transfers between devices with their start and end apart: 8 -> 10, of which waited for: 2 -> 3; matrix products, arithmetic and copies ran while one was open for 0% -> 0% of each run, Pallas kernels for 26% -> 24%
where the time goes in v5:
time: 34.4 us; the launch traced here: 34.1 us
  starting transfers between devices  16.1 us (47%)
  Pallas kernels  12 us (35%)
  waiting for transfers between devices  3.45 us (10%)
  between operations  2.66 us (8%)
    ppermute x4, starting transfers between devices, swap_ring(): return lax.ppermute(array, axis, pairs)  9.04 us
    ppermute x3, starting transfers between devices, swap(): return lax.ppermute(array, axis, [(0, 1), (1, 0)])  5.22 us
    pallas_call x1, Pallas kernels, on_device(): pl.pallas_call(project_kernel, out_shape=(shape((3 * heads, HEAD_DIM, tok...  4.05 us
    pallas_call x1, Pallas kernels, on_device(): pl.pallas_call(attend_kernel, out_shape=shape((branches * own_tokens, mod...  3.21 us
    ppermute x4, waiting for transfers between devices, swap_ring(): return lax.ppermute(array, axis, pairs)  2.41 us
    pallas_call x1, Pallas kernels, on_device(): pl.pallas_call(finish_kernel, out_shape=tuple((shape((slab_cols, wide), f...  2.02 us
    ppermute x3, starting transfers between devices, swap_across(): lax.ppermute(array, axis, [(place, place ^ step) for place in range(size)])  1.82 us
    pallas_call x1, Pallas kernels, on_device(): pl.pallas_call(prepare_kernel, out_shape=(shape((row_couples, above), f32...  1.03 us
  transfers between devices with their start and end apart: 10, of which 3 were waited for; matrix products, arithmetic and copies ran while one was open for 0% of the time, Pallas kernels for 24%

profile of v5, /device:TPU:0, one launch (start us, length us, event | category | flops | bytes accessed | tf_op | source)
XLA Modules:
  0.0 34.1 jit_solution(3176542904833462991)
XLA Ops:
  1.9 1.0 %prepare.1 = (f32[16,640]{1,0:T(8,128)S(1)}, f32[32,640]{1,0:T(8,128)S(1)}, bf16[256,1152]{1,0:T(8,128)(2,1)S(1)}, s32[8,128]{1,0:T(8,128)S(1)}, f32[4,1152]{1,0...) custom-call(s32[1]{0:T(128)S(6)} %copy.14.step_ref, s32[1]{0:T(128)S(6)} %copy.12.offset_ref, ...), custom_call_target="tpu_custom_call" | custom-call | flops 10000000 | bytes 1000000 | tf_op jit(solution)/shard_map/prepare/pallas_call | solution.py:492
  3.0 3.1 %collective-permute-start.4 = (bf16[72,1152]{1,0:T(8,128)(2,1)S(1)}, bf16[72,1152]{1,0:T(8,128)(2,1)S(1)}, u32[]{:S(2)}, u32[]{:S(2)}) collective-permute-start(bf16[72,1152]{1,0:T(8,128)(2,1)S(1)} %get-tuple-element.31), channel_id=1, source_target_pairs={{0,16},{16,0},{1,17},{17,1},{2,18},{18,2},{3,19},{19,3},{4,20},{20... | collective-permute-start | bytes 497672 | tf_op jit(solution)/shard_map/ppermute | solution.py:35
  6.0 0.0 collective-permute-start
  6.0 4.6 %collective-permute-start.1 = (f32[32,4,32]{2,1,0:T(4,128)}, f32[32,4,32]{2,1,0:T(4,128)S(1)}, u32[]{:S(2)}, u32[]{:S(2)}) collective-permute-start(f32[32,4,32]{2,1,0:T(4,128)} %latent_source.1), channel_id=1, source_target_pairs={{1,2},{2,1},{3,4},{4,3},{5,6},{6,5},{7,8},{8,7},{9,10},{10,9},{11,... | collective-permute-start | bytes 49160 | tf_op jit(solution)/shard_map/ppermute | solution.py:31
  10.7 0.0 collective-permute-done.4.weight_ref
  10.7 1.3 %collective-permute-start.6 = (bf16[72,1152]{1,0:T(8,128)(2,1)S(1)}, bf16[72,1152]{1,0:T(8,128)(2,1)S(1)}, u32[]{:S(2)}, u32[]{:S(2)}) collective-permute-start(bf16[72,1152]{1,0:T(8,128)(2,1)S(1)} %collective-permute-done.4.weight_ref), channel_id=1, source_target_pairs={{0,2},{1,3},{2,0},{3,1},{4,6},{5,7},{6,4},{7,5},{8,10},{9,11},{10,... | collective-permute-start | bytes 497672 | tf_op jit(solution)/shard_map/ppermute | solution.py:40
  12.0 0.0 collective-permute-done.near_ref
  12.0 0.9 %collective-permute-done.1.far_ref = f32[32,4,32]{2,1,0:T(4,128)S(1)} collective-permute-done((f32[32,4,32]{2,1,0:T(4,128)}, f32[32,4,32]{2,1,0:T(4,128)S(1)}, u32[]{:S(2)}, u32[]{:S(2)}) %collective-permute-start.1) | collective-permute-done | bytes 16416 | tf_op jit(solution)/shard_map/ppermute | solution.py:31
  12.9 4.1 %project.1 = (bf16[12,72,512]{2,1,0:T(8,128)(2,1)S(1)}, f32[256,1152]{1,0:T(8,128)S(1)}, bf16[2,2,288,120]{3,2,1,0:T(8,128)(2,1)S(1)}, bf16[144,512]{1,0:T(8,128)(2,1)S(1)}) custom-call(s32[8,128]{1,0:T(8,128)S(1)} %get-tuple-element.20.start_ref.start_source, f32[4,1152]{1,0:T(4,128)S(1)} %get-tuple-element.23.modulation_ref, ...), custom_call_target="tpu_custom_call" | custom-call | flops 2000000000 | bytes 8000000 | tf_op jit(solution)/shard_map/project/pallas_call | solution.py:518
  17.0 0.6 %collective-permute-start.2 = (bf16[144,512]{1,0:T(8,128)(2,1)S(1)}, bf16[144,512]{1,0:T(8,128)(2,1)S(1)}, u32[]{:S(2)}, u32[]{:S(2)}) collective-permute-start(bf16[144,512]{1,0:T(8,128)(2,1)S(1)} %get-tuple-element.30), channel_id=1, source_target_pairs={{0,16},{16,0},{1,17},{17,1},{2,18},{18,2},{3,19},{19,3},{4,20},{20... | collective-permute-start | bytes 442376 | tf_op jit(solution)/shard_map/ppermute | solution.py:35
  17.6 0.0 collective-permute-start.5
  17.6 0.0 collective-permute-done.6.cross_ref
  17.6 0.5 %collective-permute-start.7 = (bf16[72,1152]{1,0:T(8,128)(2,1)S(1)}, bf16[72,1152]{1,0:T(8,128)(2,1)S(1)}, u32[]{:S(2)}, u32[]{:S(2)}) collective-permute-start(bf16[72,1152]{1,0:T(8,128)(2,1)S(1)} %collective-permute-done.6.cross_ref), channel_id=1, source_target_pairs={{0,1},{1,0},{2,3},{3,2},{4,5},{5,4},{6,7},{7,6},{8,9},{9,8},{10,11... | collective-permute-start | bytes 497672 | tf_op jit(solution)/shard_map/ppermute | solution.py:40
  18.1 0.8 %second.1 = bf16[144,512]{1,0:T(8,128)(2,1)S(1)} custom-call(bf16[12,72,512]{2,1,0:T(8,128)(2,1)S(1)} %get-tuple-element.28.proj_ref, bf16[2,2,288,120]{3,2,1,0:T(8,128)(2,1)S(1)} %get-tuple-element.29.text_ref), custom_call_target="tpu_custom_call" | custom-call | flops 1000000000 | bytes 1000000 | tf_op jit(solution)/shard_map/second/pallas_call | solution.py:540
  18.9 1.5 %collective-permute-start.3 = (bf16[144,512]{1,0:T(8,128)(2,1)S(1)}, bf16[144,512]{1,0:T(8,128)(2,1)S(1)}, u32[]{:S(2)}, u32[]{:S(2)}) collective-permute-start(bf16[144,512]{1,0:T(8,128)(2,1)S(1)} %second.1), channel_id=1, source_target_pairs={{0,16},{16,0},{1,17},{17,1},{2,18},{18,2},{3,19},{19,3},{4,20},{20... | collective-permute-start | bytes 442376 | tf_op jit(solution)/shard_map/ppermute | solution.py:35
  21.1 0.0 copy-start
  21.1 3.2 %attend.1.mixed_ref = bf16[512,1152]{1,0:T(8,128)(2,1)S(1)} custom-call(bf16[12,72,512]{2,1,0:T(8,128)(2,1)S(1)} %get-tuple-element.28.proj_ref, bf16[2,2,288,120]{3,2,1,0:T(8,128)(2,1)S(1)} %get-tuple-element.29.text_ref, bf16[288,1152]{1,0:T(8,128)(2,1)} %weight_source.1), custom_call_target="tpu_custom_call" | custom-call | flops 1000000000 | bytes 8000000 | tf_op jit(solution)/shard_map/attend/pallas_call | solution.py:553
  24.3 0.0 collective-permute-done.2.early_ref
  24.3 1.0 %collective-permute-done.3.late_ref = bf16[144,512]{1,0:T(8,128)(2,1)S(1)} collective-permute-done((bf16[144,512]{1,0:T(8,128)(2,1)S(1)}, bf16[144,512]{1,0:T(8,128)(2,1)S(1)}, u32[]{:S(2)}, u32[]{:S(2)}) %collective-permute-start.3) | collective-permute-done | bytes 147488 | tf_op jit(solution)/shard_map/ppermute | solution.py:35
  25.4 0.0 collective-permute-done.5.core_ref
  25.4 0.0 collective-permute-done.7.core_cross_ref
  25.4 0.0 copy-done
  25.4 2.0 %finish.1 = (f32[32,128]{1,0:T(8,128)S(1)}, f32[32,128]{1,0:T(8,128)S(1)}, f32[32,128]{1,0:T(8,128)S(1)}) custom-call(s32[8,128]{1,0:T(8,128)S(1)} %get-tuple-element.20.start_ref.start_source, s32[1]{0:T(128)S(6)} %copy.13.blend_ref, f32[4,1152]{1,0:T(4,128)S(1)} %get-tuple-element.23.modulation_ref, f32[256,1152]{1,0:T(8,128)S(1)} %get-tuple-element.27.embedded_ref, ...), custom_call_target="tpu_custom_call" | custom-call | flops 1000000000 | bytes 4000000 | tf_op jit(solution)/shard_map/finish/pallas_call | solution.py:575
  27.4 0.1 collective-permute-start.8
  27.5 4.3 %collective-permute-start.9 = (f32[32,128]{1,0:T(8,128)S(1)}, f32[32,128]{1,0:T(8,128)S(1)}, u32[]{:S(2)}, u32[]{:S(2)}) collective-permute-start(f32[32,128]{1,0:T(8,128)S(1)} %get-tuple-element.34), channel_id=1, source_target_pairs={{1,2},{2,1},{3,4},{4,3},{5,6},{6,5},{7,8},{8,7},{9,10},{10,9},{11,... | collective-permute-start | bytes 49160 | tf_op jit(solution)/shard_map/ppermute | solution.py:31
  31.8 0.1 coefficient.1
  31.9 0.0 collective-permute-done.8.near_ref
  31.9 1.5 %collective-permute-done.9.far_ref = f32[32,128]{1,0:T(8,128)S(1)} collective-permute-done((f32[32,128]{1,0:T(8,128)S(1)}, f32[32,128]{1,0:T(8,128)S(1)}, u32[]{:S(2)}, u32[]{:S(2)}) %collective-permute-start.9) | collective-permute-done | bytes 16416 | tf_op jit(solution)/shard_map/ppermute | solution.py:31
  33.4 0.7 %blend.1 = (f32[4,16,32]{2,1,0:T(8,128)}, f32[4,16,32]{2,1,0:T(8,128)}) custom-call(f32[8,128]{1,0:T(8,128)S(1)} %get-tuple-element.22.plan_ref, f32[32,128]{1,0:T(8,128)S(1)} %get-tuple-element.32.center_ref, f32[32,128]{1,0:T(8,128)S(1)} %collective-permute-done.8.near_ref, f32[32,128]{1,0:T(8,128)S(1)} %collective-permute-done.9.far_ref, ...), custom_call_target="tpu_custom_call" | custom-call | tf_op jit(solution)/shard_map/blend/pallas_call | solution.py:594
Async XLA Ops:
  3.0 7.7 %collective-permute-start.4 = (bf16[72,1152]{1,0:T(8,128)(2,1)S(1)}, bf16[72,1152]{1,0:T(8,128)(2,1)S(1)}, u32[]{:S(2)}, u32[]{:S(2)}) collective-permute-start(bf16[72,1152]{1,0:T(8,128)(2,1)S(1)} %get-tuple-element.31), channel_id=1, source_target_pairs={{0,16},{16,0},{1,17},{17,1},{2,18},{18,2},{3,19},{19,3},{4,20},{20... | collective-permute-start | bytes 497672 | tf_op jit(solution)/shard_map/ppermute | solution.py:35
  6.0 6.0 %collective-permute-start = (f32[32,4,32]{2,1,0:T(4,128)}, f32[32,4,32]{2,1,0:T(4,128)S(1)}, u32[]{:S(2)}, u32[]{:S(2)}) collective-permute-start(f32[32,4,32]{2,1,0:T(4,128)} %latent_source.1), channel_id=1, source_target_pairs={{0,1},{1,0},{2,3},{3,2},{4,5},{5,4},{6,7},{7,6},{8,9},{9,8},{10,11... | collective-permute-start | bytes 49160 | tf_op jit(solution)/shard_map/ppermute | solution.py:31
  6.0 6.9 %collective-permute-start.1 = (f32[32,4,32]{2,1,0:T(4,128)}, f32[32,4,32]{2,1,0:T(4,128)S(1)}, u32[]{:S(2)}, u32[]{:S(2)}) collective-permute-start(f32[32,4,32]{2,1,0:T(4,128)} %latent_source.1), channel_id=1, source_target_pairs={{1,2},{2,1},{3,4},{4,3},{5,6},{6,5},{7,8},{8,7},{9,10},{10,9},{11,... | collective-permute-start | bytes 49160 | tf_op jit(solution)/shard_map/ppermute | solution.py:31
  10.7 7.0 %collective-permute-start.6 = (bf16[72,1152]{1,0:T(8,128)(2,1)S(1)}, bf16[72,1152]{1,0:T(8,128)(2,1)S(1)}, u32[]{:S(2)}, u32[]{:S(2)}) collective-permute-start(bf16[72,1152]{1,0:T(8,128)(2,1)S(1)} %collective-permute-done.4.weight_ref), channel_id=1, source_target_pairs={{0,2},{1,3},{2,0},{3,1},{4,6},{5,7},{6,4},{7,5},{8,10},{9,11},{10,... | collective-permute-start | bytes 497672 | tf_op jit(solution)/shard_map/ppermute | solution.py:40
  17.0 7.3 %collective-permute-start.2 = (bf16[144,512]{1,0:T(8,128)(2,1)S(1)}, bf16[144,512]{1,0:T(8,128)(2,1)S(1)}, u32[]{:S(2)}, u32[]{:S(2)}) collective-permute-start(bf16[144,512]{1,0:T(8,128)(2,1)S(1)} %get-tuple-element.30), channel_id=1, source_target_pairs={{0,16},{16,0},{1,17},{17,1},{2,18},{18,2},{3,19},{19,3},{4,20},{20... | collective-permute-start | bytes 442376 | tf_op jit(solution)/shard_map/ppermute | solution.py:35
  17.6 7.7 %collective-permute-start.5 = (bf16[72,1152]{1,0:T(8,128)(2,1)S(1)}, bf16[72,1152]{1,0:T(8,128)(2,1)S(1)}, u32[]{:S(2)}, u32[]{:S(2)}) collective-permute-start(bf16[72,1152]{1,0:T(8,128)(2,1)S(1)} %collective-permute-done.4.weight_ref), channel_id=1, source_target_pairs={{0,1},{1,0},{2,3},{3,2},{4,5},{5,4},{6,7},{7,6},{8,9},{9,8},{10,11... | collective-permute-start | bytes 497672 | tf_op jit(solution)/shard_map/ppermute | solution.py:40
  17.6 7.7 %collective-permute-start.7 = (bf16[72,1152]{1,0:T(8,128)(2,1)S(1)}, bf16[72,1152]{1,0:T(8,128)(2,1)S(1)}, u32[]{:S(2)}, u32[]{:S(2)}) collective-permute-start(bf16[72,1152]{1,0:T(8,128)(2,1)S(1)} %collective-permute-done.6.cross_ref), channel_id=1, source_target_pairs={{0,1},{1,0},{2,3},{3,2},{4,5},{5,4},{6,7},{7,6},{8,9},{9,8},{10,11... | collective-permute-start | bytes 497672 | tf_op jit(solution)/shard_map/ppermute | solution.py:40
  18.9 6.4 %collective-permute-start.3 = (bf16[144,512]{1,0:T(8,128)(2,1)S(1)}, bf16[144,512]{1,0:T(8,128)(2,1)S(1)}, u32[]{:S(2)}, u32[]{:S(2)}) collective-permute-start(bf16[144,512]{1,0:T(8,128)(2,1)S(1)} %second.1), channel_id=1, source_target_pairs={{0,16},{16,0},{1,17},{17,1},{2,18},{18,2},{3,19},{19,3},{4,20},{20... | collective-permute-start | bytes 442376 | tf_op jit(solution)/shard_map/ppermute | solution.py:35
  21.1 4.3 %copy-start = (bf16[1152,16]{0,1:T(8,128)(2,1)S(1)}, bf16[1152,16]{0,1:T(8,128)(2,1)}, u32[]{:S(2)}) copy-start(bf16[1152,16]{0,1:T(8,128)(2,1)} %param.16) | copy-start | bytes 110596
  27.4 4.5 %collective-permute-start.8 = (f32[32,128]{1,0:T(8,128)S(1)}, f32[32,128]{1,0:T(8,128)S(1)}, u32[]{:S(2)}, u32[]{:S(2)}) collective-permute-start(f32[32,128]{1,0:T(8,128)S(1)} %get-tuple-element.33), channel_id=1, source_target_pairs={{0,1},{1,0},{2,3},{3,2},{4,5},{5,4},{6,7},{7,6},{8,9},{9,8},{10,11... | collective-permute-start | bytes 49160 | tf_op jit(solution)/shard_map/ppermute | solution.py:31
  27.5 5.9 %collective-permute-start.9 = (f32[32,128]{1,0:T(8,128)S(1)}, f32[32,128]{1,0:T(8,128)S(1)}, u32[]{:S(2)}, u32[]{:S(2)}) collective-permute-start(f32[32,128]{1,0:T(8,128)S(1)} %get-tuple-element.34), channel_id=1, source_target_pairs={{1,2},{2,1},{3,4},{4,3},{5,6},{6,5},{7,8},{8,7},{9,10},{10,9},{11,... | collective-permute-start | bytes 49160 | tf_op jit(solution)/shard_map/ppermute | solution.py:31

commit v6 on v5

--- a/solution.py
+++ b/solution.py
@@ -60,8 +60,6 @@
 
 
 def prepare_kernel(
-    step_ref,
-    offset_ref,
     latent_source,
     patch_source,
     modulation_ref,
@@ -69,8 +67,7 @@
     row_ref,
     col_ref,
     patch_wide_ref,
-    start_ref,
-    modulate_copy,
+    modulation_copy,
     latent_copy,
     quarter_copy,
     patch_ref,
@@ -78,13 +75,12 @@
 ):
     count = quarter_copy.shape[0]
     quarter_first = pl.multiple_of(lax.axis_index("win") % 4 * count, 8)
-    row = step_ref[0] * STEPS // plan_length
     copies = [
         pltpu.make_async_copy(source, target, semaphores.at[place])
         for place, (source, target) in enumerate(
             (
                 (patch_source, patch_ref),
-                (modulation_ref.at[row], modulate_copy),
+                (modulation_ref, modulation_copy),
                 (latent_source, latent_copy),
                 (out_source.at[pl.ds(quarter_first, count)], quarter_copy),
             )
@@ -92,7 +88,7 @@
     ]
     for copy in copies:
         copy.start()
-    slab_cols, _, row_count = latent_copy.shape
+    _, _, row_count = latent_copy.shape
     model_width = patch_ref.shape[1]
     quarter = model_width // 4
 
@@ -106,17 +102,15 @@
 
     table(row_ref, 0)
     table(col_ref, model_width - col_ref.shape[1])
-    is_start = lax.broadcasted_iota(jnp.int32, start_ref.shape, 0) == 0
-    start_ref[...] = jnp.where(is_start, slab_cols - offset_ref[0], step_ref[0])
     copies[0].wait()
     patch_wide_ref[...] = repeat_pairs(patch_ref[...], row_count // 2)
     for copy in copies[1:]:
         copy.wait()
 
 
-def coefficient_kernel(start_ref, latent_ref, plan_ref, rows_ref):
+def coefficient_kernel(step_ref, latent_ref, plan_ref, rows_ref):
     _, channels, row_count = latent_ref.shape
-    moment = start_ref[1:2, :128]
+    moment = step_ref[0]
     index = lax.broadcasted_iota(jnp.int32, (8, 128), 0) * 128 + lax.broadcasted_iota(
         jnp.int32, (8, 128), 1
     )
@@ -150,18 +144,24 @@
         )
 
 
-def attend(proj_ref, text_ref, first, count, chosen, finished):
-    heads = proj_ref.shape[0] // 3
+def first_pair():
+    return lax.axis_index("win") % 4 // 2
+
+
+def attend(parts, text_ref, first, count, chosen, finished):
     branches = text_ref.shape[0]
     feature = (((0,), (0,)), ((), ()))
 
+    def place_of(head):
+        pair = first_pair() if head < 2 else 1 - first_pair()
+        return 2 * pair + head % 2
+
     def score(head):
-        rows = slice(head * HEAD_DIM, (head + 1) * HEAD_DIM)
-        queries = proj_ref[head, :, pl.ds(first, count)]
+        queries = parts[head // 2][head % 2, :, pl.ds(first, count)]
         return [
             lax.dot_general(keys, queries, feature, preferred_element_type=jnp.float32)
-            for keys in [proj_ref[heads + head]]
-            + [text_ref[branch, 0, rows, :] for branch in range(branches)]
+            for keys in [parts[head // 2][2 + head % 2]]
+            + [text_ref[branch, 0, place_of(head)] for branch in range(branches)]
         ]
 
     def weigh(scores):
@@ -178,14 +178,13 @@
         return own[0], texts
 
     def mix(head, own_exp, texts):
-        rows = slice(head * HEAD_DIM, (head + 1) * HEAD_DIM)
         own_mix = jnp.dot(
-            proj_ref[2 * heads + head], own_exp, preferred_element_type=jnp.float32
+            parts[head // 2][4 + head % 2], own_exp, preferred_element_type=jnp.float32
         )
         results = []
         for branch, (text_exp, lowered, inverse) in enumerate(texts):
             text_mix = jnp.dot(
-                text_ref[branch, 1, rows, :], text_exp, preferred_element_type=jnp.float32
+                text_ref[branch, 1, place_of(head)], text_exp, preferred_element_type=jnp.float32
             )
             results.append((lowered * own_mix + text_mix) * inverse)
         return jnp.concatenate(results, axis=1)
@@ -215,9 +214,34 @@
     target_ref[...] = pair
 
 
+def weight_copies(weight_source, weight_ref, half, semaphores):
+    count = weight_ref.shape[0] // 3
+    total = weight_source.shape[0] // 3
+    return [
+        pltpu.make_async_copy(
+            weight_source.at[pl.ds(pl.multiple_of(kind * total + half * count, 16), count)],
+            weight_ref.at[pl.ds(kind * count, count)],
+            semaphores.at[kind],
+        )
+        for kind in range(3)
+    ]
+
+
+def project_half(weight_ref, normed, target_ref, lanes):
+    projected = lax.dot_general(
+        weight_ref[...], normed, (((1,), (1,)), ((), ())), preferred_element_type=jnp.float32
+    )
+    for block in range(target_ref.shape[0]):
+        part = projected[block * HEAD_DIM : (block + 1) * HEAD_DIM]
+        if block < target_ref.shape[0] // 3:
+            part = part * (math.log2(math.e) / math.sqrt(HEAD_DIM))
+        target_ref[block, :, lanes] = part.astype(jnp.bfloat16)
+
+
 def project_kernel(
-    start_ref,
-    modulation_ref,
+    step_ref,
+    offset_ref,
+    modulations_ref,
     near_ref,
     own_ref,
     far_ref,
@@ -227,17 +251,25 @@
     weight_source,
     text_source,
     proj_ref,
+    normed_ref,
+    modulation_ref,
     embedded_ref,
     text_ref,
+    late_weight_ref,
     sent_ref,
     extended_ref,
     weight_ref,
     semaphores,
 ):
-    weight_copy = pltpu.make_async_copy(weight_source, weight_ref, semaphores.at[0])
-    text_copy = pltpu.make_async_copy(text_source, text_ref, semaphores.at[1])
-    weight_copy.start()
-    text_copy.start()
+    pair = first_pair()
+    copies = weight_copies(weight_source, weight_ref, pair, semaphores.at[pl.ds(0, 3)])
+    late_copies = weight_copies(
+        weight_source, late_weight_ref, 1 - pair, semaphores.at[pl.ds(3, 3)]
+    )
+    text_copy = pltpu.make_async_copy(text_source, text_ref, semaphores.at[6])
+    for copy in copies + [text_copy] + late_copies:
+        copy.start()
+    modulation_ref[...] = modulations_ref[step_ref[0] * STEPS // plan_length]
     slab_cols, channels, row_count = own_ref.shape
     col_pairs, row_couples = slab_cols, row_count // 2
     tokens = col_pairs * row_couples
@@ -253,7 +285,7 @@
                 channel * row_count : (channel + 1) * row_count,
             ] = value
     extended = extended_ref[...].astype(jnp.bfloat16)
-    start_at = start_ref[0:1, : 3 * slab_cols]
+    start_at = slab_cols - offset_ref[0]
     chosen = lax.broadcasted_iota(jnp.int32, (2 * col_pairs, 3 * slab_cols), 0)
     column = lax.broadcasted_iota(jnp.int32, (2 * col_pairs, 3 * slab_cols), 1)
     target = jnp.where(
@@ -267,7 +299,6 @@
         [jnp.where(lane_couple == couple, picked, 0.0) for couple in range(row_couples)], axis=0
     ).astype(jnp.bfloat16)
     side = lax.axis_index("cfg")
-    heads = proj_ref.shape[0] // 3
     chunks = [slice(place * own_tokens, (place + 1) * own_tokens) for place in range(2)]
 
     couples = row_couples // 2
@@ -300,68 +331,85 @@
             layer_norm(embedded) * (1.0 + modulation_ref[1:2, :]) + modulation_ref[0:1, :]
         ).astype(jnp.bfloat16)
 
-    def project(place, normed):
-        projected = lax.dot_general(
-            weight_ref[...],
-            normed,
-            (((1,), (1,)), ((), ())),
-            preferred_element_type=jnp.float32,
-        )
-        for head in range(3 * heads):
-            part = projected[head * HEAD_DIM : (head + 1) * HEAD_DIM]
-            if head < heads:
-                part = part * (math.log2(math.e) / math.sqrt(HEAD_DIM))
-            proj_ref[head, :, chunks[place]] = part.astype(jnp.bfloat16)
-
     normed = norm(embed(0))
     later = embed(1)
-    weight_copy.wait()
-    project(0, normed)
-    project(1, norm(later))
+    for copy in copies:
+        copy.wait()
+    normed_ref[chunks[0], :] = normed
+    project_half(weight_ref, normed, proj_ref, chunks[0])
+    normed = norm(later)
+    normed_ref[chunks[1], :] = normed
+    project_half(weight_ref, normed, proj_ref, chunks[1])
     first = pl.multiple_of((1 - side) * own_tokens, own_tokens)
     text_copy.wait()
-    attend(proj_ref, text_ref, first, own_tokens, range(heads // 2), functools.partial(keep_pair, sent_ref))
-
-
-def second_kernel(proj_ref, text_ref, sent_ref):
-    heads = proj_ref.shape[0] // 3
-    own_tokens = proj_ref.shape[2] // 2
+    attend(
+        [proj_ref], text_ref, first, own_tokens, range(2), functools.partial(keep_pair, sent_ref)
+    )
+    for copy in late_copies:
+        copy.wait()
+
+
+def second_kernel(
+    normed_ref, text_ref, weight_ref, out_source, proj_ref, out_ref, sent_ref, semaphore
+):
+    out_copy = pltpu.make_async_copy(out_source, out_ref, semaphore)
+    out_copy.start()
+    own_tokens = normed_ref.shape[0] // 2
+    for place in range(2):
+        chunk = slice(place * own_tokens, (place + 1) * own_tokens)
+        project_half(weight_ref, normed_ref[chunk, :], proj_ref, chunk)
     first = pl.multiple_of((1 - lax.axis_index("cfg")) * own_tokens, own_tokens)
-    attend(proj_ref, text_ref, first, own_tokens, range(heads // 2, heads), functools.partial(keep_pair, sent_ref))
-
-
-def attend_kernel(proj_ref, text_ref, weight_source, mixed_ref, weight_ref, semaphore):
-    weight_copy = pltpu.make_async_copy(weight_source, weight_ref, semaphore)
-    weight_copy.start()
-    heads = proj_ref.shape[0] // 3
-    tokens = proj_ref.shape[2]
+    attend(
+        [None, proj_ref], text_ref, first, own_tokens, range(2, 4),
+        functools.partial(keep_pair, sent_ref),
+    )
+    out_copy.wait()
+
+
+def attend_kernel(early_ref, late_ref, text_ref, weight_ref, mixed_ref):
+    tokens = early_ref.shape[2]
     own_tokens = tokens // 2
     first = pl.multiple_of(lax.axis_index("cfg") * own_tokens, own_tokens)
-    weight_copy.wait()
     pairs = []
 
     def finished(place, pair):
         pairs.append(pair)
 
-    attend(proj_ref, text_ref, first, own_tokens, range(heads), finished)
-    mixed_ref[...] = lax.dot_general(
-        jnp.concatenate(pairs, axis=0),
-        weight_ref[...],
-        (((0,), (0,)), ((), ())),
-        preferred_element_type=jnp.float32,
-    ).astype(jnp.bfloat16)
+    attend([early_ref, late_ref], text_ref, first, own_tokens, range(4), finished)
+    count = 2 * HEAD_DIM
+    mixed = []
+    for place, pair in enumerate(pairs):
+        chosen = first_pair() if place == 0 else 1 - first_pair()
+        rows = pl.ds(pl.multiple_of(chosen * count, count), count)
+        mixed.append(contract(pair, weight_ref[rows, :]))
+    mixed_ref[...] = mixed[0] + mixed[1]
+
+
+def contract(features, weight):
+    return lax.dot_general(
+        features, weight, (((0,), (0,)), ((), ())), preferred_element_type=jnp.float32
+    )
+
+
+def join(mine_ref, neighbour_ref):
+    mine, neighbour = mine_ref[...].astype(jnp.float32), neighbour_ref[...].astype(jnp.float32)
+    even_place = lax.axis_index("win") % 2 == 0
+    first = jnp.where(even_place, mine, neighbour)
+    second = jnp.where(even_place, neighbour, mine)
+    return jnp.concatenate([first, second], axis=0).astype(jnp.bfloat16)
+
+
+def partial_kernel(mixed_ref, early_ref, weight_ref, core_ref, summed_ref):
+    summed_ref[...] = mixed_ref[...] + contract(early_ref[...], join(weight_ref, core_ref))
 
 
 def finish_kernel(
-    start_source,
+    offset_ref,
     blend_ref,
     modulation_ref,
     embedded_ref,
     mixed_ref,
-    early_ref,
     late_ref,
-    weight_ref,
-    core_ref,
     cross_ref,
     core_cross_ref,
     final_ref,
@@ -369,33 +417,9 @@
     center_ref,
     far_ref,
     buffer_ref,
-    start_ref,
-    semaphore,
 ):
-    start_copy = pltpu.make_async_copy(start_source, start_ref, semaphore)
-    start_copy.start()
     even_place = lax.axis_index("win") % 2 == 0
-    lower_pair = lax.axis_index("win") % 4 < 2
-
-    def join(mine, neighbour):
-        mine, neighbour = mine[...].astype(jnp.float32), neighbour[...].astype(jnp.float32)
-        first = jnp.where(even_place, mine, neighbour)
-        second = jnp.where(even_place, neighbour, mine)
-        return jnp.concatenate([first, second], axis=0).astype(jnp.bfloat16)
-
-    feature = (((0,), (0,)), ((), ()))
-    early, late = early_ref[...], late_ref[...]
-    other = lax.dot_general(
-        jnp.where(lower_pair, early, late),
-        join(weight_ref, core_ref),
-        feature,
-        preferred_element_type=jnp.float32,
-    ) + lax.dot_general(
-        jnp.where(lower_pair, late, early),
-        join(cross_ref, core_cross_ref),
-        feature,
-        preferred_element_type=jnp.float32,
-    )
+    other = contract(late_ref[...], join(cross_ref, core_cross_ref))
     slab_cols = center_ref.shape[0]
     col_pairs = slab_cols
     own_tokens = embedded_ref.shape[0]
@@ -405,7 +429,7 @@
     predicted = []
     for branch in range(2):
         rows = slice(branch * own_tokens, (branch + 1) * own_tokens)
-        mixed = mixed_ref[rows, :].astype(jnp.float32) + other[rows]
+        mixed = mixed_ref[rows, :] + other[rows]
         residual = embedded_ref[...] + modulation_ref[2:3, :] * mixed
         final_norm = (layer_norm(residual) * (1.0 + modulation_ref[3:4, :])).astype(jnp.bfloat16)
         predicted.append(
@@ -429,8 +453,7 @@
     is_noise = lax.broadcasted_iota(jnp.int32, (col_pairs, wide), 1) < half
     even = jnp.where(is_noise, weight_value * pairs, weight_value)
     odd = jnp.where(is_noise, weight_value * pltpu.roll(pairs, half, 1), weight_value)
-    start_copy.wait()
-    start_at = start_ref[0, 0]
+    start_at = slab_cols - offset_ref[0]
     buffer_ref[...] = jnp.zeros_like(buffer_ref)
     buffer_ref[pl.ds(start_at, col_pairs, stride=2), :] = even
     buffer_ref[pl.ds(start_at + 1, col_pairs, stride=2), :] = odd
@@ -471,7 +494,7 @@
     model_width = patch_weight.shape[1]
     half_attn = out_weight.shape[0]
     heads = half_attn // HEAD_DIM
-    branches = text_kv.shape[0]
+    branches, caption = text_kv.shape[0], text_kv.shape[2]
     col_pairs, row_couples = slab_cols, row_count // 2
     tokens = col_pairs * row_couples
     own_tokens = tokens // 2
@@ -481,7 +504,7 @@
     hbm = pl.BlockSpec(memory_space=pltpu.HBM)
     keep = functools.partial(pltpu.with_memory_space_constraint, memory_space=pltpu.HBM)
     weight = jnp.transpose(qkv_weight, (1, 2, 0)).reshape(3 * half_attn, model_width)
-    text = jnp.transpose(text_kv, (0, 1, 3, 2))
+    text = jnp.transpose(text_kv, (0, 1, 3, 2)).reshape(branches, 2, heads, HEAD_DIM, caption)
     final = jnp.transpose(final_weight, (1, 0))
 
     bf16, f32 = jnp.bfloat16, jnp.float32
@@ -489,105 +512,110 @@
     wide = 2 * channels * half_rows
     half_width = model_width // 2
     below, above = half_width // 128 * 128, -(-half_width // 128) * 128
-    row_part, col_part, patch_wide, start, modulate, own, quarter = pl.pallas_call(
+    row_part, col_part, patch_wide, modulations, own, quarter = pl.pallas_call(
         prepare_kernel,
         out_shape=(
             shape((row_couples, above), f32),
             shape((col_pairs, model_width - below), f32),
             shape((2 * channels * row_count, model_width), bf16),
-            shape((8, -(-3 * slab_cols // 128) * 128), jnp.int32),
-            shape(modulation.shape[1:], f32),
+            shape(modulation.shape, f32),
             shape(latent.shape, f32),
             shape((half_attn // 4, model_width), bf16),
         ),
-        grid_spec=pltpu.PrefetchScalarGridSpec(
-            num_scalar_prefetch=2,
-            grid=(1,),
-            in_specs=[hbm] * 4,
-            out_specs=(VM,) * 7,
-            scratch_shapes=[
-                pltpu.VMEM(patch_weight.shape, bf16),
-                pltpu.SemaphoreType.DMA((4,)),
-            ],
-        ),
+        in_specs=[hbm] * 4,
+        out_specs=(VM,) * 6,
+        scratch_shapes=[pltpu.VMEM(patch_weight.shape, bf16), pltpu.SemaphoreType.DMA((4,))],
         name="prepare",
         compiler_params=pltpu.CompilerParams(vmem_limit_bytes=GRANT),
         cost_estimate=pl.CostEstimate(flops=10**7, bytes_accessed=10**6, transcendentals=10**5),
-    )(step_index, offsets, *map(keep, (latent, patch_weight, modulation, out_weight)))
+    )(*map(keep, (latent, patch_weight, modulation, out_weight)))
     other_weight = swap(quarter, "cfg")
-    projected, embedded, text, sent = pl.pallas_call(
+    projected, normed, modulate, embedded, text, late_weight, sent = pl.pallas_call(
         project_kernel,
         out_shape=(
-            shape((3 * heads, HEAD_DIM, tokens), bf16),
+            shape((3 * heads // 2, HEAD_DIM, tokens), bf16),
+            shape((tokens, model_width), bf16),
+            shape(modulation.shape[1:], f32),
             shape((own_tokens, model_width), f32),
             shape(text.shape, bf16),
+            shape((weight.shape[0] // 2, model_width), bf16),
             shape((half_attn // 2, branches * own_tokens), bf16),
         ),
-        in_specs=[VM] * 8 + [hbm] * 2,
-        out_specs=(VM,) * 4,
+        in_specs=[SM, SM] + [VM] * 7 + [hbm] * 2,
+        out_specs=(VM,) * 7,
         scratch_shapes=[
             pltpu.VMEM((3 * slab_cols, channels * row_count), f32),
-            pltpu.VMEM(weight.shape, bf16),
-            pltpu.SemaphoreType.DMA((2,)),
+            pltpu.VMEM((weight.shape[0] // 2, model_width), bf16),
+            pltpu.SemaphoreType.DMA((7,)),
         ],
         name="project",
         compiler_params=pltpu.CompilerParams(vmem_limit_bytes=GRANT),
         cost_estimate=pl.CostEstimate(flops=2 * 10**9, bytes_accessed=8 * 10**6, transcendentals=10**6),
     )(
-        start, modulate, near, own, far, row_part, col_part, patch_wide, keep(weight), keep(text)
+        step_index, offsets, modulations, near, own, far, row_part, col_part, patch_wide,
+        keep(weight), keep(text),
     )
     early = swap(sent, "cfg")
-    sent = pl.pallas_call(
+    projected_late, own_weight, sent = pl.pallas_call(
         second_kernel,
-        out_shape=shape((half_attn // 2, branches * own_tokens), bf16),
-        in_specs=[VM] * 2,
-        out_specs=VM,
+        out_shape=(
+            shape((3 * heads // 2, HEAD_DIM, tokens), bf16),
+            shape(out_weight.shape, bf16),
+            shape((half_attn // 2, branches * own_tokens), bf16),
+        ),
+        in_specs=[VM] * 3 + [hbm],
+        out_specs=(VM,) * 3,
+        scratch_shapes=[pltpu.SemaphoreType.DMA],
         name="second",
         compiler_params=pltpu.CompilerParams(vmem_limit_bytes=GRANT),
         cost_estimate=pl.CostEstimate(flops=10**9, bytes_accessed=10**6, transcendentals=10**6),
-    )(projected, text)
+    )(normed, text, late_weight, keep(out_weight))
     late = swap(sent, "cfg")
     cross_weight = swap_across(other_weight, "win", 2)
     core_weight = swap_across(other_weight, "win", 1)
     core_cross_weight = swap_across(cross_weight, "win", 1)
     mixed = pl.pallas_call(
         attend_kernel,
-        out_shape=shape((branches * own_tokens, model_width), bf16),
-        in_specs=[VM] * 2 + [hbm],
+        out_shape=shape((branches * own_tokens, model_width), f32),
+        in_specs=[VM] * 4,
         out_specs=VM,
-        scratch_shapes=[pltpu.VMEM(out_weight.shape, bf16), pltpu.SemaphoreType.DMA],
         name="attend",
         compiler_params=pltpu.CompilerParams(vmem_limit_bytes=GRANT),
         cost_estimate=pl.CostEstimate(flops=10**9, bytes_accessed=8 * 10**6, transcendentals=10**6),
-    )(projected, text, keep(out_weight))
+    )(projected, projected_late, text, own_weight)
+    mixed = pl.pallas_call(
+        partial_kernel,
+        out_shape=shape(mixed.shape, f32),
+        in_specs=[VM] * 4,
+        out_specs=VM,
+        name="partial",
+        compiler_params=pltpu.CompilerParams(vmem_limit_bytes=GRANT),
+        cost_estimate=pl.CostEstimate(flops=2 * 10**8, bytes_accessed=10**6, transcendentals=0),
+    )(mixed, early, other_weight, core_weight)
     plan_values, rows = pl.pallas_call(
         coefficient_kernel,
         out_shape=(
             shape((8, -(-slab_cols // 128) * 128), f32),
             shape((channels * half_rows, slab_cols), f32),
         ),
-        in_specs=[VM, VM],
+        in_specs=[SM, VM],
         out_specs=(VM, VM),
         name="coefficient",
         compiler_params=pltpu.CompilerParams(vmem_limit_bytes=GRANT),
         cost_estimate=pl.CostEstimate(flops=10**5, bytes_accessed=10**5, transcendentals=10**4),
-    )(start, own)
+    )(step_index, own)
     to_near, center, to_far = pl.pallas_call(
         finish_kernel,
         out_shape=tuple(shape((slab_cols, wide), f32) for _ in range(3)),
-        in_specs=[VM, SM] + [VM] * 10,
+        in_specs=[SM, SM] + [VM] * 7,
         out_specs=(VM, VM, VM),
-        scratch_shapes=[
-            pltpu.VMEM((3 * slab_cols + 8, wide), f32),
-            pltpu.SMEM(start.shape, jnp.int32),
-            pltpu.SemaphoreType.DMA,
-        ],
+        scratch_shapes=[pltpu.VMEM((3 * slab_cols + 8, wide), f32)],
         name="finish",
         compiler_params=pltpu.CompilerParams(vmem_limit_bytes=GRANT),
         cost_estimate=pl.CostEstimate(flops=10**9, bytes_accessed=4 * 10**6, transcendentals=10**3),
     )(
-        start, blend_weights, modulate, embedded, mixed, early, late,
-        other_weight, core_weight, cross_weight, core_cross_weight, final,
+        offsets, blend_weights, modulate, embedded, mixed, late,
+        cross_weight, core_cross_weight, final,
     )
     from_far = swap_ring(to_far, "win", 1)
     from_near = swap_ring(to_near, "win", 0)

time: 34.4 us -> 32.5 us (0.945)
  starting transfers between devices: 16.1 us -> 14 us
  waiting for transfers between devices: 3.45 us -> 4.45 us
  Pallas kernels: 12 us -> 11.1 us
    ppermute x3, starting transfers between devices: 1.82 us -> 0.08 us  [swap_across(): lax.ppermute(array, axis, [(place, place ^ step) for place in range(size)])]
    pallas_call x1, Pallas kernels: 3.21 us -> 2.26 us  [on_device(): pl.pallas_call(attend_kernel, out_shape=shape((branches * own_tokens, mod...]
    pallas_call x2 -> x3, Pallas kernels: 4.83 us -> 5.33 us  [the longest x1 3.3 us: on_device(): pl.pallas_call(project_kernel, out_shape=(shape((3 * heads // 2, HEAD_DIM...]
    ppermute x3, waiting for transfers between devices: 0.01 us -> 0.5 us  [swap_across(): lax.ppermute(array, axis, [(place, place ^ step) for place in range(size)])]
    pallas_call x1, Pallas kernels: 2.02 us -> 1.53 us  [on_device(): pl.pallas_call(finish_kernel, out_shape=tuple((shape((slab_cols, wide), f...]
  transfers between devices with their start and end apart: 10 -> 10, of which waited for: 3 -> 4; matrix products, arithmetic and copies ran while one was open for 0% -> 0% of each run, Pallas kernels for 24% -> 24%
where the time goes in v6:
time: 32.5 us; the launch traced here: 32.3 us
  starting transfers between devices  14 us (43%)
  Pallas kernels  11.1 us (34%)
  waiting for transfers between devices  4.45 us (14%)
  between operations  2.7 us (8%)
    ppermute x4, starting transfers between devices, swap_ring(): return lax.ppermute(array, axis, pairs)  8.72 us
    ppermute x3, starting transfers between devices, swap(): return lax.ppermute(array, axis, [(0, 1), (1, 0)])  5.22 us
    pallas_call x1, Pallas kernels, on_device(): pl.pallas_call(project_kernel, out_shape=(shape((3 * heads // 2, HEAD_DIM...  3.3 us
    ppermute x4, waiting for transfers between devices, swap_ring(): return lax.ppermute(array, axis, pairs)  2.65 us
    pallas_call x1, Pallas kernels, on_device(): pl.pallas_call(attend_kernel, out_shape=shape((branches * own_tokens, mod...  2.26 us
    pallas_call x1, Pallas kernels, on_device(): pl.pallas_call(finish_kernel, out_shape=tuple((shape((slab_cols, wide), f...  1.53 us
    pallas_call x1, Pallas kernels, on_device(): pl.pallas_call(second_kernel, out_shape=(shape((3 * heads // 2, HEAD_DIM,...  1.47 us
    ppermute x3, waiting for transfers between devices, swap(): return lax.ppermute(array, axis, [(0, 1), (1, 0)])  1.3 us
  transfers between devices with their start and end apart: 10, of which 4 were waited for; matrix products, arithmetic and copies ran while one was open for 0% of the time, Pallas kernels for 24%

profile of v6, /device:TPU:0, one launch (start us, length us, event | category | flops | bytes accessed | tf_op | source)
XLA Modules:
  0.0 32.3 jit_solution(6820462803771609809)
XLA Ops:
  0.6 1.1 %prepare.1 = (f32[16,640]{1,0:T(8,128)S(1)}, f32[32,640]{1,0:T(8,128)S(1)}, bf16[256,1152]{1,0:T(8,128)(2,1)S(1)}, f32[20,4,1152]{2,1,0:T(4,128)S(1)}, f32[32,4,...) custom-call(f32[32,4,32]{2,1,0:T(4,128)} %latent_source.1, bf16[16,1152]{1,0:T(8,128)(2,1)} %patch_source.1, ...), custom_call_target="tpu_custom_call" | custom-call | flops 10000000 | bytes 1000000 | tf_op jit(solution)/shard_map/prepare/pallas_call | solution.py:515
  1.8 3.1 %collective-permute-start.3 = (bf16[72,1152]{1,0:T(8,128)(2,1)S(1)}, bf16[72,1152]{1,0:T(8,128)(2,1)S(1)}, u32[]{:S(2)}, u32[]{:S(2)}) collective-permute-start(bf16[72,1152]{1,0:T(8,128)(2,1)S(1)} %get-tuple-element.40), channel_id=1, source_target_pairs={{0,16},{16,0},{1,17},{17,1},{2,18},{18,2},{3,19},{19,3},{4,20},{20... | collective-permute-start | bytes 497672 | tf_op jit(solution)/shard_map/ppermute | solution.py:35
  4.8 0.0 collective-permute-start
  4.8 4.6 %collective-permute-start.1 = (f32[32,4,32]{2,1,0:T(4,128)}, f32[32,4,32]{2,1,0:T(4,128)S(1)}, u32[]{:S(2)}, u32[]{:S(2)}) collective-permute-start(f32[32,4,32]{2,1,0:T(4,128)} %latent_source.1), channel_id=1, source_target_pairs={{1,2},{2,1},{3,4},{4,3},{5,6},{6,5},{7,8},{8,7},{9,10},{10,9},{11,... | collective-permute-start | bytes 49160 | tf_op jit(solution)/shard_map/ppermute | solution.py:31
  10.8 0.0 collective-permute-done.3.weight_ref
  10.8 0.1 collective-permute-start.6
  10.8 0.0 collective-permute-done.near_ref
  10.9 0.9 %collective-permute-done.1.far_ref = f32[32,4,32]{2,1,0:T(4,128)S(1)} collective-permute-done((f32[32,4,32]{2,1,0:T(4,128)}, f32[32,4,32]{2,1,0:T(4,128)S(1)}, u32[]{:S(2)}, u32[]{:S(2)}) %collective-permute-start.1) | collective-permute-done | bytes 16416 | tf_op jit(solution)/shard_map/ppermute | solution.py:31
  11.7 3.3 %project.1 = (bf16[6,72,512]{2,1,0:T(8,128)(2,1)S(1)}, bf16[512,1152]{1,0:T(8,128)(2,1)S(1)}, f32[4,1152]{1,0:T(4,128)S(1)}, f32[256,1152]{1,0:T(8,128)S(1)}, bf...) custom-call(s32[1]{0:T(128)S(6)} %copy.14.step_ref, ...), custom_call_target="tpu_custom_call" | custom-call | flops 2000000000 | bytes 8000000 | tf_op jit(solution)/shard_map/project/pallas_call | solution.py:533
  15.0 0.6 %collective-permute-start.2 = (bf16[144,512]{1,0:T(8,128)(2,1)S(1)}, bf16[144,512]{1,0:T(8,128)(2,1)S(1)}, u32[]{:S(2)}, u32[]{:S(2)}) collective-permute-start(bf16[144,512]{1,0:T(8,128)(2,1)S(1)} %get-tuple-element.39), channel_id=1, source_target_pairs={{0,16},{16,0},{1,17},{17,1},{2,18},{18,2},{3,19},{19,3},{4,20},{20... | collective-permute-start | bytes 442376 | tf_op jit(solution)/shard_map/ppermute | solution.py:35
  15.7 0.0 collective-permute-start.4
  15.7 0.5 %collective-permute-done.6.cross_ref = bf16[72,1152]{1,0:T(8,128)(2,1)S(1)} collective-permute-done((bf16[72,1152]{1,0:T(8,128)(2,1)S(1)}, bf16[72,1152]{1,0:T(8,128)(2,1)S(1)}, u32[]{:S(2)}, u32[]{:S(2)}) %collective-permute-start.6) | collective-permute-done | bytes 165920 | tf_op jit(solution)/shard_map/ppermute | solution.py:40
  16.2 0.0 collective-permute-start.7
  16.2 1.5 %second.1 = (bf16[6,72,512]{2,1,0:T(8,128)(2,1)S(1)}, bf16[288,1152]{1,0:T(8,128)(2,1)S(1)}, bf16[144,512]{1,0:T(8,128)(2,1)S(1)}) custom-call(bf16[512,1152]{1,0:T(8,128)(2,1)S(1)} %get-tuple-element.34.normed_ref, bf16[2,2,4,72,120]{4,3,2,1,0:T(8,128)(2,1)S(1)} %get-tuple-element.35.text_ref, bf16[432,1152]{1,0:T(8,128)(2,1)S(1)} %get-tuple-element.36.weight_ref, ...), custom_call_target="tpu_custom_call" | custom-call | flops 1000000000 | bytes 1000000 | tf_op jit(solution)/shard_map/second/pallas_call | solution.py:559
  17.7 1.5 %collective-permute-start.5 = (bf16[144,512]{1,0:T(8,128)(2,1)S(1)}, bf16[144,512]{1,0:T(8,128)(2,1)S(1)}, u32[]{:S(2)}, u32[]{:S(2)}) collective-permute-start(bf16[144,512]{1,0:T(8,128)(2,1)S(1)} %get-tuple-element.41), channel_id=1, source_target_pairs={{0,16},{16,0},{1,17},{17,1},{2,18},{18,2},{3,19},{19,3},{4,20},{20... | collective-permute-start | bytes 442376 | tf_op jit(solution)/shard_map/ppermute | solution.py:35
  19.8 2.3 %attend.1.mixed_ref = f32[512,1152]{1,0:T(8,128)S(1)} custom-call(bf16[6,72,512]{2,1,0:T(8,128)(2,1)S(1)} %get-tuple-element.33.early_ref, bf16[6,72,512]{2,1,0:T(8,128)(2,1)S(1)} %get-tuple-element.37.late_ref, bf16[2,2,4,72,120]{4,3,2,1,0:T(8,128)(2,1)S(1)} %get-tuple-element.35.text_ref, bf16[288,1152]{1,0:T(8,128)(2,1)S(1)} %get-tuple-element.38.weight_ref), custom_call_target="tpu_custom_call" | custom-call | flops 1000000000 | bytes 8000000 | tf_op jit(solution)/shard_map/attend/pallas_call | solution.py:577
  22.1 0.0 copy-start
  22.1 0.0 collective-permute-done.2.early_ref
  22.1 0.0 collective-permute-done.4.core_ref
  22.1 0.6 %partial.1.mixed_ref = f32[512,1152]{1,0:T(8,128)S(1)} custom-call(f32[512,1152]{1,0:T(8,128)S(1)} %attend.1.mixed_ref, bf16[144,512]{1,0:T(8,128)(2,1)S(1)} %collective-permute-done.2.early_ref, bf16[72,1152]{1,0:T(8,128)(2,1)S(1)} %collective-permute-done.3.weight_ref, bf16[72,1152]{1,0:T(8,128)(2,1)S(1)} %collective-permute-done.4.core_ref), custom_call_target="tpu_custom_call" | custom-call | flops 200000000 | bytes 1000000 | tf_op jit(solution)/shard_map/partial/pallas_call | solution.py:586
  22.7 1.3 %collective-permute-done.5.late_ref = bf16[144,512]{1,0:T(8,128)(2,1)S(1)} collective-permute-done((bf16[144,512]{1,0:T(8,128)(2,1)S(1)}, bf16[144,512]{1,0:T(8,128)(2,1)S(1)}, u32[]{:S(2)}, u32[]{:S(2)}) %collective-permute-start.5) | collective-permute-done | bytes 147488 | tf_op jit(solution)/shard_map/ppermute | solution.py:35
  24.0 0.0 collective-permute-done.7.core_cross_ref
  24.0 0.0 copy-done
  24.0 1.5 %finish.1 = (f32[32,128]{1,0:T(8,128)S(1)}, f32[32,128]{1,0:T(8,128)S(1)}, f32[32,128]{1,0:T(8,128)S(1)}) custom-call(s32[1]{0:T(128)S(6)} %copy.12.offset_ref, s32[1]{0:T(128)S(6)} %copy.13.blend_ref, f32[4,1152]{1,0:T(4,128)S(1)} %get-tuple-element.31.modulation_ref, f32[256,1152]{1,0:T(8,128)S(1)} %get-tuple-element.32.embedded_ref, ...), custom_call_target="tpu_custom_call" | custom-call | flops 1000000000 | bytes 4000000 | tf_op jit(solution)/shard_map/finish/pallas_call | solution.py:607
  25.5 0.1 collective-permute-start.8
  25.6 4.0 %collective-permute-start.9 = (f32[32,128]{1,0:T(8,128)S(1)}, f32[32,128]{1,0:T(8,128)S(1)}, u32[]{:S(2)}, u32[]{:S(2)}) collective-permute-start(f32[32,128]{1,0:T(8,128)S(1)} %get-tuple-element.44), channel_id=1, source_target_pairs={{1,2},{2,1},{3,4},{4,3},{5,6},{6,5},{7,8},{8,7},{9,10},{10,9},{11,... | collective-permute-start | bytes 49160 | tf_op jit(solution)/shard_map/ppermute | solution.py:31
  29.6 0.1 coefficient.1
  29.7 0.0 collective-permute-done.8.near_ref
  29.8 1.8 %collective-permute-done.9.far_ref = f32[32,128]{1,0:T(8,128)S(1)} collective-permute-done((f32[32,128]{1,0:T(8,128)S(1)}, f32[32,128]{1,0:T(8,128)S(1)}, u32[]{:S(2)}, u32[]{:S(2)}) %collective-permute-start.9) | collective-permute-done | bytes 16416 | tf_op jit(solution)/shard_map/ppermute | solution.py:31
  31.5 0.7 %blend.1 = (f32[4,16,32]{2,1,0:T(8,128)}, f32[4,16,32]{2,1,0:T(8,128)}) custom-call(f32[8,128]{1,0:T(8,128)S(1)} %get-tuple-element.26.plan_ref, f32[32,128]{1,0:T(8,128)S(1)} %get-tuple-element.42.center_ref, f32[32,128]{1,0:T(8,128)S(1)} %collective-permute-done.8.near_ref, f32[32,128]{1,0:T(8,128)S(1)} %collective-permute-done.9.far_ref, ...), custom_call_target="tpu_custom_call" | custom-call | tf_op jit(solution)/shard_map/blend/pallas_call | solution.py:622
Async XLA Ops:
  1.8 9.0 %collective-permute-start.3 = (bf16[72,1152]{1,0:T(8,128)(2,1)S(1)}, bf16[72,1152]{1,0:T(8,128)(2,1)S(1)}, u32[]{:S(2)}, u32[]{:S(2)}) collective-permute-start(bf16[72,1152]{1,0:T(8,128)(2,1)S(1)} %get-tuple-element.40), channel_id=1, source_target_pairs={{0,16},{16,0},{1,17},{17,1},{2,18},{18,2},{3,19},{19,3},{4,20},{20... | collective-permute-start | bytes 497672 | tf_op jit(solution)/shard_map/ppermute | solution.py:35
  4.8 6.0 %collective-permute-start = (f32[32,4,32]{2,1,0:T(4,128)}, f32[32,4,32]{2,1,0:T(4,128)S(1)}, u32[]{:S(2)}, u32[]{:S(2)}) collective-permute-start(f32[32,4,32]{2,1,0:T(4,128)} %latent_source.1), channel_id=1, source_target_pairs={{0,1},{1,0},{2,3},{3,2},{4,5},{5,4},{6,7},{7,6},{8,9},{9,8},{10,11... | collective-permute-start | bytes 49160 | tf_op jit(solution)/shard_map/ppermute | solution.py:31
  4.8 6.9 %collective-permute-start.1 = (f32[32,4,32]{2,1,0:T(4,128)}, f32[32,4,32]{2,1,0:T(4,128)S(1)}, u32[]{:S(2)}, u32[]{:S(2)}) collective-permute-start(f32[32,4,32]{2,1,0:T(4,128)} %latent_source.1), channel_id=1, source_target_pairs={{1,2},{2,1},{3,4},{4,3},{5,6},{6,5},{7,8},{8,7},{9,10},{10,9},{11,... | collective-permute-start | bytes 49160 | tf_op jit(solution)/shard_map/ppermute | solution.py:31
  10.8 5.4 %collective-permute-start.6 = (bf16[72,1152]{1,0:T(8,128)(2,1)S(1)}, bf16[72,1152]{1,0:T(8,128)(2,1)S(1)}, u32[]{:S(2)}, u32[]{:S(2)}) collective-permute-start(bf16[72,1152]{1,0:T(8,128)(2,1)S(1)} %collective-permute-done.3.weight_ref), channel_id=1, source_target_pairs={{0,2},{1,3},{2,0},{3,1},{4,6},{5,7},{6,4},{7,5},{8,10},{9,11},{10,... | collective-permute-start | bytes 497672 | tf_op jit(solution)/shard_map/ppermute | solution.py:40
  15.0 7.1 %collective-permute-start.2 = (bf16[144,512]{1,0:T(8,128)(2,1)S(1)}, bf16[144,512]{1,0:T(8,128)(2,1)S(1)}, u32[]{:S(2)}, u32[]{:S(2)}) collective-permute-start(bf16[144,512]{1,0:T(8,128)(2,1)S(1)} %get-tuple-element.39), channel_id=1, source_target_pairs={{0,16},{16,0},{1,17},{17,1},{2,18},{18,2},{3,19},{19,3},{4,20},{20... | collective-permute-start | bytes 442376 | tf_op jit(solution)/shard_map/ppermute | solution.py:35
  15.7 6.5 %collective-permute-start.4 = (bf16[72,1152]{1,0:T(8,128)(2,1)S(1)}, bf16[72,1152]{1,0:T(8,128)(2,1)S(1)}, u32[]{:S(2)}, u32[]{:S(2)}) collective-permute-start(bf16[72,1152]{1,0:T(8,128)(2,1)S(1)} %collective-permute-done.3.weight_ref), channel_id=1, source_target_pairs={{0,1},{1,0},{2,3},{3,2},{4,5},{5,4},{6,7},{7,6},{8,9},{9,8},{10,11... | collective-permute-start | bytes 497672 | tf_op jit(solution)/shard_map/ppermute | solution.py:40
  16.2 7.8 %collective-permute-start.7 = (bf16[72,1152]{1,0:T(8,128)(2,1)S(1)}, bf16[72,1152]{1,0:T(8,128)(2,1)S(1)}, u32[]{:S(2)}, u32[]{:S(2)}) collective-permute-start(bf16[72,1152]{1,0:T(8,128)(2,1)S(1)} %collective-permute-done.6.cross_ref), channel_id=1, source_target_pairs={{0,1},{1,0},{2,3},{3,2},{4,5},{5,4},{6,7},{7,6},{8,9},{9,8},{10,11... | collective-permute-start | bytes 497672 | tf_op jit(solution)/shard_map/ppermute | solution.py:40
  17.7 6.3 %collective-permute-start.5 = (bf16[144,512]{1,0:T(8,128)(2,1)S(1)}, bf16[144,512]{1,0:T(8,128)(2,1)S(1)}, u32[]{:S(2)}, u32[]{:S(2)}) collective-permute-start(bf16[144,512]{1,0:T(8,128)(2,1)S(1)} %get-tuple-element.41), channel_id=1, source_target_pairs={{0,16},{16,0},{1,17},{17,1},{2,18},{18,2},{3,19},{19,3},{4,20},{20... | collective-permute-start | bytes 442376 | tf_op jit(solution)/shard_map/ppermute | solution.py:35
  22.1 1.9 %copy-start = (bf16[1152,16]{0,1:T(8,128)(2,1)S(1)}, bf16[1152,16]{0,1:T(8,128)(2,1)}, u32[]{:S(2)}) copy-start(bf16[1152,16]{0,1:T(8,128)(2,1)} %param.16) | copy-start | bytes 110596
  25.5 4.2 %collective-permute-start.8 = (f32[32,128]{1,0:T(8,128)S(1)}, f32[32,128]{1,0:T(8,128)S(1)}, u32[]{:S(2)}, u32[]{:S(2)}) collective-permute-start(f32[32,128]{1,0:T(8,128)S(1)} %get-tuple-element.43), channel_id=1, source_target_pairs={{0,1},{1,0},{2,3},{3,2},{4,5},{5,4},{6,7},{7,6},{8,9},{9,8},{10,11... | collective-permute-start | bytes 49160 | tf_op jit(solution)/shard_map/ppermute | solution.py:31
  25.6 5.9 %collective-permute-start.9 = (f32[32,128]{1,0:T(8,128)S(1)}, f32[32,128]{1,0:T(8,128)S(1)}, u32[]{:S(2)}, u32[]{:S(2)}) collective-permute-start(f32[32,128]{1,0:T(8,128)S(1)} %get-tuple-element.44), channel_id=1, source_target_pairs={{1,2},{2,1},{3,4},{4,3},{5,6},{6,5},{7,8},{8,7},{9,10},{10,9},{11,... | collective-permute-start | bytes 49160 | tf_op jit(solution)/shard_map/ppermute | solution.py:31

commit v7 on v6

--- a/solution.py
+++ b/solution.py
@@ -148,6 +148,13 @@
     return lax.axis_index("win") % 4 // 2
 
 
+def token_lanes(side, tokens):
+    return [
+        pl.multiple_of(half * (tokens // 2) + side * (tokens // 4), tokens // 4)
+        for half in range(2)
+    ]
+
+
 def attend(parts, text_ref, first, count, chosen, finished):
     branches = text_ref.shape[0]
     feature = (((0,), (0,)), ((), ()))
@@ -157,7 +164,9 @@
         return 2 * pair + head % 2
 
     def score(head):
-        queries = parts[head // 2][head % 2, :, pl.ds(first, count)]
+        queries = jnp.concatenate(
+            [parts[head // 2][head % 2, :, pl.ds(start, count // 2)] for start in first], axis=1
+        )
         return [
             lax.dot_general(keys, queries, feature, preferred_element_type=jnp.float32)
             for keys in [parts[head // 2][2 + head % 2]]
@@ -187,7 +196,11 @@
                 text_ref[branch, 1, place_of(head)], text_exp, preferred_element_type=jnp.float32
             )
             results.append((lowered * own_mix + text_mix) * inverse)
-        return jnp.concatenate(results, axis=1)
+        return jnp.concatenate(
+            [result[:, : count // 2] for result in results]
+            + [result[:, count // 2 :] for result in results],
+            axis=1,
+        )
 
     chosen = list(chosen)
     mixed = []
@@ -288,59 +301,64 @@
     start_at = slab_cols - offset_ref[0]
     chosen = lax.broadcasted_iota(jnp.int32, (2 * col_pairs, 3 * slab_cols), 0)
     column = lax.broadcasted_iota(jnp.int32, (2 * col_pairs, 3 * slab_cols), 1)
-    target = jnp.where(
-        chosen < col_pairs, 2 * chosen, 2 * (chosen - col_pairs) + 1
-    )
+    half_pairs = col_pairs // 2
+    parity = lax.axis_index("win") % 2
+    near_first, far_first = (1 - parity) * half_pairs, parity * half_pairs
+    group, within = chosen // half_pairs, chosen % half_pairs
+    target = 2 * (within + jnp.where(group < 2, near_first, far_first)) + group % 2
     pick = jnp.where(column == target + start_at, 1.0, 0.0).astype(jnp.bfloat16)
     picked = jnp.dot(pick, extended, preferred_element_type=jnp.float32)
-    picked = jnp.concatenate([picked[:col_pairs], picked[col_pairs:]], axis=1)
-    lane_couple = lax.broadcasted_iota(jnp.int32, (col_pairs, wide), 1) % row_count // 2
-    spread = jnp.concatenate(
-        [jnp.where(lane_couple == couple, picked, 0.0) for couple in range(row_couples)], axis=0
-    ).astype(jnp.bfloat16)
+    groups = [picked[place * half_pairs : (place + 1) * half_pairs] for place in range(4)]
+    lane_couple = lax.broadcasted_iota(jnp.int32, (half_pairs, wide), 1) % row_count // 2
+    spread = []
+    for place in range(2):
+        pair = jnp.concatenate(groups[2 * place : 2 * place + 2], axis=1)
+        spread.append(
+            jnp.concatenate(
+                [jnp.where(lane_couple == couple, pair, 0.0) for couple in range(row_couples)],
+                axis=0,
+            ).astype(jnp.bfloat16)
+        )
     side = lax.axis_index("cfg")
     chunks = [slice(place * own_tokens, (place + 1) * own_tokens) for place in range(2)]
 
-    couples = row_couples // 2
     model_width = patch_ref.shape[1]
     below, above = model_width - col_ref.shape[1], row_ref.shape[1]
-    is_row = below + lax.broadcasted_iota(jnp.int32, (col_pairs, above - below), 1)
+    is_row = below + lax.broadcasted_iota(jnp.int32, (half_pairs, above - below), 1)
     is_row = is_row < model_width // 2
 
-    def position(couple):
-        line = jnp.broadcast_to(row_ref[couple : couple + 1, :], (col_pairs, above))
-        column = col_ref[...]
+    def position(place, couple):
+        line = jnp.broadcast_to(row_ref[couple : couple + 1, :], (half_pairs, above))
+        column_first = near_first if place == 0 else far_first
+        column = col_ref[pl.ds(pl.multiple_of(column_first, half_pairs), half_pairs), :]
         both = jnp.where(is_row, line[:, below:], column[:, : above - below])
         return jnp.concatenate([line[:, :below], both, column[:, above - below :]], axis=1)
 
+    gain, shift = 1.0 + modulation_ref[1:2, :], modulation_ref[0:1, :]
+
     def embed(place):
-        chunk = chunks[place]
-        embedded = jnp.dot(spread[chunk], patch_ref[...], preferred_element_type=jnp.float32)
-        embedded = embedded + jnp.concatenate(
-            [position(couple) for couple in range(row_couples)[place * couples :][:couples]], axis=0
-        )
-
-        @pl.when(side == place)
-        def _():
-            embedded_ref[...] = embedded
-
-        return embedded
-
-    def norm(embedded):
-        return (
-            layer_norm(embedded) * (1.0 + modulation_ref[1:2, :]) + modulation_ref[0:1, :]
-        ).astype(jnp.bfloat16)
-
-    normed = norm(embed(0))
+        return jnp.dot(spread[place], patch_ref[...], preferred_element_type=jnp.float32)
+
+    def norm(place, patches):
+        for first_couple in range(0, row_couples, 2):
+            rows = slice(first_couple * half_pairs, (first_couple + 2) * half_pairs)
+            target = slice(place * own_tokens + rows.start, place * own_tokens + rows.stop)
+            embedded = patches[rows] + jnp.concatenate(
+                [position(place, first_couple + next_) for next_ in range(2)], axis=0
+            )
+            embedded_ref[target, :] = embedded
+            normed = layer_norm(embedded) * gain + shift
+            normed_ref[target, :] = normed.astype(jnp.bfloat16)
+
+    early = embed(0)
     later = embed(1)
+    norm(0, early)
     for copy in copies:
         copy.wait()
-    normed_ref[chunks[0], :] = normed
-    project_half(weight_ref, normed, proj_ref, chunks[0])
-    normed = norm(later)
-    normed_ref[chunks[1], :] = normed
-    project_half(weight_ref, normed, proj_ref, chunks[1])
-    first = pl.multiple_of((1 - side) * own_tokens, own_tokens)
+    project_half(weight_ref, normed_ref[chunks[0], :], proj_ref, chunks[0])
+    norm(1, later)
+    project_half(weight_ref, normed_ref[chunks[1], :], proj_ref, chunks[1])
+    first = token_lanes(1 - side, tokens)
     text_copy.wait()
     attend(
         [proj_ref], text_ref, first, own_tokens, range(2), functools.partial(keep_pair, sent_ref)
@@ -358,7 +376,7 @@
     for place in range(2):
         chunk = slice(place * own_tokens, (place + 1) * own_tokens)
         project_half(weight_ref, normed_ref[chunk, :], proj_ref, chunk)
-    first = pl.multiple_of((1 - lax.axis_index("cfg")) * own_tokens, own_tokens)
+    first = token_lanes(1 - lax.axis_index("cfg"), 2 * own_tokens)
     attend(
         [None, proj_ref], text_ref, first, own_tokens, range(2, 4),
         functools.partial(keep_pair, sent_ref),
@@ -369,7 +387,7 @@
 def attend_kernel(early_ref, late_ref, text_ref, weight_ref, mixed_ref):
     tokens = early_ref.shape[2]
     own_tokens = tokens // 2
-    first = pl.multiple_of(lax.axis_index("cfg") * own_tokens, own_tokens)
+    first = token_lanes(lax.axis_index("cfg"), tokens)
     pairs = []
 
     def finished(place, pair):
@@ -399,42 +417,51 @@
     return jnp.concatenate([first, second], axis=0).astype(jnp.bfloat16)
 
 
+def join_kernel(mine_ref, neighbour_ref, joined_ref):
+    joined_ref[...] = join(mine_ref, neighbour_ref)
+
+
 def partial_kernel(mixed_ref, early_ref, weight_ref, core_ref, summed_ref):
     summed_ref[...] = mixed_ref[...] + contract(early_ref[...], join(weight_ref, core_ref))
 
 
 def finish_kernel(
+    half,
     offset_ref,
     blend_ref,
     modulation_ref,
     embedded_ref,
     mixed_ref,
     late_ref,
-    cross_ref,
-    core_cross_ref,
+    weight_ref,
     final_ref,
-    near_ref,
+    sent_ref,
     center_ref,
-    far_ref,
     buffer_ref,
+    final_norm_ref,
 ):
-    even_place = lax.axis_index("win") % 2 == 0
-    other = contract(late_ref[...], join(cross_ref, core_cross_ref))
-    slab_cols = center_ref.shape[0]
-    col_pairs = slab_cols
-    own_tokens = embedded_ref.shape[0]
-    couples = own_tokens // col_pairs
+    slab_cols, wide = center_ref.shape
+    half_pairs = slab_cols // 2
+    count = embedded_ref.shape[0] // 4
+    couples = count // half_pairs
     final_wide = repeat_pairs(final_ref[...], couples)
-    wide = final_wide.shape[0]
+    gate, gain = modulation_ref[2:3, :], 1.0 + modulation_ref[3:4, :]
+    side_first = pl.multiple_of(half * 2 * count + lax.axis_index("cfg") * count, count)
+    lanes = slice(half * 2 * count, (half + 1) * 2 * count)
+    other = contract(late_ref[:, lanes], weight_ref[...])
     predicted = []
+    block = slab_cols
     for branch in range(2):
-        rows = slice(branch * own_tokens, (branch + 1) * own_tokens)
-        mixed = mixed_ref[rows, :] + other[rows]
-        residual = embedded_ref[...] + modulation_ref[2:3, :] * mixed
-        final_norm = (layer_norm(residual) * (1.0 + modulation_ref[3:4, :])).astype(jnp.bfloat16)
+        for place in range(count // block):
+            rows = slice(branch * count + place * block, branch * count + (place + 1) * block)
+            mixed = mixed_ref[lanes.start + rows.start : lanes.start + rows.stop, :] + other[rows]
+            embedded = embedded_ref[pl.ds(side_first + place * block, block), :]
+            residual = embedded + gate * mixed
+            final_norm_ref[rows, :] = (layer_norm(residual) * gain).astype(jnp.bfloat16)
+        rows = slice(branch * count, (branch + 1) * count)
         predicted.append(
             lax.dot_general(
-                final_norm,
+                final_norm_ref[rows, :],
                 final_wide,
                 (((1,), (1,)), ((), ())),
                 preferred_element_type=jnp.float32,
@@ -442,30 +469,34 @@
         )
     conditional, unconditional = predicted
     guided = unconditional + guidance_scale * (conditional - unconditional)
-    lane_couple = lax.broadcasted_iota(jnp.int32, (col_pairs, wide), 1) % (2 * couples) // 2
-    pairs = jnp.zeros((col_pairs, wide), jnp.float32)
+    lane_couple = lax.broadcasted_iota(jnp.int32, (half_pairs, wide), 1) % (2 * couples) // 2
+    pairs = jnp.zeros((half_pairs, wide), jnp.float32)
     for couple in range(couples):
         pairs = pairs + jnp.where(
-            lane_couple == couple, guided[couple * col_pairs : (couple + 1) * col_pairs], 0.0
+            lane_couple == couple, guided[couple * half_pairs : (couple + 1) * half_pairs], 0.0
         )
     weight_value = blend_ref[0].astype(jnp.float32)
-    half = wide // 2
-    is_noise = lax.broadcasted_iota(jnp.int32, (col_pairs, wide), 1) < half
+    is_noise = lax.broadcasted_iota(jnp.int32, (half_pairs, wide), 1) < wide // 2
     even = jnp.where(is_noise, weight_value * pairs, weight_value)
-    odd = jnp.where(is_noise, weight_value * pltpu.roll(pairs, half, 1), weight_value)
-    start_at = slab_cols - offset_ref[0]
+    odd = jnp.where(is_noise, weight_value * pltpu.roll(pairs, wide // 2, 1), weight_value)
+    parity = lax.axis_index("win") % 2
+    right = 1 - parity if half == 0 else parity
+    start_at = slab_cols - offset_ref[0] + right * slab_cols
     buffer_ref[...] = jnp.zeros_like(buffer_ref)
-    buffer_ref[pl.ds(start_at, col_pairs, stride=2), :] = even
-    buffer_ref[pl.ds(start_at + 1, col_pairs, stride=2), :] = odd
+    buffer_ref[pl.ds(start_at, half_pairs, stride=2), :] = even
+    buffer_ref[pl.ds(start_at + 1, half_pairs, stride=2), :] = odd
     center_ref[...] = buffer_ref[slab_cols : 2 * slab_cols]
-    left, right = buffer_ref[:slab_cols], buffer_ref[2 * slab_cols : 3 * slab_cols]
-    near_ref[...] = jnp.where(even_place, right, left)
-    far_ref[...] = jnp.where(even_place, left, right)
-
-
-def blend_kernel(plan_ref, center_ref, near_ref, far_ref, rows_ref, previous_ref, noise_ref):
+    sent_ref[...] = jnp.where(
+        right == 1, buffer_ref[2 * slab_cols : 3 * slab_cols], buffer_ref[:slab_cols]
+    )
+
+
+def blend_kernel(
+    plan_ref, center_ref, near_ref, far_center_ref, far_ref, rows_ref, previous_ref, noise_ref
+):
     channels, half_rows, slab_cols = noise_ref.shape
-    total = jnp.transpose(center_ref[...] + near_ref[...] + far_ref[...], (1, 0))
+    total = (center_ref[...] + near_ref[...]) + (far_center_ref[...] + far_ref[...])
+    total = jnp.transpose(total, (1, 0))
     half = total.shape[0] // 2
     noise = total[:half] / total[half:]
     scale = plan_ref[:, :slab_cols]
@@ -536,7 +567,7 @@
             shape((3 * heads // 2, HEAD_DIM, tokens), bf16),
             shape((tokens, model_width), bf16),
             shape(modulation.shape[1:], f32),
-            shape((own_tokens, model_width), f32),
+            shape((tokens, model_width), f32),
             shape(text.shape, bf16),
             shape((weight.shape[0] // 2, model_width), bf16),
             shape((half_attn // 2, branches * own_tokens), bf16),
@@ -604,29 +635,43 @@
         compiler_params=pltpu.CompilerParams(vmem_limit_bytes=GRANT),
         cost_estimate=pl.CostEstimate(flops=10**5, bytes_accessed=10**5, transcendentals=10**4),
     )(step_index, own)
-    to_near, center, to_far = pl.pallas_call(
-        finish_kernel,
-        out_shape=tuple(shape((slab_cols, wide), f32) for _ in range(3)),
-        in_specs=[SM, SM] + [VM] * 7,
-        out_specs=(VM, VM, VM),
-        scratch_shapes=[pltpu.VMEM((3 * slab_cols + 8, wide), f32)],
-        name="finish",
-        compiler_params=pltpu.CompilerParams(vmem_limit_bytes=GRANT),
-        cost_estimate=pl.CostEstimate(flops=10**9, bytes_accessed=4 * 10**6, transcendentals=10**3),
-    )(
-        offsets, blend_weights, modulate, embedded, mixed, late,
-        cross_weight, core_cross_weight, final,
-    )
+    late_rows = pl.pallas_call(
+        join_kernel,
+        out_shape=shape((half_attn // 2, model_width), bf16),
+        in_specs=[VM] * 2,
+        out_specs=VM,
+        name="join",
+        compiler_params=pltpu.CompilerParams(vmem_limit_bytes=GRANT),
+    )(cross_weight, core_cross_weight)
+
+    def finish(half):
+        return pl.pallas_call(
+            functools.partial(finish_kernel, half),
+            out_shape=tuple(shape((slab_cols, wide), f32) for _ in range(2)),
+            in_specs=[SM, SM] + [VM] * 6,
+            out_specs=(VM, VM),
+            scratch_shapes=[
+                pltpu.VMEM((3 * slab_cols + 8, wide), f32),
+                pltpu.VMEM((own_tokens, model_width), bf16),
+            ],
+            compiler_params=pltpu.CompilerParams(vmem_limit_bytes=GRANT),
+            cost_estimate=pl.CostEstimate(
+                flops=5 * 10**8, bytes_accessed=2 * 10**6, transcendentals=10**3
+            ),
+        )(offsets, blend_weights, modulate, embedded, mixed, late, late_rows, final)
+
+    to_far, far_center = finish(1)
+    to_near, center = finish(0)
     from_far = swap_ring(to_far, "win", 1)
     from_near = swap_ring(to_near, "win", 0)
     previous, noise = pl.pallas_call(
         blend_kernel,
         out_shape=tuple(shape((channels, half_rows, slab_cols), f32) for _ in range(2)),
-        in_specs=[VM] * 5,
+        in_specs=[VM] * 6,
         out_specs=(VM, VM),
         name="blend",
         compiler_params=pltpu.CompilerParams(vmem_limit_bytes=GRANT),
-    )(plan_values, center, from_near, from_far, rows)
+    )(plan_values, center, from_near, far_center, from_far, rows)
     return (jnp.transpose(previous, (2, 0, 1)), jnp.transpose(noise, (2, 0, 1)))
 
 

time: 32.5 us -> 33.1 us (1.018)
  waiting for transfers between devices: 4.45 us -> 2.88 us
  Pallas kernels: 11.1 us -> 12.3 us
  starting transfers between devices: 14 us -> 15 us
    pallas_call x1 -> x3, Pallas kernels: 1.53 us -> 2.19 us  [the longest x2 2.09 us: finish(): pl.pallas_call(functools.partial(finish_kernel, half), out_shape=tuple((s...]
    pallas_call x1, Pallas kernels: 3.3 us -> 3.92 us  [on_device(): pl.pallas_call(project_kernel, out_shape=(shape((3 * heads // 2, HEAD_DIM...]
    ppermute x3, waiting for transfers between devices: 1.3 us -> 0.7 us  [swap(): return lax.ppermute(array, axis, [(0, 1), (1, 0)])]
    ppermute x3, starting transfers between devices: 0.08 us -> 0.58 us  [swap_across(): lax.ppermute(array, axis, [(place, place ^ step) for place in range(size)])]
    ppermute x3, waiting for transfers between devices: 0.5 us -> 0.01 us  [swap_across(): lax.ppermute(array, axis, [(place, place ^ step) for place in range(size)])]
    ppermute x4, waiting for transfers between devices: 2.65 us -> 2.17 us  [swap_ring(): return lax.ppermute(array, axis, pairs)]
    ppermute x4, starting transfers between devices: 8.72 us -> 9.17 us  [swap_ring(): return lax.ppermute(array, axis, pairs)]
  transfers between devices with their start and end apart: 10 -> 10, of which waited for: 4 -> 3; matrix products, arithmetic and copies ran while one was open for 0% -> 0% of each run, Pallas kernels for 24% -> 29%
where the time goes in v7:
time: 33.1 us; the launch traced here: 32.9 us
  starting transfers between devices  15 us (45%)
  Pallas kernels  12.3 us (37%)
  waiting for transfers between devices  2.88 us (9%)
  between operations  2.71 us (8%)
    ppermute x4, starting transfers between devices, swap_ring(): return lax.ppermute(array, axis, pairs)  9.17 us
    ppermute x3, starting transfers between devices, swap(): return lax.ppermute(array, axis, [(0, 1), (1, 0)])  5.22 us
    pallas_call x1, Pallas kernels, on_device(): pl.pallas_call(project_kernel, out_shape=(shape((3 * heads // 2, HEAD_DIM...  3.92 us
    pallas_call x1, Pallas kernels, on_device(): pl.pallas_call(attend_kernel, out_shape=shape((branches * own_tokens, mod...  2.23 us
    ppermute x4, waiting for transfers between devices, swap_ring(): return lax.ppermute(array, axis, pairs)  2.17 us
    pallas_call x2, Pallas kernels, finish(): pl.pallas_call(functools.partial(finish_kernel, half), out_shape=tuple((s...  2.09 us
    pallas_call x1, Pallas kernels, on_device(): pl.pallas_call(second_kernel, out_shape=(shape((3 * heads // 2, HEAD_DIM,...  1.46 us
    pallas_call x1, Pallas kernels, on_device(): pl.pallas_call(prepare_kernel, out_shape=(shape((row_couples, above), f32...  1.12 us
  transfers between devices with their start and end apart: 10, of which 3 were waited for; matrix products, arithmetic and copies ran while one was open for 0% of the time, Pallas kernels for 29%

profile of v7, /device:TPU:0, one launch (start us, length us, event | category | flops | bytes accessed | tf_op | source)
XLA Modules:
  0.0 32.9 jit_solution(12644177040298552772)
XLA Ops:
  0.6 1.1 %prepare.1 = (f32[16,640]{1,0:T(8,128)S(1)}, f32[32,640]{1,0:T(8,128)S(1)}, bf16[256,1152]{1,0:T(8,128)(2,1)S(1)}, f32[20,4,1152]{2,1,0:T(4,128)S(1)}, f32[32,4,...) custom-call(f32[32,4,32]{2,1,0:T(4,128)} %latent_source.1, bf16[16,1152]{1,0:T(8,128)(2,1)} %patch_source.1, ...), custom_call_target="tpu_custom_call" | custom-call | flops 10000000 | bytes 1000000 | tf_op jit(solution)/shard_map/prepare/pallas_call | solution.py:546
  1.8 3.1 %collective-permute-start.3 = (bf16[72,1152]{1,0:T(8,128)(2,1)S(1)}, bf16[72,1152]{1,0:T(8,128)(2,1)S(1)}, u32[]{:S(2)}, u32[]{:S(2)}) collective-permute-start(bf16[72,1152]{1,0:T(8,128)(2,1)S(1)} %get-tuple-element.41), channel_id=1, source_target_pairs={{0,16},{16,0},{1,17},{17,1},{2,18},{18,2},{3,19},{19,3},{4,20},{20... | collective-permute-start | bytes 497672 | tf_op jit(solution)/shard_map/ppermute | solution.py:35
  4.8 0.0 collective-permute-start
  4.8 4.6 %collective-permute-start.1 = (f32[32,4,32]{2,1,0:T(4,128)}, f32[32,4,32]{2,1,0:T(4,128)S(1)}, u32[]{:S(2)}, u32[]{:S(2)}) collective-permute-start(f32[32,4,32]{2,1,0:T(4,128)} %latent_source.1), channel_id=1, source_target_pairs={{1,2},{2,1},{3,4},{4,3},{5,6},{6,5},{7,8},{8,7},{9,10},{10,9},{11,... | collective-permute-start | bytes 49160 | tf_op jit(solution)/shard_map/ppermute | solution.py:31
  10.8 0.0 collective-permute-done.3.weight_ref
  10.8 0.1 collective-permute-start.6
  10.8 0.0 collective-permute-done.near_ref
  10.9 0.9 %collective-permute-done.1.far_ref = f32[32,4,32]{2,1,0:T(4,128)S(1)} collective-permute-done((f32[32,4,32]{2,1,0:T(4,128)}, f32[32,4,32]{2,1,0:T(4,128)S(1)}, u32[]{:S(2)}, u32[]{:S(2)}) %collective-permute-start.1) | collective-permute-done | bytes 16416 | tf_op jit(solution)/shard_map/ppermute | solution.py:31
  11.7 3.9 %project.1 = (bf16[6,72,512]{2,1,0:T(8,128)(2,1)S(1)}, bf16[512,1152]{1,0:T(8,128)(2,1)S(1)}, f32[4,1152]{1,0:T(4,128)S(1)}, f32[512,1152]{1,0:T(8,128)S(1)}, bf...) custom-call(s32[1]{0:T(128)S(6)} %copy.14.step_ref, ...), custom_call_target="tpu_custom_call" | custom-call | flops 2000000000 | bytes 8000000 | tf_op jit(solution)/shard_map/project/pallas_call | solution.py:564
  15.6 0.6 %collective-permute-start.2 = (bf16[144,512]{1,0:T(8,128)(2,1)S(1)}, bf16[144,512]{1,0:T(8,128)(2,1)S(1)}, u32[]{:S(2)}, u32[]{:S(2)}) collective-permute-start(bf16[144,512]{1,0:T(8,128)(2,1)S(1)} %get-tuple-element.40), channel_id=1, source_target_pairs={{0,16},{16,0},{1,17},{17,1},{2,18},{18,2},{3,19},{19,3},{4,20},{20... | collective-permute-start | bytes 442376 | tf_op jit(solution)/shard_map/ppermute | solution.py:35
  16.3 0.0 collective-permute-start.4
  16.3 0.0 collective-permute-done.6.mine_ref
  16.3 0.5 %collective-permute-start.7 = (bf16[72,1152]{1,0:T(8,128)(2,1)S(1)}, bf16[72,1152]{1,0:T(8,128)(2,1)S(1)}, u32[]{:S(2)}, u32[]{:S(2)}) collective-permute-start(bf16[72,1152]{1,0:T(8,128)(2,1)S(1)} %collective-permute-done.6.mine_ref), channel_id=1, source_target_pairs={{0,1},{1,0},{2,3},{3,2},{4,5},{5,4},{6,7},{7,6},{8,9},{9,8},{10,11... | collective-permute-start | bytes 497672 | tf_op jit(solution)/shard_map/ppermute | solution.py:40
  16.8 1.5 %second.1 = (bf16[6,72,512]{2,1,0:T(8,128)(2,1)S(1)}, bf16[288,1152]{1,0:T(8,128)(2,1)S(1)}, bf16[144,512]{1,0:T(8,128)(2,1)S(1)}) custom-call(bf16[512,1152]{1,0:T(8,128)(2,1)S(1)} %get-tuple-element.35.normed_ref, bf16[2,2,4,72,120]{4,3,2,1,0:T(8,128)(2,1)S(1)} %get-tuple-element.36.text_ref, bf16[432,1152]{1,0:T(8,128)(2,1)S(1)} %get-tuple-element.37.weight_ref, ...), custom_call_target="tpu_custom_call" | custom-call | flops 1000000000 | bytes 1000000 | tf_op jit(solution)/shard_map/second/pallas_call | solution.py:590
  18.3 1.5 %collective-permute-start.5 = (bf16[144,512]{1,0:T(8,128)(2,1)S(1)}, bf16[144,512]{1,0:T(8,128)(2,1)S(1)}, u32[]{:S(2)}, u32[]{:S(2)}) collective-permute-start(bf16[144,512]{1,0:T(8,128)(2,1)S(1)} %get-tuple-element.42), channel_id=1, source_target_pairs={{0,16},{16,0},{1,17},{17,1},{2,18},{18,2},{3,19},{19,3},{4,20},{20... | collective-permute-start | bytes 442376 | tf_op jit(solution)/shard_map/ppermute | solution.py:35
  20.4 2.2 %attend.1.mixed_ref = f32[512,1152]{1,0:T(8,128)S(1)} custom-call(bf16[6,72,512]{2,1,0:T(8,128)(2,1)S(1)} %get-tuple-element.34.early_ref, bf16[6,72,512]{2,1,0:T(8,128)(2,1)S(1)} %get-tuple-element.38.late_ref, bf16[2,2,4,72,120]{4,3,2,1,0:T(8,128)(2,1)S(1)} %get-tuple-element.36.text_ref, bf16[288,1152]{1,0:T(8,128)(2,1)S(1)} %get-tuple-element.39.weight_ref), custom_call_target="tpu_custom_call" | custom-call | flops 1000000000 | bytes 8000000 | tf_op jit(solution)/shard_map/attend/pallas_call | solution.py:608
  22.7 0.0 copy-start
  22.7 0.0 collective-permute-done.2.early_ref
  22.7 0.0 collective-permute-done.4.core_ref
  22.7 0.6 %partial.1.mixed_ref = f32[512,1152]{1,0:T(8,128)S(1)} custom-call(f32[512,1152]{1,0:T(8,128)S(1)} %attend.1.mixed_ref, bf16[144,512]{1,0:T(8,128)(2,1)S(1)} %collective-permute-done.2.early_ref, bf16[72,1152]{1,0:T(8,128)(2,1)S(1)} %collective-permute-done.3.weight_ref, bf16[72,1152]{1,0:T(8,128)(2,1)S(1)} %collective-permute-done.4.core_ref), custom_call_target="tpu_custom_call" | custom-call | flops 200000000 | bytes 1000000 | tf_op jit(solution)/shard_map/partial/pallas_call | solution.py:617
  23.3 0.0 collective-permute-done.7.neighbour_ref
  23.3 0.1 join.1.weight_ref
  23.4 0.7 %collective-permute-done.5.late_ref = bf16[144,512]{1,0:T(8,128)(2,1)S(1)} collective-permute-done((bf16[144,512]{1,0:T(8,128)(2,1)S(1)}, bf16[144,512]{1,0:T(8,128)(2,1)S(1)}, u32[]{:S(2)}, u32[]{:S(2)}) %collective-permute-start.5) | collective-permute-done | bytes 147488 | tf_op jit(solution)/shard_map/ppermute | solution.py:35
  24.1 0.0 copy-done
  24.1 1.0 %shard_map.113 = (f32[32,128]{1,0:T(8,128)S(1)}, f32[32,128]{1,0:T(8,128)S(1)}) custom-call(s32[1]{0:T(128)S(6)} %copy.12.offset_ref, s32[1]{0:T(128)S(6)} %copy.13.blend_ref, f32[4,1152]{1,0:T(4,128)S(1)} %get-tuple-element.32.modulation_ref, f32[512,1152]{1,0:T(8,128)S(1)} %get-tuple-element.33.embedded_ref, f32[512,1152]{1,0:T(8,128)S(1)} %partial.1.mixed_ref, ...), custom_call_target="tpu_custom_call" | custom-call | flops 500000000 | bytes 2000000 | tf_op jit(solution)/shard_map/pallas_call | solution.py:648
  25.1 0.0 collective-permute-start.8
  25.2 1.0 %shard_map.114 = (f32[32,128]{1,0:T(8,128)S(1)}, f32[32,128]{1,0:T(8,128)S(1)}) custom-call(s32[1]{0:T(128)S(6)} %copy.12.offset_ref, s32[1]{0:T(128)S(6)} %copy.13.blend_ref, f32[4,1152]{1,0:T(4,128)S(1)} %get-tuple-element.32.modulation_ref, f32[512,1152]{1,0:T(8,128)S(1)} %get-tuple-element.33.embedded_ref, f32[512,1152]{1,0:T(8,128)S(1)} %partial.1.mixed_ref, ...), custom_call_target="tpu_custom_call" | custom-call | flops 500000000 | bytes 2000000 | tf_op jit(solution)/shard_map/pallas_call | solution.py:648
  26.2 4.5 %collective-permute-start.9 = (f32[32,128]{1,0:T(8,128)S(1)}, f32[32,128]{1,0:T(8,128)S(1)}, u32[]{:S(2)}, u32[]{:S(2)}) collective-permute-start(f32[32,128]{1,0:T(8,128)S(1)} %get-tuple-element.46), channel_id=1, source_target_pairs={{1,2},{2,1},{3,4},{4,3},{5,6},{6,5},{7,8},{8,7},{9,10},{10,9},{11,... | collective-permute-start | bytes 49160 | tf_op jit(solution)/shard_map/ppermute | solution.py:31
  30.7 0.1 coefficient.1
  30.9 0.0 collective-permute-done.8.near_ref
  30.9 1.3 %collective-permute-done.9.far_ref = f32[32,128]{1,0:T(8,128)S(1)} collective-permute-done((f32[32,128]{1,0:T(8,128)S(1)}, f32[32,128]{1,0:T(8,128)S(1)}, u32[]{:S(2)}, u32[]{:S(2)}) %collective-permute-start.9) | collective-permute-done | bytes 16416 | tf_op jit(solution)/shard_map/ppermute | solution.py:31
  32.2 0.7 %blend.1 = (f32[4,16,32]{2,1,0:T(8,128)}, f32[4,16,32]{2,1,0:T(8,128)}) custom-call(f32[8,128]{1,0:T(8,128)S(1)} %get-tuple-element.27.plan_ref, f32[32,128]{1,0:T(8,128)S(1)} %get-tuple-element.43.center_ref, f32[32,128]{1,0:T(8,128)S(1)} %collective-permute-done.8.near_ref, f32[32,128]{1,0:T(8,128)S(1)} %get-tuple-element.45.far_center_ref, ...), custom_call_target="tpu_custom_call" | custom-call | tf_op jit(solution)/shard_map/blend/pallas_call | solution.py:667
Async XLA Ops:
  1.8 9.0 %collective-permute-start.3 = (bf16[72,1152]{1,0:T(8,128)(2,1)S(1)}, bf16[72,1152]{1,0:T(8,128)(2,1)S(1)}, u32[]{:S(2)}, u32[]{:S(2)}) collective-permute-start(bf16[72,1152]{1,0:T(8,128)(2,1)S(1)} %get-tuple-element.41), channel_id=1, source_target_pairs={{0,16},{16,0},{1,17},{17,1},{2,18},{18,2},{3,19},{19,3},{4,20},{20... | collective-permute-start | bytes 497672 | tf_op jit(solution)/shard_map/ppermute | solution.py:35
  4.8 6.0 %collective-permute-start = (f32[32,4,32]{2,1,0:T(4,128)}, f32[32,4,32]{2,1,0:T(4,128)S(1)}, u32[]{:S(2)}, u32[]{:S(2)}) collective-permute-start(f32[32,4,32]{2,1,0:T(4,128)} %latent_source.1), channel_id=1, source_target_pairs={{0,1},{1,0},{2,3},{3,2},{4,5},{5,4},{6,7},{7,6},{8,9},{9,8},{10,11... | collective-permute-start | bytes 49160 | tf_op jit(solution)/shard_map/ppermute | solution.py:31
  4.8 6.9 %collective-permute-start.1 = (f32[32,4,32]{2,1,0:T(4,128)}, f32[32,4,32]{2,1,0:T(4,128)S(1)}, u32[]{:S(2)}, u32[]{:S(2)}) collective-permute-start(f32[32,4,32]{2,1,0:T(4,128)} %latent_source.1), channel_id=1, source_target_pairs={{1,2},{2,1},{3,4},{4,3},{5,6},{6,5},{7,8},{8,7},{9,10},{10,9},{11,... | collective-permute-start | bytes 49160 | tf_op jit(solution)/shard_map/ppermute | solution.py:31
  10.8 5.5 %collective-permute-start.6 = (bf16[72,1152]{1,0:T(8,128)(2,1)S(1)}, bf16[72,1152]{1,0:T(8,128)(2,1)S(1)}, u32[]{:S(2)}, u32[]{:S(2)}) collective-permute-start(bf16[72,1152]{1,0:T(8,128)(2,1)S(1)} %collective-permute-done.3.weight_ref), channel_id=1, source_target_pairs={{0,2},{1,3},{2,0},{3,1},{4,6},{5,7},{6,4},{7,5},{8,10},{9,11},{10,... | collective-permute-start | bytes 497672 | tf_op jit(solution)/shard_map/ppermute | solution.py:40
  15.6 7.1 %collective-permute-start.2 = (bf16[144,512]{1,0:T(8,128)(2,1)S(1)}, bf16[144,512]{1,0:T(8,128)(2,1)S(1)}, u32[]{:S(2)}, u32[]{:S(2)}) collective-permute-start(bf16[144,512]{1,0:T(8,128)(2,1)S(1)} %get-tuple-element.40), channel_id=1, source_target_pairs={{0,16},{16,0},{1,17},{17,1},{2,18},{18,2},{3,19},{19,3},{4,20},{20... | collective-permute-start | bytes 442376 | tf_op jit(solution)/shard_map/ppermute | solution.py:35
  16.3 6.4 %collective-permute-start.4 = (bf16[72,1152]{1,0:T(8,128)(2,1)S(1)}, bf16[72,1152]{1,0:T(8,128)(2,1)S(1)}, u32[]{:S(2)}, u32[]{:S(2)}) collective-permute-start(bf16[72,1152]{1,0:T(8,128)(2,1)S(1)} %collective-permute-done.3.weight_ref), channel_id=1, source_target_pairs={{0,1},{1,0},{2,3},{3,2},{4,5},{5,4},{6,7},{7,6},{8,9},{9,8},{10,11... | collective-permute-start | bytes 497672 | tf_op jit(solution)/shard_map/ppermute | solution.py:40
  16.3 7.0 %collective-permute-start.7 = (bf16[72,1152]{1,0:T(8,128)(2,1)S(1)}, bf16[72,1152]{1,0:T(8,128)(2,1)S(1)}, u32[]{:S(2)}, u32[]{:S(2)}) collective-permute-start(bf16[72,1152]{1,0:T(8,128)(2,1)S(1)} %collective-permute-done.6.mine_ref), channel_id=1, source_target_pairs={{0,1},{1,0},{2,3},{3,2},{4,5},{5,4},{6,7},{7,6},{8,9},{9,8},{10,11... | collective-permute-start | bytes 497672 | tf_op jit(solution)/shard_map/ppermute | solution.py:40
  18.3 5.8 %collective-permute-start.5 = (bf16[144,512]{1,0:T(8,128)(2,1)S(1)}, bf16[144,512]{1,0:T(8,128)(2,1)S(1)}, u32[]{:S(2)}, u32[]{:S(2)}) collective-permute-start(bf16[144,512]{1,0:T(8,128)(2,1)S(1)} %get-tuple-element.42), channel_id=1, source_target_pairs={{0,16},{16,0},{1,17},{17,1},{2,18},{18,2},{3,19},{19,3},{4,20},{20... | collective-permute-start | bytes 442376 | tf_op jit(solution)/shard_map/ppermute | solution.py:35
  22.7 1.4 %copy-start = (bf16[1152,16]{0,1:T(8,128)(2,1)S(1)}, bf16[1152,16]{0,1:T(8,128)(2,1)}, u32[]{:S(2)}) copy-start(bf16[1152,16]{0,1:T(8,128)(2,1)} %param.16) | copy-start | bytes 110596
  25.1 5.7 %collective-permute-start.8 = (f32[32,128]{1,0:T(8,128)S(1)}, f32[32,128]{1,0:T(8,128)S(1)}, u32[]{:S(2)}, u32[]{:S(2)}) collective-permute-start(f32[32,128]{1,0:T(8,128)S(1)} %get-tuple-element.44), channel_id=1, source_target_pairs={{0,1},{1,0},{2,3},{3,2},{4,5},{5,4},{6,7},{7,6},{8,9},{9,8},{10,11... | collective-permute-start | bytes 49160 | tf_op jit(solution)/shard_map/ppermute | solution.py:31
  26.2 6.0 %collective-permute-start.9 = (f32[32,128]{1,0:T(8,128)S(1)}, f32[32,128]{1,0:T(8,128)S(1)}, u32[]{:S(2)}, u32[]{:S(2)}) collective-permute-start(f32[32,128]{1,0:T(8,128)S(1)} %get-tuple-element.46), channel_id=1, source_target_pairs={{1,2},{2,1},{3,4},{4,3},{5,6},{6,5},{7,8},{8,7},{9,10},{10,9},{11,... | collective-permute-start | bytes 49160 | tf_op jit(solution)/shard_map/ppermute | solution.py:31

commit v8 on v7

--- a/solution.py
+++ b/solution.py
@@ -60,35 +60,22 @@
 
 
 def prepare_kernel(
-    latent_source,
+    row_count,
     patch_source,
-    modulation_ref,
     out_source,
     row_ref,
     col_ref,
     patch_wide_ref,
-    modulation_copy,
-    latent_copy,
-    quarter_copy,
+    quarter_ref,
     patch_ref,
     semaphores,
 ):
-    count = quarter_copy.shape[0]
-    quarter_first = pl.multiple_of(lax.axis_index("win") % 4 * count, 8)
-    copies = [
-        pltpu.make_async_copy(source, target, semaphores.at[place])
-        for place, (source, target) in enumerate(
-            (
-                (patch_source, patch_ref),
-                (modulation_ref, modulation_copy),
-                (latent_source, latent_copy),
-                (out_source.at[pl.ds(quarter_first, count)], quarter_copy),
-            )
-        )
-    ]
-    for copy in copies:
-        copy.start()
-    _, _, row_count = latent_copy.shape
+    patch_copy = pltpu.make_async_copy(patch_source, patch_ref, semaphores.at[0])
+    patch_copy.start()
+    count = quarter_ref.shape[0]
+    first = pl.multiple_of(lax.axis_index("win") % 4 * count, 8)
+    copy = pltpu.make_async_copy(out_source.at[pl.ds(first, count)], quarter_ref, semaphores.at[1])
+    copy.start()
     model_width = patch_ref.shape[1]
     quarter = model_width // 4
 
@@ -102,10 +89,9 @@
 
     table(row_ref, 0)
     table(col_ref, model_width - col_ref.shape[1])
-    copies[0].wait()
+    patch_copy.wait()
     patch_wide_ref[...] = repeat_pairs(patch_ref[...], row_count // 2)
-    for copy in copies[1:]:
-        copy.wait()
+    copy.wait()
 
 
 def coefficient_kernel(step_ref, latent_ref, plan_ref, rows_ref):
@@ -227,22 +213,21 @@
     target_ref[...] = pair
 
 
-def weight_copies(weight_source, weight_ref, half, semaphores):
-    count = weight_ref.shape[0] // 3
-    total = weight_source.shape[0] // 3
-    return [
-        pltpu.make_async_copy(
-            weight_source.at[pl.ds(pl.multiple_of(kind * total + half * count, 16), count)],
-            weight_ref.at[pl.ds(kind * count, count)],
-            semaphores.at[kind],
-        )
-        for kind in range(3)
-    ]
-
-
-def project_half(weight_ref, normed, target_ref, lanes):
+def pair_rows(weight_ref, pair):
+    total = weight_ref.shape[0] // 3
+    count = 2 * HEAD_DIM
+    return jnp.concatenate(
+        [
+            weight_ref[pl.ds(pl.multiple_of(kind * total + pair * count, 16), count), :]
+            for kind in range(3)
+        ],
+        axis=0,
+    )
+
+
+def project_half(weight_ref, pair, normed, target_ref, lanes):
     projected = lax.dot_general(
-        weight_ref[...], normed, (((1,), (1,)), ((), ())), preferred_element_type=jnp.float32
+        pair_rows(weight_ref, pair), normed, (((1,), (1,)), ((), ())), preferred_element_type=jnp.float32
     )
     for block in range(target_ref.shape[0]):
         part = projected[block * HEAD_DIM : (block + 1) * HEAD_DIM]
@@ -261,27 +246,15 @@
     row_ref,
     col_ref,
     patch_ref,
-    weight_source,
-    text_source,
+    weight_ref,
+    text_ref,
     proj_ref,
     normed_ref,
     modulation_ref,
     embedded_ref,
-    text_ref,
-    late_weight_ref,
     sent_ref,
     extended_ref,
-    weight_ref,
-    semaphores,
 ):
-    pair = first_pair()
-    copies = weight_copies(weight_source, weight_ref, pair, semaphores.at[pl.ds(0, 3)])
-    late_copies = weight_copies(
-        weight_source, late_weight_ref, 1 - pair, semaphores.at[pl.ds(3, 3)]
-    )
-    text_copy = pltpu.make_async_copy(text_source, text_ref, semaphores.at[6])
-    for copy in copies + [text_copy] + late_copies:
-        copy.start()
     modulation_ref[...] = modulations_ref[step_ref[0] * STEPS // plan_length]
     slab_cols, channels, row_count = own_ref.shape
     col_pairs, row_couples = slab_cols, row_count // 2
@@ -353,35 +326,25 @@
     early = embed(0)
     later = embed(1)
     norm(0, early)
-    for copy in copies:
-        copy.wait()
-    project_half(weight_ref, normed_ref[chunks[0], :], proj_ref, chunks[0])
+    project_half(weight_ref, first_pair(), normed_ref[chunks[0], :], proj_ref, chunks[0])
     norm(1, later)
-    project_half(weight_ref, normed_ref[chunks[1], :], proj_ref, chunks[1])
+    project_half(weight_ref, first_pair(), normed_ref[chunks[1], :], proj_ref, chunks[1])
     first = token_lanes(1 - side, tokens)
-    text_copy.wait()
     attend(
         [proj_ref], text_ref, first, own_tokens, range(2), functools.partial(keep_pair, sent_ref)
     )
-    for copy in late_copies:
-        copy.wait()
-
-
-def second_kernel(
-    normed_ref, text_ref, weight_ref, out_source, proj_ref, out_ref, sent_ref, semaphore
-):
-    out_copy = pltpu.make_async_copy(out_source, out_ref, semaphore)
-    out_copy.start()
+
+
+def second_kernel(normed_ref, text_ref, weight_ref, proj_ref, sent_ref):
     own_tokens = normed_ref.shape[0] // 2
     for place in range(2):
         chunk = slice(place * own_tokens, (place + 1) * own_tokens)
-        project_half(weight_ref, normed_ref[chunk, :], proj_ref, chunk)
+        project_half(weight_ref, 1 - first_pair(), normed_ref[chunk, :], proj_ref, chunk)
     first = token_lanes(1 - lax.axis_index("cfg"), 2 * own_tokens)
     attend(
         [None, proj_ref], text_ref, first, own_tokens, range(2, 4),
         functools.partial(keep_pair, sent_ref),
     )
-    out_copy.wait()
 
 
 def attend_kernel(early_ref, late_ref, text_ref, weight_ref, mixed_ref):
@@ -543,64 +506,54 @@
     wide = 2 * channels * half_rows
     half_width = model_width // 2
     below, above = half_width // 128 * 128, -(-half_width // 128) * 128
-    row_part, col_part, patch_wide, modulations, own, quarter = pl.pallas_call(
-        prepare_kernel,
+    row_part, col_part, patch_wide, quarter = pl.pallas_call(
+        functools.partial(prepare_kernel, row_count),
         out_shape=(
             shape((row_couples, above), f32),
             shape((col_pairs, model_width - below), f32),
             shape((2 * channels * row_count, model_width), bf16),
-            shape(modulation.shape, f32),
-            shape(latent.shape, f32),
             shape((half_attn // 4, model_width), bf16),
         ),
-        in_specs=[hbm] * 4,
-        out_specs=(VM,) * 6,
-        scratch_shapes=[pltpu.VMEM(patch_weight.shape, bf16), pltpu.SemaphoreType.DMA((4,))],
+        in_specs=[hbm] * 2,
+        out_specs=(VM,) * 4,
+        scratch_shapes=[pltpu.VMEM(patch_weight.shape, bf16), pltpu.SemaphoreType.DMA((2,))],
         name="prepare",
         compiler_params=pltpu.CompilerParams(vmem_limit_bytes=GRANT),
-        cost_estimate=pl.CostEstimate(flops=10**7, bytes_accessed=10**6, transcendentals=10**5),
-    )(*map(keep, (latent, patch_weight, modulation, out_weight)))
+        cost_estimate=pl.CostEstimate(flops=2*10**9, bytes_accessed=10**6, transcendentals=10**5),
+    )(keep(patch_weight), keep(out_weight))
     other_weight = swap(quarter, "cfg")
-    projected, normed, modulate, embedded, text, late_weight, sent = pl.pallas_call(
+    projected, normed, modulate, embedded, sent = pl.pallas_call(
         project_kernel,
         out_shape=(
             shape((3 * heads // 2, HEAD_DIM, tokens), bf16),
             shape((tokens, model_width), bf16),
             shape(modulation.shape[1:], f32),
             shape((tokens, model_width), f32),
-            shape(text.shape, bf16),
-            shape((weight.shape[0] // 2, model_width), bf16),
             shape((half_attn // 2, branches * own_tokens), bf16),
         ),
-        in_specs=[SM, SM] + [VM] * 7 + [hbm] * 2,
-        out_specs=(VM,) * 7,
-        scratch_shapes=[
-            pltpu.VMEM((3 * slab_cols, channels * row_count), f32),
-            pltpu.VMEM((weight.shape[0] // 2, model_width), bf16),
-            pltpu.SemaphoreType.DMA((7,)),
-        ],
+        in_specs=[SM, SM] + [VM] * 9,
+        out_specs=(VM,) * 5,
+        scratch_shapes=[pltpu.VMEM((3 * slab_cols, channels * row_count), f32)],
         name="project",
         compiler_params=pltpu.CompilerParams(vmem_limit_bytes=GRANT),
         cost_estimate=pl.CostEstimate(flops=2 * 10**9, bytes_accessed=8 * 10**6, transcendentals=10**6),
     )(
-        step_index, offsets, modulations, near, own, far, row_part, col_part, patch_wide,
-        keep(weight), keep(text),
+        step_index, offsets, modulation, near, latent, far, row_part, col_part, patch_wide,
+        weight, text,
     )
     early = swap(sent, "cfg")
-    projected_late, own_weight, sent = pl.pallas_call(
+    projected_late, sent = pl.pallas_call(
         second_kernel,
         out_shape=(
             shape((3 * heads // 2, HEAD_DIM, tokens), bf16),
-            shape(out_weight.shape, bf16),
             shape((half_attn // 2, branches * own_tokens), bf16),
         ),
-        in_specs=[VM] * 3 + [hbm],
-        out_specs=(VM,) * 3,
-        scratch_shapes=[pltpu.SemaphoreType.DMA],
+        in_specs=[VM] * 3,
+        out_specs=(VM,) * 2,
         name="second",
         compiler_params=pltpu.CompilerParams(vmem_limit_bytes=GRANT),
         cost_estimate=pl.CostEstimate(flops=10**9, bytes_accessed=10**6, transcendentals=10**6),
-    )(normed, text, late_weight, keep(out_weight))
+    )(normed, text, weight)
     late = swap(sent, "cfg")
     cross_weight = swap_across(other_weight, "win", 2)
     core_weight = swap_across(other_weight, "win", 1)
@@ -613,7 +566,7 @@
         name="attend",
         compiler_params=pltpu.CompilerParams(vmem_limit_bytes=GRANT),
         cost_estimate=pl.CostEstimate(flops=10**9, bytes_accessed=8 * 10**6, transcendentals=10**6),
-    )(projected, projected_late, text, own_weight)
+    )(projected, projected_late, text, out_weight)
     mixed = pl.pallas_call(
         partial_kernel,
         out_shape=shape(mixed.shape, f32),
@@ -634,7 +587,7 @@
         name="coefficient",
         compiler_params=pltpu.CompilerParams(vmem_limit_bytes=GRANT),
         cost_estimate=pl.CostEstimate(flops=10**5, bytes_accessed=10**5, transcendentals=10**4),
-    )(step_index, own)
+    )(step_index, latent)
     late_rows = pl.pallas_call(
         join_kernel,
         out_shape=shape((half_attn // 2, model_width), bf16),

time: 33.1 us -> 31.8 us (0.961)
  starting transfers between devices: 15 us -> 12.1 us
  waiting for transfers between devices: 2.88 us -> 5.65 us
  Pallas kernels: 12.3 us -> 11.1 us
    ppermute x4, starting transfers between devices: 9.17 us -> 7.37 us  [swap_ring(): return lax.ppermute(array, axis, pairs)]
    ppermute x3, waiting for transfers between devices: 0.7 us -> 2.02 us  [swap(): return lax.ppermute(array, axis, [(0, 1), (1, 0)])]
    pallas_call x1, Pallas kernels: 3.92 us -> 2.7 us  [on_device(): pl.pallas_call(project_kernel, out_shape=(shape((3 * heads // 2, HEAD_DIM...]
    ppermute x3, waiting for transfers between devices: 0.01 us -> 1.07 us  [swap_across(): lax.ppermute(array, axis, [(place, place ^ step) for place in range(size)])]
    ppermute x3, starting transfers between devices: 5.22 us -> 4.66 us  [swap(): return lax.ppermute(array, axis, [(0, 1), (1, 0)])]
    ppermute x3, starting transfers between devices: 0.58 us -> 0.08 us  [swap_across(): lax.ppermute(array, axis, [(place, place ^ step) for place in range(size)])]
    ppermute x4, waiting for transfers between devices: 2.17 us -> 2.56 us  [swap_ring(): return lax.ppermute(array, axis, pairs)]
  transfers between devices with their start and end apart: 10 -> 10, of which waited for: 3 -> 4; matrix products, arithmetic and copies ran while one was open for 0% -> 0% of each run, Pallas kernels for 29% -> 26%
where the time goes in v8:
time: 31.8 us; the launch traced here: 31.7 us
  starting transfers between devices  12.1 us (38%)
  Pallas kernels  11.1 us (35%)
  waiting for transfers between devices  5.65 us (18%)
  between operations  2.75 us (9%)
    ppermute x4, starting transfers between devices, swap_ring(): return lax.ppermute(array, axis, pairs)  7.37 us
    ppermute x3, starting transfers between devices, swap(): return lax.ppermute(array, axis, [(0, 1), (1, 0)])  4.66 us
    pallas_call x1, Pallas kernels, on_device(): pl.pallas_call(project_kernel, out_shape=(shape((3 * heads // 2, HEAD_DIM...  2.7 us
    ppermute x4, waiting for transfers between devices, swap_ring(): return lax.ppermute(array, axis, pairs)  2.56 us
    pallas_call x1, Pallas kernels, on_device(): pl.pallas_call(attend_kernel, out_shape=shape((branches * own_tokens, mod...  2.24 us
    pallas_call x2, Pallas kernels, finish(): pl.pallas_call(functools.partial(finish_kernel, half), out_shape=tuple((s...  2.09 us
    ppermute x3, waiting for transfers between devices, swap(): return lax.ppermute(array, axis, [(0, 1), (1, 0)])  2.02 us
    pallas_call x1, Pallas kernels, on_device(): pl.pallas_call(second_kernel, out_shape=(shape((3 * heads // 2, HEAD_DIM,...  1.46 us
  transfers between devices with their start and end apart: 10, of which 4 were waited for; matrix products, arithmetic and copies ran while one was open for 0% of the time, Pallas kernels for 26%

profile of v8, /device:TPU:0, one launch (start us, length us, event | category | flops | bytes accessed | tf_op | source)
XLA Modules:
  0.0 31.7 jit_solution(16787682291644271566)
XLA Ops:
  0.6 0.0 copy-start.3
  0.6 0.0 copy-start.1
  0.7 0.0 copy-start.4
  0.7 0.0 copy-start.5
  0.7 1.1 %prepare.1 = (f32[16,640]{1,0:T(8,128)S(1)}, f32[32,640]{1,0:T(8,128)S(1)}, bf16[256,1152]{1,0:T(8,128)(2,1)S(1)}, bf16[72,1152]{1,0:T(8,128)(2,1)S(1)}) custom-call(bf16[16,1152]{1,0:T(8,128)(2,1)} %patch_source.1, bf16[288,1152]{1,0:T(8,128)(2,1)} %weight_ref.1), custom_call_target="tpu_custom_call" | custom-call | flops 2000000000 | bytes 1000000 | tf_op jit(solution)/shard_map/prepare/pallas_call | solution.py:509
  1.8 3.1 %collective-permute-start.3 = (bf16[72,1152]{1,0:T(8,128)(2,1)S(1)}, bf16[72,1152]{1,0:T(8,128)(2,1)S(1)}, u32[]{:S(2)}, u32[]{:S(2)}) collective-permute-start(bf16[72,1152]{1,0:T(8,128)(2,1)S(1)} %get-tuple-element.31), channel_id=1, source_target_pairs={{0,16},{16,0},{1,17},{17,1},{2,18},{18,2},{3,19},{19,3},{4,20},{20... | collective-permute-start | bytes 497672 | tf_op jit(solution)/shard_map/ppermute | solution.py:35
  4.8 0.0 copy-done.3
  4.8 0.0 collective-permute-start
  4.8 4.6 %collective-permute-start.1 = (f32[32,4,32]{2,1,0:T(4,128)S(1)}, f32[32,4,32]{2,1,0:T(4,128)S(1)}, u32[]{:S(2)}, u32[]{:S(2)}) collective-permute-start(f32[32,4,32]{2,1,0:T(4,128)S(1)} %copy-done.3), channel_id=1, source_target_pairs={{1,2},{2,1},{3,4},{4,3},{5,6},{6,5},{7,8},{8,7},{9,10},{10,9},{11,... | collective-permute-start | bytes 49160 | tf_op jit(solution)/shard_map/ppermute | solution.py:31
  10.8 0.0 collective-permute-done.3.weight_ref
  10.8 0.1 collective-permute-start.6
  10.9 0.0 collective-permute-done.near_ref
  10.9 0.6 %collective-permute-done.1.far_ref = f32[32,4,32]{2,1,0:T(4,128)S(1)} collective-permute-done((f32[32,4,32]{2,1,0:T(4,128)S(1)}, f32[32,4,32]{2,1,0:T(4,128)S(1)}, u32[]{:S(2)}, u32[]{:S(2)}) %collective-permute-start.1) | collective-permute-done | bytes 16416 | tf_op jit(solution)/shard_map/ppermute | solution.py:31
  11.5 0.0 copy-done.1
  11.5 0.0 copy-done.4
  11.5 0.0 copy-done.5
  11.5 2.7 %project.1 = (bf16[6,72,512]{2,1,0:T(8,128)(2,1)S(1)}, bf16[512,1152]{1,0:T(8,128)(2,1)S(1)}, f32[4,1152]{1,0:T(4,128)S(1)}, f32[512,1152]{1,0:T(8,128)S(1)}, bf16[144,512]{1,0:T(8,128)(2,1)S(1)}) custom-call(s32[1]{0:T(128)S(6)} %copy.14.step_ref, s32[1]{0:T(128)S(6)} %copy.12.offset_ref, f32[20,4,1152]{2,1,0:T(4,128)S(1)} %copy-done.5, ...), custom_call_target="tpu_custom_call" | custom-call | flops 2000000000 | bytes 8000000 | tf_op jit(solution)/shard_map/project/pallas_call | solution.py:525
  14.2 0.0 copy-start
  14.2 0.9 %collective-permute-start.2 = (bf16[144,512]{1,0:T(8,128)(2,1)S(1)}, bf16[144,512]{1,0:T(8,128)(2,1)S(1)}, u32[]{:S(2)}, u32[]{:S(2)}) collective-permute-start(bf16[144,512]{1,0:T(8,128)(2,1)S(1)} %get-tuple-element.30), channel_id=1, source_target_pairs={{0,16},{16,0},{1,17},{17,1},{2,18},{18,2},{3,19},{19,3},{4,20},{20... | collective-permute-start | bytes 442376 | tf_op jit(solution)/shard_map/ppermute | solution.py:35
  15.1 0.0 collective-permute-start.4
  15.1 1.1 %collective-permute-done.6.mine_ref = bf16[72,1152]{1,0:T(8,128)(2,1)S(1)} collective-permute-done((bf16[72,1152]{1,0:T(8,128)(2,1)S(1)}, bf16[72,1152]{1,0:T(8,128)(2,1)S(1)}, u32[]{:S(2)}, u32[]{:S(2)}) %collective-permute-start.6) | collective-permute-done | bytes 165920 | tf_op jit(solution)/shard_map/ppermute | solution.py:40
  16.2 0.0 collective-permute-start.7
  16.2 1.5 %second.1 = (bf16[6,72,512]{2,1,0:T(8,128)(2,1)S(1)}, bf16[144,512]{1,0:T(8,128)(2,1)S(1)}) custom-call(bf16[512,1152]{1,0:T(8,128)(2,1)S(1)} %get-tuple-element.28.normed_ref, bf16[2,2,4,72,120]{4,3,2,1,0:T(8,128)(2,1)S(1)} %bitcast.10, bf16[864,1152]{1,0:T(8,128)(2,1)S(1)} %bitcast.15), custom_call_target="tpu_custom_call" | custom-call | flops 1000000000 | bytes 1000000 | tf_op jit(solution)/shard_map/second/pallas_call | solution.py:545
  17.7 0.7 %collective-permute-start.5 = (bf16[144,512]{1,0:T(8,128)(2,1)S(1)}, bf16[144,512]{1,0:T(8,128)(2,1)S(1)}, u32[]{:S(2)}, u32[]{:S(2)}) collective-permute-start(bf16[144,512]{1,0:T(8,128)(2,1)S(1)} %get-tuple-element.32), channel_id=1, source_target_pairs={{0,16},{16,0},{1,17},{17,1},{2,18},{18,2},{3,19},{19,3},{4,20},{20... | collective-permute-start | bytes 442376 | tf_op jit(solution)/shard_map/ppermute | solution.py:35
  19.0 0.0 copy-done
  19.0 2.2 %attend.1.mixed_ref = f32[512,1152]{1,0:T(8,128)S(1)} custom-call(bf16[6,72,512]{2,1,0:T(8,128)(2,1)S(1)} %get-tuple-element.27.early_ref, bf16[6,72,512]{2,1,0:T(8,128)(2,1)S(1)} %get-tuple-element.29.late_ref, bf16[2,2,4,72,120]{4,3,2,1,0:T(8,128)(2,1)S(1)} %bitcast.11, bf16[288,1152]{1,0:T(8,128)(2,1)S(1)} %copy-done), custom_call_target="tpu_custom_call" | custom-call | flops 1000000000 | bytes 8000000 | tf_op jit(solution)/shard_map/attend/pallas_call | solution.py:561
  21.3 0.0 copy-start.2
  21.3 0.0 collective-permute-done.2.early_ref
  21.3 0.0 collective-permute-done.4.core_ref
  21.3 0.6 %partial.1.mixed_ref = f32[512,1152]{1,0:T(8,128)S(1)} custom-call(f32[512,1152]{1,0:T(8,128)S(1)} %attend.1.mixed_ref, bf16[144,512]{1,0:T(8,128)(2,1)S(1)} %collective-permute-done.2.early_ref, bf16[72,1152]{1,0:T(8,128)(2,1)S(1)} %collective-permute-done.3.weight_ref, bf16[72,1152]{1,0:T(8,128)(2,1)S(1)} %collective-permute-done.4.core_ref), custom_call_target="tpu_custom_call" | custom-call | flops 200000000 | bytes 1000000 | tf_op jit(solution)/shard_map/partial/pallas_call | solution.py:570
  21.9 0.0 collective-permute-done.7.neighbour_ref
  21.9 0.1 join.1.weight_ref
  22.0 2.0 %collective-permute-done.5.late_ref = bf16[144,512]{1,0:T(8,128)(2,1)S(1)} collective-permute-done((bf16[144,512]{1,0:T(8,128)(2,1)S(1)}, bf16[144,512]{1,0:T(8,128)(2,1)S(1)}, u32[]{:S(2)}, u32[]{:S(2)}) %collective-permute-start.5) | collective-permute-done | bytes 147488 | tf_op jit(solution)/shard_map/ppermute | solution.py:35
  24.0 0.0 copy-done.2
  24.0 1.0 %shard_map.114 = (f32[32,128]{1,0:T(8,128)S(1)}, f32[32,128]{1,0:T(8,128)S(1)}) custom-call(s32[1]{0:T(128)S(6)} %copy.12.offset_ref, s32[1]{0:T(128)S(6)} %copy.13.blend_ref, f32[4,1152]{1,0:T(4,128)S(1)} %get-tuple-element.25.modulation_ref, f32[512,1152]{1,0:T(8,128)S(1)} %get-tuple-element.26.embedded_ref, f32[512,1152]{1,0:T(8,128)S(1)} %partial.1.mixed_ref, ...), custom_call_target="tpu_custom_call" | custom-call | flops 500000000 | bytes 2000000 | tf_op jit(solution)/shard_map/pallas_call | solution.py:601
  25.1 2.7 %collective-permute-start.9 = (f32[32,128]{1,0:T(8,128)S(1)}, f32[32,128]{1,0:T(8,128)S(1)}, u32[]{:S(2)}, u32[]{:S(2)}) collective-permute-start(f32[32,128]{1,0:T(8,128)S(1)} %get-tuple-element.36), channel_id=1, source_target_pairs={{1,2},{2,1},{3,4},{4,3},{5,6},{6,5},{7,8},{8,7},{9,10},{10,9},{11,... | collective-permute-start | bytes 49160 | tf_op jit(solution)/shard_map/ppermute | solution.py:31
  27.8 1.0 %shard_map.113 = (f32[32,128]{1,0:T(8,128)S(1)}, f32[32,128]{1,0:T(8,128)S(1)}) custom-call(s32[1]{0:T(128)S(6)} %copy.12.offset_ref, s32[1]{0:T(128)S(6)} %copy.13.blend_ref, f32[4,1152]{1,0:T(4,128)S(1)} %get-tuple-element.25.modulation_ref, f32[512,1152]{1,0:T(8,128)S(1)} %get-tuple-element.26.embedded_ref, f32[512,1152]{1,0:T(8,128)S(1)} %partial.1.mixed_ref, ...), custom_call_target="tpu_custom_call" | custom-call | flops 500000000 | bytes 2000000 | tf_op jit(solution)/shard_map/pallas_call | solution.py:601
  28.8 0.0 collective-permute-start.8
  28.8 0.1 coefficient.1
  29.0 2.0 %collective-permute-done.9.far_ref = f32[32,128]{1,0:T(8,128)S(1)} collective-permute-done((f32[32,128]{1,0:T(8,128)S(1)}, f32[32,128]{1,0:T(8,128)S(1)}, u32[]{:S(2)}, u32[]{:S(2)}) %collective-permute-start.9) | collective-permute-done | bytes 16416 | tf_op jit(solution)/shard_map/ppermute | solution.py:31
  30.9 0.0 collective-permute-done.8.near_ref
  30.9 0.7 %blend.1 = (f32[4,16,32]{2,1,0:T(8,128)}, f32[4,16,32]{2,1,0:T(8,128)}) custom-call(f32[8,128]{1,0:T(8,128)S(1)} %get-tuple-element.21.plan_ref, f32[32,128]{1,0:T(8,128)S(1)} %get-tuple-element.33.center_ref, f32[32,128]{1,0:T(8,128)S(1)} %collective-permute-done.8.near_ref, f32[32,128]{1,0:T(8,128)S(1)} %get-tuple-element.35.far_center_ref, ...), custom_call_target="tpu_custom_call" | custom-call | tf_op jit(solution)/shard_map/blend/pallas_call | solution.py:620
Async XLA Ops:
  0.6 4.2 %copy-start.3 = (f32[32,4,32]{2,1,0:T(4,128)S(1)}, f32[32,4,32]{2,1,0:T(4,128)}, u32[]{:S(2)}) copy-start(f32[32,4,32]{2,1,0:T(4,128)} %own_ref.1) | copy-start | bytes 49156
  0.6 10.8 %copy-start.1 = (bf16[2,2,120,288]{2,3,1,0:T(8,128)(2,1)S(1)}, bf16[2,2,120,288]{2,3,1,0:T(8,128)(2,1)}, u32[]{:S(2)}) copy-start(bf16[2,2,120,288]{2,3,1,0:T(8,128)(2,1)} %param.11) | copy-start | bytes 829444
  0.7 10.8 %copy-start.4 = (bf16[1152,3,288]{0,2,1:T(8,128)(2,1)S(1)}, bf16[1152,3,288]{0,2,1:T(8,128)(2,1)}, u32[]{:S(2)}) copy-start(bf16[1152,3,288]{0,2,1:T(8,128)(2,1)} %param.13) | copy-start | bytes 5971972
  0.7 10.8 %copy-start.5 = (f32[20,4,1152]{2,1,0:T(4,128)S(1)}, f32[20,4,1152]{2,1,0:T(4,128)}, u32[]{:S(2)}) copy-start(f32[20,4,1152]{2,1,0:T(4,128)} %modulations_ref.1) | copy-start | bytes 1105924
  1.8 9.0 %collective-permute-start.3 = (bf16[72,1152]{1,0:T(8,128)(2,1)S(1)}, bf16[72,1152]{1,0:T(8,128)(2,1)S(1)}, u32[]{:S(2)}, u32[]{:S(2)}) collective-permute-start(bf16[72,1152]{1,0:T(8,128)(2,1)S(1)} %get-tuple-element.31), channel_id=1, source_target_pairs={{0,16},{16,0},{1,17},{17,1},{2,18},{18,2},{3,19},{19,3},{4,20},{20... | collective-permute-start | bytes 497672 | tf_op jit(solution)/shard_map/ppermute | solution.py:35
  4.8 6.0 %collective-permute-start = (f32[32,4,32]{2,1,0:T(4,128)S(1)}, f32[32,4,32]{2,1,0:T(4,128)S(1)}, u32[]{:S(2)}, u32[]{:S(2)}) collective-permute-start(f32[32,4,32]{2,1,0:T(4,128)S(1)} %copy-done.3), channel_id=1, source_target_pairs={{0,1},{1,0},{2,3},{3,2},{4,5},{5,4},{6,7},{7,6},{8,9},{9,8},{10,11... | collective-permute-start | bytes 49160 | tf_op jit(solution)/shard_map/ppermute | solution.py:31
  4.8 6.6 %collective-permute-start.1 = (f32[32,4,32]{2,1,0:T(4,128)S(1)}, f32[32,4,32]{2,1,0:T(4,128)S(1)}, u32[]{:S(2)}, u32[]{:S(2)}) collective-permute-start(f32[32,4,32]{2,1,0:T(4,128)S(1)} %copy-done.3), channel_id=1, source_target_pairs={{1,2},{2,1},{3,4},{4,3},{5,6},{6,5},{7,8},{8,7},{9,10},{10,9},{11,... | collective-permute-start | bytes 49160 | tf_op jit(solution)/shard_map/ppermute | solution.py:31
  10.8 5.4 %collective-permute-start.6 = (bf16[72,1152]{1,0:T(8,128)(2,1)S(1)}, bf16[72,1152]{1,0:T(8,128)(2,1)S(1)}, u32[]{:S(2)}, u32[]{:S(2)}) collective-permute-start(bf16[72,1152]{1,0:T(8,128)(2,1)S(1)} %collective-permute-done.3.weight_ref), channel_id=1, source_target_pairs={{0,2},{1,3},{2,0},{3,1},{4,6},{5,7},{6,4},{7,5},{8,10},{9,11},{10,... | collective-permute-start | bytes 497672 | tf_op jit(solution)/shard_map/ppermute | solution.py:40
  14.2 4.8 %copy-start = (bf16[288,1152]{1,0:T(8,128)(2,1)S(1)}, bf16[288,1152]{1,0:T(8,128)(2,1)}, u32[]{:S(2)}) copy-start(bf16[288,1152]{1,0:T(8,128)(2,1)} %weight_ref.1) | copy-start | bytes 1990660
  14.2 7.1 %collective-permute-start.2 = (bf16[144,512]{1,0:T(8,128)(2,1)S(1)}, bf16[144,512]{1,0:T(8,128)(2,1)S(1)}, u32[]{:S(2)}, u32[]{:S(2)}) collective-permute-start(bf16[144,512]{1,0:T(8,128)(2,1)S(1)} %get-tuple-element.30), channel_id=1, source_target_pairs={{0,16},{16,0},{1,17},{17,1},{2,18},{18,2},{3,19},{19,3},{4,20},{20... | collective-permute-start | bytes 442376 | tf_op jit(solution)/shard_map/ppermute | solution.py:35
  15.1 6.2 %collective-permute-start.4 = (bf16[72,1152]{1,0:T(8,128)(2,1)S(1)}, bf16[72,1152]{1,0:T(8,128)(2,1)S(1)}, u32[]{:S(2)}, u32[]{:S(2)}) collective-permute-start(bf16[72,1152]{1,0:T(8,128)(2,1)S(1)} %collective-permute-done.3.weight_ref), channel_id=1, source_target_pairs={{0,1},{1,0},{2,3},{3,2},{4,5},{5,4},{6,7},{7,6},{8,9},{9,8},{10,11... | collective-permute-start | bytes 497672 | tf_op jit(solution)/shard_map/ppermute | solution.py:40
  16.2 5.7 %collective-permute-start.7 = (bf16[72,1152]{1,0:T(8,128)(2,1)S(1)}, bf16[72,1152]{1,0:T(8,128)(2,1)S(1)}, u32[]{:S(2)}, u32[]{:S(2)}) collective-permute-start(bf16[72,1152]{1,0:T(8,128)(2,1)S(1)} %collective-permute-done.6.mine_ref), channel_id=1, source_target_pairs={{0,1},{1,0},{2,3},{3,2},{4,5},{5,4},{6,7},{7,6},{8,9},{9,8},{10,11... | collective-permute-start | bytes 497672 | tf_op jit(solution)/shard_map/ppermute | solution.py:40
  17.7 6.3 %collective-permute-start.5 = (bf16[144,512]{1,0:T(8,128)(2,1)S(1)}, bf16[144,512]{1,0:T(8,128)(2,1)S(1)}, u32[]{:S(2)}, u32[]{:S(2)}) collective-permute-start(bf16[144,512]{1,0:T(8,128)(2,1)S(1)} %get-tuple-element.32), channel_id=1, source_target_pairs={{0,16},{16,0},{1,17},{17,1},{2,18},{18,2},{3,19},{19,3},{4,20},{20... | collective-permute-start | bytes 442376 | tf_op jit(solution)/shard_map/ppermute | solution.py:35
  21.3 2.7 %copy-start.2 = (bf16[1152,16]{0,1:T(8,128)(2,1)S(1)}, bf16[1152,16]{0,1:T(8,128)(2,1)}, u32[]{:S(2)}) copy-start(bf16[1152,16]{0,1:T(8,128)(2,1)} %param.16) | copy-start | bytes 110596
  25.1 5.9 %collective-permute-start.9 = (f32[32,128]{1,0:T(8,128)S(1)}, f32[32,128]{1,0:T(8,128)S(1)}, u32[]{:S(2)}, u32[]{:S(2)}) collective-permute-start(f32[32,128]{1,0:T(8,128)S(1)} %get-tuple-element.36), channel_id=1, source_target_pairs={{1,2},{2,1},{3,4},{4,3},{5,6},{6,5},{7,8},{8,7},{9,10},{10,9},{11,... | collective-permute-start | bytes 49160 | tf_op jit(solution)/shard_map/ppermute | solution.py:31
  28.8 2.1 %collective-permute-start.8 = (f32[32,128]{1,0:T(8,128)S(1)}, f32[32,128]{1,0:T(8,128)S(1)}, u32[]{:S(2)}, u32[]{:S(2)}) collective-permute-start(f32[32,128]{1,0:T(8,128)S(1)} %get-tuple-element.34), channel_id=1, source_target_pairs={{0,1},{1,0},{2,3},{3,2},{4,5},{5,4},{6,7},{7,6},{8,9},{9,8},{10,11... | collective-permute-start | bytes 49160 | tf_op jit(solution)/shard_map/ppermute | solution.py:31

commit v9 on v8

--- a/solution.py
+++ b/solution.py
@@ -335,7 +335,13 @@
     )
 
 
-def second_kernel(normed_ref, text_ref, weight_ref, proj_ref, sent_ref):
+def keep_halves(near_ref, far_ref, place, pair):
+    count = near_ref.shape[1]
+    near_ref[...] = pair[:, :count]
+    far_ref[...] = pair[:, count:]
+
+
+def second_kernel(normed_ref, text_ref, weight_ref, proj_ref, near_ref, far_ref):
     own_tokens = normed_ref.shape[0] // 2
     for place in range(2):
         chunk = slice(place * own_tokens, (place + 1) * own_tokens)
@@ -343,11 +349,16 @@
     first = token_lanes(1 - lax.axis_index("cfg"), 2 * own_tokens)
     attend(
         [None, proj_ref], text_ref, first, own_tokens, range(2, 4),
-        functools.partial(keep_pair, sent_ref),
-    )
-
-
-def attend_kernel(early_ref, late_ref, text_ref, weight_ref, mixed_ref):
+        functools.partial(keep_halves, near_ref, far_ref),
+    )
+
+
+def attend_kernel(
+    early_ref, late_ref, text_ref, weight_ref, final_ref, mixed_ref, final_wide_ref
+):
+    final_wide_ref[...] = repeat_pairs(
+        final_ref[...], final_wide_ref.shape[0] // final_ref.shape[0]
+    )
     tokens = early_ref.shape[2]
     own_tokens = tokens // 2
     first = token_lanes(lax.axis_index("cfg"), tokens)
@@ -384,8 +395,17 @@
     joined_ref[...] = join(mine_ref, neighbour_ref)
 
 
-def partial_kernel(mixed_ref, early_ref, weight_ref, core_ref, summed_ref):
-    summed_ref[...] = mixed_ref[...] + contract(early_ref[...], join(weight_ref, core_ref))
+def partial_kernel(
+    half, modulation_ref, embedded_ref, mixed_ref, early_ref, weight_ref, core_ref, residual_ref
+):
+    count = residual_ref.shape[0] // 2
+    lanes = slice(half * 2 * count, (half + 1) * 2 * count)
+    mixed = contract(early_ref[:, lanes], join(weight_ref, core_ref)) + mixed_ref[lanes, :]
+    first = pl.multiple_of(half * 2 * count + lax.axis_index("cfg") * count, count)
+    embedded = embedded_ref[pl.ds(first, count), :]
+    for branch in range(2):
+        rows = slice(branch * count, (branch + 1) * count)
+        residual_ref[rows, :] = embedded + modulation_ref[2:3, :] * mixed[rows]
 
 
 def finish_kernel(
@@ -393,8 +413,7 @@
     offset_ref,
     blend_ref,
     modulation_ref,
-    embedded_ref,
-    mixed_ref,
+    residual_ref,
     late_ref,
     weight_ref,
     final_ref,
@@ -405,27 +424,22 @@
 ):
     slab_cols, wide = center_ref.shape
     half_pairs = slab_cols // 2
-    count = embedded_ref.shape[0] // 4
+    count = residual_ref.shape[0] // 2
     couples = count // half_pairs
-    final_wide = repeat_pairs(final_ref[...], couples)
     gate, gain = modulation_ref[2:3, :], 1.0 + modulation_ref[3:4, :]
-    side_first = pl.multiple_of(half * 2 * count + lax.axis_index("cfg") * count, count)
-    lanes = slice(half * 2 * count, (half + 1) * 2 * count)
-    other = contract(late_ref[:, lanes], weight_ref[...])
+    other = contract(late_ref[...], weight_ref[...])
     predicted = []
     block = slab_cols
     for branch in range(2):
         for place in range(count // block):
             rows = slice(branch * count + place * block, branch * count + (place + 1) * block)
-            mixed = mixed_ref[lanes.start + rows.start : lanes.start + rows.stop, :] + other[rows]
-            embedded = embedded_ref[pl.ds(side_first + place * block, block), :]
-            residual = embedded + gate * mixed
+            residual = residual_ref[rows, :] + gate * other[rows]
             final_norm_ref[rows, :] = (layer_norm(residual) * gain).astype(jnp.bfloat16)
         rows = slice(branch * count, (branch + 1) * count)
         predicted.append(
             lax.dot_general(
                 final_norm_ref[rows, :],
-                final_wide,
+                final_ref[...],
                 (((1,), (1,)), ((), ())),
                 preferred_element_type=jnp.float32,
             )
@@ -542,40 +556,47 @@
         weight, text,
     )
     early = swap(sent, "cfg")
-    projected_late, sent = pl.pallas_call(
+    projected_late, sent_near, sent_far = pl.pallas_call(
         second_kernel,
         out_shape=(
             shape((3 * heads // 2, HEAD_DIM, tokens), bf16),
-            shape((half_attn // 2, branches * own_tokens), bf16),
+            shape((half_attn // 2, own_tokens), bf16),
+            shape((half_attn // 2, own_tokens), bf16),
         ),
         in_specs=[VM] * 3,
-        out_specs=(VM,) * 2,
+        out_specs=(VM,) * 3,
         name="second",
         compiler_params=pltpu.CompilerParams(vmem_limit_bytes=GRANT),
         cost_estimate=pl.CostEstimate(flops=10**9, bytes_accessed=10**6, transcendentals=10**6),
     )(normed, text, weight)
-    late = swap(sent, "cfg")
+    late_far = swap(sent_far, "cfg")
+    late_near = swap(sent_near, "cfg")
     cross_weight = swap_across(other_weight, "win", 2)
     core_weight = swap_across(other_weight, "win", 1)
     core_cross_weight = swap_across(cross_weight, "win", 1)
-    mixed = pl.pallas_call(
+    mixed, final_wide = pl.pallas_call(
         attend_kernel,
-        out_shape=shape((branches * own_tokens, model_width), f32),
-        in_specs=[VM] * 4,
-        out_specs=VM,
+        out_shape=(
+            shape((branches * own_tokens, model_width), f32),
+            shape((wide, model_width), bf16),
+        ),
+        in_specs=[VM] * 5,
+        out_specs=(VM, VM),
         name="attend",
         compiler_params=pltpu.CompilerParams(vmem_limit_bytes=GRANT),
         cost_estimate=pl.CostEstimate(flops=10**9, bytes_accessed=8 * 10**6, transcendentals=10**6),
-    )(projected, projected_late, text, out_weight)
-    mixed = pl.pallas_call(
-        partial_kernel,
-        out_shape=shape(mixed.shape, f32),
-        in_specs=[VM] * 4,
-        out_specs=VM,
-        name="partial",
-        compiler_params=pltpu.CompilerParams(vmem_limit_bytes=GRANT),
-        cost_estimate=pl.CostEstimate(flops=2 * 10**8, bytes_accessed=10**6, transcendentals=0),
-    )(mixed, early, other_weight, core_weight)
+    )(projected, projected_late, text, out_weight, final)
+
+    def partial(half):
+        return pl.pallas_call(
+            functools.partial(partial_kernel, half),
+            out_shape=shape((own_tokens, model_width), f32),
+            in_specs=[VM] * 6,
+            out_specs=VM,
+            compiler_params=pltpu.CompilerParams(vmem_limit_bytes=GRANT),
+            cost_estimate=pl.CostEstimate(flops=10**8, bytes_accessed=10**6, transcendentals=0),
+        )(modulate, embedded, mixed, early, other_weight, core_weight)
+
     plan_values, rows = pl.pallas_call(
         coefficient_kernel,
         out_shape=(
@@ -597,11 +618,11 @@
         compiler_params=pltpu.CompilerParams(vmem_limit_bytes=GRANT),
     )(cross_weight, core_cross_weight)
 
-    def finish(half):
+    def finish(half, residual, late):
         return pl.pallas_call(
             functools.partial(finish_kernel, half),
             out_shape=tuple(shape((slab_cols, wide), f32) for _ in range(2)),
-            in_specs=[SM, SM] + [VM] * 6,
+            in_specs=[SM, SM] + [VM] * 5,
             out_specs=(VM, VM),
             scratch_shapes=[
                 pltpu.VMEM((3 * slab_cols + 8, wide), f32),
@@ -611,10 +632,10 @@
             cost_estimate=pl.CostEstimate(
                 flops=5 * 10**8, bytes_accessed=2 * 10**6, transcendentals=10**3
             ),
-        )(offsets, blend_weights, modulate, embedded, mixed, late, late_rows, final)
-
-    to_far, far_center = finish(1)
-    to_near, center = finish(0)
+        )(offsets, blend_weights, modulate, residual, late, late_rows, final_wide)
+
+    to_far, far_center = finish(1, partial(1), late_far)
+    to_near, center = finish(0, partial(0), late_near)
     from_far = swap_ring(to_far, "win", 1)
     from_near = swap_ring(to_near, "win", 0)
     previous, noise = pl.pallas_call(

time: 31.8 us -> 31.4 us (0.987)
  waiting for transfers between devices: 5.65 us -> 4.05 us
  starting transfers between devices: 12.1 us -> 13.1 us
    ppermute x3 -> x4, waiting for transfers between devices: 2.02 us -> 0.01 us  [swap(): return lax.ppermute(array, axis, [(0, 1), (1, 0)])]
    ppermute x3 -> x4, starting transfers between devices: 4.66 us -> 5.99 us  [swap(): return lax.ppermute(array, axis, [(0, 1), (1, 0)])]
    ppermute x3, waiting for transfers between devices: 1.07 us -> 1.7 us  [swap_across(): lax.ppermute(array, axis, [(place, place ^ step) for place in range(size)])]
    ppermute x4, starting transfers between devices: 7.37 us -> 7.02 us  [swap_ring(): return lax.ppermute(array, axis, pairs)]
    pallas_call x2 -> x3, Pallas kernels: 2.8 us -> 3.03 us  [the longest x1 2.26 us: on_device(): pl.pallas_call(attend_kernel, out_shape=(shape((branches * own_tokens, mo...]
  transfers between devices with their start and end apart: 10 -> 11, of which waited for: 4 -> 2; matrix products, arithmetic and copies ran while one was open for 0% -> 0% of each run, Pallas kernels for 26% -> 30%
where the time goes in v9:
time: 31.4 us; the launch traced here: 31.3 us
  starting transfers between devices  13.1 us (42%)
  Pallas kernels  11.3 us (36%)
  waiting for transfers between devices  4.05 us (13%)
  between operations  2.78 us (9%)
    ppermute x4, starting transfers between devices, swap_ring(): return lax.ppermute(array, axis, pairs)  7.02 us
    ppermute x4, starting transfers between devices, swap(): return lax.ppermute(array, axis, [(0, 1), (1, 0)])  5.99 us
    pallas_call x1, Pallas kernels, on_device(): pl.pallas_call(project_kernel, out_shape=(shape((3 * heads // 2, HEAD_DIM...  2.71 us
    ppermute x4, waiting for transfers between devices, swap_ring(): return lax.ppermute(array, axis, pairs)  2.34 us
    pallas_call x1, Pallas kernels, on_device(): pl.pallas_call(attend_kernel, out_shape=(shape((branches * own_tokens, mo...  2.26 us
    pallas_call x2, Pallas kernels, finish(): pl.pallas_call(functools.partial(finish_kernel, half), out_shape=tuple((s...  2.04 us
    ppermute x3, waiting for transfers between devices, swap_across(): lax.ppermute(array, axis, [(place, place ^ step) for place in range(size)])  1.7 us
    pallas_call x1, Pallas kernels, on_device(): pl.pallas_call(second_kernel, out_shape=(shape((3 * heads // 2, HEAD_DIM,...  1.46 us
  transfers between devices with their start and end apart: 11, of which 2 were waited for; matrix products, arithmetic and copies ran while one was open for 0% of the time, Pallas kernels for 30%

profile of v9, /device:TPU:0, one launch (start us, length us, event | category | flops | bytes accessed | tf_op | source)
XLA Modules:
  0.0 31.3 jit_solution(11026757755727577058)
XLA Ops:
  0.6 0.0 copy-start
  0.6 0.0 copy-start.4
  0.7 0.0 copy-start.1
  0.7 0.0 copy-start.3
  0.7 1.1 %prepare.1 = (f32[16,640]{1,0:T(8,128)S(1)}, f32[32,640]{1,0:T(8,128)S(1)}, bf16[256,1152]{1,0:T(8,128)(2,1)S(1)}, bf16[72,1152]{1,0:T(8,128)(2,1)S(1)}) custom-call(bf16[16,1152]{1,0:T(8,128)(2,1)} %patch_source.1, bf16[288,1152]{1,0:T(8,128)(2,1)} %weight_ref.1), custom_call_target="tpu_custom_call" | custom-call | flops 2000000000 | bytes 1000000 | tf_op jit(solution)/shard_map/prepare/pallas_call | solution.py:523
  1.8 3.1 %collective-permute-start.3 = (bf16[72,1152]{1,0:T(8,128)(2,1)S(1)}, bf16[72,1152]{1,0:T(8,128)(2,1)S(1)}, u32[]{:S(2)}, u32[]{:S(2)}) collective-permute-start(bf16[72,1152]{1,0:T(8,128)(2,1)S(1)} %get-tuple-element.35), channel_id=1, source_target_pairs={{0,16},{16,0},{1,17},{17,1},{2,18},{18,2},{3,19},{19,3},{4,20},{20... | collective-permute-start | bytes 497672 | tf_op jit(solution)/shard_map/ppermute | solution.py:35
  4.8 0.0 copy-done
  4.8 0.0 collective-permute-start
  4.8 4.6 %collective-permute-start.1 = (f32[32,4,32]{2,1,0:T(4,128)S(1)}, f32[32,4,32]{2,1,0:T(4,128)S(1)}, u32[]{:S(2)}, u32[]{:S(2)}) collective-permute-start(f32[32,4,32]{2,1,0:T(4,128)S(1)} %copy-done), channel_id=1, source_target_pairs={{1,2},{2,1},{3,4},{4,3},{5,6},{6,5},{7,8},{8,7},{9,10},{10,9},{11,... | collective-permute-start | bytes 49160 | tf_op jit(solution)/shard_map/ppermute | solution.py:31
  11.4 0.0 collective-permute-done.3.weight_ref
  11.4 0.1 collective-permute-start.6
  11.5 0.0 collective-permute-done.near_ref
  11.5 0.0 collective-permute-done.1.far_ref
  11.5 0.0 copy-done.4
  11.6 0.0 copy-done.1
  11.6 0.0 copy-done.3
  11.6 2.7 %project.1 = (bf16[6,72,512]{2,1,0:T(8,128)(2,1)S(1)}, bf16[512,1152]{1,0:T(8,128)(2,1)S(1)}, f32[4,1152]{1,0:T(4,128)S(1)}, f32[512,1152]{1,0:T(8,128)S(1)}, bf16[144,512]{1,0:T(8,128)(2,1)S(1)}) custom-call(s32[1]{0:T(128)S(6)} %copy.14.step_ref, s32[1]{0:T(128)S(6)} %copy.12.offset_ref, f32[20,4,1152]{2,1,0:T(4,128)S(1)} %copy-done.3, ...), custom_call_target="tpu_custom_call" | custom-call | flops 2000000000 | bytes 8000000 | tf_op jit(solution)/shard_map/project/pallas_call | solution.py:539
  14.3 0.0 copy-start.2
  14.3 0.0 copy-start.5
  14.3 0.8 %collective-permute-start.2 = (bf16[144,512]{1,0:T(8,128)(2,1)S(1)}, bf16[144,512]{1,0:T(8,128)(2,1)S(1)}, u32[]{:S(2)}, u32[]{:S(2)}) collective-permute-start(bf16[144,512]{1,0:T(8,128)(2,1)S(1)} %get-tuple-element.34), channel_id=1, source_target_pairs={{0,16},{16,0},{1,17},{17,1},{2,18},{18,2},{3,19},{19,3},{4,20},{20... | collective-permute-start | bytes 442376 | tf_op jit(solution)/shard_map/ppermute | solution.py:35
  15.2 0.0 collective-permute-start.4
  15.2 1.7 %collective-permute-done.6.mine_ref = bf16[72,1152]{1,0:T(8,128)(2,1)S(1)} collective-permute-done((bf16[72,1152]{1,0:T(8,128)(2,1)S(1)}, bf16[72,1152]{1,0:T(8,128)(2,1)S(1)}, u32[]{:S(2)}, u32[]{:S(2)}) %collective-permute-start.6) | collective-permute-done | bytes 165920 | tf_op jit(solution)/shard_map/ppermute | solution.py:40
  16.9 0.0 collective-permute-start.7
  16.9 1.5 %second.1 = (bf16[6,72,512]{2,1,0:T(8,128)(2,1)S(1)}, bf16[144,256]{1,0:T(8,128)(2,1)S(1)}, bf16[144,256]{1,0:T(8,128)(2,1)S(1)}) custom-call(bf16[512,1152]{1,0:T(8,128)(2,1)S(1)} %get-tuple-element.31.normed_ref, bf16[2,2,4,72,120]{4,3,2,1,0:T(8,128)(2,1)S(1)} %bitcast.12, bf16[864,1152]{1,0:T(8,128)(2,1)S(1)} %bitcast.10), custom_call_target="tpu_custom_call" | custom-call | flops 1000000000 | bytes 1000000 | tf_op jit(solution)/shard_map/second/pallas_call | solution.py:559
  18.3 0.6 %collective-permute-start.9 = (bf16[144,256]{1,0:T(8,128)(2,1)S(1)}, bf16[144,256]{1,0:T(8,128)(2,1)S(1)}, u32[]{:S(2)}, u32[]{:S(2)}) collective-permute-start(bf16[144,256]{1,0:T(8,128)(2,1)S(1)} %get-tuple-element.40), channel_id=1, source_target_pairs={{0,16},{16,0},{1,17},{17,1},{2,18},{18,2},{3,19},{19,3},{4,20},{20... | collective-permute-start | bytes 221192 | tf_op jit(solution)/shard_map/ppermute | solution.py:35
  18.9 1.5 %collective-permute-start.5 = (bf16[144,256]{1,0:T(8,128)(2,1)S(1)}, bf16[144,256]{1,0:T(8,128)(2,1)S(1)}, u32[]{:S(2)}, u32[]{:S(2)}) collective-permute-start(bf16[144,256]{1,0:T(8,128)(2,1)S(1)} %get-tuple-element.36), channel_id=1, source_target_pairs={{0,16},{16,0},{1,17},{17,1},{2,18},{18,2},{3,19},{19,3},{4,20},{20... | collective-permute-start | bytes 221192 | tf_op jit(solution)/shard_map/ppermute | solution.py:35
  20.4 0.0 copy-done.2
  20.4 0.0 copy-done.5
  20.4 2.3 %attend.1 = (f32[512,1152]{1,0:T(8,128)S(1)}, bf16[128,1152]{1,0:T(8,128)(2,1)S(1)}) custom-call(bf16[6,72,512]{2,1,0:T(8,128)(2,1)S(1)} %get-tuple-element.30.early_ref, bf16[6,72,512]{2,1,0:T(8,128)(2,1)S(1)} %get-tuple-element.32.late_ref, bf16[2,2,4,72,120]{4,3,2,1,0:T(8,128)(2,1)S(1)} %bitcast.13, bf16[288,1152]{1,0:T(8,128)(2,1)S(1)} %copy-done.2, ...), custom_call_target="tpu_custom_call" | custom-call | flops 1000000000 | bytes 8000000 | tf_op jit(solution)/shard_map/attend/pallas_call | solution.py:577
  22.7 0.0 collective-permute-done.2.early_ref
  22.7 0.0 collective-permute-done.4.core_ref
  22.7 0.4 %shard_map.115.residual_ref = f32[256,1152]{1,0:T(8,128)S(1)} custom-call(f32[4,1152]{1,0:T(4,128)S(1)} %get-tuple-element.28.modulation_ref, f32[512,1152]{1,0:T(8,128)S(1)} %get-tuple-element.29.embedded_ref, f32[512,1152]{1,0:T(8,128)S(1)} %get-tuple-element.33.mixed_ref, bf16[144,512]{1,0:T(8,128)(2,1)S(1)} %collective-permute-done.2.early_ref, ...), custom_call_target="tpu_custom_call" | custom-call | flops 100000000 | bytes 1000000 | tf_op jit(solution)/shard_map/pallas_call | solution.py:591
  23.1 0.4 %shard_map.113.residual_ref = f32[256,1152]{1,0:T(8,128)S(1)} custom-call(f32[4,1152]{1,0:T(4,128)S(1)} %get-tuple-element.28.modulation_ref, f32[512,1152]{1,0:T(8,128)S(1)} %get-tuple-element.29.embedded_ref, f32[512,1152]{1,0:T(8,128)S(1)} %get-tuple-element.33.mixed_ref, bf16[144,512]{1,0:T(8,128)(2,1)S(1)} %collective-permute-done.2.early_ref, ...), custom_call_target="tpu_custom_call" | custom-call | flops 100000000 | bytes 1000000 | tf_op jit(solution)/shard_map/pallas_call | solution.py:591
  23.5 0.0 collective-permute-done.7.neighbour_ref
  23.5 0.1 join.1.weight_ref
  23.6 0.0 collective-permute-done.9.late_ref
  23.6 1.0 %shard_map.116 = (f32[32,128]{1,0:T(8,128)S(1)}, f32[32,128]{1,0:T(8,128)S(1)}) custom-call(s32[1]{0:T(128)S(6)} %copy.12.offset_ref, s32[1]{0:T(128)S(6)} %copy.13.blend_ref, f32[4,1152]{1,0:T(4,128)S(1)} %get-tuple-element.28.modulation_ref, f32[256,1152]{1,0:T(8,128)S(1)} %shard_map.115.residual_ref, ...), custom_call_target="tpu_custom_call" | custom-call | flops 500000000 | bytes 2000000 | tf_op jit(solution)/shard_map/pallas_call | solution.py:622
  24.6 2.4 %collective-permute-start.10 = (f32[32,128]{1,0:T(8,128)S(1)}, f32[32,128]{1,0:T(8,128)S(1)}, u32[]{:S(2)}, u32[]{:S(2)}) collective-permute-start(f32[32,128]{1,0:T(8,128)S(1)} %get-tuple-element.42), channel_id=1, source_target_pairs={{1,2},{2,1},{3,4},{4,3},{5,6},{6,5},{7,8},{8,7},{9,10},{10,9},{11,... | collective-permute-start | bytes 49160 | tf_op jit(solution)/shard_map/ppermute | solution.py:31
  27.0 0.0 collective-permute-done.5.late_ref
  27.0 1.0 %shard_map.114 = (f32[32,128]{1,0:T(8,128)S(1)}, f32[32,128]{1,0:T(8,128)S(1)}) custom-call(s32[1]{0:T(128)S(6)} %copy.12.offset_ref, s32[1]{0:T(128)S(6)} %copy.13.blend_ref, f32[4,1152]{1,0:T(4,128)S(1)} %get-tuple-element.28.modulation_ref, f32[256,1152]{1,0:T(8,128)S(1)} %shard_map.113.residual_ref, ...), custom_call_target="tpu_custom_call" | custom-call | flops 500000000 | bytes 2000000 | tf_op jit(solution)/shard_map/pallas_call | solution.py:622
  28.0 0.0 collective-permute-start.8
  28.1 0.1 coefficient.1
  28.2 2.3 %collective-permute-done.10.far_ref = f32[32,128]{1,0:T(8,128)S(1)} collective-permute-done((f32[32,128]{1,0:T(8,128)S(1)}, f32[32,128]{1,0:T(8,128)S(1)}, u32[]{:S(2)}, u32[]{:S(2)}) %collective-permute-start.10) | collective-permute-done | bytes 16416 | tf_op jit(solution)/shard_map/ppermute | solution.py:31
  30.5 0.0 collective-permute-done.8.near_ref
  30.5 0.7 %blend.1 = (f32[4,16,32]{2,1,0:T(8,128)}, f32[4,16,32]{2,1,0:T(8,128)}) custom-call(f32[8,128]{1,0:T(8,128)S(1)} %get-tuple-element.24.plan_ref, f32[32,128]{1,0:T(8,128)S(1)} %get-tuple-element.38.center_ref, f32[32,128]{1,0:T(8,128)S(1)} %collective-permute-done.8.near_ref, f32[32,128]{1,0:T(8,128)S(1)} %get-tuple-element.41.far_center_ref, ...), custom_call_target="tpu_custom_call" | custom-call | tf_op jit(solution)/shard_map/blend/pallas_call | solution.py:641
Async XLA Ops:
  0.6 4.2 %copy-start = (f32[32,4,32]{2,1,0:T(4,128)S(1)}, f32[32,4,32]{2,1,0:T(4,128)}, u32[]{:S(2)}) copy-start(f32[32,4,32]{2,1,0:T(4,128)} %own_ref.1) | copy-start | bytes 49156
  0.6 10.9 %copy-start.4 = (bf16[2,2,120,288]{2,3,1,0:T(8,128)(2,1)S(1)}, bf16[2,2,120,288]{2,3,1,0:T(8,128)(2,1)}, u32[]{:S(2)}) copy-start(bf16[2,2,120,288]{2,3,1,0:T(8,128)(2,1)} %param.11) | copy-start | bytes 829444
  0.7 10.9 %copy-start.1 = (bf16[1152,3,288]{0,2,1:T(8,128)(2,1)S(1)}, bf16[1152,3,288]{0,2,1:T(8,128)(2,1)}, u32[]{:S(2)}) copy-start(bf16[1152,3,288]{0,2,1:T(8,128)(2,1)} %param.13) | copy-start | bytes 5971972
  0.7 10.9 %copy-start.3 = (f32[20,4,1152]{2,1,0:T(4,128)S(1)}, f32[20,4,1152]{2,1,0:T(4,128)}, u32[]{:S(2)}) copy-start(f32[20,4,1152]{2,1,0:T(4,128)} %modulations_ref.1) | copy-start | bytes 1105924
  1.8 9.7 %collective-permute-start.3 = (bf16[72,1152]{1,0:T(8,128)(2,1)S(1)}, bf16[72,1152]{1,0:T(8,128)(2,1)S(1)}, u32[]{:S(2)}, u32[]{:S(2)}) collective-permute-start(bf16[72,1152]{1,0:T(8,128)(2,1)S(1)} %get-tuple-element.35), channel_id=1, source_target_pairs={{0,16},{16,0},{1,17},{17,1},{2,18},{18,2},{3,19},{19,3},{4,20},{20... | collective-permute-start | bytes 497672 | tf_op jit(solution)/shard_map/ppermute | solution.py:35
  4.8 6.7 %collective-permute-start = (f32[32,4,32]{2,1,0:T(4,128)S(1)}, f32[32,4,32]{2,1,0:T(4,128)S(1)}, u32[]{:S(2)}, u32[]{:S(2)}) collective-permute-start(f32[32,4,32]{2,1,0:T(4,128)S(1)} %copy-done), channel_id=1, source_target_pairs={{0,1},{1,0},{2,3},{3,2},{4,5},{5,4},{6,7},{7,6},{8,9},{9,8},{10,11... | collective-permute-start | bytes 49160 | tf_op jit(solution)/shard_map/ppermute | solution.py:31
  4.8 6.7 %collective-permute-start.1 = (f32[32,4,32]{2,1,0:T(4,128)S(1)}, f32[32,4,32]{2,1,0:T(4,128)S(1)}, u32[]{:S(2)}, u32[]{:S(2)}) collective-permute-start(f32[32,4,32]{2,1,0:T(4,128)S(1)} %copy-done), channel_id=1, source_target_pairs={{1,2},{2,1},{3,4},{4,3},{5,6},{6,5},{7,8},{8,7},{9,10},{10,9},{11,... | collective-permute-start | bytes 49160 | tf_op jit(solution)/shard_map/ppermute | solution.py:31
  11.4 5.4 %collective-permute-start.6 = (bf16[72,1152]{1,0:T(8,128)(2,1)S(1)}, bf16[72,1152]{1,0:T(8,128)(2,1)S(1)}, u32[]{:S(2)}, u32[]{:S(2)}) collective-permute-start(bf16[72,1152]{1,0:T(8,128)(2,1)S(1)} %collective-permute-done.3.weight_ref), channel_id=1, source_target_pairs={{0,2},{1,3},{2,0},{3,1},{4,6},{5,7},{6,4},{7,5},{8,10},{9,11},{10,... | collective-permute-start | bytes 497672 | tf_op jit(solution)/shard_map/ppermute | solution.py:40
  14.3 6.1 %copy-start.2 = (bf16[288,1152]{1,0:T(8,128)(2,1)S(1)}, bf16[288,1152]{1,0:T(8,128)(2,1)}, u32[]{:S(2)}) copy-start(bf16[288,1152]{1,0:T(8,128)(2,1)} %weight_ref.1) | copy-start | bytes 1990660
  14.3 6.1 %copy-start.5 = (bf16[1152,16]{0,1:T(8,128)(2,1)S(1)}, bf16[1152,16]{0,1:T(8,128)(2,1)}, u32[]{:S(2)}) copy-start(bf16[1152,16]{0,1:T(8,128)(2,1)} %param.16) | copy-start | bytes 110596
  14.3 8.4 %collective-permute-start.2 = (bf16[144,512]{1,0:T(8,128)(2,1)S(1)}, bf16[144,512]{1,0:T(8,128)(2,1)S(1)}, u32[]{:S(2)}, u32[]{:S(2)}) collective-permute-start(bf16[144,512]{1,0:T(8,128)(2,1)S(1)} %get-tuple-element.34), channel_id=1, source_target_pairs={{0,16},{16,0},{1,17},{17,1},{2,18},{18,2},{3,19},{19,3},{4,20},{20... | collective-permute-start | bytes 442376 | tf_op jit(solution)/shard_map/ppermute | solution.py:35
  15.2 7.5 %collective-permute-start.4 = (bf16[72,1152]{1,0:T(8,128)(2,1)S(1)}, bf16[72,1152]{1,0:T(8,128)(2,1)S(1)}, u32[]{:S(2)}, u32[]{:S(2)}) collective-permute-start(bf16[72,1152]{1,0:T(8,128)(2,1)S(1)} %collective-permute-done.3.weight_ref), channel_id=1, source_target_pairs={{0,1},{1,0},{2,3},{3,2},{4,5},{5,4},{6,7},{7,6},{8,9},{9,8},{10,11... | collective-permute-start | bytes 497672 | tf_op jit(solution)/shard_map/ppermute | solution.py:40
  16.9 6.6 %collective-permute-start.7 = (bf16[72,1152]{1,0:T(8,128)(2,1)S(1)}, bf16[72,1152]{1,0:T(8,128)(2,1)S(1)}, u32[]{:S(2)}, u32[]{:S(2)}) collective-permute-start(bf16[72,1152]{1,0:T(8,128)(2,1)S(1)} %collective-permute-done.6.mine_ref), channel_id=1, source_target_pairs={{0,1},{1,0},{2,3},{3,2},{4,5},{5,4},{6,7},{7,6},{8,9},{9,8},{10,11... | collective-permute-start | bytes 497672 | tf_op jit(solution)/shard_map/ppermute | solution.py:40
  18.3 5.3 %collective-permute-start.9 = (bf16[144,256]{1,0:T(8,128)(2,1)S(1)}, bf16[144,256]{1,0:T(8,128)(2,1)S(1)}, u32[]{:S(2)}, u32[]{:S(2)}) collective-permute-start(bf16[144,256]{1,0:T(8,128)(2,1)S(1)} %get-tuple-element.40), channel_id=1, source_target_pairs={{0,16},{16,0},{1,17},{17,1},{2,18},{18,2},{3,19},{19,3},{4,20},{20... | collective-permute-start | bytes 221192 | tf_op jit(solution)/shard_map/ppermute | solution.py:35
  18.9 8.1 %collective-permute-start.5 = (bf16[144,256]{1,0:T(8,128)(2,1)S(1)}, bf16[144,256]{1,0:T(8,128)(2,1)S(1)}, u32[]{:S(2)}, u32[]{:S(2)}) collective-permute-start(bf16[144,256]{1,0:T(8,128)(2,1)S(1)} %get-tuple-element.36), channel_id=1, source_target_pairs={{0,16},{16,0},{1,17},{17,1},{2,18},{18,2},{3,19},{19,3},{4,20},{20... | collective-permute-start | bytes 221192 | tf_op jit(solution)/shard_map/ppermute | solution.py:35
  24.6 5.9 %collective-permute-start.10 = (f32[32,128]{1,0:T(8,128)S(1)}, f32[32,128]{1,0:T(8,128)S(1)}, u32[]{:S(2)}, u32[]{:S(2)}) collective-permute-start(f32[32,128]{1,0:T(8,128)S(1)} %get-tuple-element.42), channel_id=1, source_target_pairs={{1,2},{2,1},{3,4},{4,3},{5,6},{6,5},{7,8},{8,7},{9,10},{10,9},{11,... | collective-permute-start | bytes 49160 | tf_op jit(solution)/shard_map/ppermute | solution.py:31
  28.0 2.5 %collective-permute-start.8 = (f32[32,128]{1,0:T(8,128)S(1)}, f32[32,128]{1,0:T(8,128)S(1)}, u32[]{:S(2)}, u32[]{:S(2)}) collective-permute-start(f32[32,128]{1,0:T(8,128)S(1)} %get-tuple-element.39), channel_id=1, source_target_pairs={{0,1},{1,0},{2,3},{3,2},{4,5},{5,4},{6,7},{7,6},{8,9},{9,8},{10,11... | collective-permute-start | bytes 49160 | tf_op jit(solution)/shard_map/ppermute | solution.py:31

commit v10 on v9

--- a/solution.py
+++ b/solution.py
@@ -35,9 +35,10 @@
     return lax.ppermute(array, axis, [(0, 1), (1, 0)])
 
 
-def swap_across(array, axis, step):
+def swap_across(array, axis, even_step, odd_step):
     size = lax.axis_size(axis)
-    return lax.ppermute(array, axis, [(place, place ^ step) for place in range(size)])
+    steps = (even_step, odd_step)
+    return lax.ppermute(array, axis, [(place, place ^ steps[place % 2]) for place in range(size)])
 
 
 def layer_norm(values):
@@ -73,7 +74,8 @@
     patch_copy = pltpu.make_async_copy(patch_source, patch_ref, semaphores.at[0])
     patch_copy.start()
     count = quarter_ref.shape[0]
-    first = pl.multiple_of(lax.axis_index("win") % 4 * count, 8)
+    quarter = 2 * first_pair() + lax.axis_index("win") % 2
+    first = pl.multiple_of(quarter * count, 8)
     copy = pltpu.make_async_copy(out_source.at[pl.ds(first, count)], quarter_ref, semaphores.at[1])
     copy.start()
     model_width = patch_ref.shape[1]
@@ -131,7 +133,8 @@
 
 
 def first_pair():
-    return lax.axis_index("win") % 4 // 2
+    place = lax.axis_index("win")
+    return (place // 2 + place // 4) % 2
 
 
 def token_lanes(side, tokens):
@@ -142,6 +145,7 @@
 
 
 def attend(parts, text_ref, first, count, chosen, finished):
+    width = count // len(first)
     branches = text_ref.shape[0]
     feature = (((0,), (0,)), ((), ()))
 
@@ -151,7 +155,7 @@
 
     def score(head):
         queries = jnp.concatenate(
-            [parts[head // 2][head % 2, :, pl.ds(start, count // 2)] for start in first], axis=1
+            [parts[head // 2][head % 2, :, pl.ds(start, width)] for start in first], axis=1
         )
         return [
             lax.dot_general(keys, queries, feature, preferred_element_type=jnp.float32)
@@ -183,8 +187,11 @@
             )
             results.append((lowered * own_mix + text_mix) * inverse)
         return jnp.concatenate(
-            [result[:, : count // 2] for result in results]
-            + [result[:, count // 2 :] for result in results],
+            [
+                result[:, place * width : (place + 1) * width]
+                for place in range(len(first))
+                for result in results
+            ],
             axis=1,
         )
 
@@ -353,15 +360,16 @@
     )
 
 
-def attend_kernel(
-    early_ref, late_ref, text_ref, weight_ref, final_ref, mixed_ref, final_wide_ref
-):
-    final_wide_ref[...] = repeat_pairs(
-        final_ref[...], final_wide_ref.shape[0] // final_ref.shape[0]
-    )
+def attend_kernel(half, early_ref, late_ref, text_ref, weight_ref, final_ref, *outputs):
+    mixed_ref = outputs[0]
+    if half == 1:
+        final_wide_ref = outputs[1]
+        final_wide_ref[...] = repeat_pairs(
+            final_ref[...], final_wide_ref.shape[0] // final_ref.shape[0]
+        )
     tokens = early_ref.shape[2]
-    own_tokens = tokens // 2
-    first = token_lanes(lax.axis_index("cfg"), tokens)
+    own_tokens = tokens // 4
+    first = token_lanes(lax.axis_index("cfg"), tokens)[half : half + 1]
     pairs = []
 
     def finished(place, pair):
@@ -400,7 +408,7 @@
 ):
     count = residual_ref.shape[0] // 2
     lanes = slice(half * 2 * count, (half + 1) * 2 * count)
-    mixed = contract(early_ref[:, lanes], join(weight_ref, core_ref)) + mixed_ref[lanes, :]
+    mixed = contract(early_ref[:, lanes], join(weight_ref, core_ref)) + mixed_ref[...]
     first = pl.multiple_of(half * 2 * count + lax.axis_index("cfg") * count, count)
     embedded = embedded_ref[pl.ds(first, count), :]
     for branch in range(2):
@@ -571,23 +579,28 @@
     )(normed, text, weight)
     late_far = swap(sent_far, "cfg")
     late_near = swap(sent_near, "cfg")
-    cross_weight = swap_across(other_weight, "win", 2)
-    core_weight = swap_across(other_weight, "win", 1)
-    core_cross_weight = swap_across(cross_weight, "win", 1)
-    mixed, final_wide = pl.pallas_call(
-        attend_kernel,
-        out_shape=(
-            shape((branches * own_tokens, model_width), f32),
-            shape((wide, model_width), bf16),
-        ),
-        in_specs=[VM] * 5,
-        out_specs=(VM, VM),
-        name="attend",
-        compiler_params=pltpu.CompilerParams(vmem_limit_bytes=GRANT),
-        cost_estimate=pl.CostEstimate(flops=10**9, bytes_accessed=8 * 10**6, transcendentals=10**6),
-    )(projected, projected_late, text, out_weight, final)
-
-    def partial(half):
+    cross_weight = swap_across(other_weight, "win", 2, 4)
+    core_weight = swap_across(other_weight, "win", 1, 1)
+    core_cross_weight = swap_across(cross_weight, "win", 1, 1)
+
+    def attend_own(half):
+        return pl.pallas_call(
+            functools.partial(attend_kernel, half),
+            out_shape=(shape((own_tokens, model_width), f32), shape((wide, model_width), bf16))[
+                : half + 1
+            ],
+            in_specs=[VM] * 5,
+            out_specs=(VM, VM)[: half + 1],
+            compiler_params=pltpu.CompilerParams(vmem_limit_bytes=GRANT),
+            cost_estimate=pl.CostEstimate(
+                flops=5 * 10**8, bytes_accessed=4 * 10**6, transcendentals=5 * 10**5
+            ),
+        )(projected, projected_late, text, out_weight, final)
+
+    mixed_far, final_wide = attend_own(1)
+    (mixed_near,) = attend_own(0)
+
+    def partial(half, mixed):
         return pl.pallas_call(
             functools.partial(partial_kernel, half),
             out_shape=shape((own_tokens, model_width), f32),
@@ -634,8 +647,8 @@
             ),
         )(offsets, blend_weights, modulate, residual, late, late_rows, final_wide)
 
-    to_far, far_center = finish(1, partial(1), late_far)
-    to_near, center = finish(0, partial(0), late_near)
+    to_far, far_center = finish(1, partial(1, mixed_far), late_far)
+    to_near, center = finish(0, partial(0, mixed_near), late_near)
     from_far = swap_ring(to_far, "win", 1)
     from_near = swap_ring(to_near, "win", 0)
     previous, noise = pl.pallas_call(

time: 31.4 us -> 31.9 us (1.016)
  Pallas kernels: 11.3 us -> 11.8 us
    pallas_call x1 -> x2, Pallas kernels: 2.26 us -> 2.7 us  [attend_own(): pl.pallas_call(functools.partial(attend_kernel, half), out_shape=(shape((...]
    ppermute x4, starting transfers between devices: 5.99 us -> 5.59 us  [swap(): return lax.ppermute(array, axis, [(0, 1), (1, 0)])]
  transfers between devices with their start and end apart: 11 -> 11, of which waited for: 2 -> 3; matrix products, arithmetic and copies ran while one was open for 0% -> 0% of each run, Pallas kernels for 30% -> 31%
where the time goes in v10:
time: 31.9 us; the launch traced here: 31.8 us
  starting transfers between devices  12.9 us (40%)
  Pallas kernels  11.8 us (37%)
  waiting for transfers between devices  4.3 us (13%)
  between operations  2.74 us (9%)
    ppermute x4, starting transfers between devices, swap_ring(): return lax.ppermute(array, axis, pairs)  7.21 us
    ppermute x4, starting transfers between devices, swap(): return lax.ppermute(array, axis, [(0, 1), (1, 0)])  5.59 us
    pallas_call x1, Pallas kernels, on_device(): pl.pallas_call(project_kernel, out_shape=(shape((3 * heads // 2, HEAD_DIM...  2.7 us
    pallas_call x2, Pallas kernels, attend_own(): pl.pallas_call(functools.partial(attend_kernel, half), out_shape=(shape((...  2.7 us
    ppermute x4, waiting for transfers between devices, swap_ring(): return lax.ppermute(array, axis, pairs)  2.56 us
    pallas_call x2, Pallas kernels, finish(): pl.pallas_call(functools.partial(finish_kernel, half), out_shape=tuple((s...  2.09 us
    ppermute x3, waiting for transfers between devices, swap_across(): lax.ppermute(array, axis, [(place, place ^ steps[place % 2]) for place in...  1.73 us
    pallas_call x1, Pallas kernels, on_device(): pl.pallas_call(second_kernel, out_shape=(shape((3 * heads // 2, HEAD_DIM,...  1.45 us
  transfers between devices with their start and end apart: 11, of which 3 were waited for; matrix products, arithmetic and copies ran while one was open for 0% of the time, Pallas kernels for 31%

profile of v10, /device:TPU:0, one launch (start us, length us, event | category | flops | bytes accessed | tf_op | source)
XLA Modules:
  0.0 31.8 jit_solution(3861627110449883114)
XLA Ops:
  0.6 0.0 copy-start.3
  0.6 0.0 copy-start.1
  0.7 0.0 copy-start.4
  0.7 0.0 copy-start.5
  0.7 1.1 %prepare.1 = (f32[16,640]{1,0:T(8,128)S(1)}, f32[32,640]{1,0:T(8,128)S(1)}, bf16[256,1152]{1,0:T(8,128)(2,1)S(1)}, bf16[72,1152]{1,0:T(8,128)(2,1)S(1)}) custom-call(bf16[16,1152]{1,0:T(8,128)(2,1)} %patch_source.1, bf16[288,1152]{1,0:T(8,128)(2,1)} %weight_ref.3), custom_call_target="tpu_custom_call" | custom-call | flops 2000000000 | bytes 1000000 | tf_op jit(solution)/shard_map/prepare/pallas_call | solution.py:531
  1.8 3.1 %collective-permute-start.3 = (bf16[72,1152]{1,0:T(8,128)(2,1)S(1)}, bf16[72,1152]{1,0:T(8,128)(2,1)S(1)}, u32[]{:S(2)}, u32[]{:S(2)}) collective-permute-start(bf16[72,1152]{1,0:T(8,128)(2,1)S(1)} %get-tuple-element.34), channel_id=1, source_target_pairs={{0,16},{16,0},{1,17},{17,1},{2,18},{18,2},{3,19},{19,3},{4,20},{20... | collective-permute-start | bytes 497672 | tf_op jit(solution)/shard_map/ppermute | solution.py:35
  4.8 0.0 copy-done.3
  4.8 0.0 collective-permute-start
  4.8 4.6 %collective-permute-start.1 = (f32[32,4,32]{2,1,0:T(4,128)S(1)}, f32[32,4,32]{2,1,0:T(4,128)S(1)}, u32[]{:S(2)}, u32[]{:S(2)}) collective-permute-start(f32[32,4,32]{2,1,0:T(4,128)S(1)} %copy-done.3), channel_id=1, source_target_pairs={{1,2},{2,1},{3,4},{4,3},{5,6},{6,5},{7,8},{8,7},{9,10},{10,9},{11,... | collective-permute-start | bytes 49160 | tf_op jit(solution)/shard_map/ppermute | solution.py:31
  11.4 0.0 collective-permute-done.3.weight_ref
  11.4 0.1 collective-permute-start.6
  11.5 0.0 collective-permute-done.near_ref
  11.5 0.4 %collective-permute-done.1.far_ref = f32[32,4,32]{2,1,0:T(4,128)S(1)} collective-permute-done((f32[32,4,32]{2,1,0:T(4,128)S(1)}, f32[32,4,32]{2,1,0:T(4,128)S(1)}, u32[]{:S(2)}, u32[]{:S(2)}) %collective-permute-start.1) | collective-permute-done | bytes 16416 | tf_op jit(solution)/shard_map/ppermute | solution.py:31
  12.0 0.0 copy-done.1
  12.0 0.0 copy-done.4
  12.0 0.0 copy-done.5
  12.0 2.7 %project.1 = (bf16[6,72,512]{2,1,0:T(8,128)(2,1)S(1)}, bf16[512,1152]{1,0:T(8,128)(2,1)S(1)}, f32[4,1152]{1,0:T(4,128)S(1)}, f32[512,1152]{1,0:T(8,128)S(1)}, bf16[144,512]{1,0:T(8,128)(2,1)S(1)}) custom-call(s32[1]{0:T(128)S(6)} %copy.14.step_ref, s32[1]{0:T(128)S(6)} %copy.12.offset_ref, f32[20,4,1152]{2,1,0:T(4,128)S(1)} %copy-done.5, ...), custom_call_target="tpu_custom_call" | custom-call | flops 2000000000 | bytes 8000000 | tf_op jit(solution)/shard_map/project/pallas_call | solution.py:547
  14.7 0.4 %collective-permute-start.2 = (bf16[144,512]{1,0:T(8,128)(2,1)S(1)}, bf16[144,512]{1,0:T(8,128)(2,1)S(1)}, u32[]{:S(2)}, u32[]{:S(2)}) collective-permute-start(bf16[144,512]{1,0:T(8,128)(2,1)S(1)} %get-tuple-element.33), channel_id=1, source_target_pairs={{0,16},{16,0},{1,17},{17,1},{2,18},{18,2},{3,19},{19,3},{4,20},{20... | collective-permute-start | bytes 442376 | tf_op jit(solution)/shard_map/ppermute | solution.py:35
  15.1 0.0 collective-permute-start.4
  15.1 1.7 %collective-permute-done.6.mine_ref = bf16[72,1152]{1,0:T(8,128)(2,1)S(1)} collective-permute-done((bf16[72,1152]{1,0:T(8,128)(2,1)S(1)}, bf16[72,1152]{1,0:T(8,128)(2,1)S(1)}, u32[]{:S(2)}, u32[]{:S(2)}) %collective-permute-start.6) | collective-permute-done | bytes 165920 | tf_op jit(solution)/shard_map/ppermute | solution.py:41
  16.9 0.0 collective-permute-start.7
  16.9 0.0 copy-start
  16.9 0.0 copy-start.2
  16.9 1.5 %second.1 = (bf16[6,72,512]{2,1,0:T(8,128)(2,1)S(1)}, bf16[144,256]{1,0:T(8,128)(2,1)S(1)}, bf16[144,256]{1,0:T(8,128)(2,1)S(1)}) custom-call(bf16[512,1152]{1,0:T(8,128)(2,1)S(1)} %get-tuple-element.31.normed_ref, bf16[2,2,4,72,120]{4,3,2,1,0:T(8,128)(2,1)S(1)} %bitcast.10, bf16[864,1152]{1,0:T(8,128)(2,1)S(1)} %bitcast.16), custom_call_target="tpu_custom_call" | custom-call | flops 1000000000 | bytes 1000000 | tf_op jit(solution)/shard_map/second/pallas_call | solution.py:567
  18.3 0.6 %collective-permute-start.9 = (bf16[144,256]{1,0:T(8,128)(2,1)S(1)}, bf16[144,256]{1,0:T(8,128)(2,1)S(1)}, u32[]{:S(2)}, u32[]{:S(2)}) collective-permute-start(bf16[144,256]{1,0:T(8,128)(2,1)S(1)} %get-tuple-element.40), channel_id=1, source_target_pairs={{0,16},{16,0},{1,17},{17,1},{2,18},{18,2},{3,19},{19,3},{4,20},{20... | collective-permute-start | bytes 221192 | tf_op jit(solution)/shard_map/ppermute | solution.py:35
  18.9 1.5 %collective-permute-start.5 = (bf16[144,256]{1,0:T(8,128)(2,1)S(1)}, bf16[144,256]{1,0:T(8,128)(2,1)S(1)}, u32[]{:S(2)}, u32[]{:S(2)}) collective-permute-start(bf16[144,256]{1,0:T(8,128)(2,1)S(1)} %get-tuple-element.35), channel_id=1, source_target_pairs={{0,16},{16,0},{1,17},{17,1},{2,18},{18,2},{3,19},{19,3},{4,20},{20... | collective-permute-start | bytes 221192 | tf_op jit(solution)/shard_map/ppermute | solution.py:35
  20.4 0.0 copy-done
  20.4 0.0 copy-done.2
  20.4 1.4 %shard_map.115 = (f32[256,1152]{1,0:T(8,128)S(1)}, bf16[128,1152]{1,0:T(8,128)(2,1)S(1)}) custom-call(bf16[6,72,512]{2,1,0:T(8,128)(2,1)S(1)} %get-tuple-element.30.early_ref, bf16[6,72,512]{2,1,0:T(8,128)(2,1)S(1)} %get-tuple-element.32.late_ref, bf16[2,2,4,72,120]{4,3,2,1,0:T(8,128)(2,1)S(1)} %bitcast.11, bf16[288,1152]{1,0:T(8,128)(2,1)S(1)} %copy-done, ...), custom_call_target="tpu_custom_call" | custom-call | flops 500000000 | bytes 4000000 | tf_op jit(solution)/shard_map/pallas_call | solution.py:587
  21.8 1.3 %shard_map.113.mixed_ref = f32[256,1152]{1,0:T(8,128)S(1)} custom-call(bf16[6,72,512]{2,1,0:T(8,128)(2,1)S(1)} %get-tuple-element.30.early_ref, bf16[6,72,512]{2,1,0:T(8,128)(2,1)S(1)} %get-tuple-element.32.late_ref, bf16[2,2,4,72,120]{4,3,2,1,0:T(8,128)(2,1)S(1)} %bitcast.12, bf16[288,1152]{1,0:T(8,128)(2,1)S(1)} %copy-done, bf16[16,1152]{1,0:T(8,128)(2,1)S(1)} %bitcast.14), custom_call_target="tpu_custom_call" | custom-call | flops 500000000 | bytes 4000000 | tf_op jit(solution)/shard_map/pallas_call | solution.py:587
  23.1 0.0 collective-permute-done.2.early_ref
  23.1 0.0 collective-permute-done.4.core_ref
  23.2 0.4 %shard_map.117.residual_ref = f32[256,1152]{1,0:T(8,128)S(1)} custom-call(f32[4,1152]{1,0:T(4,128)S(1)} %get-tuple-element.28.modulation_ref, f32[512,1152]{1,0:T(8,128)S(1)} %get-tuple-element.29.embedded_ref, f32[256,1152]{1,0:T(8,128)S(1)} %get-tuple-element.39.mixed_ref, bf16[144,512]{1,0:T(8,128)(2,1)S(1)} %collective-permute-done.2.early_ref, ...), custom_call_target="tpu_custom_call" | custom-call | flops 100000000 | bytes 1000000 | tf_op jit(solution)/shard_map/pallas_call | solution.py:604
  23.6 0.4 %shard_map.114.residual_ref = f32[256,1152]{1,0:T(8,128)S(1)} custom-call(f32[4,1152]{1,0:T(4,128)S(1)} %get-tuple-element.28.modulation_ref, f32[512,1152]{1,0:T(8,128)S(1)} %get-tuple-element.29.embedded_ref, f32[256,1152]{1,0:T(8,128)S(1)} %shard_map.113.mixed_ref, bf16[144,512]{1,0:T(8,128)(2,1)S(1)} %collective-permute-done.2.early_ref, ...), custom_call_target="tpu_custom_call" | custom-call | flops 100000000 | bytes 1000000 | tf_op jit(solution)/shard_map/pallas_call | solution.py:604
  24.0 0.0 collective-permute-done.7.neighbour_ref
  24.0 0.1 join.1.weight_ref
  24.1 0.0 collective-permute-done.9.late_ref
  24.1 1.0 %shard_map.118 = (f32[32,128]{1,0:T(8,128)S(1)}, f32[32,128]{1,0:T(8,128)S(1)}) custom-call(s32[1]{0:T(128)S(6)} %copy.12.offset_ref, s32[1]{0:T(128)S(6)} %copy.13.blend_ref, f32[4,1152]{1,0:T(4,128)S(1)} %get-tuple-element.28.modulation_ref, f32[256,1152]{1,0:T(8,128)S(1)} %shard_map.117.residual_ref, ...), custom_call_target="tpu_custom_call" | custom-call | flops 500000000 | bytes 2000000 | tf_op jit(solution)/shard_map/pallas_call | solution.py:635
  25.1 2.6 %collective-permute-start.10 = (f32[32,128]{1,0:T(8,128)S(1)}, f32[32,128]{1,0:T(8,128)S(1)}, u32[]{:S(2)}, u32[]{:S(2)}) collective-permute-start(f32[32,128]{1,0:T(8,128)S(1)} %get-tuple-element.42), channel_id=1, source_target_pairs={{1,2},{2,1},{3,4},{4,3},{5,6},{6,5},{7,8},{8,7},{9,10},{10,9},{11,... | collective-permute-start | bytes 49160 | tf_op jit(solution)/shard_map/ppermute | solution.py:31
  27.7 0.0 collective-permute-done.5.late_ref
  27.7 1.0 %shard_map.116 = (f32[32,128]{1,0:T(8,128)S(1)}, f32[32,128]{1,0:T(8,128)S(1)}) custom-call(s32[1]{0:T(128)S(6)} %copy.12.offset_ref, s32[1]{0:T(128)S(6)} %copy.13.blend_ref, f32[4,1152]{1,0:T(4,128)S(1)} %get-tuple-element.28.modulation_ref, f32[256,1152]{1,0:T(8,128)S(1)} %shard_map.114.residual_ref, ...), custom_call_target="tpu_custom_call" | custom-call | flops 500000000 | bytes 2000000 | tf_op jit(solution)/shard_map/pallas_call | solution.py:635
  28.7 0.0 collective-permute-start.8
  28.8 0.1 coefficient.1
  28.9 2.1 %collective-permute-done.10.far_ref = f32[32,128]{1,0:T(8,128)S(1)} collective-permute-done((f32[32,128]{1,0:T(8,128)S(1)}, f32[32,128]{1,0:T(8,128)S(1)}, u32[]{:S(2)}, u32[]{:S(2)}) %collective-permute-start.10) | collective-permute-done | bytes 16416 | tf_op jit(solution)/shard_map/ppermute | solution.py:31
  31.0 0.0 collective-permute-done.8.near_ref
  31.0 0.7 %blend.1 = (f32[4,16,32]{2,1,0:T(8,128)}, f32[4,16,32]{2,1,0:T(8,128)}) custom-call(f32[8,128]{1,0:T(8,128)S(1)} %get-tuple-element.24.plan_ref, f32[32,128]{1,0:T(8,128)S(1)} %get-tuple-element.37.center_ref, f32[32,128]{1,0:T(8,128)S(1)} %collective-permute-done.8.near_ref, f32[32,128]{1,0:T(8,128)S(1)} %get-tuple-element.41.far_center_ref, ...), custom_call_target="tpu_custom_call" | custom-call | tf_op jit(solution)/shard_map/blend/pallas_call | solution.py:654
Async XLA Ops:
  0.6 4.2 %copy-start.3 = (f32[32,4,32]{2,1,0:T(4,128)S(1)}, f32[32,4,32]{2,1,0:T(4,128)}, u32[]{:S(2)}) copy-start(f32[32,4,32]{2,1,0:T(4,128)} %own_ref.1) | copy-start | bytes 49156
  0.6 11.3 %copy-start.1 = (bf16[2,2,120,288]{2,3,1,0:T(8,128)(2,1)S(1)}, bf16[2,2,120,288]{2,3,1,0:T(8,128)(2,1)}, u32[]{:S(2)}) copy-start(bf16[2,2,120,288]{2,3,1,0:T(8,128)(2,1)} %param.11) | copy-start | bytes 829444
  0.7 11.3 %copy-start.4 = (bf16[1152,3,288]{0,2,1:T(8,128)(2,1)S(1)}, bf16[1152,3,288]{0,2,1:T(8,128)(2,1)}, u32[]{:S(2)}) copy-start(bf16[1152,3,288]{0,2,1:T(8,128)(2,1)} %param.13) | copy-start | bytes 5971972
  0.7 11.3 %copy-start.5 = (f32[20,4,1152]{2,1,0:T(4,128)S(1)}, f32[20,4,1152]{2,1,0:T(4,128)}, u32[]{:S(2)}) copy-start(f32[20,4,1152]{2,1,0:T(4,128)} %modulations_ref.1) | copy-start | bytes 1105924
  1.8 9.7 %collective-permute-start.3 = (bf16[72,1152]{1,0:T(8,128)(2,1)S(1)}, bf16[72,1152]{1,0:T(8,128)(2,1)S(1)}, u32[]{:S(2)}, u32[]{:S(2)}) collective-permute-start(bf16[72,1152]{1,0:T(8,128)(2,1)S(1)} %get-tuple-element.34), channel_id=1, source_target_pairs={{0,16},{16,0},{1,17},{17,1},{2,18},{18,2},{3,19},{19,3},{4,20},{20... | collective-permute-start | bytes 497672 | tf_op jit(solution)/shard_map/ppermute | solution.py:35
  4.8 6.7 %collective-permute-start = (f32[32,4,32]{2,1,0:T(4,128)S(1)}, f32[32,4,32]{2,1,0:T(4,128)S(1)}, u32[]{:S(2)}, u32[]{:S(2)}) collective-permute-start(f32[32,4,32]{2,1,0:T(4,128)S(1)} %copy-done.3), channel_id=1, source_target_pairs={{0,1},{1,0},{2,3},{3,2},{4,5},{5,4},{6,7},{7,6},{8,9},{9,8},{10,11... | collective-permute-start | bytes 49160 | tf_op jit(solution)/shard_map/ppermute | solution.py:31
  4.8 7.1 %collective-permute-start.1 = (f32[32,4,32]{2,1,0:T(4,128)S(1)}, f32[32,4,32]{2,1,0:T(4,128)S(1)}, u32[]{:S(2)}, u32[]{:S(2)}) collective-permute-start(f32[32,4,32]{2,1,0:T(4,128)S(1)} %copy-done.3), channel_id=1, source_target_pairs={{1,2},{2,1},{3,4},{4,3},{5,6},{6,5},{7,8},{8,7},{9,10},{10,9},{11,... | collective-permute-start | bytes 49160 | tf_op jit(solution)/shard_map/ppermute | solution.py:31
  11.4 5.4 %collective-permute-start.6 = (bf16[72,1152]{1,0:T(8,128)(2,1)S(1)}, bf16[72,1152]{1,0:T(8,128)(2,1)S(1)}, u32[]{:S(2)}, u32[]{:S(2)}) collective-permute-start(bf16[72,1152]{1,0:T(8,128)(2,1)S(1)} %collective-permute-done.3.weight_ref), channel_id=1, source_target_pairs={{0,2},{1,5},{2,0},{3,7},{4,6},{5,1},{6,4},{7,3},{8,10},{9,13},{10,... | collective-permute-start | bytes 497672 | tf_op jit(solution)/shard_map/ppermute | solution.py:41
  14.7 8.4 %collective-permute-start.2 = (bf16[144,512]{1,0:T(8,128)(2,1)S(1)}, bf16[144,512]{1,0:T(8,128)(2,1)S(1)}, u32[]{:S(2)}, u32[]{:S(2)}) collective-permute-start(bf16[144,512]{1,0:T(8,128)(2,1)S(1)} %get-tuple-element.33), channel_id=1, source_target_pairs={{0,16},{16,0},{1,17},{17,1},{2,18},{18,2},{3,19},{19,3},{4,20},{20... | collective-permute-start | bytes 442376 | tf_op jit(solution)/shard_map/ppermute | solution.py:35
  15.1 8.0 %collective-permute-start.4 = (bf16[72,1152]{1,0:T(8,128)(2,1)S(1)}, bf16[72,1152]{1,0:T(8,128)(2,1)S(1)}, u32[]{:S(2)}, u32[]{:S(2)}) collective-permute-start(bf16[72,1152]{1,0:T(8,128)(2,1)S(1)} %collective-permute-done.3.weight_ref), channel_id=1, source_target_pairs={{0,1},{1,0},{2,3},{3,2},{4,5},{5,4},{6,7},{7,6},{8,9},{9,8},{10,11... | collective-permute-start | bytes 497672 | tf_op jit(solution)/shard_map/ppermute | solution.py:41
  16.9 7.1 %collective-permute-start.7 = (bf16[72,1152]{1,0:T(8,128)(2,1)S(1)}, bf16[72,1152]{1,0:T(8,128)(2,1)S(1)}, u32[]{:S(2)}, u32[]{:S(2)}) collective-permute-start(bf16[72,1152]{1,0:T(8,128)(2,1)S(1)} %collective-permute-done.6.mine_ref), channel_id=1, source_target_pairs={{0,1},{1,0},{2,3},{3,2},{4,5},{5,4},{6,7},{7,6},{8,9},{9,8},{10,11... | collective-permute-start | bytes 497672 | tf_op jit(solution)/shard_map/ppermute | solution.py:41
  16.9 3.6 %copy-start = (bf16[288,1152]{1,0:T(8,128)(2,1)S(1)}, bf16[288,1152]{1,0:T(8,128)(2,1)}, u32[]{:S(2)}) copy-start(bf16[288,1152]{1,0:T(8,128)(2,1)} %weight_ref.3) | copy-start | bytes 1990660
  16.9 3.6 %copy-start.2 = (bf16[1152,16]{0,1:T(8,128)(2,1)S(1)}, bf16[1152,16]{0,1:T(8,128)(2,1)}, u32[]{:S(2)}) copy-start(bf16[1152,16]{0,1:T(8,128)(2,1)} %param.16) | copy-start | bytes 110596
  18.3 5.8 %collective-permute-start.9 = (bf16[144,256]{1,0:T(8,128)(2,1)S(1)}, bf16[144,256]{1,0:T(8,128)(2,1)S(1)}, u32[]{:S(2)}, u32[]{:S(2)}) collective-permute-start(bf16[144,256]{1,0:T(8,128)(2,1)S(1)} %get-tuple-element.40), channel_id=1, source_target_pairs={{0,16},{16,0},{1,17},{17,1},{2,18},{18,2},{3,19},{19,3},{4,20},{20... | collective-permute-start | bytes 221192 | tf_op jit(solution)/shard_map/ppermute | solution.py:35
  18.9 8.8 %collective-permute-start.5 = (bf16[144,256]{1,0:T(8,128)(2,1)S(1)}, bf16[144,256]{1,0:T(8,128)(2,1)S(1)}, u32[]{:S(2)}, u32[]{:S(2)}) collective-permute-start(bf16[144,256]{1,0:T(8,128)(2,1)S(1)} %get-tuple-element.35), channel_id=1, source_target_pairs={{0,16},{16,0},{1,17},{17,1},{2,18},{18,2},{3,19},{19,3},{4,20},{20... | collective-permute-start | bytes 221192 | tf_op jit(solution)/shard_map/ppermute | solution.py:35
  25.1 5.9 %collective-permute-start.10 = (f32[32,128]{1,0:T(8,128)S(1)}, f32[32,128]{1,0:T(8,128)S(1)}, u32[]{:S(2)}, u32[]{:S(2)}) collective-permute-start(f32[32,128]{1,0:T(8,128)S(1)} %get-tuple-element.42), channel_id=1, source_target_pairs={{1,2},{2,1},{3,4},{4,3},{5,6},{6,5},{7,8},{8,7},{9,10},{10,9},{11,... | collective-permute-start | bytes 49160 | tf_op jit(solution)/shard_map/ppermute | solution.py:31
  28.7 2.3 %collective-permute-start.8 = (f32[32,128]{1,0:T(8,128)S(1)}, f32[32,128]{1,0:T(8,128)S(1)}, u32[]{:S(2)}, u32[]{:S(2)}) collective-permute-start(f32[32,128]{1,0:T(8,128)S(1)} %get-tuple-element.38), channel_id=1, source_target_pairs={{0,1},{1,0},{2,3},{3,2},{4,5},{5,4},{6,7},{7,6},{8,9},{9,8},{10,11... | collective-permute-start | bytes 49160 | tf_op jit(solution)/shard_map/ppermute | solution.py:31

commit v11 on v10

--- a/solution.py
+++ b/solution.py
@@ -476,6 +476,38 @@
     )
 
 
+def near_kernel(
+    offset_ref,
+    blend_ref,
+    modulation_ref,
+    embedded_ref,
+    first_ref,
+    second_ref,
+    text_ref,
+    own_weight_ref,
+    early_ref,
+    weight_ref,
+    core_ref,
+    late_ref,
+    late_weight_ref,
+    final_ref,
+    sent_ref,
+    center_ref,
+    mixed_ref,
+    residual_ref,
+    buffer_ref,
+    final_norm_ref,
+):
+    attend_kernel(0, first_ref, second_ref, text_ref, own_weight_ref, None, mixed_ref)
+    partial_kernel(
+        0, modulation_ref, embedded_ref, mixed_ref, early_ref, weight_ref, core_ref, residual_ref
+    )
+    finish_kernel(
+        0, offset_ref, blend_ref, modulation_ref, residual_ref, late_ref, late_weight_ref,
+        final_ref, sent_ref, center_ref, buffer_ref, final_norm_ref,
+    )
+
+
 def blend_kernel(
     plan_ref, center_ref, near_ref, far_center_ref, far_ref, rows_ref, previous_ref, noise_ref
 ):
@@ -598,7 +630,6 @@
         )(projected, projected_late, text, out_weight, final)
 
     mixed_far, final_wide = attend_own(1)
-    (mixed_near,) = attend_own(0)
 
     def partial(half, mixed):
         return pl.pallas_call(
@@ -648,7 +679,26 @@
         )(offsets, blend_weights, modulate, residual, late, late_rows, final_wide)
 
     to_far, far_center = finish(1, partial(1, mixed_far), late_far)
-    to_near, center = finish(0, partial(0, mixed_near), late_near)
+    to_near, center = pl.pallas_call(
+        near_kernel,
+        out_shape=tuple(shape((slab_cols, wide), f32) for _ in range(2)),
+        in_specs=[SM, SM] + [VM] * 12,
+        out_specs=(VM, VM),
+        scratch_shapes=[
+            pltpu.VMEM((own_tokens, model_width), f32),
+            pltpu.VMEM((own_tokens, model_width), f32),
+            pltpu.VMEM((3 * slab_cols + 8, wide), f32),
+            pltpu.VMEM((own_tokens, model_width), bf16),
+        ],
+        name="near",
+        compiler_params=pltpu.CompilerParams(vmem_limit_bytes=GRANT),
+        cost_estimate=pl.CostEstimate(
+            flops=10**9, bytes_accessed=6 * 10**6, transcendentals=5 * 10**5
+        ),
+    )(
+        offsets, blend_weights, modulate, embedded, projected, projected_late, text, out_weight,
+        early, other_weight, core_weight, late_near, late_rows, final_wide,
+    )
     from_far = swap_ring(to_far, "win", 1)
     from_near = swap_ring(to_near, "win", 0)
     previous, noise = pl.pallas_call(

time: 31.9 us -> 33 us (1.034)
  starting transfers between devices: 12.9 us -> 13.7 us
  waiting for transfers between devices: 4.3 us -> 5.07 us
  Pallas kernels: 11.8 us -> 11.3 us
    pallas_call x0 -> x1, Pallas kernels: none -> 2.29 us  [on_device(): pl.pallas_call(near_kernel, out_shape=tuple((shape((slab_cols, wide), f32...]
    pallas_call x2 -> x1, Pallas kernels: 2.7 us -> 1.36 us  [attend_own(): pl.pallas_call(functools.partial(attend_kernel, half), out_shape=(shape((...]
    pallas_call x2 -> x1, Pallas kernels: 2.09 us -> 0.99 us  [finish(): pl.pallas_call(functools.partial(finish_kernel, half), out_shape=tuple((s...]
    ppermute x4, waiting for transfers between devices: 2.56 us -> 3.49 us  [swap_ring(): return lax.ppermute(array, axis, pairs)]
    ppermute x4, starting transfers between devices: 7.21 us -> 7.9 us  [swap_ring(): return lax.ppermute(array, axis, pairs)]
    ppermute x3, waiting for transfers between devices: 1.73 us -> 1.07 us  [swap_across(): lax.ppermute(array, axis, [(place, place ^ steps[place % 2]) for place in...]
    ppermute x4, waiting for transfers between devices: 0.01 us -> 0.51 us  [swap(): return lax.ppermute(array, axis, [(0, 1), (1, 0)])]
    pallas_call x2 -> x1, Pallas kernels: 0.8 us -> 0.39 us  [partial(): pl.pallas_call(functools.partial(partial_kernel, half), out_shape=shape((...]
  transfers between devices with their start and end apart: 11 -> 11, of which waited for: 3 -> 4; matrix products, arithmetic and copies ran while one was open for 0% -> 0% of each run, Pallas kernels for 31% -> 29%
where the time goes in v11:
time: 33 us; the launch traced here: 32.8 us
  starting transfers between devices  13.7 us (42%)
  Pallas kernels  11.3 us (34%)
  waiting for transfers between devices  5.07 us (15%)
  between operations  2.74 us (8%)
    ppermute x4, starting transfers between devices, swap_ring(): return lax.ppermute(array, axis, pairs)  7.9 us
    ppermute x4, starting transfers between devices, swap(): return lax.ppermute(array, axis, [(0, 1), (1, 0)])  5.67 us
    ppermute x4, waiting for transfers between devices, swap_ring(): return lax.ppermute(array, axis, pairs)  3.49 us
    pallas_call x1, Pallas kernels, on_device(): pl.pallas_call(project_kernel, out_shape=(shape((3 * heads // 2, HEAD_DIM...  2.7 us
    pallas_call x1, Pallas kernels, on_device(): pl.pallas_call(near_kernel, out_shape=tuple((shape((slab_cols, wide), f32...  2.29 us
    pallas_call x1, Pallas kernels, on_device(): pl.pallas_call(second_kernel, out_shape=(shape((3 * heads // 2, HEAD_DIM,...  1.46 us
    pallas_call x1, Pallas kernels, attend_own(): pl.pallas_call(functools.partial(attend_kernel, half), out_shape=(shape((...  1.36 us
    pallas_call x1, Pallas kernels, on_device(): pl.pallas_call(functools.partial(prepare_kernel, row_count), out_shape=(s...  1.1 us
  transfers between devices with their start and end apart: 11, of which 4 were waited for; matrix products, arithmetic and copies ran while one was open for 0% of the time, Pallas kernels for 29%

profile of v11, /device:TPU:0, one launch (start us, length us, event | category | flops | bytes accessed | tf_op | source)
XLA Modules:
  0.0 32.8 jit_solution(6839141294973570910)
XLA Ops:
  0.6 0.0 copy-start.2
  0.6 0.0 copy-start.4
  0.7 0.0 copy-start.5
  0.7 0.0 copy-start.1
  0.7 1.1 %prepare.1 = (f32[16,640]{1,0:T(8,128)S(1)}, f32[32,640]{1,0:T(8,128)S(1)}, bf16[256,1152]{1,0:T(8,128)(2,1)S(1)}, bf16[72,1152]{1,0:T(8,128)(2,1)S(1)}) custom-call(bf16[16,1152]{1,0:T(8,128)(2,1)} %patch_source.1, bf16[288,1152]{1,0:T(8,128)(2,1)} %own_weight_ref.1), custom_call_target="tpu_custom_call" | custom-call | flops 2000000000 | bytes 1000000 | tf_op jit(solution)/shard_map/prepare/pallas_call | solution.py:563
  1.8 3.1 %collective-permute-start.3 = (bf16[72,1152]{1,0:T(8,128)(2,1)S(1)}, bf16[72,1152]{1,0:T(8,128)(2,1)S(1)}, u32[]{:S(2)}, u32[]{:S(2)}) collective-permute-start(bf16[72,1152]{1,0:T(8,128)(2,1)S(1)} %get-tuple-element.34), channel_id=1, source_target_pairs={{0,16},{16,0},{1,17},{17,1},{2,18},{18,2},{3,19},{19,3},{4,20},{20... | collective-permute-start | bytes 497672 | tf_op jit(solution)/shard_map/ppermute | solution.py:35
  4.8 0.0 copy-done.2
  4.8 0.0 collective-permute-start
  4.8 4.6 %collective-permute-start.1 = (f32[32,4,32]{2,1,0:T(4,128)S(1)}, f32[32,4,32]{2,1,0:T(4,128)S(1)}, u32[]{:S(2)}, u32[]{:S(2)}) collective-permute-start(f32[32,4,32]{2,1,0:T(4,128)S(1)} %copy-done.2), channel_id=1, source_target_pairs={{1,2},{2,1},{3,4},{4,3},{5,6},{6,5},{7,8},{8,7},{9,10},{10,9},{11,... | collective-permute-start | bytes 49160 | tf_op jit(solution)/shard_map/ppermute | solution.py:31
  10.8 0.0 collective-permute-done.3.weight_ref
  10.8 0.1 collective-permute-start.6
  10.9 0.1 collective-permute-start.4
  11.0 0.0 collective-permute-done.near_ref
  11.0 1.0 %collective-permute-done.1.far_ref = f32[32,4,32]{2,1,0:T(4,128)S(1)} collective-permute-done((f32[32,4,32]{2,1,0:T(4,128)S(1)}, f32[32,4,32]{2,1,0:T(4,128)S(1)}, u32[]{:S(2)}, u32[]{:S(2)}) %collective-permute-start.1) | collective-permute-done | bytes 16416 | tf_op jit(solution)/shard_map/ppermute | solution.py:31
  12.0 0.0 copy-done.4
  12.0 0.0 copy-done.5
  12.0 0.0 copy-done.1
  12.0 2.7 %project.1 = (bf16[6,72,512]{2,1,0:T(8,128)(2,1)S(1)}, bf16[512,1152]{1,0:T(8,128)(2,1)S(1)}, f32[4,1152]{1,0:T(4,128)S(1)}, f32[512,1152]{1,0:T(8,128)S(1)}, bf16[144,512]{1,0:T(8,128)(2,1)S(1)}) custom-call(s32[1]{0:T(128)S(6)} %copy.14.step_ref, s32[1]{0:T(128)S(6)} %copy.12.offset_ref, f32[20,4,1152]{2,1,0:T(4,128)S(1)} %copy-done.5, ...), custom_call_target="tpu_custom_call" | custom-call | flops 2000000000 | bytes 8000000 | tf_op jit(solution)/shard_map/project/pallas_call | solution.py:579
  14.7 0.5 %collective-permute-start.2 = (bf16[144,512]{1,0:T(8,128)(2,1)S(1)}, bf16[144,512]{1,0:T(8,128)(2,1)S(1)}, u32[]{:S(2)}, u32[]{:S(2)}) collective-permute-start(bf16[144,512]{1,0:T(8,128)(2,1)S(1)} %get-tuple-element.33), channel_id=1, source_target_pairs={{0,16},{16,0},{1,17},{17,1},{2,18},{18,2},{3,19},{19,3},{4,20},{20... | collective-permute-start | bytes 442376 | tf_op jit(solution)/shard_map/ppermute | solution.py:35
  15.1 1.1 %collective-permute-done.6.mine_ref = bf16[72,1152]{1,0:T(8,128)(2,1)S(1)} collective-permute-done((bf16[72,1152]{1,0:T(8,128)(2,1)S(1)}, bf16[72,1152]{1,0:T(8,128)(2,1)S(1)}, u32[]{:S(2)}, u32[]{:S(2)}) %collective-permute-start.6) | collective-permute-done | bytes 165920 | tf_op jit(solution)/shard_map/ppermute | solution.py:41
  16.2 0.0 collective-permute-start.7
  16.2 0.0 copy-start
  16.2 0.0 copy-start.3
  16.2 1.5 %second.1 = (bf16[6,72,512]{2,1,0:T(8,128)(2,1)S(1)}, bf16[144,256]{1,0:T(8,128)(2,1)S(1)}, bf16[144,256]{1,0:T(8,128)(2,1)S(1)}) custom-call(bf16[512,1152]{1,0:T(8,128)(2,1)S(1)} %get-tuple-element.31.normed_ref, bf16[2,2,4,72,120]{4,3,2,1,0:T(8,128)(2,1)S(1)} %bitcast.10, bf16[864,1152]{1,0:T(8,128)(2,1)S(1)} %bitcast.15), custom_call_target="tpu_custom_call" | custom-call | flops 1000000000 | bytes 1000000 | tf_op jit(solution)/shard_map/second/pallas_call | solution.py:599
  17.7 0.7 %collective-permute-start.5 = (bf16[144,256]{1,0:T(8,128)(2,1)S(1)}, bf16[144,256]{1,0:T(8,128)(2,1)S(1)}, u32[]{:S(2)}, u32[]{:S(2)}) collective-permute-start(bf16[144,256]{1,0:T(8,128)(2,1)S(1)} %get-tuple-element.35), channel_id=1, source_target_pairs={{0,16},{16,0},{1,17},{17,1},{2,18},{18,2},{3,19},{19,3},{4,20},{20... | collective-permute-start | bytes 221192 | tf_op jit(solution)/shard_map/ppermute | solution.py:35
  19.0 1.5 %collective-permute-start.9 = (bf16[144,256]{1,0:T(8,128)(2,1)S(1)}, bf16[144,256]{1,0:T(8,128)(2,1)S(1)}, u32[]{:S(2)}, u32[]{:S(2)}) collective-permute-start(bf16[144,256]{1,0:T(8,128)(2,1)S(1)} %get-tuple-element.40), channel_id=1, source_target_pairs={{0,16},{16,0},{1,17},{17,1},{2,18},{18,2},{3,19},{19,3},{4,20},{20... | collective-permute-start | bytes 221192 | tf_op jit(solution)/shard_map/ppermute | solution.py:35
  20.5 0.0 copy-done
  20.5 0.0 copy-done.3
  20.5 1.4 %shard_map.113 = (f32[256,1152]{1,0:T(8,128)S(1)}, bf16[128,1152]{1,0:T(8,128)(2,1)S(1)}) custom-call(bf16[6,72,512]{2,1,0:T(8,128)(2,1)S(1)} %get-tuple-element.30.early_ref.first_ref, bf16[6,72,512]{2,1,0:T(8,128)(2,1)S(1)} %get-tuple-element.32.late_ref.second_ref, bf16[2,2,4,72,120]{4,3,2,1,0:T(8,128)(2,1)S(1)} %bitcast.11, ...), custom_call_target="tpu_custom_call" | custom-call | flops 500000000 | bytes 4000000 | tf_op jit(solution)/shard_map/pallas_call | solution.py:619
  21.9 0.0 collective-permute-done.2.early_ref
  21.9 0.0 collective-permute-done.4.core_ref
  21.9 0.4 %shard_map.114.residual_ref = f32[256,1152]{1,0:T(8,128)S(1)} custom-call(f32[4,1152]{1,0:T(4,128)S(1)} %get-tuple-element.28.modulation_ref, f32[512,1152]{1,0:T(8,128)S(1)} %get-tuple-element.29.embedded_ref, f32[256,1152]{1,0:T(8,128)S(1)} %get-tuple-element.39.mixed_ref, bf16[144,512]{1,0:T(8,128)(2,1)S(1)} %collective-permute-done.2.early_ref, ...), custom_call_target="tpu_custom_call" | custom-call | flops 100000000 | bytes 1000000 | tf_op jit(solution)/shard_map/pallas_call | solution.py:635
  22.3 0.0 collective-permute-done.7.neighbour_ref
  22.3 0.1 join.1.late_weight_ref.weight_ref
  22.4 0.5 %collective-permute-done.5.late_ref = bf16[144,256]{1,0:T(8,128)(2,1)S(1)} collective-permute-done((bf16[144,256]{1,0:T(8,128)(2,1)S(1)}, bf16[144,256]{1,0:T(8,128)(2,1)S(1)}, u32[]{:S(2)}, u32[]{:S(2)}) %collective-permute-start.5) | collective-permute-done | bytes 73760 | tf_op jit(solution)/shard_map/ppermute | solution.py:35
  22.9 2.3 %near.1 = (f32[32,128]{1,0:T(8,128)S(1)}, f32[32,128]{1,0:T(8,128)S(1)}) custom-call(s32[1]{0:T(128)S(6)} %copy.12.offset_ref, s32[1]{0:T(128)S(6)} %copy.13.blend_ref, f32[4,1152]{1,0:T(4,128)S(1)} %get-tuple-element.28.modulation_ref, f32[512,1152]{1,0:T(8,128)S(1)} %get-tuple-element.29.embedded_ref, ...), custom_call_target="tpu_custom_call" | custom-call | flops 1000000000 | bytes 6000000 | tf_op jit(solution)/shard_map/near/pallas_call | solution.py:682
  25.2 0.0 collective-permute-start.8
  25.2 0.0 collective-permute-done.9.late_ref
  25.2 1.0 %shard_map.115 = (f32[32,128]{1,0:T(8,128)S(1)}, f32[32,128]{1,0:T(8,128)S(1)}) custom-call(s32[1]{0:T(128)S(6)} %copy.12.offset_ref, s32[1]{0:T(128)S(6)} %copy.13.blend_ref, f32[4,1152]{1,0:T(4,128)S(1)} %get-tuple-element.28.modulation_ref, f32[256,1152]{1,0:T(8,128)S(1)} %shard_map.114.residual_ref, ...), custom_call_target="tpu_custom_call" | custom-call | flops 500000000 | bytes 2000000 | tf_op jit(solution)/shard_map/pallas_call | solution.py:666
  26.2 3.2 %collective-permute-start.10 = (f32[32,128]{1,0:T(8,128)S(1)}, f32[32,128]{1,0:T(8,128)S(1)}, u32[]{:S(2)}, u32[]{:S(2)}) collective-permute-start(f32[32,128]{1,0:T(8,128)S(1)} %get-tuple-element.42), channel_id=1, source_target_pairs={{1,2},{2,1},{3,4},{4,3},{5,6},{6,5},{7,8},{8,7},{9,10},{10,9},{11,... | collective-permute-start | bytes 49160 | tf_op jit(solution)/shard_map/ppermute | solution.py:31
  29.4 0.1 coefficient.1
  29.6 0.0 collective-permute-done.8.near_ref
  29.6 2.5 %collective-permute-done.10.far_ref = f32[32,128]{1,0:T(8,128)S(1)} collective-permute-done((f32[32,128]{1,0:T(8,128)S(1)}, f32[32,128]{1,0:T(8,128)S(1)}, u32[]{:S(2)}, u32[]{:S(2)}) %collective-permute-start.10) | collective-permute-done | bytes 16416 | tf_op jit(solution)/shard_map/ppermute | solution.py:31
  32.1 0.7 %blend.1 = (f32[4,16,32]{2,1,0:T(8,128)}, f32[4,16,32]{2,1,0:T(8,128)}) custom-call(f32[8,128]{1,0:T(8,128)S(1)} %get-tuple-element.24.plan_ref, f32[32,128]{1,0:T(8,128)S(1)} %get-tuple-element.37.center_ref, f32[32,128]{1,0:T(8,128)S(1)} %collective-permute-done.8.near_ref, f32[32,128]{1,0:T(8,128)S(1)} %get-tuple-element.41.far_center_ref, ...), custom_call_target="tpu_custom_call" | custom-call | tf_op jit(solution)/shard_map/blend/pallas_call | solution.py:704
Async XLA Ops:
  0.6 4.2 %copy-start.2 = (f32[32,4,32]{2,1,0:T(4,128)S(1)}, f32[32,4,32]{2,1,0:T(4,128)}, u32[]{:S(2)}) copy-start(f32[32,4,32]{2,1,0:T(4,128)} %own_ref.1) | copy-start | bytes 49156
  0.6 11.3 %copy-start.4 = (bf16[1152,3,288]{0,2,1:T(8,128)(2,1)S(1)}, bf16[1152,3,288]{0,2,1:T(8,128)(2,1)}, u32[]{:S(2)}) copy-start(bf16[1152,3,288]{0,2,1:T(8,128)(2,1)} %param.13) | copy-start | bytes 5971972
  0.7 11.3 %copy-start.5 = (f32[20,4,1152]{2,1,0:T(4,128)S(1)}, f32[20,4,1152]{2,1,0:T(4,128)}, u32[]{:S(2)}) copy-start(f32[20,4,1152]{2,1,0:T(4,128)} %modulations_ref.1) | copy-start | bytes 1105924
  0.7 11.3 %copy-start.1 = (bf16[2,2,120,288]{2,3,1,0:T(8,128)(2,1)S(1)}, bf16[2,2,120,288]{2,3,1,0:T(8,128)(2,1)}, u32[]{:S(2)}) copy-start(bf16[2,2,120,288]{2,3,1,0:T(8,128)(2,1)} %param.11) | copy-start | bytes 829444
  1.8 9.0 %collective-permute-start.3 = (bf16[72,1152]{1,0:T(8,128)(2,1)S(1)}, bf16[72,1152]{1,0:T(8,128)(2,1)S(1)}, u32[]{:S(2)}, u32[]{:S(2)}) collective-permute-start(bf16[72,1152]{1,0:T(8,128)(2,1)S(1)} %get-tuple-element.34), channel_id=1, source_target_pairs={{0,16},{16,0},{1,17},{17,1},{2,18},{18,2},{3,19},{19,3},{4,20},{20... | collective-permute-start | bytes 497672 | tf_op jit(solution)/shard_map/ppermute | solution.py:35
  4.8 6.1 %collective-permute-start = (f32[32,4,32]{2,1,0:T(4,128)S(1)}, f32[32,4,32]{2,1,0:T(4,128)S(1)}, u32[]{:S(2)}, u32[]{:S(2)}) collective-permute-start(f32[32,4,32]{2,1,0:T(4,128)S(1)} %copy-done.2), channel_id=1, source_target_pairs={{0,1},{1,0},{2,3},{3,2},{4,5},{5,4},{6,7},{7,6},{8,9},{9,8},{10,11... | collective-permute-start | bytes 49160 | tf_op jit(solution)/shard_map/ppermute | solution.py:31
  4.8 7.1 %collective-permute-start.1 = (f32[32,4,32]{2,1,0:T(4,128)S(1)}, f32[32,4,32]{2,1,0:T(4,128)S(1)}, u32[]{:S(2)}, u32[]{:S(2)}) collective-permute-start(f32[32,4,32]{2,1,0:T(4,128)S(1)} %copy-done.2), channel_id=1, source_target_pairs={{1,2},{2,1},{3,4},{4,3},{5,6},{6,5},{7,8},{8,7},{9,10},{10,9},{11,... | collective-permute-start | bytes 49160 | tf_op jit(solution)/shard_map/ppermute | solution.py:31
  10.8 5.4 %collective-permute-start.6 = (bf16[72,1152]{1,0:T(8,128)(2,1)S(1)}, bf16[72,1152]{1,0:T(8,128)(2,1)S(1)}, u32[]{:S(2)}, u32[]{:S(2)}) collective-permute-start(bf16[72,1152]{1,0:T(8,128)(2,1)S(1)} %collective-permute-done.3.weight_ref), channel_id=1, source_target_pairs={{0,2},{1,5},{2,0},{3,7},{4,6},{5,1},{6,4},{7,3},{8,10},{9,13},{10,... | collective-permute-start | bytes 497672 | tf_op jit(solution)/shard_map/ppermute | solution.py:41
  10.9 11.0 %collective-permute-start.4 = (bf16[72,1152]{1,0:T(8,128)(2,1)S(1)}, bf16[72,1152]{1,0:T(8,128)(2,1)S(1)}, u32[]{:S(2)}, u32[]{:S(2)}) collective-permute-start(bf16[72,1152]{1,0:T(8,128)(2,1)S(1)} %collective-permute-done.3.weight_ref), channel_id=1, source_target_pairs={{0,1},{1,0},{2,3},{3,2},{4,5},{5,4},{6,7},{7,6},{8,9},{9,8},{10,11... | collective-permute-start | bytes 497672 | tf_op jit(solution)/shard_map/ppermute | solution.py:41
  14.7 7.2 %collective-permute-start.2 = (bf16[144,512]{1,0:T(8,128)(2,1)S(1)}, bf16[144,512]{1,0:T(8,128)(2,1)S(1)}, u32[]{:S(2)}, u32[]{:S(2)}) collective-permute-start(bf16[144,512]{1,0:T(8,128)(2,1)S(1)} %get-tuple-element.33), channel_id=1, source_target_pairs={{0,16},{16,0},{1,17},{17,1},{2,18},{18,2},{3,19},{19,3},{4,20},{20... | collective-permute-start | bytes 442376 | tf_op jit(solution)/shard_map/ppermute | solution.py:35
  16.2 6.1 %collective-permute-start.7 = (bf16[72,1152]{1,0:T(8,128)(2,1)S(1)}, bf16[72,1152]{1,0:T(8,128)(2,1)S(1)}, u32[]{:S(2)}, u32[]{:S(2)}) collective-permute-start(bf16[72,1152]{1,0:T(8,128)(2,1)S(1)} %collective-permute-done.6.mine_ref), channel_id=1, source_target_pairs={{0,1},{1,0},{2,3},{3,2},{4,5},{5,4},{6,7},{7,6},{8,9},{9,8},{10,11... | collective-permute-start | bytes 497672 | tf_op jit(solution)/shard_map/ppermute | solution.py:41
  16.2 4.3 %copy-start = (bf16[288,1152]{1,0:T(8,128)(2,1)S(1)}, bf16[288,1152]{1,0:T(8,128)(2,1)}, u32[]{:S(2)}) copy-start(bf16[288,1152]{1,0:T(8,128)(2,1)} %own_weight_ref.1) | copy-start | bytes 1990660
  16.2 4.3 %copy-start.3 = (bf16[1152,16]{0,1:T(8,128)(2,1)S(1)}, bf16[1152,16]{0,1:T(8,128)(2,1)}, u32[]{:S(2)}) copy-start(bf16[1152,16]{0,1:T(8,128)(2,1)} %param.16) | copy-start | bytes 110596
  17.7 5.2 %collective-permute-start.5 = (bf16[144,256]{1,0:T(8,128)(2,1)S(1)}, bf16[144,256]{1,0:T(8,128)(2,1)S(1)}, u32[]{:S(2)}, u32[]{:S(2)}) collective-permute-start(bf16[144,256]{1,0:T(8,128)(2,1)S(1)} %get-tuple-element.35), channel_id=1, source_target_pairs={{0,16},{16,0},{1,17},{17,1},{2,18},{18,2},{3,19},{19,3},{4,20},{20... | collective-permute-start | bytes 221192 | tf_op jit(solution)/shard_map/ppermute | solution.py:35
  19.0 6.2 %collective-permute-start.9 = (bf16[144,256]{1,0:T(8,128)(2,1)S(1)}, bf16[144,256]{1,0:T(8,128)(2,1)S(1)}, u32[]{:S(2)}, u32[]{:S(2)}) collective-permute-start(bf16[144,256]{1,0:T(8,128)(2,1)S(1)} %get-tuple-element.40), channel_id=1, source_target_pairs={{0,16},{16,0},{1,17},{17,1},{2,18},{18,2},{3,19},{19,3},{4,20},{20... | collective-permute-start | bytes 221192 | tf_op jit(solution)/shard_map/ppermute | solution.py:35
  25.2 4.4 %collective-permute-start.8 = (f32[32,128]{1,0:T(8,128)S(1)}, f32[32,128]{1,0:T(8,128)S(1)}, u32[]{:S(2)}, u32[]{:S(2)}) collective-permute-start(f32[32,128]{1,0:T(8,128)S(1)} %get-tuple-element.38), channel_id=1, source_target_pairs={{0,1},{1,0},{2,3},{3,2},{4,5},{5,4},{6,7},{7,6},{8,9},{9,8},{10,11... | collective-permute-start | bytes 49160 | tf_op jit(solution)/shard_map/ppermute | solution.py:31
  26.2 5.9 %collective-permute-start.10 = (f32[32,128]{1,0:T(8,128)S(1)}, f32[32,128]{1,0:T(8,128)S(1)}, u32[]{:S(2)}, u32[]{:S(2)}) collective-permute-start(f32[32,128]{1,0:T(8,128)S(1)} %get-tuple-element.42), channel_id=1, source_target_pairs={{1,2},{2,1},{3,4},{4,3},{5,6},{6,5},{7,8},{8,7},{9,10},{10,9},{11,... | collective-permute-start | bytes 49160 | tf_op jit(solution)/shard_map/ppermute | solution.py:31

commit v12 on v11

--- a/solution.py
+++ b/solution.py
@@ -399,10 +399,6 @@
     return jnp.concatenate([first, second], axis=0).astype(jnp.bfloat16)
 
 
-def join_kernel(mine_ref, neighbour_ref, joined_ref):
-    joined_ref[...] = join(mine_ref, neighbour_ref)
-
-
 def partial_kernel(
     half, modulation_ref, embedded_ref, mixed_ref, early_ref, weight_ref, core_ref, residual_ref
 ):
@@ -423,7 +419,8 @@
     modulation_ref,
     residual_ref,
     late_ref,
-    weight_ref,
+    cross_ref,
+    core_cross_ref,
     final_ref,
     sent_ref,
     center_ref,
@@ -435,7 +432,7 @@
     count = residual_ref.shape[0] // 2
     couples = count // half_pairs
     gate, gain = modulation_ref[2:3, :], 1.0 + modulation_ref[3:4, :]
-    other = contract(late_ref[...], weight_ref[...])
+    other = contract(late_ref[...], join(cross_ref, core_cross_ref))
     predicted = []
     block = slab_cols
     for branch in range(2):
@@ -489,7 +486,8 @@
     weight_ref,
     core_ref,
     late_ref,
-    late_weight_ref,
+    cross_ref,
+    core_cross_ref,
     final_ref,
     sent_ref,
     center_ref,
@@ -503,8 +501,8 @@
         0, modulation_ref, embedded_ref, mixed_ref, early_ref, weight_ref, core_ref, residual_ref
     )
     finish_kernel(
-        0, offset_ref, blend_ref, modulation_ref, residual_ref, late_ref, late_weight_ref,
-        final_ref, sent_ref, center_ref, buffer_ref, final_norm_ref,
+        0, offset_ref, blend_ref, modulation_ref, residual_ref, late_ref, cross_ref,
+        core_cross_ref, final_ref, sent_ref, center_ref, buffer_ref, final_norm_ref,
     )
 
 
@@ -653,20 +651,12 @@
         compiler_params=pltpu.CompilerParams(vmem_limit_bytes=GRANT),
         cost_estimate=pl.CostEstimate(flops=10**5, bytes_accessed=10**5, transcendentals=10**4),
     )(step_index, latent)
-    late_rows = pl.pallas_call(
-        join_kernel,
-        out_shape=shape((half_attn // 2, model_width), bf16),
-        in_specs=[VM] * 2,
-        out_specs=VM,
-        name="join",
-        compiler_params=pltpu.CompilerParams(vmem_limit_bytes=GRANT),
-    )(cross_weight, core_cross_weight)
 
     def finish(half, residual, late):
         return pl.pallas_call(
             functools.partial(finish_kernel, half),
             out_shape=tuple(shape((slab_cols, wide), f32) for _ in range(2)),
-            in_specs=[SM, SM] + [VM] * 5,
+            in_specs=[SM, SM] + [VM] * 6,
             out_specs=(VM, VM),
             scratch_shapes=[
                 pltpu.VMEM((3 * slab_cols + 8, wide), f32),
@@ -676,13 +666,13 @@
             cost_estimate=pl.CostEstimate(
                 flops=5 * 10**8, bytes_accessed=2 * 10**6, transcendentals=10**3
             ),
-        )(offsets, blend_weights, modulate, residual, late, late_rows, final_wide)
+        )(offsets, blend_weights, modulate, residual, late, cross_weight, core_cross_weight, final_wide)
 
     to_far, far_center = finish(1, partial(1, mixed_far), late_far)
     to_near, center = pl.pallas_call(
         near_kernel,
         out_shape=tuple(shape((slab_cols, wide), f32) for _ in range(2)),
-        in_specs=[SM, SM] + [VM] * 12,
+        in_specs=[SM, SM] + [VM] * 13,
         out_specs=(VM, VM),
         scratch_shapes=[
             pltpu.VMEM((own_tokens, model_width), f32),
@@ -697,7 +687,7 @@
         ),
     )(
         offsets, blend_weights, modulate, embedded, projected, projected_late, text, out_weight,
-        early, other_weight, core_weight, late_near, late_rows, final_wide,
+        early, other_weight, core_weight, late_near, cross_weight, core_cross_weight, final_wide,
     )
     from_far = swap_ring(to_far, "win", 1)
     from_near = swap_ring(to_near, "win", 0)

time: 33 us -> 33.1 us (level)
  no operation moved by 1% of the time
where the time goes in v12:
time: 33.1 us; the launch traced here: 32.9 us
  starting transfers between devices  13.6 us (41%)
  Pallas kernels  11.3 us (34%)
  waiting for transfers between devices  5.33 us (16%)
  between operations  2.73 us (8%)
    ppermute x4, starting transfers between devices, swap_ring(): return lax.ppermute(array, axis, pairs)  7.78 us
    ppermute x4, starting transfers between devices, swap(): return lax.ppermute(array, axis, [(0, 1), (1, 0)])  5.66 us
    ppermute x4, waiting for transfers between devices, swap_ring(): return lax.ppermute(array, axis, pairs)  3.62 us
    pallas_call x1, Pallas kernels, on_device(): pl.pallas_call(project_kernel, out_shape=(shape((3 * heads // 2, HEAD_DIM...  2.67 us
    pallas_call x1, Pallas kernels, on_device(): pl.pallas_call(near_kernel, out_shape=tuple((shape((slab_cols, wide), f32...  2.36 us
    pallas_call x1, Pallas kernels, on_device(): pl.pallas_call(second_kernel, out_shape=(shape((3 * heads // 2, HEAD_DIM,...  1.46 us
    pallas_call x1, Pallas kernels, attend_own(): pl.pallas_call(functools.partial(attend_kernel, half), out_shape=(shape((...  1.36 us
    ppermute x3, waiting for transfers between devices, swap_across(): lax.ppermute(array, axis, [(place, place ^ steps[place % 2]) for place in...  1.11 us
  transfers between devices with their start and end apart: 11, of which 4 were waited for; matrix products, arithmetic and copies ran while one was open for 0% of the time, Pallas kernels for 29%

profile of v12, /device:TPU:0, one launch (start us, length us, event | category | flops | bytes accessed | tf_op | source)
XLA Modules:
  0.0 32.9 jit_solution(18028806623605986266)
XLA Ops:
  0.6 0.0 copy-start.2
  0.6 0.0 copy-start.4
  0.7 0.0 copy-start.5
  0.7 0.0 copy-start.1
  0.7 1.1 %prepare.1 = (f32[16,640]{1,0:T(8,128)S(1)}, f32[32,640]{1,0:T(8,128)S(1)}, bf16[256,1152]{1,0:T(8,128)(2,1)S(1)}, bf16[72,1152]{1,0:T(8,128)(2,1)S(1)}) custom-call(bf16[16,1152]{1,0:T(8,128)(2,1)} %patch_source.1, bf16[288,1152]{1,0:T(8,128)(2,1)} %own_weight_ref.1), custom_call_target="tpu_custom_call" | custom-call | flops 2000000000 | bytes 1000000 | tf_op jit(solution)/shard_map/prepare/pallas_call | solution.py:561
  1.8 3.1 %collective-permute-start.3 = (bf16[72,1152]{1,0:T(8,128)(2,1)S(1)}, bf16[72,1152]{1,0:T(8,128)(2,1)S(1)}, u32[]{:S(2)}, u32[]{:S(2)}) collective-permute-start(bf16[72,1152]{1,0:T(8,128)(2,1)S(1)} %get-tuple-element.34), channel_id=1, source_target_pairs={{0,16},{16,0},{1,17},{17,1},{2,18},{18,2},{3,19},{19,3},{4,20},{20... | collective-permute-start | bytes 497672 | tf_op jit(solution)/shard_map/ppermute | solution.py:35
  4.8 0.0 copy-done.2
  4.8 0.0 collective-permute-start
  4.8 4.6 %collective-permute-start.1 = (f32[32,4,32]{2,1,0:T(4,128)S(1)}, f32[32,4,32]{2,1,0:T(4,128)S(1)}, u32[]{:S(2)}, u32[]{:S(2)}) collective-permute-start(f32[32,4,32]{2,1,0:T(4,128)S(1)} %copy-done.2), channel_id=1, source_target_pairs={{1,2},{2,1},{3,4},{4,3},{5,6},{6,5},{7,8},{8,7},{9,10},{10,9},{11,... | collective-permute-start | bytes 49160 | tf_op jit(solution)/shard_map/ppermute | solution.py:31
  10.8 0.0 collective-permute-done.3.weight_ref
  10.8 0.1 collective-permute-start.6
  10.9 0.1 collective-permute-start.4
  11.0 0.0 collective-permute-done.near_ref
  11.0 1.0 %collective-permute-done.1.far_ref = f32[32,4,32]{2,1,0:T(4,128)S(1)} collective-permute-done((f32[32,4,32]{2,1,0:T(4,128)S(1)}, f32[32,4,32]{2,1,0:T(4,128)S(1)}, u32[]{:S(2)}, u32[]{:S(2)}) %collective-permute-start.1) | collective-permute-done | bytes 16416 | tf_op jit(solution)/shard_map/ppermute | solution.py:31
  12.0 0.0 copy-done.4
  12.0 0.0 copy-done.5
  12.0 0.0 copy-done.1
  12.0 2.7 %project.1 = (bf16[6,72,512]{2,1,0:T(8,128)(2,1)S(1)}, bf16[512,1152]{1,0:T(8,128)(2,1)S(1)}, f32[4,1152]{1,0:T(4,128)S(1)}, f32[512,1152]{1,0:T(8,128)S(1)}, bf16[144,512]{1,0:T(8,128)(2,1)S(1)}) custom-call(s32[1]{0:T(128)S(6)} %copy.14.step_ref, s32[1]{0:T(128)S(6)} %copy.12.offset_ref, f32[20,4,1152]{2,1,0:T(4,128)S(1)} %copy-done.5, ...), custom_call_target="tpu_custom_call" | custom-call | flops 2000000000 | bytes 8000000 | tf_op jit(solution)/shard_map/project/pallas_call | solution.py:577
  14.7 0.4 %collective-permute-start.2 = (bf16[144,512]{1,0:T(8,128)(2,1)S(1)}, bf16[144,512]{1,0:T(8,128)(2,1)S(1)}, u32[]{:S(2)}, u32[]{:S(2)}) collective-permute-start(bf16[144,512]{1,0:T(8,128)(2,1)S(1)} %get-tuple-element.33), channel_id=1, source_target_pairs={{0,16},{16,0},{1,17},{17,1},{2,18},{18,2},{3,19},{19,3},{4,20},{20... | collective-permute-start | bytes 442376 | tf_op jit(solution)/shard_map/ppermute | solution.py:35
  15.1 1.1 %collective-permute-done.6.cross_ref = bf16[72,1152]{1,0:T(8,128)(2,1)S(1)} collective-permute-done((bf16[72,1152]{1,0:T(8,128)(2,1)S(1)}, bf16[72,1152]{1,0:T(8,128)(2,1)S(1)}, u32[]{:S(2)}, u32[]{:S(2)}) %collective-permute-start.6) | collective-permute-done | bytes 165920 | tf_op jit(solution)/shard_map/ppermute | solution.py:41
  16.2 0.0 collective-permute-start.7
  16.2 0.0 copy-start
  16.2 0.0 copy-start.3
  16.2 1.5 %second.1 = (bf16[6,72,512]{2,1,0:T(8,128)(2,1)S(1)}, bf16[144,256]{1,0:T(8,128)(2,1)S(1)}, bf16[144,256]{1,0:T(8,128)(2,1)S(1)}) custom-call(bf16[512,1152]{1,0:T(8,128)(2,1)S(1)} %get-tuple-element.31.normed_ref, bf16[2,2,4,72,120]{4,3,2,1,0:T(8,128)(2,1)S(1)} %bitcast.10, bf16[864,1152]{1,0:T(8,128)(2,1)S(1)} %bitcast.15), custom_call_target="tpu_custom_call" | custom-call | flops 1000000000 | bytes 1000000 | tf_op jit(solution)/shard_map/second/pallas_call | solution.py:597
  17.7 0.6 %collective-permute-start.5 = (bf16[144,256]{1,0:T(8,128)(2,1)S(1)}, bf16[144,256]{1,0:T(8,128)(2,1)S(1)}, u32[]{:S(2)}, u32[]{:S(2)}) collective-permute-start(bf16[144,256]{1,0:T(8,128)(2,1)S(1)} %get-tuple-element.35), channel_id=1, source_target_pairs={{0,16},{16,0},{1,17},{17,1},{2,18},{18,2},{3,19},{19,3},{4,20},{20... | collective-permute-start | bytes 221192 | tf_op jit(solution)/shard_map/ppermute | solution.py:35
  19.0 1.5 %collective-permute-start.9 = (bf16[144,256]{1,0:T(8,128)(2,1)S(1)}, bf16[144,256]{1,0:T(8,128)(2,1)S(1)}, u32[]{:S(2)}, u32[]{:S(2)}) collective-permute-start(bf16[144,256]{1,0:T(8,128)(2,1)S(1)} %get-tuple-element.40), channel_id=1, source_target_pairs={{0,16},{16,0},{1,17},{17,1},{2,18},{18,2},{3,19},{19,3},{4,20},{20... | collective-permute-start | bytes 221192 | tf_op jit(solution)/shard_map/ppermute | solution.py:35
  20.5 0.0 copy-done
  20.5 0.0 copy-done.3
  20.5 1.4 %shard_map.113 = (f32[256,1152]{1,0:T(8,128)S(1)}, bf16[128,1152]{1,0:T(8,128)(2,1)S(1)}) custom-call(bf16[6,72,512]{2,1,0:T(8,128)(2,1)S(1)} %get-tuple-element.30.early_ref.first_ref, bf16[6,72,512]{2,1,0:T(8,128)(2,1)S(1)} %get-tuple-element.32.late_ref.second_ref, bf16[2,2,4,72,120]{4,3,2,1,0:T(8,128)(2,1)S(1)} %bitcast.11, ...), custom_call_target="tpu_custom_call" | custom-call | flops 500000000 | bytes 4000000 | tf_op jit(solution)/shard_map/pallas_call | solution.py:617
  21.9 0.0 collective-permute-done.2.early_ref
  21.9 0.0 collective-permute-done.4.core_ref
  21.9 0.4 %shard_map.114.residual_ref = f32[256,1152]{1,0:T(8,128)S(1)} custom-call(f32[4,1152]{1,0:T(4,128)S(1)} %get-tuple-element.28.modulation_ref, f32[512,1152]{1,0:T(8,128)S(1)} %get-tuple-element.29.embedded_ref, f32[256,1152]{1,0:T(8,128)S(1)} %get-tuple-element.39.mixed_ref, bf16[144,512]{1,0:T(8,128)(2,1)S(1)} %collective-permute-done.2.early_ref, ...), custom_call_target="tpu_custom_call" | custom-call | flops 100000000 | bytes 1000000 | tf_op jit(solution)/shard_map/pallas_call | solution.py:633
  22.3 0.6 %collective-permute-done.5.late_ref = bf16[144,256]{1,0:T(8,128)(2,1)S(1)} collective-permute-done((bf16[144,256]{1,0:T(8,128)(2,1)S(1)}, bf16[144,256]{1,0:T(8,128)(2,1)S(1)}, u32[]{:S(2)}, u32[]{:S(2)}) %collective-permute-start.5) | collective-permute-done | bytes 73760 | tf_op jit(solution)/shard_map/ppermute | solution.py:35
  22.9 0.0 collective-permute-done.7.core_cross_ref
  22.9 2.4 %near.1 = (f32[32,128]{1,0:T(8,128)S(1)}, f32[32,128]{1,0:T(8,128)S(1)}) custom-call(s32[1]{0:T(128)S(6)} %copy.12.offset_ref, s32[1]{0:T(128)S(6)} %copy.13.blend_ref, f32[4,1152]{1,0:T(4,128)S(1)} %get-tuple-element.28.modulation_ref, f32[512,1152]{1,0:T(8,128)S(1)} %get-tuple-element.29.embedded_ref, ...), custom_call_target="tpu_custom_call" | custom-call | flops 1000000000 | bytes 6000000 | tf_op jit(solution)/shard_map/near/pallas_call | solution.py:672
  25.2 0.0 collective-permute-start.8
  25.3 0.0 collective-permute-done.9.late_ref
  25.3 1.1 %shard_map.115 = (f32[32,128]{1,0:T(8,128)S(1)}, f32[32,128]{1,0:T(8,128)S(1)}) custom-call(s32[1]{0:T(128)S(6)} %copy.12.offset_ref, s32[1]{0:T(128)S(6)} %copy.13.blend_ref, f32[4,1152]{1,0:T(4,128)S(1)} %get-tuple-element.28.modulation_ref, f32[256,1152]{1,0:T(8,128)S(1)} %shard_map.114.residual_ref, ...), custom_call_target="tpu_custom_call" | custom-call | flops 500000000 | bytes 2000000 | tf_op jit(solution)/shard_map/pallas_call | solution.py:656
  26.3 3.1 %collective-permute-start.10 = (f32[32,128]{1,0:T(8,128)S(1)}, f32[32,128]{1,0:T(8,128)S(1)}, u32[]{:S(2)}, u32[]{:S(2)}) collective-permute-start(f32[32,128]{1,0:T(8,128)S(1)} %get-tuple-element.42), channel_id=1, source_target_pairs={{1,2},{2,1},{3,4},{4,3},{5,6},{6,5},{7,8},{8,7},{9,10},{10,9},{11,... | collective-permute-start | bytes 49160 | tf_op jit(solution)/shard_map/ppermute | solution.py:31
  29.4 0.1 coefficient.1
  29.6 0.0 collective-permute-done.8.near_ref
  29.6 2.6 %collective-permute-done.10.far_ref = f32[32,128]{1,0:T(8,128)S(1)} collective-permute-done((f32[32,128]{1,0:T(8,128)S(1)}, f32[32,128]{1,0:T(8,128)S(1)}, u32[]{:S(2)}, u32[]{:S(2)}) %collective-permute-start.10) | collective-permute-done | bytes 16416 | tf_op jit(solution)/shard_map/ppermute | solution.py:31
  32.2 0.7 %blend.1 = (f32[4,16,32]{2,1,0:T(8,128)}, f32[4,16,32]{2,1,0:T(8,128)}) custom-call(f32[8,128]{1,0:T(8,128)S(1)} %get-tuple-element.24.plan_ref, f32[32,128]{1,0:T(8,128)S(1)} %get-tuple-element.37.center_ref, f32[32,128]{1,0:T(8,128)S(1)} %collective-permute-done.8.near_ref, f32[32,128]{1,0:T(8,128)S(1)} %get-tuple-element.41.far_center_ref, ...), custom_call_target="tpu_custom_call" | custom-call | tf_op jit(solution)/shard_map/blend/pallas_call | solution.py:694
Async XLA Ops:
  0.6 4.2 %copy-start.2 = (f32[32,4,32]{2,1,0:T(4,128)S(1)}, f32[32,4,32]{2,1,0:T(4,128)}, u32[]{:S(2)}) copy-start(f32[32,4,32]{2,1,0:T(4,128)} %own_ref.1) | copy-start | bytes 49156
  0.6 11.3 %copy-start.4 = (bf16[1152,3,288]{0,2,1:T(8,128)(2,1)S(1)}, bf16[1152,3,288]{0,2,1:T(8,128)(2,1)}, u32[]{:S(2)}) copy-start(bf16[1152,3,288]{0,2,1:T(8,128)(2,1)} %param.13) | copy-start | bytes 5971972
  0.7 11.3 %copy-start.5 = (f32[20,4,1152]{2,1,0:T(4,128)S(1)}, f32[20,4,1152]{2,1,0:T(4,128)}, u32[]{:S(2)}) copy-start(f32[20,4,1152]{2,1,0:T(4,128)} %modulations_ref.1) | copy-start | bytes 1105924
  0.7 11.3 %copy-start.1 = (bf16[2,2,120,288]{2,3,1,0:T(8,128)(2,1)S(1)}, bf16[2,2,120,288]{2,3,1,0:T(8,128)(2,1)}, u32[]{:S(2)}) copy-start(bf16[2,2,120,288]{2,3,1,0:T(8,128)(2,1)} %param.11) | copy-start | bytes 829444
  1.8 9.0 %collective-permute-start.3 = (bf16[72,1152]{1,0:T(8,128)(2,1)S(1)}, bf16[72,1152]{1,0:T(8,128)(2,1)S(1)}, u32[]{:S(2)}, u32[]{:S(2)}) collective-permute-start(bf16[72,1152]{1,0:T(8,128)(2,1)S(1)} %get-tuple-element.34), channel_id=1, source_target_pairs={{0,16},{16,0},{1,17},{17,1},{2,18},{18,2},{3,19},{19,3},{4,20},{20... | collective-permute-start | bytes 497672 | tf_op jit(solution)/shard_map/ppermute | solution.py:35
  4.8 6.1 %collective-permute-start = (f32[32,4,32]{2,1,0:T(4,128)S(1)}, f32[32,4,32]{2,1,0:T(4,128)S(1)}, u32[]{:S(2)}, u32[]{:S(2)}) collective-permute-start(f32[32,4,32]{2,1,0:T(4,128)S(1)} %copy-done.2), channel_id=1, source_target_pairs={{0,1},{1,0},{2,3},{3,2},{4,5},{5,4},{6,7},{7,6},{8,9},{9,8},{10,11... | collective-permute-start | bytes 49160 | tf_op jit(solution)/shard_map/ppermute | solution.py:31
  4.8 7.1 %collective-permute-start.1 = (f32[32,4,32]{2,1,0:T(4,128)S(1)}, f32[32,4,32]{2,1,0:T(4,128)S(1)}, u32[]{:S(2)}, u32[]{:S(2)}) collective-permute-start(f32[32,4,32]{2,1,0:T(4,128)S(1)} %copy-done.2), channel_id=1, source_target_pairs={{1,2},{2,1},{3,4},{4,3},{5,6},{6,5},{7,8},{8,7},{9,10},{10,9},{11,... | collective-permute-start | bytes 49160 | tf_op jit(solution)/shard_map/ppermute | solution.py:31
  10.8 5.4 %collective-permute-start.6 = (bf16[72,1152]{1,0:T(8,128)(2,1)S(1)}, bf16[72,1152]{1,0:T(8,128)(2,1)S(1)}, u32[]{:S(2)}, u32[]{:S(2)}) collective-permute-start(bf16[72,1152]{1,0:T(8,128)(2,1)S(1)} %collective-permute-done.3.weight_ref), channel_id=1, source_target_pairs={{0,2},{1,5},{2,0},{3,7},{4,6},{5,1},{6,4},{7,3},{8,10},{9,13},{10,... | collective-permute-start | bytes 497672 | tf_op jit(solution)/shard_map/ppermute | solution.py:41
  10.9 11.0 %collective-permute-start.4 = (bf16[72,1152]{1,0:T(8,128)(2,1)S(1)}, bf16[72,1152]{1,0:T(8,128)(2,1)S(1)}, u32[]{:S(2)}, u32[]{:S(2)}) collective-permute-start(bf16[72,1152]{1,0:T(8,128)(2,1)S(1)} %collective-permute-done.3.weight_ref), channel_id=1, source_target_pairs={{0,1},{1,0},{2,3},{3,2},{4,5},{5,4},{6,7},{7,6},{8,9},{9,8},{10,11... | collective-permute-start | bytes 497672 | tf_op jit(solution)/shard_map/ppermute | solution.py:41
  14.7 7.2 %collective-permute-start.2 = (bf16[144,512]{1,0:T(8,128)(2,1)S(1)}, bf16[144,512]{1,0:T(8,128)(2,1)S(1)}, u32[]{:S(2)}, u32[]{:S(2)}) collective-permute-start(bf16[144,512]{1,0:T(8,128)(2,1)S(1)} %get-tuple-element.33), channel_id=1, source_target_pairs={{0,16},{16,0},{1,17},{17,1},{2,18},{18,2},{3,19},{19,3},{4,20},{20... | collective-permute-start | bytes 442376 | tf_op jit(solution)/shard_map/ppermute | solution.py:35
  16.2 6.7 %collective-permute-start.7 = (bf16[72,1152]{1,0:T(8,128)(2,1)S(1)}, bf16[72,1152]{1,0:T(8,128)(2,1)S(1)}, u32[]{:S(2)}, u32[]{:S(2)}) collective-permute-start(bf16[72,1152]{1,0:T(8,128)(2,1)S(1)} %collective-permute-done.6.cross_ref), channel_id=1, source_target_pairs={{0,1},{1,0},{2,3},{3,2},{4,5},{5,4},{6,7},{7,6},{8,9},{9,8},{10,11... | collective-permute-start | bytes 497672 | tf_op jit(solution)/shard_map/ppermute | solution.py:41
  16.2 4.3 %copy-start = (bf16[288,1152]{1,0:T(8,128)(2,1)S(1)}, bf16[288,1152]{1,0:T(8,128)(2,1)}, u32[]{:S(2)}) copy-start(bf16[288,1152]{1,0:T(8,128)(2,1)} %own_weight_ref.1) | copy-start | bytes 1990660
  16.2 4.3 %copy-start.3 = (bf16[1152,16]{0,1:T(8,128)(2,1)S(1)}, bf16[1152,16]{0,1:T(8,128)(2,1)}, u32[]{:S(2)}) copy-start(bf16[1152,16]{0,1:T(8,128)(2,1)} %param.16) | copy-start | bytes 110596
  17.7 5.2 %collective-permute-start.5 = (bf16[144,256]{1,0:T(8,128)(2,1)S(1)}, bf16[144,256]{1,0:T(8,128)(2,1)S(1)}, u32[]{:S(2)}, u32[]{:S(2)}) collective-permute-start(bf16[144,256]{1,0:T(8,128)(2,1)S(1)} %get-tuple-element.35), channel_id=1, source_target_pairs={{0,16},{16,0},{1,17},{17,1},{2,18},{18,2},{3,19},{19,3},{4,20},{20... | collective-permute-start | bytes 221192 | tf_op jit(solution)/shard_map/ppermute | solution.py:35
  19.0 6.3 %collective-permute-start.9 = (bf16[144,256]{1,0:T(8,128)(2,1)S(1)}, bf16[144,256]{1,0:T(8,128)(2,1)S(1)}, u32[]{:S(2)}, u32[]{:S(2)}) collective-permute-start(bf16[144,256]{1,0:T(8,128)(2,1)S(1)} %get-tuple-element.40), channel_id=1, source_target_pairs={{0,16},{16,0},{1,17},{17,1},{2,18},{18,2},{3,19},{19,3},{4,20},{20... | collective-permute-start | bytes 221192 | tf_op jit(solution)/shard_map/ppermute | solution.py:35
  25.2 4.3 %collective-permute-start.8 = (f32[32,128]{1,0:T(8,128)S(1)}, f32[32,128]{1,0:T(8,128)S(1)}, u32[]{:S(2)}, u32[]{:S(2)}) collective-permute-start(f32[32,128]{1,0:T(8,128)S(1)} %get-tuple-element.38), channel_id=1, source_target_pairs={{0,1},{1,0},{2,3},{3,2},{4,5},{5,4},{6,7},{7,6},{8,9},{9,8},{10,11... | collective-permute-start | bytes 49160 | tf_op jit(solution)/shard_map/ppermute | solution.py:31
  26.3 5.9 %collective-permute-start.10 = (f32[32,128]{1,0:T(8,128)S(1)}, f32[32,128]{1,0:T(8,128)S(1)}, u32[]{:S(2)}, u32[]{:S(2)}) collective-permute-start(f32[32,128]{1,0:T(8,128)S(1)} %get-tuple-element.42), channel_id=1, source_target_pairs={{1,2},{2,1},{3,4},{4,3},{5,6},{6,5},{7,8},{8,7},{9,10},{10,9},{11,... | collective-permute-start | bytes 49160 | tf_op jit(solution)/shard_map/ppermute | solution.py:31
